TPU v7x, 32 devices: a whole 2x2x4 slice. The times are simulated.
32 devices in a mesh: dp: 16 (over z, y, core), head: 2 (over x).
Axes of the slice: x: 2, y: 2, z: 4, core: 2. Of those that a mesh axis runs over, the one named last changes fastest.
Arguments:
- tokens: bfloat16 [16, 256, 512], P('dp', 'head'), may hold values from -6 to 6
- lengths: int32 [16], P('dp'), may hold values from 32 to 256, as said below
- cotangent: bfloat16 [16, 256, 512], P('dp', 'head'), may hold values from -6 to 6
- glu_weight: bfloat16 [512, 1024], replicated, may hold values from -0.25 to 0.25
- glu_bias: bfloat16 [1024], replicated, may hold values from -1.75 to 1.75
- norm_gain: bfloat16 [4, 512], replicated, may hold values from 0.25 to 1.75
- norm_bias: bfloat16 [4, 512], replicated, may hold values from -1.75 to 1.75
- mid_gain: bfloat16 [2048], replicated, may hold values from 0.25 to 1.75
- mid_bias: bfloat16 [2048], replicated, may hold values from -1.75 to 1.75
- left_weight: bfloat16 [512, 2048], replicated, may hold values from -0.25 to 0.25
- left_bias: bfloat16 [2048], replicated, may hold values from -1.75 to 1.75
- conv_weight: bfloat16 [3, 512, 256], replicated, may hold values from -0.15625 to 0.15625
- conv_bias: bfloat16 [256], replicated, may hold values from -1.75 to 1.75
- depth_weight: bfloat16 [9, 2048], replicated, may hold values from -2 to 2
- point_weight: bfloat16 [2048, 256], replicated, may hold values from -0.125 to 0.125
- point_bias: bfloat16 [256], replicated, may hold values from -1.75 to 1.75
- qkv_weight: bfloat16 [512, 1536], replicated, may hold values from -0.375 to 0.375
- out_weight: bfloat16 [512, 512], replicated, may hold values from -1 to 1
- ffn_in_weight: bfloat16 [512, 2048], replicated, may hold values from -0.25 to 0.25
- ffn_in_bias: bfloat16 [2048], replicated, may hold values from -1.75 to 1.75
- ffn_out_weight: bfloat16 [2048, 512], replicated, may hold values from -0.125 to 0.125
- ffn_out_bias: bfloat16 [512], replicated, may hold values from -1.75 to 1.75
Outputs:
- out_tokens: bfloat16 [16, 256, 512], P('dp', 'head')
- grad_tokens: float32 [16, 256, 512], P('dp', 'head')
- grad_glu_weight: float32 [512, 1024], P('dp')
- grad_glu_bias: float32 [1024], P('dp')
- grad_norm_gain: float32 [4, 512], P(None, 'dp')
- grad_norm_bias: float32 [4, 512], P(None, 'dp')
- grad_mid_gain: float32 [2048], P('dp')
- grad_mid_bias: float32 [2048], P('dp')
- grad_left_weight: float32 [512, 2048], P('dp')
- grad_left_bias: float32 [2048], P('dp')
- grad_conv_weight: float32 [3, 512, 256], P(None, 'dp')
- grad_conv_bias: float32 [256], replicated
- grad_depth_weight: float32 [9, 2048], P(None, 'dp')
- grad_point_weight: float32 [2048, 256], P('dp')
- grad_point_bias: float32 [256], replicated
- grad_qkv_weight: float32 [512, 1536], P('dp')
- grad_out_weight: float32 [512, 512], P('dp')
- grad_ffn_in_weight: float32 [512, 2048], P('dp')
- grad_ffn_in_bias: float32 [2048], P('dp')
- grad_ffn_out_weight: float32 [2048, 512], P('dp')
- grad_ffn_out_bias: float32 [512], P('dp')
Inputs may be any that keep to these rules, and one draw needn't show every extreme that they name: `lengths`: counted from the start of the row; some row is full.
All inputs are finite; a program needn't handle non-finite values.
Results may differ from a plain program's by a relative error of at most 0.03.
The roundings to bfloat16 on the way count: a program that leaves them out, or rounds other values in their place, can miss the bound.
Values may be sent and summed in bfloat16 or wider, within the bound.
No kernel may reach another device: no remote copies, remote signals or barrier semaphores. Data moves between devices by JAX's collectives and lax.ppermute only.
A program may use at most 128 MiB of HBM per device.

v0:
```python
import jax
import jax.numpy as jnp
from jax import lax
from jax.sharding import PartitionSpec as P

HEAD_DIM = 64


EPSILON = 1e-06


def padded(cells, sides, width):
    for axis, dim in sides:
        count = lax.axis_size(axis)
        ends = count - 1
        head = lax.slice_in_dim(cells, 0, width, axis=dim)
        tail = lax.slice_in_dim(cells, cells.shape[dim] - width, cells.shape[dim], axis=dim)
        cells = jnp.concatenate(
            [
                lax.ppermute(tail, axis, [(i, (i + 1) % count) for i in range(ends)]),
                cells,
                lax.ppermute(head, axis, [((i + 1) % count, i) for i in range(ends)]),
            ],
            axis=dim,
        )
    return cells


def layer_norm(inputs, gain_vec, bias_vec):
    average = jnp.mean(inputs, axis=-1, keepdims=True)
    centred = inputs - average
    spread = jnp.mean(centred * centred, axis=-1, keepdims=True)
    return centred * lax.rsqrt(spread + EPSILON) * gain_vec + bias_vec


def project(inputs, weight):
    return jnp.dot(inputs, weight, preferred_element_type=jnp.float32)


def project_back(incoming, weight):
    return jnp.einsum("bte,de->btd", incoming, weight, preferred_element_type=jnp.float32)


def weight_grad(inputs, incoming):
    return jnp.einsum("btd,bte->de", inputs, incoming, preferred_element_type=jnp.float32)


def token_sum(incoming):
    return jnp.sum(incoming.astype(jnp.float32), axis=(0, 1))


def norm_back(inputs, gain_vec, bias_vec, incoming):
    unused, pullback = jax.vjp(layer_norm, inputs, gain_vec, bias_vec)
    return pullback(incoming)


def per_device(
    tokens,
    lengths,
    cotangent,
    glu_weight,
    glu_bias,
    norm_gain,
    norm_bias,
    mid_gain,
    mid_bias,
    left_weight,
    left_bias,
    conv_weight,
    conv_bias,
    depth_weight,
    point_weight,
    point_bias,
    qkv_weight,
    out_weight,
    ffn_in_weight,
    ffn_in_bias,
    ffn_out_weight,
    ffn_out_bias,
):
    row_count, part_len, width = tokens.shape
    groups = lax.axis_size("head")
    seq_len = part_len * groups
    local_width = width // groups
    local_heads = local_width // HEAD_DIM
    half_width = conv_weight.shape[2]
    ffn_width = left_weight.shape[1]
    scale = HEAD_DIM ** (-0.5)
    begin = lax.axis_index("head") * part_len
    places = begin + jnp.arange(part_len, dtype=jnp.int32)
    columns = (places[None, :] < lengths[:, None]).astype(jnp.float32)[:, :, None]
    keys_open = (jnp.arange(seq_len, dtype=jnp.int32)[None, :] < lengths[:, None])[:, None, None, :]
    gains = norm_gain.astype(jnp.float32)
    shifts = norm_bias.astype(jnp.float32)
    mid_gains = mid_gain.astype(jnp.float32)
    mid_shifts = mid_bias.astype(jnp.float32)
    taps = depth_weight.astype(jnp.float32)
    conv_flat = conv_weight.reshape(3 * width, half_width)
    stream_in = tokens.astype(jnp.float32)
    first_norm = layer_norm(stream_in, gains[0], shifts[0]).astype(jnp.bfloat16)
    joined = project(first_norm, glu_weight) + glu_bias.astype(jnp.float32)
    values_part = joined[..., :width]
    gate_part = jax.nn.sigmoid(joined[..., width:])
    after_glu = stream_in + values_part * gate_part
    second_norm = (layer_norm(after_glu, gains[1], shifts[1]) * columns).astype(jnp.bfloat16)
    left_pre = project(second_norm, left_weight) + left_bias.astype(jnp.float32)
    rimmed_second = padded(second_norm, (("head", 1),), 1)
    window = jnp.concatenate(
        [rimmed_second[:, :-2], rimmed_second[:, 1:-1], rimmed_second[:, 2:]], axis=-1
    )
    right_pre = project(window, conv_flat) + conv_bias.astype(jnp.float32)
    combined = jnp.where(left_pre > 0.0, left_pre, 0.0) + jnp.pad(
        jnp.where(right_pre > 0.0, right_pre, 0.0), ((0, 0), (0, 0), (0, ffn_width - half_width))
    )
    third_norm = layer_norm(combined, mid_gains, mid_shifts) * columns
    rimmed_third = padded(third_norm.astype(jnp.bfloat16), (("head", 1),), 4).astype(
        third_norm.dtype
    )
    depthwise = rimmed_third[:, 0:part_len] * taps[0]
    for offset in range(1, 9):
        depthwise = depthwise + rimmed_third[:, offset : offset + part_len] * taps[offset]
    depth_low = depthwise.astype(jnp.bfloat16)
    separable = project(depth_low, point_weight) + point_bias.astype(jnp.float32)
    after_conv = after_glu + jnp.pad(separable, ((0, 0), (0, 0), (0, width - half_width)))
    fourth_norm = layer_norm(after_conv, gains[2], shifts[2]).astype(jnp.bfloat16)
    packed = (
        project(fourth_norm, qkv_weight).astype(jnp.bfloat16).reshape(row_count, part_len, 3, width)
    )
    spread_out = lax.all_to_all(packed, "head", split_axis=3, concat_axis=1, tiled=True)
    shaped = spread_out.reshape(row_count, seq_len, 3, local_heads, HEAD_DIM)
    queries = shaped[:, :, 0]
    keyset = shaped[:, :, 1]
    valueset = shaped[:, :, 2]

    def masked_scores():
        raw_scores = (
            jnp.einsum("bqhd,bkhd->bhqk", queries, keyset, preferred_element_type=jnp.float32)
            * scale
        )
        return jnp.where(keys_open, raw_scores, -1000000000.0)

    scores = masked_scores()
    largest = jnp.max(scores, axis=-1, keepdims=True)
    raised = jnp.exp(scores - largest)
    totals = jnp.sum(raised, axis=-1, keepdims=True)
    log_total = largest + jnp.log(totals)
    context = jnp.einsum(
        "bhqk,bkhd->bqhd",
        (raised / totals).astype(jnp.bfloat16),
        valueset,
        preferred_element_type=jnp.float32,
    )
    context = context.astype(jnp.bfloat16).reshape(row_count, seq_len, local_width)
    returned = lax.all_to_all(context, "head", split_axis=1, concat_axis=2, tiled=True)
    after_attn = after_conv + project(returned, out_weight)
    fifth_norm = layer_norm(after_attn, gains[3], shifts[3]).astype(jnp.bfloat16)
    hidden_pre = project(fifth_norm, ffn_in_weight) + ffn_in_bias.astype(jnp.float32)
    hidden = jnp.where(hidden_pre > 0.0, hidden_pre, 0.0).astype(jnp.bfloat16)
    block_out = after_attn + project(hidden, ffn_out_weight) + ffn_out_bias.astype(jnp.float32)
    grad_stream = cotangent.astype(jnp.float32)
    g_ffn_out = weight_grad(hidden, cotangent)
    g_ffn_out_bias = token_sum(cotangent)
    d_hidden = jnp.where(hidden_pre > 0.0, project_back(cotangent, ffn_out_weight), 0.0).astype(
        jnp.bfloat16
    )
    g_ffn_in = weight_grad(fifth_norm, d_hidden)
    g_ffn_in_bias = token_sum(d_hidden)
    d_fifth, gain_three, shift_three = norm_back(
        after_attn, gains[3], shifts[3], project_back(d_hidden, ffn_in_weight)
    )
    d_after_attn = grad_stream + d_fifth
    d_attn = d_after_attn.astype(jnp.bfloat16)
    g_out = weight_grad(returned, d_attn)
    d_returned = project_back(d_attn, out_weight).astype(jnp.bfloat16)
    d_context = lax.all_to_all(d_returned, "head", split_axis=2, concat_axis=1, tiled=True)
    d_context = d_context.reshape(row_count, seq_len, local_heads, HEAD_DIM)
    probs = jnp.exp(masked_scores() - log_total)
    d_values = jnp.einsum(
        "bhqk,bqhd->bkhd", probs.astype(jnp.bfloat16), d_context, preferred_element_type=jnp.float32
    )
    d_probs = jnp.einsum("bqhd,bkhd->bhqk", d_context, valueset, preferred_element_type=jnp.float32)
    delta = jnp.sum(d_probs * probs, axis=-1, keepdims=True)
    d_scores = (probs * (d_probs - delta)).astype(jnp.bfloat16)
    d_queries = (
        jnp.einsum("bhqk,bkhd->bqhd", d_scores, keyset, preferred_element_type=jnp.float32) * scale
    )
    d_keys = (
        jnp.einsum("bhqk,bqhd->bkhd", d_scores, queries, preferred_element_type=jnp.float32) * scale
    )
    d_spread = jnp.stack([d_queries, d_keys, d_values], axis=2).astype(jnp.bfloat16)
    d_spread = d_spread.reshape(row_count, seq_len, 3, local_width)
    d_packed = lax.all_to_all(d_spread, "head", split_axis=1, concat_axis=3, tiled=True)
    d_packed = d_packed.reshape(row_count, part_len, 3 * width)
    g_qkv = weight_grad(fourth_norm, d_packed)
    upper = (g_ffn_out, g_ffn_out_bias, g_ffn_in, g_ffn_in_bias, g_out, g_qkv)
    d_fourth, gain_two, shift_two = norm_back(
        after_conv, gains[2], shifts[2], project_back(d_packed, qkv_weight)
    )
    d_after_conv = d_after_attn + d_fourth
    d_sep = d_after_conv[..., :half_width].astype(jnp.bfloat16)
    g_point = weight_grad(depth_low, d_sep)
    g_point_bias = token_sum(d_sep)
    d_depth = project_back(d_sep, point_weight)
    g_depth = jnp.stack(
        [
            jnp.sum(d_depth * rimmed_third[:, offset : offset + part_len], axis=(0, 1))
            for offset in range(9)
        ]
    )
    d_rimmed = padded(d_depth.astype(jnp.bfloat16), (("head", 1),), 4).astype(d_depth.dtype)
    d_third = d_rimmed[:, 8 : 8 + part_len] * taps[0]
    for offset in range(1, 9):
        d_third = d_third + d_rimmed[:, 8 - offset : 8 - offset + part_len] * taps[offset]
    d_third = d_third * columns
    d_combined, g_mid_gain, g_mid_bias = norm_back(combined, mid_gains, mid_shifts, d_third)
    d_left = jnp.where(left_pre > 0.0, d_combined, 0.0).astype(jnp.bfloat16)
    d_right = jnp.where(right_pre > 0.0, d_combined[..., :half_width], 0.0).astype(jnp.bfloat16)
    g_left = weight_grad(second_norm, d_left)
    g_left_bias = token_sum(d_left)
    g_conv = weight_grad(window, d_right).reshape(3, width, half_width)
    g_conv_bias = token_sum(d_right)
    d_window = project_back(d_right, conv_flat)
    side_taps = jnp.stack([d_window[..., :width], d_window[..., 2 * width :]], axis=0)
    side_rimmed = padded(side_taps.astype(jnp.bfloat16), (("head", 2),), 1).astype(side_taps.dtype)
    d_second = project_back(d_left, left_weight) + d_window[..., width : 2 * width]
    d_second = d_second + side_rimmed[0][:, 2:] + side_rimmed[1][:, :-2]
    d_second = d_second * columns
    d_norm_one, gain_one, shift_one = norm_back(after_glu, gains[1], shifts[1], d_second)
    d_after_glu = d_after_conv + d_norm_one
    d_values_part = d_after_glu * gate_part
    d_gate_part = d_after_glu * values_part * gate_part * (1.0 - gate_part)
    d_joined = jnp.concatenate([d_values_part, d_gate_part], axis=-1).astype(jnp.bfloat16)
    g_glu = weight_grad(first_norm, d_joined)
    g_glu_bias = token_sum(d_joined)
    d_norm_zero, gain_zero, shift_zero = norm_back(
        stream_in, gains[0], shifts[0], project_back(d_joined, glu_weight)
    )
    grad_input = d_after_glu + d_norm_zero
    g_gains = jnp.stack([gain_zero, gain_one, gain_two, gain_three])
    g_shifts = jnp.stack([shift_zero, shift_one, shift_two, shift_three])
    bias_totals = lax.psum((g_conv_bias, g_point_bias), ("dp", "head"))
    summed = (
        lax.psum_scatter(upper[0], "dp", scatter_dimension=0, tiled=True),
        lax.psum_scatter(upper[1], "dp", scatter_dimension=0, tiled=True),
        lax.psum_scatter(upper[2], "dp", scatter_dimension=0, tiled=True),
        lax.psum_scatter(upper[3], "dp", scatter_dimension=0, tiled=True),
        lax.psum_scatter(upper[4], "dp", scatter_dimension=0, tiled=True),
        lax.psum_scatter(upper[5], "dp", scatter_dimension=0, tiled=True),
        lax.psum_scatter(g_glu, "dp", scatter_dimension=0, tiled=True),
        lax.psum_scatter(g_glu_bias, "dp", scatter_dimension=0, tiled=True),
        lax.psum_scatter(g_gains, "dp", scatter_dimension=1, tiled=True),
        lax.psum_scatter(g_shifts, "dp", scatter_dimension=1, tiled=True),
        lax.psum_scatter(g_mid_gain, "dp", scatter_dimension=0, tiled=True),
        lax.psum_scatter(g_mid_bias, "dp", scatter_dimension=0, tiled=True),
        lax.psum_scatter(g_left, "dp", scatter_dimension=0, tiled=True),
        lax.psum_scatter(g_left_bias, "dp", scatter_dimension=0, tiled=True),
        lax.psum_scatter(g_conv, "dp", scatter_dimension=1, tiled=True),
        lax.psum_scatter(g_depth, "dp", scatter_dimension=1, tiled=True),
        lax.psum_scatter(g_point, "dp", scatter_dimension=0, tiled=True),
    )
    final = (
        lax.psum(summed[0].astype(jnp.bfloat16), "head").astype(jnp.float32),
        lax.psum(summed[1].astype(jnp.bfloat16), "head").astype(jnp.float32),
        lax.psum(summed[2].astype(jnp.bfloat16), "head").astype(jnp.float32),
        lax.psum(summed[3].astype(jnp.bfloat16), "head").astype(jnp.float32),
        lax.psum(summed[4].astype(jnp.bfloat16), "head").astype(jnp.float32),
        lax.psum(summed[5].astype(jnp.bfloat16), "head").astype(jnp.float32),
        lax.psum(summed[6].astype(jnp.bfloat16), "head").astype(jnp.float32),
        lax.psum(summed[7].astype(jnp.bfloat16), "head").astype(jnp.float32),
        lax.psum(summed[8].astype(jnp.bfloat16), "head").astype(jnp.float32),
        lax.psum(summed[9].astype(jnp.bfloat16), "head").astype(jnp.float32),
        lax.psum(summed[10].astype(jnp.bfloat16), "head").astype(jnp.float32),
        lax.psum(summed[11].astype(jnp.bfloat16), "head").astype(jnp.float32),
        lax.psum(summed[12].astype(jnp.bfloat16), "head").astype(jnp.float32),
        lax.psum(summed[13].astype(jnp.bfloat16), "head").astype(jnp.float32),
        lax.psum(summed[14].astype(jnp.bfloat16), "head").astype(jnp.float32),
        lax.psum(summed[15].astype(jnp.bfloat16), "head").astype(jnp.float32),
        lax.psum(summed[16].astype(jnp.bfloat16), "head").astype(jnp.float32),
    )
    return (
        block_out.astype(jnp.bfloat16),
        grad_input,
        final[6],
        final[7],
        final[8],
        final[9],
        final[10],
        final[11],
        final[12],
        final[13],
        final[14],
        bias_totals[0],
        final[15],
        final[16],
        bias_totals[1],
        final[5],
        final[4],
        final[2],
        final[3],
        final[0],
        final[1],
    )


def solution(mesh):
    return jax.shard_map(
        per_device,
        mesh=mesh,
        in_specs=(
            P("dp", "head", None),
            P("dp"),
            P("dp", "head", None),
            P(),
            P(),
            P(),
            P(),
            P(),
            P(),
            P(),
            P(),
            P(),
            P(),
            P(),
            P(),
            P(),
            P(),
            P(),
            P(),
            P(),
            P(),
            P(),
        ),
        out_specs=(
            P("dp", "head", None),
            P("dp", "head", None),
            P("dp", None),
            P("dp"),
            P(None, "dp"),
            P(None, "dp"),
            P("dp"),
            P("dp"),
            P("dp", None),
            P("dp"),
            P(None, "dp", None),
            P(),
            P(None, "dp"),
            P("dp", None),
            P(),
            P("dp", None),
            P("dp", None),
            P("dp", None),
            P("dp"),
            P("dp", None),
            P("dp"),
        ),
        check_vma=False,
    )
```

profile of v0, /device:TPU:0, one launch (start us, length us, event | category | flops | bytes accessed | tf_op | source)
XLA Modules:
  0.0 969.6 jit_solution(5460570614094923607)
XLA Ops:
  17.2 5.0 collective-permute-start
  23.6 4.0 collective-permute-done.1
  33.2 4.1 collective-permute-done.3
  45.6 4.2 all-to-all-start
  49.8 6.7 all-to-all-done
  69.6 4.0 all-to-all-start.1
  73.7 4.5 all-to-all-done.1
  94.0 3.0 reduce.42
  98.6 4.0 all-to-all-start.2
  102.8 4.3 all-to-all-done.2
  124.4 9.0 all_to_all.60
  136.2 3.0 fusion.65
  153.7 3.3 multiply_reduce_fusion
  159.6 3.8 collective-permute-start.6
  164.8 4.2 collective-permute-done.7
  185.3 2.7 fusion.42
  193.5 2.8 fusion.106
  197.5 3.6 fusion.71
  201.1 3.8 fusion.39
  209.2 58.8 %all-reduce.9 = (bf16[1024]{0:T(1024)(128)(2,1)}, bf16[2048]{0:T(1024)(128)(2,1)}, bf16[2048]{0:T(1024)(128)(2,1)}, bf16[2048]{0:T(1024)(128)(2,1)}, bf16[2048]{0:T(1024)(128)(2,1)}, /*index=5*/bf16[512]{0:T(512)(128)(2,1)}) all-reduce(f32[1024]{0:T(1024)S(1)} %convert_reduce_fusion.2, ...), channel_id=3, replica_groups=mesh['dp'=16,'head'=2] {'dp'}, use_global_device_ids=true, to_apply=%region_26.27.clone | all-reduce | flops 9728 | bytes 58368
  277.0 10.3 %reduce-scatter.34.cloned.1.call-done = f32[32,4]{1,0:T(8,128)} async-done(((f32[512,4]{1,0:T(8,128)}), f32[32,4]{1,0:T(8,128)}) %reduce-scatter.34.cloned.1.call-update) | async-done | bytes 528
  288.6 53.8 %reduce-scatter.22.cloned.1.call-done = f32[9,128]{1,0:T(8,128)} async-done(((f32[9,2048]{1,0:T(8,128)}), f32[9,128]{1,0:T(8,128)}) %reduce-scatter.22.cloned.1.call-update) | async-done | bytes 4624 | tf_op jit(solution)/shard_map/reduce_scatter | solution.py:258
  343.7 59.1 %reduce-scatter.28.cloned.1.call-done = f32[32,512]{1,0:T(8,128)} async-done(((f32[512,512]{1,0:T(8,128)}), f32[32,512]{1,0:T(8,128)}) %reduce-scatter.28.cloned.1.call-update) | async-done | bytes 65552 | tf_op jit(solution)/shard_map/reduce_scatter | solution.py:247
  404.2 60.5 %reduce-scatter.20.cloned.1.call-done = f32[3,32,256]{2,1,0:T(8,128)} async-done(((f32[3,512,256]{2,1,0:T(8,128)}), f32[3,32,256]{2,1,0:T(8,128)}) %reduce-scatter.20.cloned.1.call-update) | async-done | bytes 98320 | tf_op jit(solution)/shard_map/reduce_scatter | solution.py:257
  467.0 62.3 %reduce-scatter.24.cloned.1.call-done = f32[128,256]{1,0:T(8,128)} async-done(((f32[2048,256]{1,0:T(8,128)}), f32[128,256]{1,0:T(8,128)}) %reduce-scatter.24.cloned.1.call-update) | async-done | bytes 131088 | tf_op jit(solution)/shard_map/reduce_scatter | solution.py:259
  530.9 62.8 %reduce-scatter.16.cloned.1.call-done = f32[32,1024]{1,0:T(8,128)} async-done(((f32[512,1024]{1,0:T(8,128)}), f32[32,1024]{1,0:T(8,128)}) %reduce-scatter.16.cloned.1.call-update) | async-done | bytes 131088 | tf_op jit(solution)/shard_map/reduce_scatter | solution.py:249
  595.2 68.0 %reduce-scatter.26.cloned.1.call-done = f32[32,1536]{1,0:T(8,128)} async-done(((f32[512,1536]{1,0:T(8,128)}), f32[32,1536]{1,0:T(8,128)}) %reduce-scatter.26.cloned.1.call-update) | async-done | bytes 196624 | tf_op jit(solution)/shard_map/reduce_scatter | solution.py:248
  664.8 74.4 %reduce-scatter.30.cloned.1.call-done = f32[32,2048]{1,0:T(8,128)} async-done(((f32[512,2048]{1,0:T(8,128)}), f32[32,2048]{1,0:T(8,128)}) %reduce-scatter.30.cloned.1.call-update) | async-done | bytes 262160 | tf_op jit(solution)/shard_map/reduce_scatter | solution.py:245
  740.8 73.6 %reduce-scatter.32.cloned.1.call-done = f32[128,512]{1,0:T(8,128)} async-done(((f32[2048,512]{1,0:T(8,128)}), f32[128,512]{1,0:T(8,128)}) %reduce-scatter.32.cloned.1.call-update) | async-done | bytes 262160 | tf_op jit(solution)/shard_map/reduce_scatter | solution.py:243
  816.0 74.6 %reduce-scatter.18.cloned.1.call-done = f32[32,2048]{1,0:T(8,128)} async-done(((f32[512,2048]{1,0:T(8,128)}), f32[32,2048]{1,0:T(8,128)}) %reduce-scatter.18.cloned.1.call-update) | async-done | bytes 262160 | tf_op jit(solution)/shard_map/reduce_scatter | solution.py:255
  894.3 40.0 %all-reduce.8 = (f32[256]{0:T(256)}, f32[256]{0:T(256)}) all-reduce(f32[256]{0:T(256)} %get-tuple-element.67, f32[256]{0:T(256)S(1)} %convert_reduce_fusion.5), channel_id=1, replica_groups=mesh['dp'=16,'head'=2] {'dp','head'}, use_global_device_ids=true, to_apply=%region_54.55 | all-reduce | flops 512 | bytes 4096 | tf_op jit(solution)/shard_map/psum | solution.py:241
  950.2 3.4 all-reduce.17.cloned.1.call-done
  (455 shorter events, 169.7 us)
Async XLA Ops:
  7.2 78.2 %copy-start = (bf16[2048,512]{1,0:T(8,128)(2,1)S(1)}, bf16[2048,512]{1,0:T(8,128)(2,1)}, u32[]{:S(2)}) copy-start(bf16[2048,512]{1,0:T(8,128)(2,1)} %param.42) | copy-start | bytes 6291460
  7.3 20.4 %copy-start.51 = (bf16[3,512,256]{2,1,0:T(8,128)(2,1)S(1)}, bf16[3,512,256]{2,1,0:T(8,128)(2,1)}, u32[]{:S(2)}) copy-start(bf16[3,512,256]{2,1,0:T(8,128)(2,1)} %param.33) | copy-start | bytes 2359300
  16.1 22.9 %copy-start.10 = (f32[1,128,512]{2,1,0:T(8,128)}, f32[1,128,512]{2,1,0:T(8,128)S(1)}, u32[]{:S(2)}) copy-start(f32[1,128,512]{2,1,0:T(8,128)S(1)} %get-tuple-element.86) | copy-start | bytes 786436
  17.2 6.4 collective-permute-start
  22.2 5.5 collective-permute-start.1
  30.0 3.1 collective-permute-start.2
  31.7 5.6 collective-permute-start.3
  39.5 99.6 %copy-start.85 = (f32[128]{0:T(128)}, f32[128]{0:T(128)S(1)}, u32[]{:S(2)}) copy-start(f32[128]{0:T(128)S(1)} %broadcast_multiply_fusion.2) | copy-start | bytes 1540
  39.7 99.5 %copy-start.96 = (f32[128]{0:T(128)}, f32[128]{0:T(128)S(1)}, u32[]{:S(2)}) copy-start(f32[128]{0:T(128)S(1)} %fusion.96) | copy-start | bytes 1540
  45.6 10.9 %all-to-all-start = ((bf16[1,128,3,512]{1,2,0,3:T(4,128)(2,1)}), bf16[1,128,3,512]{1,2,0,3:T(4,128)(2,1)}, u32[]{:S(2)}, u32[]{:S(2)}) async-start(bf16[1,128,3,512]{1,2,0,3:T(4,128)(2,1)} %copy.95), calls=%async_computation | async-start | bytes 1048576 | tf_op jit(solution)/shard_map/all_to_all | solution.py:129
  64.4 18.9 %copy-start.76 = (f32[1,512]{1,0:T(1,128)S(1)}, f32[1,512]{1,0:T(1,128)}, u32[]{:S(2)}) copy-start(f32[1,512]{1,0:T(1,128)} %get-tuple-element.114) | copy-start | bytes 6148
  69.6 8.6 all-to-all-start.1
  98.6 8.6 all-to-all-start.2
  102.6 173.1 %reduce-scatter.36.cloned.1.call-start = ((), (), s32[]{:S(2)}) async-start(), calls=%async_computation.25 | async-start | bytes 278528
  144.0 7.0 collective-permute-start.4
  146.5 5.9 collective-permute-start.5
  159.6 5.1 collective-permute-start.6
  163.4 5.5 collective-permute-start.7
  173.5 113.7 %reduce-scatter.34.cloned.1.call-start = ((), (), s32[]{:S(2)}) async-start(), calls=%async_computation.24 | async-start | bytes 278528
  175.9 166.5 %reduce-scatter.22.cloned.1.call-start = ((), (), s32[]{:S(2)}) async-start(), calls=%async_computation.18 | async-start | bytes 139264 | tf_op jit(solution)/shard_map/reduce_scatter | solution.py:258
  178.2 224.6 %reduce-scatter.28.cloned.1.call-start = ((), (), s32[]{:S(2)}) async-start(), calls=%async_computation.21 | async-start | bytes 1114112 | tf_op jit(solution)/shard_map/reduce_scatter | solution.py:247
  179.6 285.2 %reduce-scatter.20.cloned.1.call-start = ((), (), s32[]{:S(2)}) async-start(), calls=%async_computation.17 | async-start | bytes 1671168 | tf_op jit(solution)/shard_map/reduce_scatter | solution.py:257
  185.0 344.4 %reduce-scatter.24.cloned.1.call-start = ((), (), s32[]{:S(2)}) async-start(), calls=%async_computation.19 | async-start | bytes 2228224 | tf_op jit(solution)/shard_map/reduce_scatter | solution.py:259
  188.0 405.7 %reduce-scatter.16.cloned.1.call-start = ((), (), s32[]{:S(2)}) async-start(), calls=%async_computation.15 | async-start | bytes 2228224 | tf_op jit(solution)/shard_map/reduce_scatter | solution.py:249
  190.0 473.2 %reduce-scatter.26.cloned.1.call-start = ((), (), s32[]{:S(2)}) async-start(), calls=%async_computation.20 | async-start | bytes 3342336 | tf_op jit(solution)/shard_map/reduce_scatter | solution.py:248
  192.4 546.7 %reduce-scatter.30.cloned.1.call-start = ((), (), s32[]{:S(2)}) async-start(), calls=%async_computation.22 | async-start | bytes 4456448 | tf_op jit(solution)/shard_map/reduce_scatter | solution.py:245
  196.3 618.1 %reduce-scatter.32.cloned.1.call-start = ((), (), s32[]{:S(2)}) async-start(), calls=%async_computation.23 | async-start | bytes 4456448 | tf_op jit(solution)/shard_map/reduce_scatter | solution.py:243
  201.1 689.5 %reduce-scatter.18.cloned.1.call-start = ((), (), s32[]{:S(2)}) async-start(), calls=%async_computation.16 | async-start | bytes 4456448 | tf_op jit(solution)/shard_map/reduce_scatter | solution.py:255
  205.0 731.8 %all-reduce.15.cloned.1.call-start = ((), (), s32[]{:S(2)}) async-start(), calls=%async_computation.26 | async-start | bytes 182272 | tf_op jit(solution)/shard_map/psum | solution.py:269
  466.3 487.3 %all-reduce.17.cloned.1.call-start = ((), (), s32[]{:S(2)}) async-start(), calls=%async_computation.27 | async-start | bytes 1245184 | tf_op jit(solution)/shard_map/psum | solution.py:268
  892.2 42.7 %copy-start.73 = (f32[128]{0:T(128)S(1)}, f32[128]{0:T(128)}, u32[]{:S(2)}) copy-start(f32[128]{0:T(128)} %copy-done.71) | copy-start | bytes 1540
  892.2 42.7 %copy-start.82 = (f32[128]{0:T(128)S(1)}, f32[128]{0:T(128)}, u32[]{:S(2)}) copy-start(f32[128]{0:T(128)} %copy-done.80) | copy-start | bytes 1540
  (117 other events, 628.6 us)
Sparse Core Ops, SparseCore 0:
  173.7 55.6 reduce-scatter.35
  232.9 54.3 reduce-scatter.33
  291.2 51.1 reduce-scatter.21
  346.3 56.4 reduce-scatter.27
  406.3 58.3 reduce-scatter.19
  468.8 60.5 reduce-scatter.23
  533.1 60.5 reduce-scatter.15
  598.0 65.1 reduce-scatter.25
  667.6 71.5 reduce-scatter.29
  742.9 71.4 reduce-scatter.31
  818.7 71.8 reduce-scatter.17
  895.1 21.7 all-reduce.14
  921.3 32.2 all-reduce.16
where the time goes:
time: 973 us; the launch traced here: 970 us
  waiting for transfers between devices  632 us (65%)
  blocking collectives  108 us (11%)
  other arithmetic  68.7 us (7%)
  local copies, waits for them, and re-layouts  62.2 us (6%)
  matrix products  48.9 us (5%)
  starting transfers between devices  31.3 us (3%)
  between operations  18.4 us (2%)
    reduce_scatter x1, waiting for transfers between devices, per_device(): lax.psum_scatter(g_left, 'dp', scatter_dimension=0, tiled=True)  74.6 us
    reduce_scatter x1, waiting for transfers between devices, per_device(): lax.psum_scatter(upper[2], 'dp', scatter_dimension=0, tiled=True)  74.4 us
    reduce_scatter x1, waiting for transfers between devices, per_device(): lax.psum_scatter(upper[0], 'dp', scatter_dimension=0, tiled=True)  73.6 us
    reduce_scatter x1, waiting for transfers between devices, per_device(): lax.psum_scatter(upper[5], 'dp', scatter_dimension=0, tiled=True)  68 us
    reduce_scatter x1, waiting for transfers between devices, per_device(): lax.psum_scatter(g_glu, 'dp', scatter_dimension=0, tiled=True)  62.8 us
    reduce_scatter x1, waiting for transfers between devices, per_device(): lax.psum_scatter(g_point, 'dp', scatter_dimension=0, tiled=True)  62.3 us
    reduce_scatter x1, waiting for transfers between devices, per_device(): lax.psum_scatter(g_conv, 'dp', scatter_dimension=1, tiled=True)  60.5 us
    reduce_scatter x1, waiting for transfers between devices, per_device(): lax.psum_scatter(upper[4], 'dp', scatter_dimension=0, tiled=True)  59.1 us
  transfers between devices with their start and end apart: 24, of which 18 were waited for; matrix products, arithmetic and copies ran while one was open for 8% of the time, Pallas kernels for 0%

commit v1 on v0

v1 whole, which is shorter than its diff:
```python
import jax
import jax.numpy as jnp
from jax import lax
from jax.sharding import PartitionSpec as P

HEAD_DIM = 64


EPSILON = 1e-06


def layer_norm(inputs, gain_vec, bias_vec):
    average = jnp.mean(inputs, axis=-1, keepdims=True)
    centred = inputs - average
    spread = jnp.mean(centred * centred, axis=-1, keepdims=True)
    return centred * lax.rsqrt(spread + EPSILON) * gain_vec + bias_vec


def project(inputs, weight):
    return jnp.dot(inputs, weight, preferred_element_type=jnp.float32)


def project_back(incoming, weight):
    return jnp.einsum("te,de->td", incoming, weight, preferred_element_type=jnp.float32)


def weight_grad(inputs, incoming):
    return jnp.einsum("td,te->de", inputs, incoming, preferred_element_type=jnp.float32).astype(
        jnp.bfloat16
    )


def token_sum(incoming):
    return jnp.sum(incoming.astype(jnp.float32), axis=0)


def norm_back(inputs, gain_vec, bias_vec, incoming):
    unused, pullback = jax.vjp(layer_norm, inputs, gain_vec, bias_vec)
    return pullback(incoming)


def shifted(cells, offset):
    if offset == 0:
        return cells
    blank = jnp.zeros_like(cells[: abs(offset)])
    if offset > 0:
        return jnp.concatenate([cells[offset:], blank], axis=0)
    return jnp.concatenate([blank, cells[:offset]], axis=0)


def per_device(
    tokens,
    lengths,
    cotangent,
    glu_weight,
    glu_bias,
    norm_gain,
    norm_bias,
    mid_gain,
    mid_bias,
    left_weight,
    left_bias,
    conv_weight,
    conv_bias,
    depth_weight,
    point_weight,
    point_bias,
    qkv_weight,
    out_weight,
    ffn_in_weight,
    ffn_in_bias,
    ffn_out_weight,
    ffn_out_bias,
):
    row_count, part_len, width = tokens.shape
    assert row_count == 1 and lax.axis_size("head") == 2
    seq_len = part_len * 2
    shards = lax.axis_size("dp")
    heads = width // HEAD_DIM
    half_width = conv_weight.shape[2]
    ffn_width = left_weight.shape[1]
    scale = HEAD_DIM ** (-0.5)
    side = lax.axis_index("head")
    swap = [(0, 1), (1, 0)]
    bf16 = jnp.bfloat16

    def whole_row(part):
        other = lax.ppermute(part, "head", swap)
        return jnp.where(
            side == 0,
            jnp.concatenate([part, other], axis=0),
            jnp.concatenate([other, part], axis=0),
        )

    def own_tokens(full):
        return lax.dynamic_slice_in_dim(full, side * part_len, part_len, axis=0)[None]

    def own_columns(full):
        count = full.shape[1] // 2
        return lax.dynamic_slice_in_dim(full, side * count, count, axis=1)

    tokens = whole_row(tokens[0])
    cotangent = whole_row(cotangent[0])
    keys_valid = jnp.arange(seq_len, dtype=jnp.int32) < lengths[0]
    columns = keys_valid.astype(jnp.float32)[:, None]
    keys_open = keys_valid[None, None, :]
    gains = norm_gain.astype(jnp.float32)
    shifts = norm_bias.astype(jnp.float32)
    mid_gains = mid_gain.astype(jnp.float32)
    mid_shifts = mid_bias.astype(jnp.float32)
    taps = depth_weight.astype(jnp.float32)
    conv_flat = conv_weight.reshape(3 * width, half_width)
    stream_in = tokens.astype(jnp.float32)
    first_norm = layer_norm(stream_in, gains[0], shifts[0]).astype(bf16)
    joined = project(first_norm, glu_weight) + glu_bias.astype(jnp.float32)
    values_part = joined[..., :width]
    gate_part = jax.nn.sigmoid(joined[..., width:])
    after_glu = stream_in + values_part * gate_part
    second_norm = (layer_norm(after_glu, gains[1], shifts[1]) * columns).astype(bf16)
    left_pre = project(second_norm, left_weight) + left_bias.astype(jnp.float32)
    window = jnp.concatenate([shifted(second_norm, -1), second_norm, shifted(second_norm, 1)], axis=-1)
    right_pre = project(window, conv_flat) + conv_bias.astype(jnp.float32)
    combined = jnp.where(left_pre > 0.0, left_pre, 0.0) + jnp.pad(
        jnp.where(right_pre > 0.0, right_pre, 0.0), ((0, 0), (0, ffn_width - half_width))
    )
    third_norm = layer_norm(combined, mid_gains, mid_shifts) * columns
    depthwise = shifted(third_norm, -4) * taps[0]
    for offset in range(1, 9):
        depthwise = depthwise + shifted(third_norm, offset - 4) * taps[offset]
    depth_low = depthwise.astype(bf16)
    separable = project(depth_low, point_weight) + point_bias.astype(jnp.float32)
    after_conv = after_glu + jnp.pad(separable, ((0, 0), (0, width - half_width)))
    fourth_norm = layer_norm(after_conv, gains[2], shifts[2]).astype(bf16)
    packed = project(fourth_norm, qkv_weight).astype(bf16)
    shaped = packed.reshape(seq_len, 3, heads, HEAD_DIM)
    queries = shaped[:, 0]
    keyset = shaped[:, 1]
    valueset = shaped[:, 2]
    scores = jnp.einsum("qhd,khd->hqk", queries, keyset, preferred_element_type=jnp.float32) * scale
    scores = jnp.where(keys_open, scores, -1000000000.0)
    largest = jnp.max(scores, axis=-1, keepdims=True)
    raised = jnp.exp(scores - largest)
    probs = raised / jnp.sum(raised, axis=-1, keepdims=True)
    probs_low = probs.astype(bf16)
    context = jnp.einsum("hqk,khd->qhd", probs_low, valueset, preferred_element_type=jnp.float32)
    context = context.astype(bf16).reshape(seq_len, width)
    after_attn = after_conv + project(context, out_weight)
    fifth_norm = layer_norm(after_attn, gains[3], shifts[3]).astype(bf16)
    hidden_pre = project(fifth_norm, ffn_in_weight) + ffn_in_bias.astype(jnp.float32)
    hidden = jnp.where(hidden_pre > 0.0, hidden_pre, 0.0).astype(bf16)
    block_out = own_tokens(after_attn) + project(own_tokens(hidden)[0], ffn_out_weight)[None] + ffn_out_bias.astype(jnp.float32)

    grad_stream = cotangent.astype(jnp.float32)
    g_ffn_out = weight_grad(hidden, own_columns(cotangent))
    g_ffn_out_bias = token_sum(cotangent)
    d_hidden = jnp.where(hidden_pre > 0.0, project_back(cotangent, ffn_out_weight), 0.0).astype(bf16)
    g_ffn_in = weight_grad(fifth_norm, own_columns(d_hidden))
    g_ffn_in_bias = token_sum(d_hidden)
    d_fifth, gain_three, shift_three = norm_back(
        after_attn, gains[3], shifts[3], project_back(d_hidden, ffn_in_weight)
    )
    d_after_attn = grad_stream + d_fifth
    d_attn = d_after_attn.astype(bf16)
    g_out = weight_grad(context, own_columns(d_attn))
    d_context = project_back(d_attn, out_weight).astype(bf16).reshape(seq_len, heads, HEAD_DIM)
    d_values = jnp.einsum("hqk,qhd->khd", probs_low, d_context, preferred_element_type=jnp.float32)
    d_probs = jnp.einsum("qhd,khd->hqk", d_context, valueset, preferred_element_type=jnp.float32)
    delta = jnp.sum(d_probs * probs, axis=-1, keepdims=True)
    d_scores = (probs * (d_probs - delta)).astype(bf16)
    d_queries = jnp.einsum("hqk,khd->qhd", d_scores, keyset, preferred_element_type=jnp.float32) * scale
    d_keys = jnp.einsum("hqk,qhd->khd", d_scores, queries, preferred_element_type=jnp.float32) * scale
    d_packed = jnp.stack([d_queries, d_keys, d_values], axis=1).astype(bf16)
    d_packed = d_packed.reshape(seq_len, 3 * width)
    g_qkv = weight_grad(fourth_norm, own_columns(d_packed))
    d_fourth, gain_two, shift_two = norm_back(
        after_conv, gains[2], shifts[2], project_back(d_packed, qkv_weight)
    )
    d_after_conv = d_after_attn + d_fourth
    d_sep = d_after_conv[..., :half_width].astype(bf16)
    g_point = weight_grad(depth_low, own_columns(d_sep))
    g_point_bias = token_sum(d_sep)
    d_depth = project_back(d_sep, point_weight)
    g_depth = []
    d_third = None
    for offset in range(9):
        moved = shifted(d_depth, 4 - offset)
        g_depth.append(jnp.sum(moved * third_norm, axis=0))
        term = moved * taps[offset]
        d_third = term if d_third is None else d_third + term
    g_depth = jnp.stack(g_depth)
    d_third = d_third * columns
    d_combined, g_mid_gain, g_mid_bias = norm_back(combined, mid_gains, mid_shifts, d_third)
    d_left = jnp.where(left_pre > 0.0, d_combined, 0.0).astype(bf16)
    d_right = jnp.where(right_pre > 0.0, d_combined[..., :half_width], 0.0).astype(bf16)
    g_left = weight_grad(second_norm, own_columns(d_left))
    g_left_bias = token_sum(d_left)
    g_conv = weight_grad(window, own_columns(d_right))
    g_conv_bias = token_sum(d_right)
    d_window = project_back(d_right, conv_flat)
    d_second = project_back(d_left, left_weight) + d_window[..., width : 2 * width]
    d_second = d_second + shifted(d_window[..., :width], 1) + shifted(d_window[..., 2 * width :], -1)
    d_second = d_second * columns
    d_norm_one, gain_one, shift_one = norm_back(after_glu, gains[1], shifts[1], d_second)
    d_after_glu = d_after_conv + d_norm_one
    d_values_part = d_after_glu * gate_part
    d_gate_part = d_after_glu * values_part * gate_part * (1.0 - gate_part)
    d_joined = jnp.concatenate([d_values_part, d_gate_part], axis=-1).astype(bf16)
    g_glu = weight_grad(first_norm, own_columns(d_joined))
    g_glu_bias = token_sum(d_joined)
    d_norm_zero, gain_zero, shift_zero = norm_back(
        stream_in, gains[0], shifts[0], project_back(d_joined, glu_weight)
    )
    grad_input = own_tokens(d_after_glu + d_norm_zero)
    g_gains = jnp.stack([gain_zero, gain_one, gain_two, gain_three])
    g_shifts = jnp.stack([shift_zero, shift_one, shift_two, shift_three])

    lanes = 128

    def by_rows(grad):
        return grad.reshape(shards, -1, lanes)

    def by_columns(grad):
        return jnp.moveaxis(grad.reshape(-1, shards, grad.shape[-1] // shards), 1, 0).reshape(shards, -1)

    large = [
        by_rows(g_ffn_out),
        by_rows(g_ffn_in),
        by_rows(g_out),
        by_rows(g_qkv),
        by_rows(g_point),
        by_rows(g_left),
        jnp.moveaxis(g_conv.reshape(3, shards, width // shards, half_width // 2), 1, 0).reshape(
            shards, -1, lanes
        ),
        by_rows(g_glu),
    ]
    small = [
        by_columns(g[None] if g.ndim == 1 else g)
        for g in (
            g_glu_bias,
            g_gains,
            g_shifts,
            g_mid_gain,
            g_mid_bias,
            g_left_bias,
            g_depth,
            g_ffn_in_bias,
            g_ffn_out_bias,
        )
    ] + [
        jnp.broadcast_to(g[None], (shards, half_width)) for g in (g_conv_bias, g_point_bias)
    ]
    small_sizes = [s.shape[1] for s in small]
    small = jnp.concatenate(small, axis=1).astype(bf16)
    filler = -small.shape[1] % (16 * lanes)
    small = jnp.pad(small, ((0, 0), (0, filler))).reshape(shards, -1, lanes)
    buffer = jnp.concatenate(large + [small], axis=1)
    total = lax.psum_scatter(buffer, "dp", scatter_dimension=0, tiled=True)[0]
    large_rows = sum(g.shape[1] for g in large)
    mine = total[:large_rows]
    theirs = lax.ppermute(mine, "head", swap)
    lefts = jnp.where(side == 0, mine, theirs).astype(jnp.float32)
    rights = jnp.where(side == 0, theirs, mine).astype(jnp.float32)
    joined_up = []
    start = 0
    for grad, shape in zip(
        large,
        (
            (ffn_width // shards, width // 2),
            (width // shards, ffn_width // 2),
            (width // shards, width // 2),
            (width // shards, 3 * width // 2),
            (ffn_width // shards, half_width // 2),
            (width // shards, ffn_width // 2),
            (3, width // shards, half_width // 2),
            (width // shards, width),
        ),
    ):
        stop = start + grad.shape[1]
        joined_up.append(
            jnp.concatenate([lefts[start:stop].reshape(shape), rights[start:stop].reshape(shape)], axis=-1)
        )
        start = stop
    ffn_out, ffn_in, out, qkv, point, left, conv, glu = joined_up
    flat = total[large_rows:].reshape(-1).astype(jnp.float32)
    pieces = []
    start = 0
    for size in small_sizes:
        pieces.append(flat[start : start + size])
        start += size
    (
        s_glu_bias,
        s_gains,
        s_shifts,
        s_mid_gain,
        s_mid_bias,
        s_left_bias,
        s_depth,
        s_ffn_in_bias,
        s_ffn_out_bias,
        s_conv_bias,
        s_point_bias,
    ) = pieces
    return (
        block_out.astype(bf16),
        grad_input,
        glu,
        s_glu_bias,
        s_gains.reshape(4, -1),
        s_shifts.reshape(4, -1),
        s_mid_gain,
        s_mid_bias,
        left,
        s_left_bias,
        conv,
        s_conv_bias,
        s_depth.reshape(9, -1),
        point,
        s_point_bias,
        qkv,
        out,
        ffn_in,
        s_ffn_in_bias,
        ffn_out,
        s_ffn_out_bias,
    )


def solution(mesh):
    return jax.shard_map(
        per_device,
        mesh=mesh,
        in_specs=(P("dp", "head", None), P("dp"), P("dp", "head", None)) + (P(),) * 19,
        out_specs=(
            P("dp", "head", None),
            P("dp", "head", None),
            P("dp", None),
            P("dp"),
            P(None, "dp"),
            P(None, "dp"),
            P("dp"),
            P("dp"),
            P("dp", None),
            P("dp"),
            P(None, "dp", None),
            P(),
            P(None, "dp"),
            P("dp", None),
            P(),
            P("dp", None),
            P("dp", None),
            P("dp", None),
            P("dp"),
            P("dp", None),
            P("dp"),
        ),
        check_vma=False,
    )
```

time: 973 us -> 246 us (0.25)
  waiting for transfers between devices: 632 us -> 85 us
  blocking collectives: 108 us -> 0 us
  starting transfers between devices: 31.3 us -> 4.72 us
  other arithmetic: 68.7 us -> 43.7 us
  local copies, waits for them, and re-layouts: 62.2 us -> 52.1 us
    reduce_scatter x9 -> x1, waiting for transfers between devices: 589 us -> 78.5 us  [per_device(): total = lax.psum_scatter(buffer, 'dp', scatter_dimension=0, tiled=True)[0]]
    unnamed x1 -> x0, blocking collectives: 58.8 us -> none
    psum x1 -> x0, blocking collectives: 40 us -> none  [per_device(): bias_totals = lax.psum((g_conv_bias, g_point_bias), ('dp', 'head'))]
    convert_element_type x34 -> x7, other arithmetic: 39.8 us -> 5.18 us  [the longest x1 2.72 us: per_device(): depth_low = depthwise.astype(bf16)]
    all_to_all x3 -> x0, waiting for transfers between devices: 15.5 us -> none  [the longest x1 6.65 us: per_device(): lax.all_to_all(packed, 'head', split_axis=3, concat_axis=1, tiled=True)]
    unnamed x268 -> x328, local copies, waits for them, and re-layouts: 31.1 us -> 16.3 us
    ppermute x8 -> x3, starting transfers between devices: 18.1 us -> 4.68 us  [the longest x2 3.08 us: whole_row(): other = lax.ppermute(part, 'head', swap)]
    all_to_all x3 -> x0, starting transfers between devices: 12.2 us -> none  [the longest x1 4.23 us: per_device(): lax.all_to_all(packed, 'head', split_axis=3, concat_axis=1, tiled=True)]
  transfers between devices with their start and end apart: 24 -> 4, of which waited for: 18 -> 2; matrix products, arithmetic and copies ran while one was open for 8% -> 18% of each run, Pallas kernels for 0% -> 0%
where the time goes in v1:
time: 246 us; the launch traced here: 244 us
  waiting for transfers between devices  85 us (35%)
  local copies, waits for them, and re-layouts  52.1 us (21%)
  other arithmetic  43.7 us (18%)
  matrix products  42.2 us (17%)
  between operations  16.7 us (7%)
  starting transfers between devices  4.72 us (2%)
    reduce_scatter x1, waiting for transfers between devices, per_device(): total = lax.psum_scatter(buffer, 'dp', scatter_dimension=0, tiled=True)[0]  78.5 us
    unnamed x328, local copies, waits for them, and re-layouts  16.3 us
    dot_general x8, matrix products, project_back(): jnp.einsum('te,de->td', incoming, weight, preferred_element_type=jnp.floa...  11.8 us
    dot_general x8, matrix products, weight_grad(): jnp.einsum('td,te->de', inputs, incoming, preferred_element_type=jnp.floa...  11.2 us
    reshape x6, local copies, waits for them, and re-layouts, by_rows(): return grad.reshape(shards, -1, lanes)  10.3 us
    dot_general x8, matrix products, project(): return jnp.dot(inputs, weight, preferred_element_type=jnp.float32)  10.1 us
    concatenate x8, other arithmetic, per_device(): jnp.concatenate([lefts[start:stop].reshape(shape), rights[start:stop].res...  7.13 us
    ppermute x1, waiting for transfers between devices, per_device(): theirs = lax.ppermute(mine, 'head', swap)  6.55 us
  transfers between devices with their start and end apart: 4, of which 2 were waited for; matrix products, arithmetic and copies ran while one was open for 18% of the time, Pallas kernels for 0%

profile of v1, /device:TPU:0, one launch (start us, length us, event | category | flops | bytes accessed | tf_op | source)
XLA Modules:
  0.0 244.5 jit_solution(8396324077766099176)
XLA Ops:
  7.3 3.0 %collective-permute-start = (bf16[128,512]{1,0:T(8,128)(2,1)}, bf16[128,512]{1,0:T(8,128)(2,1)S(1)}, u32[]{:S(2)}, u32[]{:S(2)}) collective-permute-start(bf16[128,512]{1,0:T(8,128)(2,1)} %bitcast.171), channel_id=1, source_target_pairs={{0,1},{1,0},{2,3},{3,2},{4,5},{5,4},{6,7},{7,6},{8,9},{9,8},{10,11... | collective-permute-start | bytes 393224 | tf_op jit(solution)/shard_map/ppermute | solution.py:88
  13.9 1.7 fusion.110
  26.2 1.9 convolution_add_fusion.2
  36.6 2.7 %add_convert_fusion = bf16[256,2048]{1,0:T(8,128)(2,1)S(1)} fusion(f32[252,2048]{1,0:T(8,128)S(1)} %get-tuple-element.80, f32[253,2048]{1,0:T(8,128)S(1)} %get-tuple-element.82, f32[254,2048]{1,0:T(8,128)S(1)} %get-tuple-element.84, f32[255,2048]{1,0:T(8,128)S(1)} %get-tuple-element.86, f32[256,2048]{1,0:T(8,128)S(1)} %add_multiply_fusion.1, ...), kind=kLoop, calls=%fused_computation.32 | loop fusion | flops 9437184 | bytes 19832832 | tf_op jit(solution)/shard_map/convert_element_type | solution.py:130
  41.1 1.5 convolution_convert_fusion.1
  42.6 2.3 copy.64
  44.9 3.8 %fusion.115 = (f32[8,256]{1,0:T(8,128)}, f32[8,256,256]{1,2,0:T(8,128)}) fusion(pred[256]{0:T(512)(128)(4,1)S(1)} %copy-done.154, bf16[256,3,8,64]{0,3,2,1:T(8,128)(2,1)} %bitcast.165), kind=kOutput, calls=%fused_computation.256 | convolution fusion | flops 69206272 | bytes 2629888 | tf_op jit(solution)/shard_map/sub | solution.py:142
  48.8 2.0 convolution_convert_fusion.11
  51.5 1.8 fusion.4
  53.3 1.7 fusion.85
  59.5 2.2 fusion.14
  70.9 3.6 %multiply_reduce_fusion = (bf16[2048]{0:T(1024)(128)(2,1)}, bf16[2048]{0:T(1024)(128)(2,1)}, bf16[2048]{0:T(1024)(128)(2,1)}, bf16[2048]{0:T(1024)(128)(2,1)}, b...) fusion(f32[256,2048]{1,0:T(8,128)S(1)} %copy-done.3, ...), kind=kLoop, calls=%fused_computation.16 | loop fusion | flops 9418752 | bytes 20844544 | tf_op jit(solution)/shard_map/reduce_sum | solution.py:187
  74.6 5.5 %multiply_reduce_fusion.9 = (bf16[2048]{0:T(1024)(128)(2,1)}, f32[256]{0:T(256)S(1)}, bf16[2048]{0:T(1024)(128)(2,1)}, f32[256,2048]{1,0:T(8,128)S(1)}) fusion(f32[256]{0:T(256)S(1)} %copy-done.110, f32[256]{0:T(256)S(1)} %copy-done.91, f32[256,256]{1,0:T(8,128)S(1)} %copy-done.18, f32[256,2048]{1,0:T(8,128)S(1)} %copy-done.5, ...), kind=kLoop, calls=%fused_computation.25 | loop fusion | flops 15200000 | bytes 23261184 | tf_op jit(solution)/shard_map/transpose(jvp())/reduce_sum | solution.py:16
  82.3 2.2 fusion.86
  86.3 1.6 fusion.119
  89.5 1.5 convolution_convert_fusion
  91.0 2.2 reshape.395
  93.3 1.7 convolution_convert_fusion.5
  97.4 2.5 %convolution_convert_fusion.6 = bf16[512,768]{1,0:T(8,128)(2,1)} fusion(bf16[256,1536]{0,1:T(8,128)(2,1)} %bitcast.180, s32[]{:T(128)S(6)} %select_n.83, f32[256,512]{1,0:T(8,128)S(1)} %get-tuple-element.68, f32[512]{0:T(512)S(1)} %bitcast.224, f32[512]{0:T(512)S(1)} %bitcast.218, f32[256]{0:T(256)S(1)} %copy-done.98, f32[256]{0:T(256)S(1)} %copy-done.85), kind=kOutput, calls=%fused_computation.42 | convolution fusion | flops 202375168 | bytes 1710084 | tf_op jit(solution)/shard_map/td,te->de/dot_general | solution.py:28
  100.0 2.5 %reshape.398 = bf16[16,192,128]{2,1,0:T(8,128)(2,1)} reshape(bf16[512,768]{1,0:T(8,128)(2,1)} %convolution_convert_fusion.6) | data formatting | bytes 1572864 | tf_op jit(solution)/shard_map/reshape | solution.py:220
  102.6 1.8 copy.70
  104.6 1.5 convolution_convert_fusion.4
  106.1 2.4 reshape.400
  108.5 1.4 fusion.103
  110.4 2.2 multiply_reduce_fusion.15
  116.0 3.2 %fusion.32 = (bf16[512]{0:T(512)(128)(2,1)S(1)}, f32[256]{0:T(256)}, bf16[512]{0:T(512)(128)(2,1)S(1)}, f32[256,512]{1,0:T(8,128)}) fusion(f32[256]{0:T(256)S(1)} %copy-done.140, f32[256]{0:T(256)S(1)} %copy-done.121, bf16[128,512]{1,0:T(8,128)(2,1)S(1)} %bitcast.177, bf16[128,512]{1,0:T(8,128)(2,1)S(1)} %copy-done.39, pred[]{:T(512)S(6)} %eq.2, ...), kind=kOutput, calls=%fused_computation.93 | convolution fusion | flops 271842048 | bytes 2366465 | tf_op jit(solution)/shard_map/te,de->td/dot_general | solution.py:24
  132.7 2.1 fusion.18
  135.7 78.5 %reduce-scatter.2.cloned.1.call-done = bf16[1,1408,128]{2,1,0:T(8,128)(2,1)} async-done(((bf16[16,1408,128]{2,1,0:T(8,128)(2,1)}), bf16[1,1408,128]{2,1,0:T(8,128)(2,1)}) %reduce-scatter.2.cloned.1.call-update) | async-done | bytes 360464 | tf_op jit(solution)/shard_map/reduce_scatter | solution.py:258
  218.2 1.6 collective-permute-start.2
  221.1 6.5 %collective-permute-done.2 = bf16[1376,128]{1,0:T(8,128)(2,1)S(1)} collective-permute-done((bf16[1376,128]{1,0:T(8,128)(2,1)S(1)}, bf16[1376,128]{1,0:T(8,128)(2,1)S(1)}, u32[]{:S(2)}, u32[]{:S(2)}) %collective-permute-start.2) | collective-permute-done | bytes 352288 | tf_op jit(solution)/shard_map/ppermute | solution.py:261
  230.5 1.5 pad_maximum_fusion.10
  232.0 1.4 pad_maximum_fusion.9
  (478 shorter events, 75.7 us)
Async XLA Ops:
  7.2 44.3 %copy-start = (bf16[512,2048]{1,0:T(8,128)(2,1)S(1)}, bf16[512,2048]{1,0:T(8,128)(2,1)}, u32[]{:S(2)}) copy-start(bf16[512,2048]{1,0:T(8,128)(2,1)} %param.40) | copy-start | bytes 6291460
  7.2 20.9 %copy-start.37 = (bf16[1,128,512]{2,1,0:T(8,128)(2,1)S(1)}, bf16[1,128,512]{2,1,0:T(8,128)(2,1)}, u32[]{:S(2)}) copy-start(bf16[1,128,512]{2,1,0:T(8,128)(2,1)} %param.22) | copy-start | bytes 393220
  7.2 206.9 %reduce-scatter.2.cloned.1.call-start = ((), (), s32[]{:S(2)}) async-start(), calls=%async_computation.1 | async-start | bytes 6127616 | tf_op jit(solution)/shard_map/reduce_scatter | solution.py:258
  7.3 16.5 %collective-permute-start = (bf16[128,512]{1,0:T(8,128)(2,1)}, bf16[128,512]{1,0:T(8,128)(2,1)S(1)}, u32[]{:S(2)}, u32[]{:S(2)}) collective-permute-start(bf16[128,512]{1,0:T(8,128)(2,1)} %bitcast.171), channel_id=1, source_target_pairs={{0,1},{1,0},{2,3},{3,2},{4,5},{5,4},{6,7},{7,6},{8,9},{9,8},{10,11... | collective-permute-start | bytes 393224 | tf_op jit(solution)/shard_map/ppermute | solution.py:88
  10.3 43.0 %collective-permute-start.1 = (bf16[128,512]{1,0:T(8,128)(2,1)}, bf16[128,512]{1,0:T(8,128)(2,1)}, u32[]{:S(2)}, u32[]{:S(2)}) collective-permute-start(bf16[128,512]{1,0:T(8,128)(2,1)} %bitcast.192), channel_id=1, source_target_pairs={{0,1},{1,0},{2,3},{3,2},{4,5},{5,4},{6,7},{7,6},{8,9},{9,8},{10,11... | collective-permute-start | bytes 393224 | tf_op jit(solution)/shard_map/ppermute | solution.py:88
  12.4 15.9 %copy-start.134 = (f32[1,512]{1,0:T(1,128)}, f32[1,512]{1,0:T(1,128)S(1)}, u32[]{:S(2)}) copy-start(f32[1,512]{1,0:T(1,128)S(1)} %get-tuple-element.125) | copy-start | bytes 6148
  12.4 16.2 %copy-start.74 = (f32[1,512]{1,0:T(1,128)}, f32[1,512]{1,0:T(1,128)S(1)}, u32[]{:S(2)}) copy-start(f32[1,512]{1,0:T(1,128)S(1)} %get-tuple-element.124) | copy-start | bytes 6148
  13.9 14.5 %copy-start.144 = (f32[1,512]{1,0:T(1,128)}, f32[1,512]{1,0:T(1,128)S(1)}, u32[]{:S(2)}) copy-start(f32[1,512]{1,0:T(1,128)S(1)} %get-tuple-element.129) | copy-start | bytes 6148
  23.8 9.0 %copy-start.104 = (f32[256]{0:T(256)}, f32[256]{0:T(256)S(1)}, u32[]{:S(2)}) copy-start(f32[256]{0:T(256)S(1)} %fusion.76) | copy-start | bytes 3076
  39.9 5.0 %copy-start.83 = (f32[256]{0:T(256)}, f32[256]{0:T(256)S(1)}, u32[]{:S(2)}) copy-start(f32[256]{0:T(256)S(1)} %broadcast_multiply_fusion.2) | copy-start | bytes 3076
  51.2 6.6 %copy-start.6 = (f32[256,512]{1,0:T(8,128)}, f32[256,512]{1,0:T(8,128)S(1)}, u32[]{:S(2)}) copy-start(f32[256,512]{1,0:T(8,128)S(1)} %get-tuple-element.137) | copy-start | bytes 1572868
  51.2 6.6 %copy-start.86 = (f32[256]{0:T(256)}, f32[256]{0:T(256)S(1)}, u32[]{:S(2)}) copy-start(f32[256]{0:T(256)S(1)} %broadcast_multiply_fusion.1) | copy-start | bytes 3076
  51.4 6.4 %copy-start.99 = (f32[256]{0:T(256)}, f32[256]{0:T(256)S(1)}, u32[]{:S(2)}) copy-start(f32[256]{0:T(256)S(1)} %fusion.71) | copy-start | bytes 3076
  74.6 5.5 %copy-start.9 = (bf16[256,2048]{1,0:T(8,128)(2,1)S(1)}, bf16[256,2048]{1,0:T(8,128)(2,1)}, u32[]{:S(2)}) copy-start(bf16[256,2048]{1,0:T(8,128)(2,1)} %copy-done.8) | copy-start | bytes 3145732
  74.6 6.8 %copy-start.130 = (f32[256]{0:T(256)S(1)}, f32[256]{0:T(256)}, u32[]{:S(2)}) copy-start(f32[256]{0:T(256)} %copy-done.129) | copy-start | bytes 3076
  96.3 6.1 %copy-start.151 = (bf16[512]{0:T(512)(128)(2,1)S(1)}, bf16[512]{0:T(512)(128)(2,1)}, u32[]{:S(2)}) copy-start(bf16[512]{0:T(512)(128)(2,1)} %get-tuple-element.35) | copy-start | bytes 3076
  96.3 6.2 %copy-start.150 = (bf16[512]{0:T(512)(128)(2,1)S(1)}, bf16[512]{0:T(512)(128)(2,1)}, u32[]{:S(2)}) copy-start(bf16[512]{0:T(512)(128)(2,1)} %get-tuple-element.43) | copy-start | bytes 3076
  97.3 7.1 %copy-start.119 = (bf16[2048]{0:T(1024)(128)(2,1)S(1)}, bf16[2048]{0:T(1024)(128)(2,1)}, u32[]{:S(2)}) copy-start(bf16[2048]{0:T(1024)(128)(2,1)} %get-tuple-element.31) | copy-start | bytes 12292
  97.3 7.1 %copy-start.118 = (bf16[2048]{0:T(1024)(128)(2,1)S(1)}, bf16[2048]{0:T(1024)(128)(2,1)}, u32[]{:S(2)}) copy-start(bf16[2048]{0:T(1024)(128)(2,1)} %get-tuple-element.30) | copy-start | bytes 12292
  97.3 7.1 %copy-start.117 = (bf16[2048]{0:T(1024)(128)(2,1)S(1)}, bf16[2048]{0:T(1024)(128)(2,1)}, u32[]{:S(2)}) copy-start(bf16[2048]{0:T(1024)(128)(2,1)} %get-tuple-element.29) | copy-start | bytes 12292
  97.4 7.1 %copy-start.116 = (bf16[2048]{0:T(1024)(128)(2,1)S(1)}, bf16[2048]{0:T(1024)(128)(2,1)}, u32[]{:S(2)}) copy-start(bf16[2048]{0:T(1024)(128)(2,1)} %get-tuple-element.28) | copy-start | bytes 12292
  97.4 7.1 %copy-start.115 = (bf16[2048]{0:T(1024)(128)(2,1)S(1)}, bf16[2048]{0:T(1024)(128)(2,1)}, u32[]{:S(2)}) copy-start(bf16[2048]{0:T(1024)(128)(2,1)} %get-tuple-element.27) | copy-start | bytes 12292
  97.4 7.1 %copy-start.114 = (bf16[2048]{0:T(1024)(128)(2,1)S(1)}, bf16[2048]{0:T(1024)(128)(2,1)}, u32[]{:S(2)}) copy-start(bf16[2048]{0:T(1024)(128)(2,1)} %get-tuple-element.26) | copy-start | bytes 12292
  97.4 7.1 %copy-start.113 = (bf16[2048]{0:T(1024)(128)(2,1)S(1)}, bf16[2048]{0:T(1024)(128)(2,1)}, u32[]{:S(2)}) copy-start(bf16[2048]{0:T(1024)(128)(2,1)} %get-tuple-element.25) | copy-start | bytes 12292
  97.4 7.1 %copy-start.112 = (bf16[2048]{0:T(1024)(128)(2,1)S(1)}, bf16[2048]{0:T(1024)(128)(2,1)}, u32[]{:S(2)}) copy-start(bf16[2048]{0:T(1024)(128)(2,1)} %get-tuple-element.24) | copy-start | bytes 12292
  97.4 7.1 %copy-start.111 = (bf16[2048]{0:T(1024)(128)(2,1)S(1)}, bf16[2048]{0:T(1024)(128)(2,1)}, u32[]{:S(2)}) copy-start(bf16[2048]{0:T(1024)(128)(2,1)} %get-tuple-element.23) | copy-start | bytes 12292
  97.4 7.2 %copy-start.15 = (bf16[256,2048]{1,0:T(8,128)(2,1)S(1)}, bf16[256,2048]{1,0:T(8,128)(2,1)}, u32[]{:S(2)}) copy-start(bf16[256,2048]{1,0:T(8,128)(2,1)} %get-tuple-element.52) | copy-start | bytes 3145732
  116.0 4.9 %copy-start.102 = (bf16[2048]{0:T(1024)(128)(2,1)S(1)}, bf16[2048]{0:T(1024)(128)(2,1)}, u32[]{:S(2)}) copy-start(bf16[2048]{0:T(1024)(128)(2,1)} %get-tuple-element.21) | copy-start | bytes 12292
  116.0 4.9 %copy-start.103 = (bf16[2048]{0:T(1024)(128)(2,1)S(1)}, bf16[2048]{0:T(1024)(128)(2,1)}, u32[]{:S(2)}) copy-start(bf16[2048]{0:T(1024)(128)(2,1)} %get-tuple-element.32) | copy-start | bytes 12292
  116.0 5.8 %copy-start.21 = (bf16[16,256,128]{2,1,0:T(8,128)(2,1)S(1)}, bf16[16,256,128]{2,1,0:T(8,128)(2,1)}, u32[]{:S(2)}) copy-start(bf16[16,256,128]{2,1,0:T(8,128)(2,1)} %reshape.395) | copy-start | bytes 3145732
  218.2 9.5 %collective-permute-start.2 = (bf16[1376,128]{1,0:T(8,128)(2,1)S(1)}, bf16[1376,128]{1,0:T(8,128)(2,1)S(1)}, u32[]{:S(2)}, u32[]{:S(2)}) collective-permute-start(bf16[1376,128]{1,0:T(8,128)(2,1)S(1)} %slice_bitcast_fusion), channel_id=1, source_target_pairs={{0,1},{1,0},{2,3},{3,2},{4,5},{5,4},{6,7},{7,6},{8,9},{9,8},{10,11... | collective-permute-start | bytes 1056776 | tf_op jit(solution)/shard_map/ppermute | solution.py:261
  230.3 7.4 %copy-start.1 = (bf16[512,2048]{1,0:T(8,128)(2,1)S(1)}, bf16[512,2048]{1,0:T(8,128)(2,1)}, u32[]{:S(2)}) copy-start(bf16[512,2048]{1,0:T(8,128)(2,1)} %param.40) | copy-start | bytes 6291460
  (127 other events, 296.5 us)
Sparse Core Ops, SparseCore 0:
  130.8 83.3 reduce-scatter.1

commit v2 on v1

v2 whole, which is shorter than its diff:
```python
import functools

import jax
import jax.numpy as jnp
from jax import lax
from jax.experimental import pallas as pl
from jax.experimental.pallas import tpu as pltpu
from jax.sharding import PartitionSpec as P

HEAD_DIM = 64
EPSILON = 1e-06
LANES = 128
TILE = 256
GROUPS = 16
F32 = jnp.float32
BF16 = jnp.bfloat16
VMEM_BYTES = 50 * 1024 * 1024


def mm(a, b):
    return lax.dot_general(a, b, (((1,), (0,)), ((), ())), preferred_element_type=F32)


def mm_nt(a, b):
    return lax.dot_general(a, b, (((1,), (1,)), ((), ())), preferred_element_type=F32)


def mm_tn(a, b):
    return lax.dot_general(a, b, (((0,), (0,)), ((), ())), preferred_element_type=F32)


def mean(v):
    return jnp.mean(v, axis=-1, keepdims=True)


def normalized(v):
    centred = v - mean(v)
    rate = lax.rsqrt(mean(centred * centred) + EPSILON)
    return centred * rate, rate


def norm_back(vhat, rate, gained):
    return (gained - mean(gained) - vhat * mean(gained * vhat)) * rate


def sum_tokens(v):
    return jnp.sum(v, axis=0, keepdims=True)


def row_blocks(total, step, body, carry=0):
    def visit(i, c):
        return body(pl.multiple_of(i * step, step), c)

    return lax.fori_loop(0, total // step, visit, carry)


def valid_rows(start, count, length):
    places = start + lax.broadcasted_iota(jnp.int32, (count, 1), 0)
    return (places < length).astype(F32)


def col(n, width=TILE):
    return slice(n * width, (n + 1) * width)


def place_rows(meta, grad, keep, send, at, rows):
    def visit(p, c):
        for slot, out in ((2, keep), (2 + GROUPS // 2, send)):
            block = meta[slot + p]
            out[p, at : at + rows, :] = grad[
                pl.ds(pl.multiple_of(block * rows, rows), rows), :
            ].astype(BF16)
        return c

    lax.fori_loop(0, GROUPS // 2, visit, 0)


def for_slots(meta, keep, send, body):
    def visit(p, c):
        for slot, out in ((2, keep), (2 + GROUPS // 2, send)):
            body(p, meta[slot + p], out)
        return c

    lax.fori_loop(0, GROUPS // 2, visit, 0)


def forward_kernel(
    meta,
    mine,
    other,
    cot_mine,
    cot_other,
    vec,
    gains,
    shifts,
    depth_w,
    glu_w,
    left_w,
    conv_w,
    point_w,
    qkv_w,
    out_w,
    ffn_in_w,
    ffn_out_w,
    out_tokens,
    stream,
    first,
    joined,
    after_glu,
    second,
    left_pre,
    right_pre,
    depth_low,
    after_conv,
    fourth,
    packed,
    probs,
    context,
    d_after,
    small,
    keep,
    send,
    third,
    sides,
    after_attn,
    fifth,
    hidden,
    cot,
    d_hidden,
    d_fifth,
    grad,
):
    part, width = mine.shape
    seq = 2 * part
    ffn = left_w.shape[1]
    half = conv_w.shape[2]
    side = meta[0]
    length = meta[1]
    own = pl.ds(pl.multiple_of(side * part, part), part)
    opposite = pl.ds(pl.multiple_of((1 - side) * part, part), part)
    stream[own, :] = mine[...]
    stream[opposite, :] = other[...]
    cot[own, :] = cot_mine[...]
    cot[opposite, :] = cot_other[...]
    gain = [gains[k : k + 1, :].astype(F32) for k in range(4)]
    shift = [shifts[k : k + 1, :].astype(F32) for k in range(4)]

    def first_rows(r, c):
        rows = pl.ds(r, 64)
        vhat, _ = normalized(stream[rows, :].astype(F32))
        first[rows, :] = (vhat * gain[0] + shift[0]).astype(BF16)
        return c

    row_blocks(seq, 64, first_rows)
    for n in range(2 * width // TILE):
        joined[:, col(n)] = mm(first[...], glu_w[:, col(n)]) + vec[4:5, col(n)]

    def glu_rows(r, c):
        rows = pl.ds(r, 32)
        gate = jax.nn.sigmoid(joined[rows, width:])
        joined[rows, width:] = gate
        v = stream[rows, :].astype(F32) + joined[rows, :width] * gate
        after_glu[rows, :] = v
        vhat, _ = normalized(v)
        second[rows, :] = ((vhat * gain[1] + shift[1]) * valid_rows(r, 32, length)).astype(BF16)
        return c

    row_blocks(seq, 32, glu_rows)
    blank = jnp.zeros((8, half), F32)
    for k in range(2):
        sides[k, 0:8, :] = blank
        sides[k, 8 + seq : 16 + seq, :] = blank
    sides[0, 8 : 8 + seq, :] = mm(second[...], conv_w[0])
    sides[1, 8 : 8 + seq, :] = mm(second[...], conv_w[2])
    right_pre[...] = mm(second[...], conv_w[1]) + vec[4:5, 2 * width : 2 * width + half]
    right_pre[...] = right_pre[...] + sides[0, 7 : 7 + seq, :] + sides[1, 9 : 9 + seq, :]
    for n in range(ffn // TILE):
        left_pre[:, col(n)] = mm(second[...], left_w[:, col(n)]) + vec[2:3, col(n)]
    chunks = ffn // LANES
    edge = jnp.zeros((8, LANES), F32)
    for k in range(chunks):
        third[k, 0:8, :] = edge
        third[k, 8 + seq : 16 + seq, :] = edge

    def mid_rows(r, c):
        rows = pl.ds(r, 16)
        vhat, _ = normalized(combine(left_pre[rows, :], right_pre[rows, :]))
        v = (vhat * vec[0:1, :] + vec[1:2, :]) * valid_rows(r, 16, length)
        for k in range(chunks):
            third[k, pl.ds(pl.multiple_of(8 + r, 8), 16), :] = v[:, col(k, LANES)]
        return c

    row_blocks(seq, 16, mid_rows)

    def depth_lanes(k, c):
        lanes = pl.ds(pl.multiple_of(k * LANES, LANES), LANES)
        taps = depth_w[:, lanes].astype(F32)
        total = third[k, 4 : 4 + seq, :] * taps[0:1, :]
        for j in range(1, 9):
            total = total + third[k, 4 + j : 4 + j + seq, :] * taps[j : j + 1, :]
        depth_low[:, lanes] = total.astype(BF16)
        return c

    lax.fori_loop(0, chunks, depth_lanes, 0)
    after_conv[:, :half] = (
        after_glu[:, :half] + mm(depth_low[...], point_w[...]) + vec[4:5, 2 * width + half : 2 * width + 2 * half]
    )
    after_conv[:, half:] = after_glu[:, half:]

    def fourth_rows(r, c):
        rows = pl.ds(r, 64)
        vhat, _ = normalized(after_conv[rows, :])
        fourth[rows, :] = (vhat * gain[2] + shift[2]).astype(BF16)
        return c

    row_blocks(seq, 64, fourth_rows)
    for n in range(3 * width // TILE):
        packed[:, col(n)] = mm(fourth[...], qkv_w[:, col(n)]).astype(BF16)

    low_lanes = lax.broadcasted_iota(jnp.int32, (1, LANES), 1) < HEAD_DIM
    scale = HEAD_DIM ** (-0.5)

    def head_pair(p, c):
        lanes = pl.ds(pl.multiple_of(p * LANES, LANES), LANES)
        q = packed[:, lanes].astype(F32)
        k = packed[:, pl.ds(pl.multiple_of(width + p * LANES, LANES), LANES)]
        v = packed[:, pl.ds(pl.multiple_of(2 * width + p * LANES, LANES), LANES)]
        open_keys = lax.broadcasted_iota(jnp.int32, (1, seq), 1) < length
        results = []
        for e in range(2):
            q_one = jnp.where(low_lanes if e == 0 else ~low_lanes, q, 0.0).astype(BF16)
            s = jnp.where(open_keys, mm_nt(q_one, k) * scale, -1000000000.0)
            raised = jnp.exp(s - jnp.max(s, axis=-1, keepdims=True))
            chance = raised / jnp.sum(raised, axis=-1, keepdims=True)
            probs[2 * p + e] = chance
            results.append(mm(chance.astype(BF16), v))
        context[:, lanes] = jnp.where(low_lanes, results[0], results[1]).astype(BF16)
        return c

    lax.fori_loop(0, width // LANES, head_pair, 0)
    for n in range(width // TILE):
        after_attn[:, col(n)] = after_conv[:, col(n)] + mm(context[...], out_w[:, col(n)])

    def fifth_rows(r, c):
        rows = pl.ds(r, 64)
        vhat, _ = normalized(after_attn[rows, :])
        fifth[rows, :] = (vhat * gain[3] + shift[3]).astype(BF16)
        return c

    row_blocks(seq, 64, fifth_rows)
    for n in range(ffn // TILE):
        pre = mm(fifth[...], ffn_in_w[:, col(n)]) + vec[3:4, col(n)]
        hidden[:, col(n)] = jnp.where(pre > 0.0, pre, 0.0).astype(BF16)
    for n in range(width // TILE):
        out_tokens[:, col(n)] = (
            after_attn[own, col(n)]
            + mm(hidden[own, :], ffn_out_w[:, col(n)])
            + vec[4:5, 3 * width + n * TILE : 3 * width + (n + 1) * TILE]
        ).astype(BF16)

    for n in range(ffn // TILE):
        back = mm_nt(cot[...], ffn_out_w[col(n), :])
        back = jnp.where(hidden[:, col(n)].astype(F32) > 0.0, back, 0.0).astype(BF16)
        d_hidden[:, col(n)] = back
        small[0:1, col(n)] = sum_tokens(back.astype(F32))
    for n in range(width // TILE):
        d_fifth[:, col(n)] = mm_nt(d_hidden[...], ffn_in_w[col(n), :])

    def fifth_back(r, c):
        g_gain, g_shift, g_out = c
        rows = pl.ds(r, 32)
        vhat, rate = normalized(after_attn[rows, :])
        e = d_fifth[rows, :]
        given = cot[rows, :].astype(F32)
        d_after[rows, :] = given + norm_back(vhat, rate, e * gain[3])
        return g_gain + sum_tokens(e * vhat), g_shift + sum_tokens(e), g_out + sum_tokens(given)

    nothing = jnp.zeros((1, width), F32)
    g_gain, g_shift, g_out = row_blocks(seq, 32, fifth_back, (nothing,) * 3)
    small[1:2, 0:width] = g_gain
    small[1:2, width : 2 * width] = g_shift
    small[1:2, 2 * width : 3 * width] = g_out

    cot_half = cot[:, pl.ds(pl.multiple_of(side * (width // 2), width // 2), width // 2)]
    per_row = ffn // GROUPS

    def ffn_out_slot(p, block, out):
        out[p, 0:per_row, :] = mm_tn(
            hidden[:, pl.ds(pl.multiple_of(block * per_row, per_row), per_row)], cot_half
        ).astype(BF16)

    for_slots(meta, keep, send, ffn_out_slot)
    rows = width // GROUPS
    for j in range(ffn // 2 // TILE):
        at = pl.multiple_of(side * (ffn // 2) + j * TILE, TILE)
        grad[...] = mm_tn(fifth[...], d_hidden[:, pl.ds(at, TILE)])
        place_rows(meta, grad, keep, send, per_row + j * rows, rows)


def combine(left_pre, right_pre):
    half = right_pre.shape[1]
    left = jnp.maximum(left_pre, 0.0)
    return jnp.concatenate([left[:, :half] + jnp.maximum(right_pre, 0.0), left[:, half:]], axis=1)


def attention_back_kernel(
    meta,
    gains,
    d_after,
    packed,
    probs,
    context,
    fourth,
    after_conv,
    depth_low,
    qkv_w,
    out_w,
    d_after_conv,
    small,
    keep,
    send,
    d_attn,
    d_context,
    d_packed,
    d_fourth,
    d_sep,
    grad,
):
    seq, width = d_after.shape
    side = meta[0]
    half = d_sep.shape[1]
    ffn = depth_low.shape[1]
    rows = width // GROUPS
    d_attn[...] = d_after[...].astype(BF16)
    for n in range(width // TILE):
        d_context[:, col(n)] = mm_nt(d_attn[...], out_w[col(n), :]).astype(BF16)
    low_lanes = lax.broadcasted_iota(jnp.int32, (1, LANES), 1) < HEAD_DIM
    scale = HEAD_DIM ** (-0.5)

    def head_pair(p, c):
        lanes = pl.ds(pl.multiple_of(p * LANES, LANES), LANES)
        k_lanes = pl.ds(pl.multiple_of(width + p * LANES, LANES), LANES)
        v_lanes = pl.ds(pl.multiple_of(2 * width + p * LANES, LANES), LANES)
        q = packed[:, lanes]
        k = packed[:, k_lanes]
        v = packed[:, v_lanes]
        given = d_context[:, lanes]
        wide = given.astype(F32)
        dq, dk, dv = [], [], []
        for e in range(2):
            one = jnp.where(low_lanes if e == 0 else ~low_lanes, wide, 0.0).astype(BF16)
            chance = probs[2 * p + e]
            d_probs = mm_nt(one, v)
            delta = jnp.sum(d_probs * chance, axis=-1, keepdims=True)
            d_scores = (chance * (d_probs - delta)).astype(BF16)
            dv.append(mm_tn(chance.astype(BF16), given))
            dq.append(mm(d_scores, k))
            dk.append(mm_tn(d_scores, q))
        d_packed[:, lanes] = (jnp.where(low_lanes, dq[0], dq[1]) * scale).astype(BF16)
        d_packed[:, k_lanes] = (jnp.where(low_lanes, dk[0], dk[1]) * scale).astype(BF16)
        d_packed[:, v_lanes] = jnp.where(low_lanes, dv[0], dv[1]).astype(BF16)
        return c

    lax.fori_loop(0, width // LANES, head_pair, 0)
    for n in range(width // TILE):
        d_fourth[:, col(n)] = mm_nt(d_packed[...], qkv_w[col(n), :])
    gain = gains[2:3, :].astype(F32)

    def fourth_back(r, c):
        g_gain, g_shift, g_point = c
        block = pl.ds(r, 32)
        vhat, rate = normalized(after_conv[block, :])
        e = d_fourth[block, :]
        total = d_after[block, :] + norm_back(vhat, rate, e * gain)
        d_after_conv[block, :] = total
        sep = total[:, :half].astype(BF16)
        d_sep[block, :] = sep
        return (
            g_gain + sum_tokens(e * vhat),
            g_shift + sum_tokens(e),
            g_point + sum_tokens(sep.astype(F32)),
        )

    nothing = jnp.zeros((1, width), F32)
    g_gain, g_shift, g_point = row_blocks(
        seq, 32, fourth_back, (nothing, nothing, jnp.zeros((1, half), F32))
    )
    small[0:1, 0:width] = g_gain
    small[0:1, width : 2 * width] = g_shift
    small[0:1, 2 * width : 2 * width + half] = g_point

    at = pl.multiple_of(side * (width // 2), width // 2)
    grad[...] = mm_tn(context[...], d_attn[:, pl.ds(at, width // 2)])
    place_rows(meta, grad, keep, send, 0, rows)
    for j in range(3 * width // 2 // TILE):
        at = pl.multiple_of(side * (3 * width // 2) + j * TILE, TILE)
        grad[...] = mm_tn(fourth[...], d_packed[:, pl.ds(at, TILE)])
        place_rows(meta, grad, keep, send, (1 + j) * rows, rows)
    sep_half = d_sep[:, pl.ds(pl.multiple_of(side * (half // 2), half // 2), half // 2)]
    per_row = ffn // GROUPS

    def point_slot(p, block, out):
        g = mm_tn(
            depth_low[:, pl.ds(pl.multiple_of(block * per_row, per_row), per_row)], sep_half
        ).astype(BF16)
        out[p, 4 * rows : 4 * rows + per_row // 2, 0:LANES] = g[: per_row // 2]
        out[p, 4 * rows : 4 * rows + per_row // 2, LANES : 2 * LANES] = g[per_row // 2 :]

    for_slots(meta, keep, send, point_slot)


def conv_back_kernel(
    meta,
    vec,
    depth_w,
    d_after_conv,
    left_pre,
    right_pre,
    second,
    point_w,
    left_w,
    conv_w,
    d_second,
    small,
    keep,
    send,
    vhat3,
    third,
    d_depth,
    d_third,
    rates,
    sums,
    d_left,
    d_right,
    taps_right,
    grad,
    grad_conv,
):
    seq, width = d_after_conv.shape
    ffn = left_pre.shape[1]
    half = right_pre.shape[1]
    side = meta[0]
    length = meta[1]
    chunks = ffn // LANES
    edge = jnp.zeros((8, LANES), F32)
    for k in range(chunks):
        d_depth[k, 0:8, :] = edge
        d_depth[k, 8 + seq : 16 + seq, :] = edge
    d_sep = d_after_conv[:, :half].astype(BF16)
    for n in range(ffn // TILE):
        block = mm_nt(d_sep, point_w[col(n), :])
        for m in range(TILE // LANES):
            d_depth[n * (TILE // LANES) + m, 8 : 8 + seq, :] = block[:, col(m, LANES)]

    def mid_rows(r, c):
        rows = pl.ds(r, 16)
        vhat, rate = normalized(combine(left_pre[rows, :], right_pre[rows, :]))
        v = (vhat * vec[0:1, :] + vec[1:2, :]) * valid_rows(r, 16, length)
        rates[rows, :] = jnp.broadcast_to(rate, (16, LANES))
        for k in range(chunks):
            third[k, rows, :] = v[:, col(k, LANES)]
            vhat3[k, rows, :] = vhat[:, col(k, LANES)]
        return c

    row_blocks(seq, 16, mid_rows)
    sums[...] = jnp.zeros(sums.shape, F32)
    valid = valid_rows(0, seq, length)

    def depth_lanes(k, c):
        lanes = pl.ds(pl.multiple_of(k * LANES, LANES), LANES)
        taps = depth_w[:, lanes].astype(F32)
        total = None
        here = third[k]
        for j in range(9):
            moved = d_depth[k, 12 - j : 12 - j + seq, :]
            small[j : j + 1, lanes] = sum_tokens(moved * here)
            term = moved * taps[j : j + 1, :]
            total = term if total is None else total + term
        total = total * valid
        vhat = vhat3[k]
        small[9:10, lanes] = sum_tokens(total * vhat)
        small[10:11, lanes] = sum_tokens(total)
        gained = total * vec[0:1, lanes]
        d_third[k] = gained
        sums[0] = sums[0] + gained
        sums[1] = sums[1] + gained * vhat
        return c

    lax.fori_loop(0, chunks, depth_lanes, 0)
    inverse = 1.0 / ffn
    sums[0] = jnp.broadcast_to(jnp.sum(sums[0], axis=-1, keepdims=True) * inverse, (seq, LANES))
    sums[1] = jnp.broadcast_to(jnp.sum(sums[1], axis=-1, keepdims=True) * inverse, (seq, LANES))

    def combined_lanes(k):
        return (d_third[k] - sums[0] - vhat3[k] * sums[1]) * rates[...]

    def left_lanes(k, c):
        lanes = pl.ds(pl.multiple_of(k * LANES, LANES), LANES)
        v = jnp.where(left_pre[:, lanes] > 0.0, combined_lanes(k), 0.0).astype(BF16)
        d_left[:, lanes] = v
        small[11:12, lanes] = sum_tokens(v.astype(F32))
        return c

    lax.fori_loop(0, chunks, left_lanes, 0)
    blank = jnp.zeros((8, half), F32)
    d_right[0:8, :] = blank
    d_right[8 + seq : 16 + seq, :] = blank
    for k in range(half // LANES):
        v = jnp.where(right_pre[:, col(k, LANES)] > 0.0, combined_lanes(k), 0.0).astype(BF16)
        v = v.astype(F32)
        d_right[8 : 8 + seq, col(k, LANES)] = v
        small[12:13, col(k, LANES)] = sum_tokens(v)
    taps_right[0] = d_right[9 : 9 + seq, :].astype(BF16)
    taps_right[1] = d_right[8 : 8 + seq, :].astype(BF16)
    taps_right[2] = d_right[7 : 7 + seq, :].astype(BF16)
    for n in range(width // TILE):
        total = mm_nt(d_left[...], left_w[col(n), :])
        for tap in range(3):
            total = total + mm_nt(taps_right[tap], conv_w[tap, col(n), :])
        d_second[:, col(n)] = total * valid

    rows = width // GROUPS
    for j in range(ffn // 2 // TILE):
        at = pl.multiple_of(side * (ffn // 2) + j * TILE, TILE)
        grad[...] = mm_tn(second[...], d_left[:, pl.ds(at, TILE)])
        place_rows(meta, grad, keep, send, j * rows, rows)
    start = ffn // 2 // TILE * rows
    half_lanes = pl.ds(pl.multiple_of(side * (half // 2), half // 2), half // 2)
    for tap in range(3):
        grad_conv[tap] = mm_tn(second[...], taps_right[tap, :, half_lanes])

    def conv_slot(p, block, out):
        at = pl.multiple_of(block * rows, rows)
        middle = pl.multiple_of(block * rows + rows // 2, rows // 2)
        h = rows // 2
        out[p, start : start + rows, 0:LANES] = grad_conv[0, pl.ds(at, rows), :].astype(BF16)
        out[p, start + rows : start + rows + h, 0:LANES] = grad_conv[1, pl.ds(at, h), :].astype(BF16)
        out[p, start : start + h, LANES : 2 * LANES] = grad_conv[1, pl.ds(middle, h), :].astype(BF16)
        out[p, start + h : start + h + rows, LANES : 2 * LANES] = grad_conv[
            2, pl.ds(at, rows), :
        ].astype(BF16)

    for_slots(meta, keep, send, conv_slot)


def glu_back_kernel(
    meta,
    gains,
    d_second,
    d_after_conv,
    after_glu,
    joined,
    first,
    stream,
    glu_w,
    small_ffn,
    small_attn,
    small_conv,
    grad_tokens,
    keep,
    send,
    d_joined,
    d_after_glu,
    d_first,
    rolled,
    blocks,
    grad,
):
    seq, width = d_second.shape
    part = seq // 2
    side = meta[0]
    gain = [gains[k : k + 1, :].astype(F32) for k in range(2)]

    def glu_rows(r, c):
        g_gain, g_shift, g_value, g_gate = c
        rows = pl.ds(r, 32)
        vhat, rate = normalized(after_glu[rows, :])
        e = d_second[rows, :]
        total = d_after_conv[rows, :] + norm_back(vhat, rate, e * gain[1])
        d_after_glu[rows, :] = total
        value = joined[rows, :width]
        gate = joined[rows, width:]
        d_value = (total * gate).astype(BF16)
        d_gate = (total * value * gate * (1.0 - gate)).astype(BF16)
        d_joined[rows, :width] = d_value
        d_joined[rows, width:] = d_gate
        return (
            g_gain + sum_tokens(e * vhat),
            g_shift + sum_tokens(e),
            g_value + sum_tokens(d_value.astype(F32)),
            g_gate + sum_tokens(d_gate.astype(F32)),
        )

    nothing = jnp.zeros((1, width), F32)
    gain_one, shift_one, g_value, g_gate = row_blocks(seq, 32, glu_rows, (nothing,) * 4)
    for n in range(width // TILE):
        d_first[:, col(n)] = mm_nt(d_joined[...], glu_w[col(n), :])

    def first_back(r, c):
        g_gain, g_shift = c
        rows = pl.ds(r, 32)
        vhat, rate = normalized(stream[rows, :].astype(F32))
        e = d_first[rows, :]
        d_after_glu[rows, :] = d_after_glu[rows, :] + norm_back(vhat, rate, e * gain[0])
        return g_gain + sum_tokens(e * vhat), g_shift + sum_tokens(e)

    gain_zero, shift_zero = row_blocks(seq, 32, first_back, (nothing,) * 2)
    grad_tokens[...] = d_after_glu[pl.ds(pl.multiple_of(side * part, part), part), :]

    rows = width // GROUPS
    for j in range(width // TILE):
        at = pl.multiple_of(side * width + j * TILE, TILE)
        grad[...] = mm_tn(first[...], d_joined[:, pl.ds(at, TILE)])
        place_rows(meta, grad, keep, send, j * rows, rows)

    blocks[...] = jnp.zeros(blocks.shape, F32)
    rolled[...] = jnp.zeros(rolled.shape, F32)
    vectors = (
        (gain_zero, gain_one, small_attn[0:1, 0:width], small_ffn[1:2, 0:width]),
        (shift_zero, shift_one, small_attn[0:1, width : 2 * width], small_ffn[1:2, width : 2 * width]),
    )
    tiles = width // LANES
    lane = lax.broadcasted_iota(jnp.int32, (8, LANES), 1)
    quarter = LANES // tiles
    for kind, four in enumerate(vectors):
        for k, vector in enumerate(four):
            for t in range(tiles):
                rolled[kind, 8 * k + t : 8 * k + t + 1, :] = vector[:, col(t, LANES)]
        for q in range(tiles):
            total = jnp.zeros((8, LANES), F32)
            for k in range(4):
                moved = pltpu.roll(rolled[kind, 8 * k : 8 * k + 8, :], (quarter * (k - q)) % LANES, 1)
                total = jnp.where((lane >= quarter * k) & (lane < quarter * (k + 1)), moved, total)
            for t in range(tiles):
                blocks[tiles * t + q, 13 + kind : 14 + kind, 0:LANES] = total[t : t + 1, :]
    lane = lane[0:1, :]
    g_out = small_ffn[1:2, 2 * width : 3 * width]
    for s in range(GROUPS):
        source = g_value if s < GROUPS // 2 else g_gate
        place = (s % (GROUPS // 2)) * (2 * width // GROUPS)
        block = source[:, place // LANES * LANES : place // LANES * LANES + LANES]
        glu_part = block if place % LANES == 0 else pltpu.roll(block, LANES - place % LANES, 1)
        place = s * (width // GROUPS)
        block = g_out[:, place // LANES * LANES : place // LANES * LANES + LANES]
        moved = (LANES // 2 - place % LANES) % LANES
        out_part = block if moved == 0 else pltpu.roll(block, moved, 1)
        blocks[s, 15:16, 0:LANES] = jnp.where(
            lane < LANES // 2, glu_part, jnp.where(lane < LANES // 2 + quarter, out_part, 0.0)
        )
        blocks[s, 0:12, 0:LANES] = small_conv[0:12, col(s, LANES)]
        blocks[s, 12:13, 0:LANES] = small_ffn[0:1, col(s, LANES)]
        for k in range(2):
            blocks[s, k : k + 1, LANES : 2 * LANES] = small_conv[12:13, col(k, LANES)]
            blocks[s, 2 + k : 3 + k, LANES : 2 * LANES] = small_attn[
                0:1, 2 * width + k * LANES : 2 * width + (k + 1) * LANES
            ]
    start = width // TILE * rows

    def small_slot(p, block, out):
        out[p, start : start + 16, :] = blocks[block].astype(BF16)

    for_slots(meta, keep, send, small_slot)


def finish_early_kernel(meta, mine_ffn, other_ffn, mine_attn, other_attn, ffn_out, ffn_in, out, qkv, point):
    side = meta[0]
    for who, ffn_grads, attn_grads in ((side, mine_ffn, mine_attn), (1 - side, other_ffn, other_attn)):
        per_row, width = ffn_out.shape
        rows = ffn_in.shape[0]
        at = pl.ds(pl.multiple_of(who * TILE, TILE), TILE)
        ffn_out[:, at] = ffn_grads[0:per_row, :].astype(F32)
        out[:, at] = attn_grads[0:rows, :].astype(F32)
        count = ffn_in.shape[1] // 2 // TILE
        for j in range(count):
            at = pl.ds(pl.multiple_of((who * count + j) * TILE, TILE), TILE)
            ffn_in[:, at] = ffn_grads[per_row + j * rows : per_row + (j + 1) * rows, :].astype(F32)
        count = qkv.shape[1] // 2 // TILE
        for j in range(count):
            at = pl.ds(pl.multiple_of((who * count + j) * TILE, TILE), TILE)
            qkv[:, at] = attn_grads[(1 + j) * rows : (2 + j) * rows, :].astype(F32)
        at = pl.ds(pl.multiple_of(who * LANES, LANES), LANES)
        start = 4 * rows
        point[0 : per_row // 2, at] = attn_grads[start : start + per_row // 2, 0:LANES].astype(F32)
        point[per_row // 2 :, at] = attn_grads[start : start + per_row // 2, LANES : 2 * LANES].astype(F32)


def finish_late_kernel(
    meta,
    mine_conv,
    other_conv,
    mine_glu,
    other_glu,
    left,
    conv,
    glu,
    gains,
    shifts,
    depth,
    vectors,
):
    side = meta[0]
    rows = left.shape[0]
    h = rows // 2
    for who, conv_grads, glu_grads in ((side, mine_conv, mine_glu), (1 - side, other_conv, other_glu)):
        count = left.shape[1] // 2 // TILE
        for j in range(count):
            at = pl.ds(pl.multiple_of((who * count + j) * TILE, TILE), TILE)
            left[:, at] = conv_grads[j * rows : (j + 1) * rows, :].astype(F32)
        start = count * rows
        at = pl.ds(pl.multiple_of(who * LANES, LANES), LANES)
        low = conv_grads[start : start + 3 * h, 0:LANES].astype(F32)
        high = conv_grads[start : start + 3 * h, LANES : 2 * LANES].astype(F32)
        conv[0, :, at] = low[0:rows]
        conv[1, 0:h, at] = low[rows:]
        conv[1, h:rows, at] = high[0:h]
        conv[2, :, at] = high[h:]
        count = glu.shape[1] // 2 // TILE
        for j in range(count):
            at = pl.ds(pl.multiple_of((who * count + j) * TILE, TILE), TILE)
            glu[:, at] = glu_grads[j * rows : (j + 1) * rows, :].astype(F32)
    start = glu.shape[1] // 2 // TILE * rows
    block = mine_glu[start : start + 16, :].astype(F32)
    depth[...] = block[0:9, 0:LANES]
    for k in range(4):
        gains[k : k + 1, :] = block[13:14, k * rows : (k + 1) * rows]
        shifts[k : k + 1, :] = block[14:15, k * rows : (k + 1) * rows]
    vectors[...] = block


def call(kernel, outs, scratch, *args):
    smem = pl.BlockSpec(memory_space=pltpu.SMEM)
    vmem = pl.BlockSpec(memory_space=pltpu.VMEM)
    return pl.pallas_call(
        kernel,
        out_shape=tuple(jax.ShapeDtypeStruct(shape, dtype) for shape, dtype in outs),
        in_specs=[smem] + [vmem] * (len(args) - 1),
        out_specs=(vmem,) * len(outs),
        scratch_shapes=[pltpu.VMEM(shape, dtype) for shape, dtype in scratch],
        compiler_params=pltpu.CompilerParams(vmem_limit_bytes=VMEM_BYTES),
        name=kernel.__name__,
    )(*args)


def per_device(
    tokens,
    lengths,
    cotangent,
    glu_weight,
    glu_bias,
    norm_gain,
    norm_bias,
    mid_gain,
    mid_bias,
    left_weight,
    left_bias,
    conv_weight,
    conv_bias,
    depth_weight,
    point_weight,
    point_bias,
    qkv_weight,
    out_weight,
    ffn_in_weight,
    ffn_in_bias,
    ffn_out_weight,
    ffn_out_bias,
):
    row_count, part, width = tokens.shape
    assert row_count == 1 and lax.axis_size("head") == 2
    seq = 2 * part
    shards = lax.axis_size("dp")
    below = shards // GROUPS
    assert below * GROUPS == shards
    heads = width // HEAD_DIM
    half = conv_weight.shape[2]
    ffn = left_weight.shape[1]
    side = lax.axis_index("head")
    group = lax.axis_index("dp") // below
    swap = [(0, 1), (1, 0)]
    slots = []
    for bit in (0, 1):
        for p in range(GROUPS // 2):
            slots.append(bit | ((p >> 2) & 1) << 1 | ((p >> 1) & 1) << 2 | (p & 1) << 3)
    meta = jnp.concatenate(
        [
            jnp.stack([side.astype(jnp.int32), lengths[0]]),
            group.astype(jnp.int32) ^ jnp.array(slots, jnp.int32),
        ]
    )

    mine = tokens[0]
    cot_mine = cotangent[0]
    other = lax.ppermute(mine, "head", swap)
    cot_other = lax.ppermute(cot_mine, "head", swap)
    vec = (
        jnp.concatenate(
            [mid_gain, mid_bias, left_bias, ffn_in_bias, glu_bias, conv_bias, point_bias, ffn_out_bias]
        )
        .astype(F32)
        .reshape(5, ffn)
    )

    def slot_outs(rows):
        return [((GROUPS // 2, rows, TILE), BF16)] * 2

    rows = width // GROUPS
    per_row = ffn // GROUPS
    ffn_rows = per_row + ffn // 2 // TILE * rows
    (
        out_tokens,
        stream,
        first,
        joined,
        after_glu,
        second,
        left_pre,
        right_pre,
        depth_low,
        after_conv,
        fourth,
        packed,
        probs,
        context,
        d_after,
        small_ffn,
        keep_ffn,
        send_ffn,
    ) = call(
        forward_kernel,
        [
            ((part, width), BF16),
            ((seq, width), BF16),
            ((seq, width), BF16),
            ((seq, 2 * width), F32),
            ((seq, width), F32),
            ((seq, width), BF16),
            ((seq, ffn), F32),
            ((seq, half), F32),
            ((seq, ffn), BF16),
            ((seq, width), F32),
            ((seq, width), BF16),
            ((seq, 3 * width), BF16),
            ((heads, seq, seq), F32),
            ((seq, width), BF16),
            ((seq, width), F32),
            ((8, ffn), F32),
        ]
        + slot_outs(ffn_rows),
        [
            ((ffn // LANES, seq + 16, LANES), F32),
            ((2, seq + 16, half), F32),
            ((seq, width), F32),
            ((seq, width), BF16),
            ((seq, ffn), BF16),
            ((seq, width), BF16),
            ((seq, ffn), BF16),
            ((seq, width), F32),
            ((width, TILE), F32),
        ],
        meta,
        mine,
        other,
        cot_mine,
        cot_other,
        vec,
        norm_gain,
        norm_bias,
        depth_weight,
        glu_weight,
        left_weight,
        conv_weight,
        point_weight,
        qkv_weight,
        out_weight,
        ffn_in_weight,
        ffn_out_weight,
    )
    d_after_conv, small_attn, keep_attn, send_attn = call(
        attention_back_kernel,
        [((seq, width), F32), ((8, ffn), F32)] + slot_outs(4 * rows + per_row // 2),
        [
            ((seq, width), BF16),
            ((seq, width), BF16),
            ((seq, 3 * width), BF16),
            ((seq, width), F32),
            ((seq, half), BF16),
            ((width, TILE), F32),
        ],
        meta,
        norm_gain,
        d_after,
        packed,
        probs,
        context,
        fourth,
        after_conv,
        depth_low,
        qkv_weight,
        out_weight,
    )
    d_second, small_conv, keep_conv, send_conv = call(
        conv_back_kernel,
        [((seq, width), F32), ((16, ffn), F32)] + slot_outs(ffn // 2 // TILE * rows + 3 * rows // 2),
        [
            ((ffn // LANES, seq, LANES), F32),
            ((ffn // LANES, seq, LANES), F32),
            ((ffn // LANES, seq + 16, LANES), F32),
            ((ffn // LANES, seq, LANES), F32),
            ((seq, LANES), F32),
            ((2, seq, LANES), F32),
            ((seq, ffn), BF16),
            ((seq + 16, half), F32),
            ((3, seq, half), BF16),
            ((width, TILE), F32),
            ((3, width, LANES), F32),
        ],
        meta,
        vec,
        depth_weight,
        d_after_conv,
        left_pre,
        right_pre,
        second,
        point_weight,
        left_weight,
        conv_weight,
    )
    grad_tokens, keep_glu, send_glu = call(
        glu_back_kernel,
        [((part, width), F32)] + slot_outs(width // TILE * rows + 16),
        [
            ((seq, 2 * width), BF16),
            ((seq, width), F32),
            ((seq, width), F32),
            ((2, 32, LANES), F32),
            ((GROUPS, 16, 2 * LANES), F32),
            ((width, TILE), F32),
        ],
        meta,
        norm_gain,
        d_second,
        d_after_conv,
        after_glu,
        joined,
        first,
        stream,
        glu_weight,
        small_ffn,
        small_attn,
        small_conv,
    )

    def reduced(keep, send):
        count = GROUPS // 2
        for bit in range(4):
            step = below << bit
            got = lax.ppermute(send, "dp", [(i, i ^ step) for i in range(shards)])
            count = count // 2

            def total(piece):
                return (keep[piece].astype(F32) + got[piece].astype(F32)).astype(BF16)

            if count == 0:
                keep = total(slice(0, 1))
            else:
                send = total(slice(count, 2 * count))
                keep = total(slice(0, count))
        keep = keep[0]
        step = 1
        while step < below:
            keep = keep + lax.ppermute(keep, "dp", [(i, i ^ step) for i in range(shards)])
            step *= 2
        return keep

    mine_ffn = reduced(keep_ffn, send_ffn)
    other_ffn = lax.ppermute(mine_ffn, "head", swap)
    mine_attn = reduced(keep_attn, send_attn)
    other_attn = lax.ppermute(mine_attn, "head", swap)
    mine_conv = reduced(keep_conv, send_conv)
    other_conv = lax.ppermute(mine_conv, "head", swap)
    mine_glu = reduced(keep_glu, send_glu)
    other_glu = lax.ppermute(mine_glu, "head", swap)
    ffn_out, ffn_in, out, qkv, point = call(
        finish_early_kernel,
        [
            ((per_row, width), F32),
            ((rows, ffn), F32),
            ((rows, width), F32),
            ((rows, 3 * width), F32),
            ((per_row, half), F32),
        ],
        [],
        meta,
        mine_ffn,
        other_ffn,
        mine_attn,
        other_attn,
    )
    left, conv, glu, gains, shifts, depth, vectors = call(
        finish_late_kernel,
        [
            ((rows, ffn), F32),
            ((3, rows, half), F32),
            ((rows, 2 * width), F32),
            ((4, rows), F32),
            ((4, rows), F32),
            ((9, LANES), F32),
            ((16, 2 * LANES), F32),
        ],
        [],
        meta,
        mine_conv,
        other_conv,
        mine_glu,
        other_glu,
    )
    results = (
        (glu, 0),
        (vectors[15, 0 : 2 * rows], 0),
        (gains, 1),
        (shifts, 1),
        (vectors[9, 0:LANES], 0),
        (vectors[10, 0:LANES], 0),
        (left, 0),
        (vectors[11, 0:LANES], 0),
        (conv, 1),
        (vectors[0:2, LANES:].reshape(-1), None),
        (depth, 1),
        (point, 0),
        (vectors[2:4, LANES:].reshape(-1), None),
        (qkv, 0),
        (out, 0),
        (ffn_in, 0),
        (vectors[12, 0:LANES], 0),
        (ffn_out, 0),
        (vectors[15, 2 * rows : 3 * rows], 0),
    )
    final = []
    for value, axis in results:
        if axis is not None and below > 1:
            size = value.shape[axis] // below
            value = lax.dynamic_slice_in_dim(value, lax.axis_index("dp") % below * size, size, axis)
        final.append(value)
    return (out_tokens[None], grad_tokens[None], *final)


def solution(mesh):
    return jax.shard_map(
        per_device,
        mesh=mesh,
        in_specs=(P("dp", "head", None), P("dp"), P("dp", "head", None)) + (P(),) * 19,
        out_specs=(
            P("dp", "head", None),
            P("dp", "head", None),
            P("dp", None),
            P("dp"),
            P(None, "dp"),
            P(None, "dp"),
            P("dp"),
            P("dp"),
            P("dp", None),
            P("dp"),
            P(None, "dp", None),
            P(),
            P(None, "dp"),
            P("dp", None),
            P(),
            P("dp", None),
            P("dp", None),
            P("dp", None),
            P("dp"),
            P("dp", None),
            P("dp"),
        ),
        check_vma=False,
    )
```

time: 246 us -> 154 us (0.63)
  Pallas kernels: 0 us -> 72.4 us
  waiting for transfers between devices: 85 us -> 35.2 us
  matrix products: 42.2 us -> 0 us
  other arithmetic: 43.7 us -> 2.16 us
  local copies, waits for them, and re-layouts: 52.1 us -> 12.3 us
  starting transfers between devices: 4.72 us -> 29.6 us
  between operations: 16.7 us -> 1.47 us
    reduce_scatter x1 -> x0, waiting for transfers between devices: 78.5 us -> none  [per_device(): total = lax.psum_scatter(buffer, 'dp', scatter_dimension=0, tiled=True)[0]]
    pallas_call x0 -> x6, Pallas kernels: none -> 72.4 us  [call(): pl.pallas_call(kernel, out_shape=tuple((jax.ShapeDtypeStruct(shape, dtype...]
    dot_general x29 -> x0, matrix products: 38.4 us -> none  [the longest x8 11.8 us: project_back(): jnp.einsum('te,de->td', incoming, weight, preferred_element_type=jnp.floa...]
    ppermute x3 -> x22, waiting for transfers between devices: 6.55 us -> 35.2 us  [the longest x16 30.3 us: reduced(): got = lax.ppermute(send, 'dp', [(i, i ^ step) for i in range(shards)])]
    ppermute x3 -> x22, starting transfers between devices: 4.68 us -> 29.6 us  [the longest x16 20.1 us: reduced(): got = lax.ppermute(send, 'dp', [(i, i ^ step) for i in range(shards)])]
    reduce_sum x20 -> x0, other arithmetic: 21 us -> none  [the longest x1 5.51 us: layer_norm(): return centred * lax.rsqrt(spread + EPSILON) * gain_vec + bias_vec]
    slice x27 -> x0, local copies, waits for them, and re-layouts: 14.7 us -> none  [the longest x5 3.4 us: shifted(): return jnp.concatenate([cells[offset:], blank], axis=0)]
    reshape x22 -> x1, local copies, waits for them, and re-layouts: 13.2 us -> 0.57 us  [per_device(): vectors[2:4, LANES:].reshape(-1)]
  transfers between devices with their start and end apart: 4 -> 22, of which waited for: 2 -> 12; matrix products, arithmetic and copies ran while one was open for 18% -> 7% of each run, Pallas kernels for 0% -> 1%
where the time goes in v2:
time: 154 us; the launch traced here: 153 us
  Pallas kernels  72.4 us (47%)
  waiting for transfers between devices  35.2 us (23%)
  starting transfers between devices  29.6 us (19%)
  local copies, waits for them, and re-layouts  12.3 us (8%)
  other arithmetic  2.16 us (1%)
    pallas_call x6, Pallas kernels, call(): pl.pallas_call(kernel, out_shape=tuple((jax.ShapeDtypeStruct(shape, dtype...  72.4 us
    ppermute x16, waiting for transfers between devices, reduced(): got = lax.ppermute(send, 'dp', [(i, i ^ step) for i in range(shards)])  30.3 us
    ppermute x16, starting transfers between devices, reduced(): got = lax.ppermute(send, 'dp', [(i, i ^ step) for i in range(shards)])  20.1 us
    unnamed x29, local copies, waits for them, and re-layouts  9.21 us
  transfers between devices with their start and end apart: 22, of which 12 were waited for; matrix products, arithmetic and copies ran while one was open for 7% of the time, Pallas kernels for 1%

profile of v2, /device:TPU:0, one launch (start us, length us, event | category | flops | bytes accessed | tf_op | source)
XLA Modules:
  0.0 153.1 jit_solution(15182058364671661737)
XLA Ops:
  0.7 3.0 %collective-permute-start = (bf16[128,512]{1,0:T(8,128)(2,1)}, bf16[128,512]{1,0:T(8,128)(2,1)S(1)}, u32[]{:S(2)}, u32[]{:S(2)}) collective-permute-start(bf16[128,512]{1,0:T(8,128)(2,1)} %bitcast.29), channel_id=1, source_target_pairs={{0,1},{1,0},{2,3},{3,2},{4,5},{5,4},{6,7},{7,6},{8,9},{9,8},{10,11... | collective-permute-start | bytes 393224 | tf_op jit(solution)/shard_map/ppermute | solution.py:793
  15.2 31.7 %forward_kernel.1 = (bf16[128,512]{1,0:T(8,128)(2,1)}, bf16[256,512]{1,0:T(8,128)(2,1)S(1)}, bf16[256,512]{1,0:T(8,128)(2,1)S(1)}, f32[256,1024]{1,0:T(8,128)}, ...) custom-call(s32[18]{0:T(128)S(1)} %pad_add_fusion.meta, ...), custom_call_target="tpu_custom_call" | custom-call | tf_op jit(solution)/shard_map/forward_kernel/pallas_call | solution.py:733
  47.0 13.3 %attention_back_kernel.1 = (f32[256,512]{1,0:T(8,128)S(1)}, f32[8,2048]{1,0:T(8,128)S(1)}, bf16[8,192,256]{2,1,0:T(8,128)(2,1)S(1)}, bf16[8,192,256]{2,1,0:T(8,128)(2,1)}) custom-call(s32[18]{0:T(128)S(1)} %pad_add_fusion.meta, bf16[4,512]{1,0:T(4,128)(2,1)S(1)} %copy-done.6, f32[256,512]{1,0:T(8,128)S(1)} %get-tuple-element.63.d_after, ...), custom_call_target="tpu_custom_call" | custom-call | tf_op jit(solution)/shard_map/attention_back_kernel/pallas_call | solution.py:733
  60.3 16.5 %conv_back_kernel.1 = (f32[256,512]{1,0:T(8,128)S(1)}, f32[16,2048]{1,0:T(8,128)S(1)}, bf16[8,176,256]{2,1,0:T(8,128)(2,1)S(1)}, bf16[8,176,256]{2,1,0:T(8,128)(2,1)S(1)}) custom-call(s32[18]{0:T(128)S(1)} %pad_add_fusion.meta, f32[5,2048]{1,0:T(8,128)S(1)} %reshape.54.vec, bf16[9,2048]{1,0:T(8,128)(2,1)S(1)} %copy-done.3, ...), custom_call_target="tpu_custom_call" | custom-call | tf_op jit(solution)/shard_map/conv_back_kernel/pallas_call | solution.py:733
  76.8 8.0 %glu_back_kernel.1 = (f32[128,512]{1,0:T(8,128)}, bf16[8,80,256]{2,1,0:T(8,128)(2,1)S(1)}, bf16[8,80,256]{2,1,0:T(8,128)(2,1)S(1)}) custom-call(s32[18]{0:T(128)S(1)} %pad_add_fusion.meta, bf16[4,512]{1,0:T(4,128)(2,1)S(1)} %copy-done.6, f32[256,512]{1,0:T(8,128)S(1)} %get-tuple-element.74.d_second, f32[256,512]{1,0:T(8,128)S(1)} %get-tuple-element.70.d_after_conv, ...), custom_call_target="tpu_custom_call" | custom-call | tf_op jit(solution)/shard_map/glu_back_kernel/pallas_call | solution.py:733
  85.3 1.1 collective-permute-done.7
  86.5 2.0 %collective-permute-start.8 = (bf16[4,80,256]{2,1,0:T(8,128)(2,1)S(1)}, bf16[4,80,256]{2,1,0:T(8,128)(2,1)S(1)}, u32[]{:S(2)}, u32[]{:S(2)}) collective-permute-start(bf16[4,80,256]{2,1,0:T(8,128)(2,1)S(1)} %get-tuple-element.116), channel_id=1, source_target_pairs={{0,4},{2,6},{4,0},{6,2},{8,12},{10,14},{12,8},{14,10},{16,20},{18,... | collective-permute-start | bytes 491528 | tf_op jit(solution)/shard_map/ppermute | solution.py:957
  88.5 4.5 %collective-permute-done.8 = bf16[4,80,256]{2,1,0:T(8,128)(2,1)S(1)} collective-permute-done((bf16[4,80,256]{2,1,0:T(8,128)(2,1)S(1)}, bf16[4,80,256]{2,1,0:T(8,128)(2,1)S(1)}, u32[]{:S(2)}, u32[]{:S(2)}) %collective-permute-start.8) | collective-permute-done | bytes 163872 | tf_op jit(solution)/shard_map/ppermute | solution.py:957
  93.1 1.9 %collective-permute-start.9 = (bf16[2,80,256]{2,1,0:T(8,128)(2,1)S(1)}, bf16[2,80,256]{2,1,0:T(8,128)(2,1)S(1)}, u32[]{:S(2)}, u32[]{:S(2)}) collective-permute-start(bf16[2,80,256]{2,1,0:T(8,128)(2,1)S(1)} %get-tuple-element.118), channel_id=1, source_target_pairs={{0,8},{2,10},{4,12},{6,14},{8,0},{10,2},{12,4},{14,6},{16,24},{18,... | collective-permute-start | bytes 245768 | tf_op jit(solution)/shard_map/ppermute | solution.py:957
  95.5 2.1 %collective-permute-done.9 = bf16[2,80,256]{2,1,0:T(8,128)(2,1)S(1)} collective-permute-done((bf16[2,80,256]{2,1,0:T(8,128)(2,1)S(1)}, bf16[2,80,256]{2,1,0:T(8,128)(2,1)S(1)}, u32[]{:S(2)}, u32[]{:S(2)}) %collective-permute-start.9) | collective-permute-done | bytes 81952 | tf_op jit(solution)/shard_map/ppermute | solution.py:957
  97.6 2.9 %collective-permute-start.10 = (bf16[1,80,256]{2,1,0:T(8,128)(2,1)S(1)}, bf16[1,80,256]{2,1,0:T(8,128)(2,1)S(1)}, u32[]{:S(2)}, u32[]{:S(2)}) collective-permute-start(bf16[1,80,256]{2,1,0:T(8,128)(2,1)S(1)} %add_convert_fusion.26), channel_id=1, source_target_pairs={{0,16},{2,18},{4,20},{6,22},{8,24},{10,26},{12,28},{14,30},{16,0},... | collective-permute-start | bytes 122888 | tf_op jit(solution)/shard_map/ppermute | solution.py:957
  100.7 1.6 %collective-permute-start.3 = (bf16[4,176,256]{2,1,0:T(8,128)(2,1)S(1)}, bf16[4,176,256]{2,1,0:T(8,128)(2,1)S(1)}, u32[]{:S(2)}, u32[]{:S(2)}) collective-permute-start(bf16[4,176,256]{2,1,0:T(8,128)(2,1)S(1)} %get-tuple-element.108), channel_id=1, source_target_pairs={{0,4},{2,6},{4,0},{6,2},{8,12},{10,14},{12,8},{14,10},{16,20},{18,... | collective-permute-start | bytes 1081352 | tf_op jit(solution)/shard_map/ppermute | solution.py:957
  102.6 1.8 %collective-permute-start.11 = (bf16[80,256]{1,0:T(8,128)(2,1)S(1)}, bf16[80,256]{1,0:T(8,128)(2,1)S(1)}, u32[]{:S(2)}, u32[]{:S(2)}) collective-permute-start(bf16[80,256]{1,0:T(8,128)(2,1)S(1)} %fusion.3.mine_glu), channel_id=1, source_target_pairs={{0,1},{1,0},{2,3},{3,2},{4,5},{5,4},{6,7},{7,6},{8,9},{9,8},{10,11... | collective-permute-start | bytes 122888 | tf_op jit(solution)/shard_map/ppermute | solution.py:982
  104.6 1.6 %collective-permute-start.18 = (bf16[4,192,256]{2,1,0:T(8,128)(2,1)S(1)}, bf16[4,192,256]{2,1,0:T(8,128)(2,1)S(1)}, u32[]{:S(2)}, u32[]{:S(2)}) collective-permute-start(bf16[4,192,256]{2,1,0:T(8,128)(2,1)S(1)} %get-tuple-element.106), channel_id=1, source_target_pairs={{0,4},{2,6},{4,0},{6,2},{8,12},{10,14},{12,8},{14,10},{16,20},{18,... | collective-permute-start | bytes 1179656 | tf_op jit(solution)/shard_map/ppermute | solution.py:957
  106.2 5.9 %collective-permute-done.3 = bf16[4,176,256]{2,1,0:T(8,128)(2,1)S(1)} collective-permute-done((bf16[4,176,256]{2,1,0:T(8,128)(2,1)S(1)}, bf16[4,176,256]{2,1,0:T(8,128)(2,1)S(1)}, u32[]{:S(2)}, u32[]{:S(2)}) %collective-permute-start.3) | collective-permute-done | bytes 360480 | tf_op jit(solution)/shard_map/ppermute | solution.py:957
  112.2 1.6 %collective-permute-start.4 = (bf16[2,176,256]{2,1,0:T(8,128)(2,1)S(1)}, bf16[2,176,256]{2,1,0:T(8,128)(2,1)S(1)}, u32[]{:S(2)}, u32[]{:S(2)}) collective-permute-start(bf16[2,176,256]{2,1,0:T(8,128)(2,1)S(1)} %get-tuple-element.114), channel_id=1, source_target_pairs={{0,8},{2,10},{4,12},{6,14},{8,0},{10,2},{12,4},{14,6},{16,24},{18,... | collective-permute-start | bytes 540680 | tf_op jit(solution)/shard_map/ppermute | solution.py:957
  114.2 1.6 %collective-permute-start.13 = (bf16[4,256,256]{2,1,0:T(8,128)(2,1)S(1)}, bf16[4,256,256]{2,1,0:T(8,128)(2,1)S(1)}, u32[]{:S(2)}, u32[]{:S(2)}) collective-permute-start(bf16[4,256,256]{2,1,0:T(8,128)(2,1)S(1)} %get-tuple-element.104), channel_id=1, source_target_pairs={{0,4},{2,6},{4,0},{6,2},{8,12},{10,14},{12,8},{14,10},{16,20},{18,... | collective-permute-start | bytes 1572872 | tf_op jit(solution)/shard_map/ppermute | solution.py:957
  115.8 2.6 %collective-permute-done.4 = bf16[2,176,256]{2,1,0:T(8,128)(2,1)S(1)} collective-permute-done((bf16[2,176,256]{2,1,0:T(8,128)(2,1)S(1)}, bf16[2,176,256]{2,1,0:T(8,128)(2,1)S(1)}, u32[]{:S(2)}, u32[]{:S(2)}) %collective-permute-start.4) | collective-permute-done | bytes 180256 | tf_op jit(solution)/shard_map/ppermute | solution.py:957
  119.2 1.4 collective-permute-done.18
  120.7 1.6 %collective-permute-start.19 = (bf16[2,192,256]{2,1,0:T(8,128)(2,1)S(1)}, bf16[2,192,256]{2,1,0:T(8,128)(2,1)S(1)}, u32[]{:S(2)}, u32[]{:S(2)}) collective-permute-start(bf16[2,192,256]{2,1,0:T(8,128)(2,1)S(1)} %get-tuple-element.112), channel_id=1, source_target_pairs={{0,8},{2,10},{4,12},{6,14},{8,0},{10,2},{12,4},{14,6},{16,24},{18,... | collective-permute-start | bytes 589832 | tf_op jit(solution)/shard_map/ppermute | solution.py:957
  122.3 3.7 %collective-permute-done.5 = bf16[1,176,256]{2,1,0:T(8,128)(2,1)S(1)} collective-permute-done((bf16[1,176,256]{2,1,0:T(8,128)(2,1)S(1)}, bf16[1,176,256]{2,1,0:T(8,128)(2,1)S(1)}, u32[]{:S(2)}, u32[]{:S(2)}) %collective-permute-start.5) | collective-permute-done | bytes 90144 | tf_op jit(solution)/shard_map/ppermute | solution.py:957
  126.0 1.6 %collective-permute-start.6 = (bf16[176,256]{1,0:T(8,128)(2,1)S(1)}, bf16[176,256]{1,0:T(8,128)(2,1)S(1)}, u32[]{:S(2)}, u32[]{:S(2)}) collective-permute-start(bf16[176,256]{1,0:T(8,128)(2,1)S(1)} %fusion.2.mine_conv), channel_id=1, source_target_pairs={{0,1},{1,0},{2,3},{3,2},{4,5},{5,4},{6,7},{7,6},{8,9},{9,8},{10,11... | collective-permute-start | bytes 270344 | tf_op jit(solution)/shard_map/ppermute | solution.py:980
  127.6 1.2 collective-permute-start.20
  128.8 1.8 %collective-permute-done.6.other_conv = bf16[176,256]{1,0:T(8,128)(2,1)S(1)} collective-permute-done((bf16[176,256]{1,0:T(8,128)(2,1)S(1)}, bf16[176,256]{1,0:T(8,128)(2,1)S(1)}, u32[]{:S(2)}, u32[]{:S(2)}) %collective-permute-start.6) | collective-permute-done | bytes 90144 | tf_op jit(solution)/shard_map/ppermute | solution.py:980
  130.6 1.4 finish_late_kernel.1
  134.2 4.9 %collective-permute-done.14 = bf16[2,256,256]{2,1,0:T(8,128)(2,1)S(1)} collective-permute-done((bf16[2,256,256]{2,1,0:T(8,128)(2,1)S(1)}, bf16[2,256,256]{2,1,0:T(8,128)(2,1)S(1)}, u32[]{:S(2)}, u32[]{:S(2)}) %collective-permute-start.14) | collective-permute-done | bytes 262176 | tf_op jit(solution)/shard_map/ppermute | solution.py:957
  139.1 2.0 %collective-permute-start.15 = (bf16[1,256,256]{2,1,0:T(8,128)(2,1)S(1)}, bf16[1,256,256]{2,1,0:T(8,128)(2,1)S(1)}, u32[]{:S(2)}, u32[]{:S(2)}) collective-permute-start(bf16[1,256,256]{2,1,0:T(8,128)(2,1)S(1)} %add_convert_fusion.15), channel_id=1, source_target_pairs={{0,16},{2,18},{4,20},{6,22},{8,24},{10,26},{12,28},{14,30},{16,0},... | collective-permute-start | bytes 393224 | tf_op jit(solution)/shard_map/ppermute | solution.py:957
  141.2 1.6 %collective-permute-start.21 = (bf16[192,256]{1,0:T(8,128)(2,1)S(1)}, bf16[192,256]{1,0:T(8,128)(2,1)S(1)}, u32[]{:S(2)}, u32[]{:S(2)}) collective-permute-start(bf16[192,256]{1,0:T(8,128)(2,1)S(1)} %fusion.1.mine_attn), channel_id=1, source_target_pairs={{0,1},{1,0},{2,3},{3,2},{4,5},{5,4},{6,7},{7,6},{8,9},{9,8},{10,11... | collective-permute-start | bytes 294920 | tf_op jit(solution)/shard_map/ppermute | solution.py:978
  142.7 3.7 %collective-permute-done.15 = bf16[1,256,256]{2,1,0:T(8,128)(2,1)S(1)} collective-permute-done((bf16[1,256,256]{2,1,0:T(8,128)(2,1)S(1)}, bf16[1,256,256]{2,1,0:T(8,128)(2,1)S(1)}, u32[]{:S(2)}, u32[]{:S(2)}) %collective-permute-start.15) | collective-permute-done | bytes 131104 | tf_op jit(solution)/shard_map/ppermute | solution.py:957
  146.5 1.4 collective-permute-start.16
  148.5 3.1 %collective-permute-done.16.other_ffn = bf16[256,256]{1,0:T(8,128)(2,1)S(1)} collective-permute-done((bf16[256,256]{1,0:T(8,128)(2,1)S(1)}, bf16[256,256]{1,0:T(8,128)(2,1)S(1)}, u32[]{:S(2)}, u32[]{:S(2)}) %collective-permute-start.16) | collective-permute-done | bytes 131104 | tf_op jit(solution)/shard_map/ppermute | solution.py:976
  151.5 1.5 finish_early_kernel.1
  (71 shorter events, 17.0 us)
Async XLA Ops:
  0.7 10.5 %collective-permute-start = (bf16[128,512]{1,0:T(8,128)(2,1)}, bf16[128,512]{1,0:T(8,128)(2,1)S(1)}, u32[]{:S(2)}, u32[]{:S(2)}) collective-permute-start(bf16[128,512]{1,0:T(8,128)(2,1)} %bitcast.29), channel_id=1, source_target_pairs={{0,1},{1,0},{2,3},{3,2},{4,5},{5,4},{6,7},{7,6},{8,9},{9,8},{10,11... | collective-permute-start | bytes 393224 | tf_op jit(solution)/shard_map/ppermute | solution.py:793
  3.7 7.5 %collective-permute-start.1 = (bf16[128,512]{1,0:T(8,128)(2,1)}, bf16[128,512]{1,0:T(8,128)(2,1)S(1)}, u32[]{:S(2)}, u32[]{:S(2)}) collective-permute-start(bf16[128,512]{1,0:T(8,128)(2,1)} %bitcast.31), channel_id=1, source_target_pairs={{0,1},{1,0},{2,3},{3,2},{4,5},{5,4},{6,7},{7,6},{8,9},{9,8},{10,11... | collective-permute-start | bytes 393224 | tf_op jit(solution)/shard_map/ppermute | solution.py:794
  11.1 35.8 %copy-start.1 = (bf16[512,512]{1,0:T(8,128)(2,1)S(1)}, bf16[512,512]{1,0:T(8,128)(2,1)}, u32[]{:S(2)}) copy-start(bf16[512,512]{1,0:T(8,128)(2,1)} %out_w.3) | copy-start | bytes 1572868
  11.2 0.9 copy-start.3
  12.1 0.9 copy-start.4
  13.0 0.9 copy-start.5
  13.9 0.7 copy-start.6
  47.0 13.3 %copy-start = (bf16[3,512,256]{2,1,0:T(8,128)(2,1)S(1)}, bf16[3,512,256]{2,1,0:T(8,128)(2,1)}, u32[]{:S(2)}) copy-start(bf16[3,512,256]{2,1,0:T(8,128)(2,1)} %conv_w.3) | copy-start | bytes 2359300
  60.3 16.5 %copy-start.2 = (f32[256,1024]{1,0:T(8,128)S(1)}, f32[256,1024]{1,0:T(8,128)}, u32[]{:S(2)}) copy-start(f32[256,1024]{1,0:T(8,128)} %get-tuple-element.76.joined) | copy-start | bytes 3145732
  76.8 18.2 %copy-start.10 = (bf16[8,192,256]{2,1,0:T(8,128)(2,1)S(1)}, bf16[8,192,256]{2,1,0:T(8,128)(2,1)}, u32[]{:S(2)}) copy-start(bf16[8,192,256]{2,1,0:T(8,128)(2,1)} %get-tuple-element.97) | copy-start | bytes 2359300
  76.8 18.2 %copy-start.9 = (bf16[8,256,256]{2,1,0:T(8,128)(2,1)S(1)}, bf16[8,256,256]{2,1,0:T(8,128)(2,1)}, u32[]{:S(2)}) copy-start(bf16[8,256,256]{2,1,0:T(8,128)(2,1)} %get-tuple-element.95) | copy-start | bytes 3145732
  84.8 1.6 %collective-permute-start.7 = (bf16[8,80,256]{2,1,0:T(8,128)(2,1)S(1)}, bf16[8,80,256]{2,1,0:T(8,128)(2,1)S(1)}, u32[]{:S(2)}, u32[]{:S(2)}) collective-permute-start(bf16[8,80,256]{2,1,0:T(8,128)(2,1)S(1)} %get-tuple-element.86), channel_id=1, source_target_pairs={{0,2},{2,0},{4,6},{6,4},{8,10},{10,8},{12,14},{14,12},{16,18},{18,... | collective-permute-start | bytes 983048 | tf_op jit(solution)/shard_map/ppermute | solution.py:957
  84.8 15.7 %collective-permute-start.2 = (bf16[8,176,256]{2,1,0:T(8,128)(2,1)S(1)}, bf16[8,176,256]{2,1,0:T(8,128)(2,1)S(1)}, u32[]{:S(2)}, u32[]{:S(2)}) collective-permute-start(bf16[8,176,256]{2,1,0:T(8,128)(2,1)S(1)} %get-tuple-element.84), channel_id=1, source_target_pairs={{0,2},{2,0},{4,6},{6,4},{8,10},{10,8},{12,14},{14,12},{16,18},{18,... | collective-permute-start | bytes 2162696 | tf_op jit(solution)/shard_map/ppermute | solution.py:957
  86.5 6.5 %collective-permute-start.8 = (bf16[4,80,256]{2,1,0:T(8,128)(2,1)S(1)}, bf16[4,80,256]{2,1,0:T(8,128)(2,1)S(1)}, u32[]{:S(2)}, u32[]{:S(2)}) collective-permute-start(bf16[4,80,256]{2,1,0:T(8,128)(2,1)S(1)} %get-tuple-element.116), channel_id=1, source_target_pairs={{0,4},{2,6},{4,0},{6,2},{8,12},{10,14},{12,8},{14,10},{16,20},{18,... | collective-permute-start | bytes 491528 | tf_op jit(solution)/shard_map/ppermute | solution.py:957
  93.1 4.5 %collective-permute-start.9 = (bf16[2,80,256]{2,1,0:T(8,128)(2,1)S(1)}, bf16[2,80,256]{2,1,0:T(8,128)(2,1)S(1)}, u32[]{:S(2)}, u32[]{:S(2)}) collective-permute-start(bf16[2,80,256]{2,1,0:T(8,128)(2,1)S(1)} %get-tuple-element.118), channel_id=1, source_target_pairs={{0,8},{2,10},{4,12},{6,14},{8,0},{10,2},{12,4},{14,6},{16,24},{18,... | collective-permute-start | bytes 245768 | tf_op jit(solution)/shard_map/ppermute | solution.py:957
  95.0 9.4 %collective-permute-start.17 = (bf16[8,192,256]{2,1,0:T(8,128)(2,1)S(1)}, bf16[8,192,256]{2,1,0:T(8,128)(2,1)S(1)}, u32[]{:S(2)}, u32[]{:S(2)}) collective-permute-start(bf16[8,192,256]{2,1,0:T(8,128)(2,1)S(1)} %copy-done.10), channel_id=1, source_target_pairs={{0,2},{2,0},{4,6},{6,4},{8,10},{10,8},{12,14},{14,12},{16,18},{18,... | collective-permute-start | bytes 2359304 | tf_op jit(solution)/shard_map/ppermute | solution.py:957
  95.0 18.9 %collective-permute-start.12 = (bf16[8,256,256]{2,1,0:T(8,128)(2,1)S(1)}, bf16[8,256,256]{2,1,0:T(8,128)(2,1)S(1)}, u32[]{:S(2)}, u32[]{:S(2)}) collective-permute-start(bf16[8,256,256]{2,1,0:T(8,128)(2,1)S(1)} %copy-done.9), channel_id=1, source_target_pairs={{0,2},{2,0},{4,6},{6,4},{8,10},{10,8},{12,14},{14,12},{16,18},{18,... | collective-permute-start | bytes 3145736 | tf_op jit(solution)/shard_map/ppermute | solution.py:957
  97.6 5.0 %collective-permute-start.10 = (bf16[1,80,256]{2,1,0:T(8,128)(2,1)S(1)}, bf16[1,80,256]{2,1,0:T(8,128)(2,1)S(1)}, u32[]{:S(2)}, u32[]{:S(2)}) collective-permute-start(bf16[1,80,256]{2,1,0:T(8,128)(2,1)S(1)} %add_convert_fusion.26), channel_id=1, source_target_pairs={{0,16},{2,18},{4,20},{6,22},{8,24},{10,26},{12,28},{14,30},{16,0},... | collective-permute-start | bytes 122888 | tf_op jit(solution)/shard_map/ppermute | solution.py:957
  100.7 13.2 %copy-start.8 = (bf16[8,256,256]{2,1,0:T(8,128)(2,1)S(1)}, bf16[8,256,256]{2,1,0:T(8,128)(2,1)}, u32[]{:S(2)}) copy-start(bf16[8,256,256]{2,1,0:T(8,128)(2,1)} %get-tuple-element.94) | copy-start | bytes 3145732
  100.7 11.4 %collective-permute-start.3 = (bf16[4,176,256]{2,1,0:T(8,128)(2,1)S(1)}, bf16[4,176,256]{2,1,0:T(8,128)(2,1)S(1)}, u32[]{:S(2)}, u32[]{:S(2)}) collective-permute-start(bf16[4,176,256]{2,1,0:T(8,128)(2,1)S(1)} %get-tuple-element.108), channel_id=1, source_target_pairs={{0,4},{2,6},{4,0},{6,2},{8,12},{10,14},{12,8},{14,10},{16,20},{18,... | collective-permute-start | bytes 1081352 | tf_op jit(solution)/shard_map/ppermute | solution.py:957
  102.6 26.2 %collective-permute-start.11 = (bf16[80,256]{1,0:T(8,128)(2,1)S(1)}, bf16[80,256]{1,0:T(8,128)(2,1)S(1)}, u32[]{:S(2)}, u32[]{:S(2)}) collective-permute-start(bf16[80,256]{1,0:T(8,128)(2,1)S(1)} %fusion.3.mine_glu), channel_id=1, source_target_pairs={{0,1},{1,0},{2,3},{3,2},{4,5},{5,4},{6,7},{7,6},{8,9},{9,8},{10,11... | collective-permute-start | bytes 122888 | tf_op jit(solution)/shard_map/ppermute | solution.py:982
  104.6 15.9 %collective-permute-start.18 = (bf16[4,192,256]{2,1,0:T(8,128)(2,1)S(1)}, bf16[4,192,256]{2,1,0:T(8,128)(2,1)S(1)}, u32[]{:S(2)}, u32[]{:S(2)}) collective-permute-start(bf16[4,192,256]{2,1,0:T(8,128)(2,1)S(1)} %get-tuple-element.106), channel_id=1, source_target_pairs={{0,4},{2,6},{4,0},{6,2},{8,12},{10,14},{12,8},{14,10},{16,20},{18,... | collective-permute-start | bytes 1179656 | tf_op jit(solution)/shard_map/ppermute | solution.py:957
  112.2 6.2 %collective-permute-start.4 = (bf16[2,176,256]{2,1,0:T(8,128)(2,1)S(1)}, bf16[2,176,256]{2,1,0:T(8,128)(2,1)S(1)}, u32[]{:S(2)}, u32[]{:S(2)}) collective-permute-start(bf16[2,176,256]{2,1,0:T(8,128)(2,1)S(1)} %get-tuple-element.114), channel_id=1, source_target_pairs={{0,8},{2,10},{4,12},{6,14},{8,0},{10,2},{12,4},{14,6},{16,24},{18,... | collective-permute-start | bytes 540680 | tf_op jit(solution)/shard_map/ppermute | solution.py:957
  114.2 18.3 %collective-permute-start.13 = (bf16[4,256,256]{2,1,0:T(8,128)(2,1)S(1)}, bf16[4,256,256]{2,1,0:T(8,128)(2,1)S(1)}, u32[]{:S(2)}, u32[]{:S(2)}) collective-permute-start(bf16[4,256,256]{2,1,0:T(8,128)(2,1)S(1)} %get-tuple-element.104), channel_id=1, source_target_pairs={{0,4},{2,6},{4,0},{6,2},{8,12},{10,14},{12,8},{14,10},{16,20},{18,... | collective-permute-start | bytes 1572872 | tf_op jit(solution)/shard_map/ppermute | solution.py:957
  118.4 7.5 %collective-permute-start.5 = (bf16[1,176,256]{2,1,0:T(8,128)(2,1)S(1)}, bf16[1,176,256]{2,1,0:T(8,128)(2,1)S(1)}, u32[]{:S(2)}, u32[]{:S(2)}) collective-permute-start(bf16[1,176,256]{2,1,0:T(8,128)(2,1)S(1)} %add_convert_fusion.21), channel_id=1, source_target_pairs={{0,16},{2,18},{4,20},{6,22},{8,24},{10,26},{12,28},{14,30},{16,0},... | collective-permute-start | bytes 270344 | tf_op jit(solution)/shard_map/ppermute | solution.py:957
  120.7 6.9 %collective-permute-start.19 = (bf16[2,192,256]{2,1,0:T(8,128)(2,1)S(1)}, bf16[2,192,256]{2,1,0:T(8,128)(2,1)S(1)}, u32[]{:S(2)}, u32[]{:S(2)}) collective-permute-start(bf16[2,192,256]{2,1,0:T(8,128)(2,1)S(1)} %get-tuple-element.112), channel_id=1, source_target_pairs={{0,8},{2,10},{4,12},{6,14},{8,0},{10,2},{12,4},{14,6},{16,24},{18,... | collective-permute-start | bytes 589832 | tf_op jit(solution)/shard_map/ppermute | solution.py:957
  126.0 4.6 %collective-permute-start.6 = (bf16[176,256]{1,0:T(8,128)(2,1)S(1)}, bf16[176,256]{1,0:T(8,128)(2,1)S(1)}, u32[]{:S(2)}, u32[]{:S(2)}) collective-permute-start(bf16[176,256]{1,0:T(8,128)(2,1)S(1)} %fusion.2.mine_conv), channel_id=1, source_target_pairs={{0,1},{1,0},{2,3},{3,2},{4,5},{5,4},{6,7},{7,6},{8,9},{9,8},{10,11... | collective-permute-start | bytes 270344 | tf_op jit(solution)/shard_map/ppermute | solution.py:980
  127.6 13.5 %collective-permute-start.20 = (bf16[1,192,256]{2,1,0:T(8,128)(2,1)S(1)}, bf16[1,192,256]{2,1,0:T(8,128)(2,1)S(1)}, u32[]{:S(2)}, u32[]{:S(2)}) collective-permute-start(bf16[1,192,256]{2,1,0:T(8,128)(2,1)S(1)} %add_convert_fusion.18), channel_id=1, source_target_pairs={{0,16},{2,18},{4,20},{6,22},{8,24},{10,26},{12,28},{14,30},{16,0},... | collective-permute-start | bytes 294920 | tf_op jit(solution)/shard_map/ppermute | solution.py:957
  132.6 6.4 %collective-permute-start.14 = (bf16[2,256,256]{2,1,0:T(8,128)(2,1)S(1)}, bf16[2,256,256]{2,1,0:T(8,128)(2,1)S(1)}, u32[]{:S(2)}, u32[]{:S(2)}) collective-permute-start(bf16[2,256,256]{2,1,0:T(8,128)(2,1)S(1)} %get-tuple-element.110), channel_id=1, source_target_pairs={{0,8},{2,10},{4,12},{6,14},{8,0},{10,2},{12,4},{14,6},{16,24},{18,... | collective-permute-start | bytes 786440 | tf_op jit(solution)/shard_map/ppermute | solution.py:957
  139.1 7.3 %collective-permute-start.15 = (bf16[1,256,256]{2,1,0:T(8,128)(2,1)S(1)}, bf16[1,256,256]{2,1,0:T(8,128)(2,1)S(1)}, u32[]{:S(2)}, u32[]{:S(2)}) collective-permute-start(bf16[1,256,256]{2,1,0:T(8,128)(2,1)S(1)} %add_convert_fusion.15), channel_id=1, source_target_pairs={{0,16},{2,18},{4,20},{6,22},{8,24},{10,26},{12,28},{14,30},{16,0},... | collective-permute-start | bytes 393224 | tf_op jit(solution)/shard_map/ppermute | solution.py:957
  141.2 7.3 %collective-permute-start.21 = (bf16[192,256]{1,0:T(8,128)(2,1)S(1)}, bf16[192,256]{1,0:T(8,128)(2,1)S(1)}, u32[]{:S(2)}, u32[]{:S(2)}) collective-permute-start(bf16[192,256]{1,0:T(8,128)(2,1)S(1)} %fusion.1.mine_attn), channel_id=1, source_target_pairs={{0,1},{1,0},{2,3},{3,2},{4,5},{5,4},{6,7},{7,6},{8,9},{9,8},{10,11... | collective-permute-start | bytes 294920 | tf_op jit(solution)/shard_map/ppermute | solution.py:978
  146.5 5.0 %collective-permute-start.16 = (bf16[256,256]{1,0:T(8,128)(2,1)S(1)}, bf16[256,256]{1,0:T(8,128)(2,1)S(1)}, u32[]{:S(2)}, u32[]{:S(2)}) collective-permute-start(bf16[256,256]{1,0:T(8,128)(2,1)S(1)} %fusion.mine_ffn), channel_id=1, source_target_pairs={{0,1},{1,0},{2,3},{3,2},{4,5},{5,4},{6,7},{7,6},{8,9},{9,8},{10,11... | collective-permute-start | bytes 393224 | tf_op jit(solution)/shard_map/ppermute | solution.py:976
  (1 other events, 0.7 us)

commit v3 on v2

v3 whole, which is shorter than its diff:
```python
import functools

import jax
import jax.numpy as jnp
from jax import lax
from jax.experimental import pallas as pl
from jax.experimental.pallas import tpu as pltpu
from jax.sharding import PartitionSpec as P

HEAD_DIM = 64
EPSILON = 1e-06
LANES = 128
TILE = 256
GROUPS = 16
F32 = jnp.float32
BF16 = jnp.bfloat16
VMEM_BYTES = 40 * 1024 * 1024
FFN_BITS = (2, 1, 3)
ATTN_BITS = (1, 2, 3)
CONV_BITS = (1, 2, 3)
GLU_BITS = (1, 2, 3)


def mm(a, b):
    return lax.dot_general(a, b, (((1,), (0,)), ((), ())), preferred_element_type=F32)


def mm_nt(a, b):
    return lax.dot_general(a, b, (((1,), (1,)), ((), ())), preferred_element_type=F32)


def mm_tn(a, b):
    return lax.dot_general(a, b, (((0,), (0,)), ((), ())), preferred_element_type=F32)


def mean(v):
    return jnp.mean(v, axis=-1, keepdims=True)


def normalized(v):
    centred = v - mean(v)
    rate = lax.rsqrt(mean(centred * centred) + EPSILON)
    return centred * rate, rate


def norm_back(vhat, rate, gained):
    return (gained - mean(gained) - vhat * mean(gained * vhat)) * rate


def sum_tokens(v):
    return jnp.sum(v, axis=0, keepdims=True)


def part_sums(v):
    return jnp.sum(v.reshape(v.shape[0] // 8, 8, v.shape[1]), axis=0)


def row_blocks(total, step, body, carry=0, unroll=1):
    def visit(i, c):
        return body(pl.multiple_of(i * step, step), c)

    return lax.fori_loop(0, total // step, visit, carry, unroll=unroll)


def valid_rows(start, count, length):
    places = start + lax.broadcasted_iota(jnp.int32, (count, 1), 0)
    return (places < length).astype(F32)


def col(n, width=TILE):
    return slice(n * width, (n + 1) * width)


def vector(ref):
    return ref[...].astype(F32).reshape(1, ref.shape[0])


def slot_block(p, sent, bits):
    group = lax.axis_index("dp") // (lax.axis_size("dp") // GROUPS)
    wanted = ((p >> 2) & 1) << bits[0] | ((p >> 1) & 1) << bits[1] | (p & 1) << bits[2]
    return group ^ (wanted | sent)


def for_slots(keep, send, bits, body):
    def visit(p, c):
        for sent, out in ((0, keep), (1, send)):
            body(p, slot_block(p, sent, bits), out)
        return c

    lax.fori_loop(0, GROUPS // 2, visit, 0)


def place_rows(grad, keep, send, bits, at, rows):
    def one(p, block, out):
        out[p, at : at + rows, :] = grad[pl.ds(pl.multiple_of(block * rows, rows), rows), :].astype(BF16)

    for_slots(keep, send, bits, one)


def forward_kernel(
    lengths,
    other,
    cot_other,
    far,
    out_tokens,
    stream,
    first,
    joined,
    after_glu,
    second,
    left_pre,
    right_pre,
    depth_low,
    after_conv,
    fourth,
    packed,
    probs,
    context,
    d_after,
    small,
    keep,
    send,
    third,
    sides,
    after_attn,
    fifth,
    hidden,
    cot,
    d_hidden,
    d_fifth,
    grad,
):
    part, width = other.shape
    seq = 2 * part
    ffn = left_pre.shape[1]
    half = right_pre.shape[1]
    side = lax.axis_index("head")
    length = lengths[0]
    own = pl.ds(pl.multiple_of(side * part, part), part)
    opposite = pl.ds(pl.multiple_of((1 - side) * part, part), part)
    (
        mine,
        gains,
        shifts,
        glu_bias,
        glu_w,
        conv_bias,
        conv_w,
        left_bias,
        left_w,
        mid_gain,
        mid_bias,
        depth_w,
        point_bias,
        point_w,
        qkv_w,
        out_w,
        ffn_in_bias,
        ffn_in_w,
        ffn_out_bias,
        ffn_out_w,
        cot_mine,
    ) = far
    stream[opposite, :] = other[...]
    cot[opposite, :] = cot_other[...]
    stream[own, :] = mine()[...]
    gains, shifts = gains(), shifts()
    gain = [gains[k : k + 1, :].astype(F32) for k in range(4)]
    shift = [shifts[k : k + 1, :].astype(F32) for k in range(4)]

    def first_rows(r, c):
        rows = pl.ds(r, 64)
        vhat, _ = normalized(stream[rows, :].astype(F32))
        first[rows, :] = (vhat * gain[0] + shift[0]).astype(BF16)
        return c

    row_blocks(seq, 64, first_rows, unroll=2)
    glu_b, glu_w = vector(glu_bias()), glu_w()
    for n in range(2 * width // TILE):
        joined[:, col(n)] = mm(first[...], glu_w[:, col(n)]) + glu_b[:, col(n)]

    def glu_rows(r, c):
        rows = pl.ds(r, 32)
        gate = jax.nn.sigmoid(joined[rows, width:])
        joined[rows, width:] = gate
        v = stream[rows, :].astype(F32) + joined[rows, :width] * gate
        after_glu[rows, :] = v
        vhat, _ = normalized(v)
        second[rows, :] = ((vhat * gain[1] + shift[1]) * valid_rows(r, 32, length)).astype(BF16)
        return c

    row_blocks(seq, 32, glu_rows, unroll=2)
    blank = jnp.zeros((8, half), F32)
    for k in range(2):
        sides[k, 0:8, :] = blank
        sides[k, 8 + seq : 16 + seq, :] = blank
    conv_w = conv_w()
    sides[0, 8 : 8 + seq, :] = mm(second[...], conv_w[0])
    sides[1, 8 : 8 + seq, :] = mm(second[...], conv_w[2])
    right_pre[...] = mm(second[...], conv_w[1]) + vector(conv_bias())
    right_pre[...] = right_pre[...] + sides[0, 7 : 7 + seq, :] + sides[1, 9 : 9 + seq, :]
    left_b, left_w = vector(left_bias()), left_w()
    for n in range(ffn // TILE):
        left_pre[:, col(n)] = mm(second[...], left_w[:, col(n)]) + left_b[:, col(n)]
    mid_g, mid_b, depth_w = vector(mid_gain()), vector(mid_bias()), depth_w()
    chunks = ffn // LANES
    edge = jnp.zeros((8, LANES), F32)
    for k in range(chunks):
        third[k, 0:8, :] = edge
        third[k, 8 + seq : 16 + seq, :] = edge

    def mid_rows(r, c):
        rows = pl.ds(r, 16)
        vhat, _ = normalized(combine(left_pre[rows, :], right_pre[rows, :]))
        v = (vhat * mid_g + mid_b) * valid_rows(r, 16, length)
        for k in range(chunks):
            third[k, pl.ds(pl.multiple_of(8 + r, 8), 16), :] = v[:, col(k, LANES)]
        return c

    row_blocks(seq, 16, mid_rows, unroll=2)

    def depth_lanes(k, c):
        lanes = pl.ds(pl.multiple_of(k * LANES, LANES), LANES)
        taps = depth_w[:, lanes].astype(F32)
        total = third[k, 4 : 4 + seq, :] * taps[0:1, :]
        for j in range(1, 9):
            total = total + third[k, 4 + j : 4 + j + seq, :] * taps[j : j + 1, :]
        depth_low[:, lanes] = total.astype(BF16)
        return c

    lax.fori_loop(0, chunks, depth_lanes, 0)
    after_conv[:, :half] = (
        after_glu[:, :half] + mm(depth_low[...], point_w()[...]) + vector(point_bias())
    )
    after_conv[:, half:] = after_glu[:, half:]

    def fourth_rows(r, c):
        rows = pl.ds(r, 64)
        vhat, _ = normalized(after_conv[rows, :])
        fourth[rows, :] = (vhat * gain[2] + shift[2]).astype(BF16)
        return c

    row_blocks(seq, 64, fourth_rows, unroll=2)
    qkv_w = qkv_w()
    for n in range(3 * width // TILE):
        packed[:, col(n)] = mm(fourth[...], qkv_w[:, col(n)]).astype(BF16)

    low_lanes = lax.broadcasted_iota(jnp.int32, (1, LANES), 1) < HEAD_DIM
    scale = HEAD_DIM ** (-0.5)

    def head_pair(p, c):
        lanes = pl.ds(pl.multiple_of(p * LANES, LANES), LANES)
        q = packed[:, lanes].astype(F32) * scale
        k = packed[:, pl.ds(pl.multiple_of(width + p * LANES, LANES), LANES)]
        v = packed[:, pl.ds(pl.multiple_of(2 * width + p * LANES, LANES), LANES)]
        open_keys = lax.broadcasted_iota(jnp.int32, (seq, 1), 0) < length
        results = []
        for e in range(2):
            q_one = jnp.where(low_lanes if e == 0 else ~low_lanes, q, 0.0).astype(BF16)
            s = jnp.where(open_keys, mm_nt(k, q_one), -1000000000.0)
            raised = jnp.exp(s - jnp.max(s, axis=0, keepdims=True))
            chance = raised * (1.0 / jnp.sum(raised, axis=0, keepdims=True))
            probs[2 * p + e] = chance
            results.append(mm_tn(v, chance.astype(BF16)))
        both = jnp.concatenate([results[0][:HEAD_DIM], results[1][HEAD_DIM:]], axis=0)
        context[:, lanes] = both.T.astype(BF16)
        return c

    lax.fori_loop(0, width // LANES, head_pair, 0)
    out_w = out_w()
    for n in range(width // TILE):
        after_attn[:, col(n)] = after_conv[:, col(n)] + mm(context[...], out_w[:, col(n)])

    def fifth_rows(r, c):
        rows = pl.ds(r, 64)
        vhat, _ = normalized(after_attn[rows, :])
        fifth[rows, :] = (vhat * gain[3] + shift[3]).astype(BF16)
        return c

    row_blocks(seq, 64, fifth_rows, unroll=2)
    ffn_in_b, ffn_in_w = vector(ffn_in_bias()), ffn_in_w()
    for n in range(ffn // TILE):
        pre = mm(fifth[...], ffn_in_w[:, col(n)]) + ffn_in_b[:, col(n)]
        hidden[:, col(n)] = jnp.where(pre > 0.0, pre, 0.0).astype(BF16)
    ffn_out_b, ffn_out_w = vector(ffn_out_bias()), ffn_out_w()
    for n in range(width // TILE):
        out_tokens[:, col(n)] = (
            after_attn[own, col(n)]
            + mm(hidden[own, :], ffn_out_w[:, col(n)])
            + ffn_out_b[:, col(n)]
        ).astype(BF16)

    cot[own, :] = cot_mine()[...]
    for n in range(ffn // TILE):
        back = mm_nt(cot[...], ffn_out_w[col(n), :])
        back = jnp.where(hidden[:, col(n)].astype(F32) > 0.0, back, 0.0).astype(BF16)
        d_hidden[:, col(n)] = back
        small[0:1, col(n)] = sum_tokens(back.astype(F32))
    for n in range(width // TILE):
        d_fifth[:, col(n)] = mm_nt(d_hidden[...], ffn_in_w[col(n), :])

    cot_half = cot[:, pl.ds(pl.multiple_of(side * (width // 2), width // 2), width // 2)]
    per_row = ffn // GROUPS
    sums = [jnp.zeros((8, width), F32)] * 3
    for p in range(GROUPS // 2):
        block = slice(p * seq // 8, (p + 1) * seq // 8)
        vhat, rate = normalized(after_attn[block, :])
        e = d_fifth[block, :]
        given = cot[block, :].astype(F32)
        d_after[block, :] = given + norm_back(vhat, rate, e * gain[3])
        sums = [total + part_sums(v) for total, v in zip(sums, (e * vhat, e, given))]
        for sent, out in ((0, keep), (1, send)):
            at = pl.multiple_of(slot_block(p, sent, FFN_BITS) * per_row, per_row)
            out[p, 0:per_row, :] = mm_tn(hidden[:, pl.ds(at, per_row)], cot_half).astype(BF16)
    for k in range(3):
        small[1:2, k * width : (k + 1) * width] = sum_tokens(sums[k])

    rows = width // GROUPS
    for j in range(ffn // 2 // TILE):
        at = pl.multiple_of(side * (ffn // 2) + j * TILE, TILE)
        grad[...] = mm_tn(fifth[...], d_hidden[:, pl.ds(at, TILE)])
        place_rows(grad, keep, send, FFN_BITS, per_row + j * rows, rows)


def combine(left_pre, right_pre):
    half = right_pre.shape[1]
    left = jnp.maximum(left_pre, 0.0)
    return jnp.concatenate([left[:, :half] + jnp.maximum(right_pre, 0.0), left[:, half:]], axis=1)


def attention_back_kernel(
    d_after,
    packed,
    probs,
    context,
    fourth,
    after_conv,
    depth_low,
    far,
    d_after_conv,
    small,
    keep,
    send,
    d_attn,
    d_context,
    d_packed,
    d_fourth,
    d_sep,
    grad,
):
    seq, width = d_after.shape
    side = lax.axis_index("head")
    out_w, qkv_w, gains = far
    half = d_sep.shape[1]
    ffn = depth_low.shape[1]
    rows = width // GROUPS
    d_attn[...] = d_after[...].astype(BF16)
    out_w = out_w()
    for n in range(width // TILE):
        d_context[:, col(n)] = mm_nt(d_attn[...], out_w[col(n), :]).astype(BF16)
    low_lanes = lax.broadcasted_iota(jnp.int32, (1, LANES), 1) < HEAD_DIM
    scale = HEAD_DIM ** (-0.5)

    def head_pair(p, c):
        lanes = pl.ds(pl.multiple_of(p * LANES, LANES), LANES)
        k_lanes = pl.ds(pl.multiple_of(width + p * LANES, LANES), LANES)
        v_lanes = pl.ds(pl.multiple_of(2 * width + p * LANES, LANES), LANES)
        q = packed[:, lanes]
        k = packed[:, k_lanes]
        v = packed[:, v_lanes].astype(F32)
        given = d_context[:, lanes]
        dq, dk, dv = [], [], []
        for e in range(2):
            one = jnp.where(low_lanes if e == 0 else ~low_lanes, v, 0.0).astype(BF16)
            chance = probs[2 * p + e]
            d_probs = mm_nt(one, given)
            delta = jnp.sum(d_probs * chance, axis=0, keepdims=True)
            d_scores = (chance * (d_probs - delta)).astype(BF16)
            dv.append(mm(chance.astype(BF16), given))
            dk.append(mm(d_scores, q))
            dq.append(mm_tn(k, d_scores))
        both = jnp.concatenate([dq[0][:HEAD_DIM], dq[1][HEAD_DIM:]], axis=0)
        d_packed[:, lanes] = (both.T * scale).astype(BF16)
        d_packed[:, k_lanes] = (jnp.where(low_lanes, dk[0], dk[1]) * scale).astype(BF16)
        d_packed[:, v_lanes] = jnp.where(low_lanes, dv[0], dv[1]).astype(BF16)
        return c

    lax.fori_loop(0, width // LANES, head_pair, 0)
    qkv_w = qkv_w()
    for n in range(width // TILE):
        d_fourth[:, col(n)] = mm_nt(d_packed[...], qkv_w[col(n), :])
    gain = gains()[2:3, :].astype(F32)

    sums = [jnp.zeros((8, width), F32)] * 2
    g_point = jnp.zeros((8, half), F32)
    at = pl.multiple_of(side * (width // 2), width // 2)
    sides = [(context, d_attn, at)]
    for j in range(3 * width // 2 // TILE):
        sides.append((fourth, d_packed, pl.multiple_of(side * (3 * width // 2) + j * TILE, TILE)))
    for p in range(2 * len(sides)):
        block = slice(p * seq // 8, (p + 1) * seq // 8)
        vhat, rate = normalized(after_conv[block, :])
        e = d_fourth[block, :]
        total = d_after[block, :] + norm_back(vhat, rate, e * gain)
        d_after_conv[block, :] = total
        sep = total[:, :half].astype(BF16)
        d_sep[block, :] = sep
        sums = [total + part_sums(v) for total, v in zip(sums, (e * vhat, e))]
        g_point = g_point + part_sums(sep.astype(F32))
        values, incoming, at = sides[p // 2]
        part = slice(p % 2 * (width // 2), (p % 2 + 1) * (width // 2))
        grad[p // 2, part, :] = mm_tn(values[:, part], incoming[:, pl.ds(at, TILE)])
    small[0:1, 0:width] = sum_tokens(sums[0])
    small[0:1, width : 2 * width] = sum_tokens(sums[1])
    small[0:1, 2 * width : 2 * width + half] = sum_tokens(g_point)
    for j in range(len(sides)):
        place_rows(grad.at[j], keep, send, ATTN_BITS, j * rows, rows)
    sep_half = d_sep[:, pl.ds(pl.multiple_of(side * (half // 2), half // 2), half // 2)]
    per_row = ffn // GROUPS

    def point_slot(p, block, out):
        g = mm_tn(
            depth_low[:, pl.ds(pl.multiple_of(block * per_row, per_row), per_row)], sep_half
        ).astype(BF16)
        out[p, 4 * rows : 4 * rows + per_row // 2, 0:LANES] = g[: per_row // 2]
        out[p, 4 * rows : 4 * rows + per_row // 2, LANES : 2 * LANES] = g[per_row // 2 :]

    for_slots(keep, send, ATTN_BITS, point_slot)


def middle_back_kernel(
    lengths,
    d_after_conv,
    left_pre,
    right_pre,
    far,
    d_left,
    taps_right,
    small,
    vhat3,
    third,
    d_depth,
    d_third,
    rates,
    sums,
    d_right,
    mid_row,
):
    seq, width = d_after_conv.shape
    ffn = left_pre.shape[1]
    half = right_pre.shape[1]
    length = lengths[0]
    point_w, mid_gain, mid_bias, depth_w = far
    chunks = ffn // LANES
    edge = jnp.zeros((8, LANES), F32)
    for k in range(chunks):
        d_depth[k, 0:8, :] = edge
        d_depth[k, 8 + seq : 16 + seq, :] = edge
    d_sep = d_after_conv[:, :half].astype(BF16)
    point_w = point_w()
    for n in range(ffn // TILE):
        block = mm_nt(d_sep, point_w[col(n), :])
        for m in range(TILE // LANES):
            d_depth[n * (TILE // LANES) + m, 8 : 8 + seq, :] = block[:, col(m, LANES)]

    mid_g, mid_b, depth_w = vector(mid_gain()), vector(mid_bias()), depth_w()
    mid_row[...] = mid_g

    def mid_rows(r, c):
        rows = pl.ds(r, 16)
        vhat, rate = normalized(combine(left_pre[rows, :], right_pre[rows, :]))
        v = (vhat * mid_g + mid_b) * valid_rows(r, 16, length)
        rates[rows, :] = jnp.broadcast_to(rate, (16, LANES))
        for k in range(chunks):
            third[k, rows, :] = v[:, col(k, LANES)]
            vhat3[k, rows, :] = vhat[:, col(k, LANES)]
        return c

    row_blocks(seq, 16, mid_rows, unroll=2)
    sums[...] = jnp.zeros(sums.shape, F32)
    step = 64

    def depth_lanes(k, c):
        lanes = pl.ds(pl.multiple_of(k * LANES, LANES), LANES)
        taps = depth_w[:, lanes].astype(F32)
        mid_lanes = mid_row[0:1, lanes]
        totals = [jnp.zeros((8, LANES), F32)] * 11
        for r in range(0, seq, step):
            block = slice(r, r + step)
            here = third[k, block, :]
            total = None
            for j in range(9):
                moved = d_depth[k, 12 - j + r : 12 - j + r + step, :]
                totals[j] = totals[j] + part_sums(moved * here)
                term = moved * taps[j : j + 1, :]
                total = term if total is None else total + term
            total = total * valid_rows(r, step, length)
            vhat = vhat3[k, block, :]
            totals[9] = totals[9] + part_sums(total * vhat)
            totals[10] = totals[10] + part_sums(total)
            gained = total * mid_lanes
            d_third[k, block, :] = gained
            sums[0, block, :] = sums[0, block, :] + gained
            sums[1, block, :] = sums[1, block, :] + gained * vhat
        for j in range(11):
            small[j : j + 1, lanes] = sum_tokens(totals[j])
        return c

    lax.fori_loop(0, chunks, depth_lanes, 0)
    inverse = 1.0 / ffn
    sums[0] = jnp.broadcast_to(jnp.sum(sums[0], axis=-1, keepdims=True) * inverse, (seq, LANES))
    sums[1] = jnp.broadcast_to(jnp.sum(sums[1], axis=-1, keepdims=True) * inverse, (seq, LANES))

    def combined_lanes(k):
        return (d_third[k] - sums[0] - vhat3[k] * sums[1]) * rates[...]

    def left_lanes(k, c):
        lanes = pl.ds(pl.multiple_of(k * LANES, LANES), LANES)
        v = jnp.where(left_pre[:, lanes] > 0.0, combined_lanes(k), 0.0).astype(BF16)
        d_left[:, lanes] = v
        small[11:12, lanes] = sum_tokens(v.astype(F32))
        return c

    lax.fori_loop(0, chunks, left_lanes, 0)
    blank = jnp.zeros((8, half), F32)
    d_right[0:8, :] = blank
    d_right[8 + seq : 16 + seq, :] = blank
    for k in range(half // LANES):
        v = jnp.where(right_pre[:, col(k, LANES)] > 0.0, combined_lanes(k), 0.0).astype(BF16)
        v = v.astype(F32)
        d_right[8 : 8 + seq, col(k, LANES)] = v
        small[12:13, col(k, LANES)] = sum_tokens(v)
    taps_right[0] = d_right[9 : 9 + seq, :].astype(BF16)
    taps_right[1] = d_right[8 : 8 + seq, :].astype(BF16)
    taps_right[2] = d_right[7 : 7 + seq, :].astype(BF16)


def conv_back_kernel(
    lengths,
    d_left,
    taps_right,
    second,
    far,
    d_second,
    keep,
    send,
    grad,
    grad_conv,
):
    seq, width = d_second.shape
    ffn = d_left.shape[1]
    half = taps_right.shape[2]
    side = lax.axis_index("head")
    valid = valid_rows(0, seq, lengths[0])
    rows = width // GROUPS
    for j in range(ffn // 2 // TILE):
        at = pl.multiple_of(side * (ffn // 2) + j * TILE, TILE)
        grad[...] = mm_tn(second[...], d_left[:, pl.ds(at, TILE)])
        place_rows(grad, keep, send, CONV_BITS, j * rows, rows)
    start = ffn // 2 // TILE * rows
    half_lanes = pl.ds(pl.multiple_of(side * (half // 2), half // 2), half // 2)
    for tap in range(3):
        grad_conv[tap] = mm_tn(second[...], taps_right[tap, :, half_lanes])

    def conv_slot(p, block, out):
        at = pl.multiple_of(block * rows, rows)
        middle = pl.multiple_of(block * rows + rows // 2, rows // 2)
        h = rows // 2
        out[p, start : start + rows, 0:LANES] = grad_conv[0, pl.ds(at, rows), :].astype(BF16)
        out[p, start + rows : start + rows + h, 0:LANES] = grad_conv[1, pl.ds(at, h), :].astype(BF16)
        out[p, start : start + h, LANES : 2 * LANES] = grad_conv[1, pl.ds(middle, h), :].astype(BF16)
        out[p, start + h : start + h + rows, LANES : 2 * LANES] = grad_conv[
            2, pl.ds(at, rows), :
        ].astype(BF16)

    for_slots(keep, send, CONV_BITS, conv_slot)
    left_w, conv_w = (get() for get in far)
    for n in range(width // TILE):
        total = mm_nt(d_left[...], left_w[col(n), :])
        for tap in range(3):
            total = total + mm_nt(taps_right[tap], conv_w[tap, col(n), :])
        d_second[:, col(n)] = total * valid


def glu_back_kernel(
    d_second,
    d_after_conv,
    after_glu,
    joined,
    first,
    stream,
    small_ffn,
    small_attn,
    small_conv,
    far,
    grad_tokens,
    keep,
    send,
    d_joined,
    d_after_glu,
    d_first,
    rolled,
    blocks,
    grad,
):
    seq, width = d_second.shape
    part = seq // 2
    side = lax.axis_index("head")
    gains, glu_w = far
    gains = gains()
    gain = [gains[k : k + 1, :].astype(F32) for k in range(2)]

    def glu_rows(r, c):
        g_gain, g_shift, g_value, g_gate = c
        rows = pl.ds(r, 32)
        vhat, rate = normalized(after_glu[rows, :])
        e = d_second[rows, :]
        total = d_after_conv[rows, :] + norm_back(vhat, rate, e * gain[1])
        d_after_glu[rows, :] = total
        value = joined[rows, :width]
        gate = joined[rows, width:]
        d_value = (total * gate).astype(BF16)
        d_gate = (total * value * gate * (1.0 - gate)).astype(BF16)
        d_joined[rows, :width] = d_value
        d_joined[rows, width:] = d_gate
        return (
            g_gain + part_sums(e * vhat),
            g_shift + part_sums(e),
            g_value + part_sums(d_value.astype(F32)),
            g_gate + part_sums(d_gate.astype(F32)),
        )

    nothing = jnp.zeros((8, width), F32)
    sums = row_blocks(seq, 32, glu_rows, (nothing,) * 4, unroll=2)
    gain_one, shift_one, g_value, g_gate = (sum_tokens(v) for v in sums)
    glu_w = glu_w()
    for n in range(width // TILE):
        d_first[:, col(n)] = mm_nt(d_joined[...], glu_w[col(n), :])

    sums = [nothing] * 2
    rows = width // GROUPS
    columns = [pl.ds(pl.multiple_of(side * width + j * TILE, TILE), TILE) for j in range(width // TILE)]
    for p in range(8):
        block = slice(p * seq // 8, (p + 1) * seq // 8)
        vhat, rate = normalized(stream[block, :].astype(F32))
        e = d_first[block, :]
        d_after_glu[block, :] = d_after_glu[block, :] + norm_back(vhat, rate, e * gain[0])
        sums = [total + part_sums(v) for total, v in zip(sums, (e * vhat, e))]
        if p < 2 * len(columns):
            part_rows = slice(p % 2 * (width // 2), (p % 2 + 1) * (width // 2))
            grad[p // 2, part_rows, :] = mm_tn(first[:, part_rows], d_joined[:, columns[p // 2]])
    gain_zero, shift_zero = (sum_tokens(v) for v in sums)
    grad_tokens[...] = d_after_glu[pl.ds(pl.multiple_of(side * part, part), part), :]
    for j in range(len(columns)):
        place_rows(grad.at[j], keep, send, GLU_BITS, j * rows, rows)

    blocks[...] = jnp.zeros(blocks.shape, F32)
    rolled[...] = jnp.zeros(rolled.shape, F32)
    vectors = (
        (gain_zero, gain_one, small_attn[0:1, 0:width], small_ffn[1:2, 0:width]),
        (shift_zero, shift_one, small_attn[0:1, width : 2 * width], small_ffn[1:2, width : 2 * width]),
    )
    tiles = width // LANES
    lane = lax.broadcasted_iota(jnp.int32, (8, LANES), 1)
    quarter = LANES // tiles
    for kind, four in enumerate(vectors):
        for k, vector in enumerate(four):
            for t in range(tiles):
                rolled[kind, 8 * k + t : 8 * k + t + 1, :] = vector[:, col(t, LANES)]
        for q in range(tiles):
            total = jnp.zeros((8, LANES), F32)
            for k in range(4):
                moved = pltpu.roll(rolled[kind, 8 * k : 8 * k + 8, :], (quarter * (k - q)) % LANES, 1)
                total = jnp.where((lane >= quarter * k) & (lane < quarter * (k + 1)), moved, total)
            for t in range(tiles):
                blocks[tiles * t + q, 13 + kind : 14 + kind, 0:LANES] = total[t : t + 1, :]
    lane = lane[0:1, :]
    g_out = small_ffn[1:2, 2 * width : 3 * width]
    for s in range(GROUPS):
        source = g_value if s < GROUPS // 2 else g_gate
        place = (s % (GROUPS // 2)) * (2 * width // GROUPS)
        block = source[:, place // LANES * LANES : place // LANES * LANES + LANES]
        glu_part = block if place % LANES == 0 else pltpu.roll(block, LANES - place % LANES, 1)
        place = s * (width // GROUPS)
        block = g_out[:, place // LANES * LANES : place // LANES * LANES + LANES]
        moved = (LANES // 2 - place % LANES) % LANES
        out_part = block if moved == 0 else pltpu.roll(block, moved, 1)
        blocks[s, 15:16, 0:LANES] = jnp.where(
            lane < LANES // 2, glu_part, jnp.where(lane < LANES // 2 + quarter, out_part, 0.0)
        )
        blocks[s, 0:12, 0:LANES] = small_conv[0:12, col(s, LANES)]
        blocks[s, 12:13, 0:LANES] = small_ffn[0:1, col(s, LANES)]
        for k in range(2):
            blocks[s, k : k + 1, LANES : 2 * LANES] = small_conv[12:13, col(k, LANES)]
            blocks[s, 2 + k : 3 + k, LANES : 2 * LANES] = small_attn[
                0:1, 2 * width + k * LANES : 2 * width + (k + 1) * LANES
            ]
    start = width // TILE * rows

    def small_slot(p, block, out):
        out[p, start : start + 16, :] = blocks[block].astype(BF16)

    for_slots(keep, send, GLU_BITS, small_slot)


def add_kernel(*refs):
    *inputs, far, keep, send = refs
    at = 0
    for kept, got in zip(inputs[::2], inputs[1::2]):
        rows = kept.shape[1]
        for out, place in ((keep, 0), (send, 1)):
            total = kept[place].astype(F32) + got[place].astype(F32)
            out[0, at : at + rows, :] = total.astype(BF16)
        at += rows


def finish_early_kernel(mine, other, far, ffn_out, ffn_in, out, qkv, point):
    side = lax.axis_index("head")
    per_row, width = ffn_out.shape
    rows = ffn_in.shape[0]
    for who, grads in ((side, mine), (1 - side, other)):
        count = ffn_in.shape[1] // 2 // TILE
        at = pl.ds(pl.multiple_of(who * TILE, TILE), TILE)
        start = per_row + count * rows
        ffn_out[:, at] = grads[0:per_row, :].astype(F32)
        out[:, at] = grads[start : start + rows, :].astype(F32)
        for j in range(count):
            at = pl.ds(pl.multiple_of((who * count + j) * TILE, TILE), TILE)
            ffn_in[:, at] = grads[per_row + j * rows : per_row + (j + 1) * rows, :].astype(F32)
        count = qkv.shape[1] // 2 // TILE
        for j in range(count):
            at = pl.ds(pl.multiple_of((who * count + j) * TILE, TILE), TILE)
            qkv[:, at] = grads[start + (1 + j) * rows : start + (2 + j) * rows, :].astype(F32)
        start = start + (1 + count) * rows
        at = pl.ds(pl.multiple_of(who * LANES, LANES), LANES)
        point[0 : per_row // 2, at] = grads[start : start + per_row // 2, 0:LANES].astype(F32)
        point[per_row // 2 :, at] = grads[start : start + per_row // 2, LANES : 2 * LANES].astype(F32)


def finish_late_kernel(
    mine,
    other,
    far,
    left,
    conv,
    glu,
    gains,
    shifts,
    depth,
    mid_gain,
    mid_bias,
    left_bias,
    ffn_in_bias,
    glu_bias,
    ffn_out_bias,
    conv_bias,
    point_bias,
):
    side = lax.axis_index("head")
    rows = glu.shape[0]
    h = rows // 2
    count = left.shape[1] // 2 // TILE
    behind = count * rows + 3 * h
    wide = glu.shape[1] // 2 // TILE
    for who, grads in ((side, mine), (1 - side, other)):
        for j in range(count):
            at = pl.ds(pl.multiple_of((who * count + j) * TILE, TILE), TILE)
            left[:, at] = grads[j * rows : (j + 1) * rows, :].astype(F32)
        start = count * rows
        at = pl.ds(pl.multiple_of(who * LANES, LANES), LANES)
        low = grads[start : start + 3 * h, 0:LANES].astype(F32)
        high = grads[start : start + 3 * h, LANES : 2 * LANES].astype(F32)
        conv[0, :, at] = low[0:rows]
        conv[1, 0:h, at] = low[rows:]
        conv[1, h:rows, at] = high[0:h]
        conv[2, :, at] = high[h:]
        for j in range(wide):
            at = pl.ds(pl.multiple_of((who * wide + j) * TILE, TILE), TILE)
            glu[:, at] = grads[behind + j * rows : behind + (j + 1) * rows, :].astype(F32)
    start = behind + wide * rows
    block = mine[start : start + 16, :].astype(F32)
    depth[...] = block[0:9, 0:LANES]
    for k in range(4):
        gains[k : k + 1, :] = block[13:14, k * rows : (k + 1) * rows]
        shifts[k : k + 1, :] = block[14:15, k * rows : (k + 1) * rows]
    mid_gain[...] = block[9, 0:LANES]
    mid_bias[...] = block[10, 0:LANES]
    left_bias[...] = block[11, 0:LANES]
    ffn_in_bias[...] = block[12, 0:LANES]
    glu_bias[...] = block[15, 0 : 2 * rows]
    ffn_out_bias[...] = block[15, 2 * rows : 3 * rows]
    for k in range(2):
        conv_bias[col(k, LANES)] = block[k, LANES : 2 * LANES]
        point_bias[col(k, LANES)] = block[2 + k, LANES : 2 * LANES]


def call(kernel, outs, scratch, near, far, micros=2, scalars=0):
    smem = pl.BlockSpec(memory_space=pltpu.SMEM)
    vmem = pl.BlockSpec(memory_space=pltpu.VMEM)
    anywhere = pl.BlockSpec(memory_space=pltpu.HBM)

    def body(*refs):
        inputs = refs[: len(near)]
        sources = refs[len(near) : len(near) + len(far)]
        results = refs[len(near) + len(far) : len(near) + len(far) + len(outs)]
        rest = refs[len(near) + len(far) + len(outs) :]
        if not far:
            kernel(*inputs, (), *results, *rest)
            return
        *rest, done = rest
        buffers = rest[len(scratch) :]
        copies = [
            pltpu.make_async_copy(source, buffer, done.at[i])
            for i, (source, buffer) in enumerate(zip(sources, buffers))
        ]
        for copy in copies:
            copy.start()

        def fetched(copy, buffer):
            def get():
                copy.wait()
                return buffer

            return get

        kernel(*inputs, tuple(map(fetched, copies, buffers)), *results, *rest[: len(scratch)])

    temporaries = [pltpu.VMEM(shape, dtype) for shape, dtype in scratch]
    if far:
        temporaries += [pltpu.VMEM(v.shape, v.dtype) for v in far]
        temporaries.append(pltpu.SemaphoreType.DMA((len(far),)))
    return pl.pallas_call(
        body,
        out_shape=tuple(jax.ShapeDtypeStruct(shape, dtype) for shape, dtype in outs),
        in_specs=[smem] * scalars + [vmem] * (len(near) - scalars) + [anywhere] * len(far),
        out_specs=(vmem,) * len(outs),
        scratch_shapes=temporaries,
        compiler_params=pltpu.CompilerParams(vmem_limit_bytes=VMEM_BYTES),
        cost_estimate=pl.CostEstimate(
            flops=micros * 10**9, transcendentals=0, bytes_accessed=micros * 3 * 10**6
        ),
        name=kernel.__name__,
    )(*near, *[pltpu.with_memory_space_constraint(v, pltpu.HBM) for v in far])


def per_device(
    tokens,
    lengths,
    cotangent,
    glu_weight,
    glu_bias,
    norm_gain,
    norm_bias,
    mid_gain,
    mid_bias,
    left_weight,
    left_bias,
    conv_weight,
    conv_bias,
    depth_weight,
    point_weight,
    point_bias,
    qkv_weight,
    out_weight,
    ffn_in_weight,
    ffn_in_bias,
    ffn_out_weight,
    ffn_out_bias,
):
    row_count, part, width = tokens.shape
    assert row_count == 1 and lax.axis_size("head") == 2
    seq = 2 * part
    shards = lax.axis_size("dp")
    below = shards // GROUPS
    assert below * GROUPS == shards
    heads = width // HEAD_DIM
    half = conv_weight.shape[2]
    ffn = left_weight.shape[1]
    swap = [(0, 1), (1, 0)]
    mine = tokens[0]
    cot_mine = cotangent[0]
    other = lax.ppermute(mine, "head", swap)
    cot_other = lax.ppermute(cot_mine, "head", swap)

    def slot_outs(rows):
        return [((GROUPS // 2, rows, TILE), BF16)] * 2

    rows = width // GROUPS
    per_row = ffn // GROUPS
    ffn_rows = per_row + ffn // 2 // TILE * rows
    (
        out_tokens,
        stream,
        first_norm,
        joined,
        after_glu,
        second,
        left_pre,
        right_pre,
        depth_low,
        after_conv,
        fourth,
        packed,
        probs,
        context,
        d_after,
        small_ffn,
        keep_ffn,
        send_ffn,
    ) = call(
        forward_kernel,
        [
            ((part, width), BF16),
            ((seq, width), BF16),
            ((seq, width), BF16),
            ((seq, 2 * width), F32),
            ((seq, width), F32),
            ((seq, width), BF16),
            ((seq, ffn), F32),
            ((seq, half), F32),
            ((seq, ffn), BF16),
            ((seq, width), F32),
            ((seq, width), BF16),
            ((seq, 3 * width), BF16),
            ((heads, seq, seq), F32),
            ((seq, width), BF16),
            ((seq, width), F32),
            ((8, ffn), F32),
        ]
        + slot_outs(ffn_rows),
        [
            ((ffn // LANES, seq + 16, LANES), F32),
            ((2, seq + 16, half), F32),
            ((seq, width), F32),
            ((seq, width), BF16),
            ((seq, ffn), BF16),
            ((seq, width), BF16),
            ((seq, ffn), BF16),
            ((seq, width), F32),
            ((width, TILE), F32),
        ],
        [lengths, other, cot_other],
        [
            mine,
            norm_gain,
            norm_bias,
            glu_bias,
            glu_weight,
            conv_bias,
            conv_weight,
            left_bias,
            left_weight,
            mid_gain,
            mid_bias,
            depth_weight,
            point_bias,
            point_weight,
            qkv_weight,
            out_weight,
            ffn_in_bias,
            ffn_in_weight,
            ffn_out_bias,
            ffn_out_weight,
            cot_mine,
        ],
        micros=25,
        scalars=1,
    )
    class Chunk:
        def __init__(self, keep, send, bits):
            self.keep, self.send, self.bits = keep, send, list(bits)

        def start(self):
            if not self.bits:
                self.got = lax.ppermute(self.keep, "head", swap)
                return
            step = below << self.bits.pop(0)
            self.got = lax.ppermute(self.send, "dp", [(i, i ^ step) for i in range(shards)])

        def add(self):
            n = self.keep.shape[0] // 2

            def total(piece):
                return (self.keep[piece].astype(F32) + self.got[piece].astype(F32)).astype(BF16)

            if n > 0:
                self.keep, self.send = total(slice(0, n)), total(slice(n, 2 * n))
                return
            total = total(slice(0, 1))[0]
            step = 1
            while step < below:
                total = total + lax.ppermute(total, "dp", [(i, i ^ step) for i in range(shards)])
                step *= 2
            self.keep, self.send = total, total

    def wave(held, *chunks, joined=False):
        gots = [c.got for c in chunks]
        held, gots = lax.optimization_barrier((held, gots))
        for c, got in zip(chunks, gots):
            c.got = got
        if joined:
            total = ((1, sum(c.keep.shape[1] for c in chunks), TILE), BF16)
            pair = call(add_kernel, [total, total], [], [v for c in chunks for v in (c.keep, c.got)], [])
            chunks = [Chunk(*pair, chunks[0].bits)]
        else:
            for c in chunks:
                c.add()
        held, pairs = lax.optimization_barrier((held, [(c.keep, c.send) for c in chunks]))
        for c, pair in zip(chunks, pairs):
            c.keep, c.send = pair
            c.start()
        return (held, chunks[0]) if joined else held

    ffn_grads = Chunk(keep_ffn, send_ffn, (0, *FFN_BITS))
    ffn_grads.start()
    d_after_conv, small_attn, keep_attn, send_attn = call(
        attention_back_kernel,
        [((seq, width), F32), ((8, ffn), F32)] + slot_outs(4 * rows + per_row // 2),
        [
            ((seq, width), BF16),
            ((seq, width), BF16),
            ((seq, 3 * width), BF16),
            ((seq, width), F32),
            ((seq, half), BF16),
            ((4, width, TILE), F32),
        ],
        [d_after, packed, probs, context, fourth, after_conv, depth_low],
        [out_weight, qkv_weight, norm_gain],
        micros=10,
    )
    d_after_conv = wave(d_after_conv, ffn_grads)
    attn_grads = Chunk(keep_attn, send_attn, (0, *ATTN_BITS))
    attn_grads.start()
    d_after_conv = wave(d_after_conv, attn_grads)
    d_left, taps_right, small_conv = call(
        middle_back_kernel,
        [((seq, ffn), BF16), ((3, seq, half), BF16), ((16, ffn), F32)],
        [
            ((ffn // LANES, seq, LANES), F32),
            ((ffn // LANES, seq, LANES), F32),
            ((ffn // LANES, seq + 16, LANES), F32),
            ((ffn // LANES, seq, LANES), F32),
            ((seq, LANES), F32),
            ((2, seq, LANES), F32),
            ((seq + 16, half), F32),
            ((1, ffn), F32),
        ],
        [lengths, d_after_conv, left_pre, right_pre],
        [point_weight, mid_gain, mid_bias, depth_weight],
        micros=10,
        scalars=1,
    )
    d_left = wave(d_left, ffn_grads, attn_grads)
    d_second, keep_conv, send_conv = call(
        conv_back_kernel,
        [((seq, width), F32)] + slot_outs(ffn // 2 // TILE * rows + 3 * rows // 2),
        [((width, TILE), F32), ((3, width, LANES), F32)],
        [lengths, d_left, taps_right, second],
        [left_weight, conv_weight],
        micros=5,
        scalars=1,
    )
    conv_grads = Chunk(keep_conv, send_conv, (0, *CONV_BITS))
    conv_grads.start()
    d_second = wave(d_second, conv_grads)
    grad_tokens, keep_glu, send_glu = call(
        glu_back_kernel,
        [((part, width), F32)] + slot_outs(width // TILE * rows + 16),
        [
            ((seq, 2 * width), BF16),
            ((seq, width), F32),
            ((seq, width), F32),
            ((2, 32, LANES), F32),
            ((GROUPS, 16, 2 * LANES), F32),
            ((width // TILE, width, TILE), F32),
        ],
        [
            d_second,
            d_after_conv,
            after_glu,
            joined,
            first_norm,
            stream,
            small_ffn,
            small_attn,
            small_conv,
        ],
        [norm_gain, glu_weight],
        micros=7,
    )
    glu_grads = Chunk(keep_glu, send_glu, (0, *GLU_BITS))
    glu_grads.start()
    held, early = wave(grad_tokens, ffn_grads, attn_grads, joined=True)
    held = wave(held, glu_grads)
    held = wave(held, conv_grads)
    held = wave(held, glu_grads)
    held, late = wave(held, conv_grads, glu_grads, joined=True)
    held = wave(held, early)
    held, other = lax.optimization_barrier((held, early.got))
    grad_tokens = wave(held, late)
    ffn_out, ffn_in, out, qkv, point = call(
        finish_early_kernel,
        [
            ((per_row, width), F32),
            ((rows, ffn), F32),
            ((rows, width), F32),
            ((rows, 3 * width), F32),
            ((per_row, half), F32),
        ],
        [],
        [early.keep, other],
        [],
    )
    (
        left,
        conv,
        glu,
        g_gains,
        g_shifts,
        g_depth,
        g_mid_gain,
        g_mid_bias,
        g_left_bias,
        g_ffn_in_bias,
        g_glu_bias,
        g_ffn_out_bias,
        g_conv_bias,
        g_point_bias,
    ) = call(
        finish_late_kernel,
        [
            ((rows, ffn), F32),
            ((3, rows, half), F32),
            ((rows, 2 * width), F32),
            ((4, rows), F32),
            ((4, rows), F32),
            ((9, LANES), F32),
            ((LANES,), F32),
            ((LANES,), F32),
            ((LANES,), F32),
            ((LANES,), F32),
            ((2 * rows,), F32),
            ((rows,), F32),
            ((half,), F32),
            ((half,), F32),
        ],
        [],
        [late.keep, late.got],
        [],
    )
    results = (
        (glu, 0),
        (g_glu_bias, 0),
        (g_gains, 1),
        (g_shifts, 1),
        (g_mid_gain, 0),
        (g_mid_bias, 0),
        (left, 0),
        (g_left_bias, 0),
        (conv, 1),
        (g_conv_bias, None),
        (g_depth, 1),
        (point, 0),
        (g_point_bias, None),
        (qkv, 0),
        (out, 0),
        (ffn_in, 0),
        (g_ffn_in_bias, 0),
        (ffn_out, 0),
        (g_ffn_out_bias, 0),
    )
    final = []
    for value, axis in results:
        if axis is not None and below > 1:
            size = value.shape[axis] // below
            value = lax.dynamic_slice_in_dim(value, lax.axis_index("dp") % below * size, size, axis)
        final.append(value)
    return (out_tokens[None], grad_tokens[None], *final)


def solution(mesh):
    return jax.shard_map(
        per_device,
        mesh=mesh,
        in_specs=(P("dp", "head", None), P("dp"), P("dp", "head", None)) + (P(),) * 19,
        out_specs=(
            P("dp", "head", None),
            P("dp", "head", None),
            P("dp", None),
            P("dp"),
            P(None, "dp"),
            P(None, "dp"),
            P("dp"),
            P("dp"),
            P("dp", None),
            P("dp"),
            P(None, "dp", None),
            P(),
            P(None, "dp"),
            P("dp", None),
            P(),
            P("dp", None),
            P("dp", None),
            P("dp", None),
            P("dp"),
            P("dp", None),
            P("dp"),
        ),
        check_vma=False,
    )
```

time: 154 us -> 106 us (0.69)
  Pallas kernels: 72.4 us -> 46.2 us
  local copies, waits for them, and re-layouts: 12.3 us -> 0 us
  starting transfers between devices: 29.6 us -> 19.5 us
  waiting for transfers between devices: 35.2 us -> 37.3 us
    pallas_call x6 -> x9, Pallas kernels: 72.4 us -> 46.2 us  [call(): pl.pallas_call(body, out_shape=tuple((jax.ShapeDtypeStruct(shape, dtype)...]
    ppermute x20 -> x16, starting transfers between devices: 26.5 us -> 16.5 us  [the longest x14 13.1 us: start(): lax.ppermute(self.send, 'dp', [(i, i ^ step) for i in range(shards)])]
    unnamed x29 -> x0, local copies, waits for them, and re-layouts: 9.21 us -> none
    ppermute x1, waiting for transfers between devices: 0.01 us -> 3.8 us  [per_device(): other = lax.ppermute(mine, 'head', swap)]
    ppermute x20 -> x16, waiting for transfers between devices: 35.2 us -> 31.5 us  [the longest x14 23.3 us: start(): lax.ppermute(self.send, 'dp', [(i, i ^ step) for i in range(shards)])]
    ppermute x1, waiting for transfers between devices: 0.01 us -> 1.98 us  [per_device(): cot_other = lax.ppermute(cot_mine, 'head', swap)]
    squeeze x3 -> x0, local copies, waits for them, and re-layouts: 1.62 us -> none  [the longest x1 0.58 us: per_device(): vectors[15, 2 * rows:3 * rows]]
  transfers between devices with their start and end apart: 22 -> 18, of which waited for: 12 -> 13; matrix products, arithmetic and copies ran while one was open for 7% -> 1% of each run, Pallas kernels for 1% -> 22%
where the time goes in v3:
time: 106 us
  Pallas kernels  46.2 us (44%)
  waiting for transfers between devices  37.3 us (35%)
  starting transfers between devices  19.5 us (18%)
  between operations  1.61 us (2%)
  other arithmetic  1.13 us (1%)
    pallas_call x9, Pallas kernels, call(): pl.pallas_call(body, out_shape=tuple((jax.ShapeDtypeStruct(shape, dtype)...  46.2 us
    ppermute x14, waiting for transfers between devices, start(): lax.ppermute(self.send, 'dp', [(i, i ^ step) for i in range(shards)])  23.3 us
    ppermute x14, starting transfers between devices, start(): lax.ppermute(self.send, 'dp', [(i, i ^ step) for i in range(shards)])  13.1 us
    ppermute x2, waiting for transfers between devices, start(): self.got = lax.ppermute(self.keep, 'head', swap)  8.16 us
    ppermute x1, waiting for transfers between devices, per_device(): other = lax.ppermute(mine, 'head', swap)  3.8 us
    ppermute x2, starting transfers between devices, start(): self.got = lax.ppermute(self.keep, 'head', swap)  3.38 us
    ppermute x1, starting transfers between devices, per_device(): other = lax.ppermute(mine, 'head', swap)  3 us
  transfers between devices with their start and end apart: 18, of which 13 were waited for; matrix products, arithmetic and copies ran while one was open for 1% of the time, Pallas kernels for 22%

profile of v3, /device:TPU:0, one launch (start us, length us, event | category | flops | bytes accessed | tf_op | source)
XLA Modules:
  0.0 105.8 jit_solution(4132704646753822361)
XLA Ops:
  0.7 3.0 %collective-permute-start = (bf16[128,512]{1,0:T(8,128)(2,1)}, bf16[128,512]{1,0:T(8,128)(2,1)S(1)}, u32[]{:S(2)}, u32[]{:S(2)}) collective-permute-start(bf16[128,512]{1,0:T(8,128)(2,1)} %bitcast.8), channel_id=1, source_target_pairs={{0,1},{1,0},{2,3},{3,2},{4,5},{5,4},{6,7},{7,6},{8,9},{9,8},{10,11... | collective-permute-start | bytes 393224 | tf_op jit(solution)/shard_map/ppermute | solution.py:882
  4.4 3.8 %collective-permute-done.refs_1_ = bf16[128,512]{1,0:T(8,128)(2,1)S(1)} collective-permute-done((bf16[128,512]{1,0:T(8,128)(2,1)}, bf16[128,512]{1,0:T(8,128)(2,1)S(1)}, u32[]{:S(2)}, u32[]{:S(2)}) %collective-permute-start) | collective-permute-done | bytes 131104 | tf_op jit(solution)/shard_map/ppermute | solution.py:882
  8.2 2.0 %collective-permute-done.1.refs_2_ = bf16[128,512]{1,0:T(8,128)(2,1)S(1)} collective-permute-done((bf16[128,512]{1,0:T(8,128)(2,1)}, bf16[128,512]{1,0:T(8,128)(2,1)S(1)}, u32[]{:S(2)}, u32[]{:S(2)}) %collective-permute-start.1) | collective-permute-done | bytes 131104 | tf_op jit(solution)/shard_map/ppermute | solution.py:883
  10.2 19.2 %forward_kernel.1 = (bf16[128,512]{1,0:T(8,128)(2,1)}, bf16[256,512]{1,0:T(8,128)(2,1)S(1)}, bf16[256,512]{1,0:T(8,128)(2,1)S(1)}, f32[256,1024]{1,0:T(8,128)S(1...) custom-call(s32[1]{0:T(128)S(6)} %copy.43.refs_0_, ...), custom_call_target="tpu_custom_call" | custom-call | flops 24999999488 | bytes 75000000 | tf_op jit(solution)/shard_map/forward_kernel/pallas_call | solution.py:832
  29.5 8.9 %attention_back_kernel.1 = (f32[256,512]{1,0:T(8,128)S(1)}, f32[8,2048]{1,0:T(8,128)S(1)}, bf16[8,192,256]{2,1,0:T(8,128)(2,1)S(1)}, bf16[8,192,256]{2,1,0:T(8,128)(2,1)S(1)}) custom-call(f32[256,512]{1,0:T(8,128)S(1)} %get-tuple-element.136.refs_0_, bf16[256,1536]{1,0:T(8,128)(2,1)S(1)} %get-tuple-element.137.refs_1_, ...), custom_call_target="tpu_custom_call" | custom-call | flops 10000000000 | bytes 30000000 | tf_op jit(solution)/shard_map/attention_back_kernel/pallas_call | solution.py:832
  38.3 0.6 collective-permute-start.3
  39.1 1.9 %collective-permute-start.4 = (bf16[4,256,256]{2,1,0:T(8,128)(2,1)S(1)}, bf16[4,256,256]{2,1,0:T(8,128)(2,1)S(1)}, u32[]{:S(2)}, u32[]{:S(2)}) collective-permute-start(bf16[4,256,256]{2,1,0:T(8,128)(2,1)S(1)} %get-tuple-element.157), channel_id=1, source_target_pairs={{0,8},{2,10},{4,12},{6,14},{8,0},{10,2},{12,4},{14,6},{16,24},{18,... | collective-permute-start | bytes 1572872 | tf_op jit(solution)/shard_map/ppermute | solution.py:978
  41.3 1.6 %collective-permute-start.5 = (bf16[4,192,256]{2,1,0:T(8,128)(2,1)S(1)}, bf16[4,192,256]{2,1,0:T(8,128)(2,1)S(1)}, u32[]{:S(2)}, u32[]{:S(2)}) collective-permute-start(bf16[4,192,256]{2,1,0:T(8,128)(2,1)S(1)} %get-tuple-element.158), channel_id=1, source_target_pairs={{0,4},{2,6},{4,0},{6,2},{8,12},{10,14},{12,8},{14,10},{16,20},{18,... | collective-permute-start | bytes 1179656 | tf_op jit(solution)/shard_map/ppermute | solution.py:978
  42.9 9.1 %middle_back_kernel.1 = (bf16[256,2048]{1,0:T(8,128)(2,1)S(1)}, bf16[3,256,256]{2,1,0:T(8,128)(2,1)S(1)}, f32[16,2048]{1,0:T(8,128)S(1)}) custom-call(s32[1]{0:T(128)S(6)} %copy.43.refs_0_, f32[256,512]{1,0:T(8,128)S(1)} %get-tuple-element.153.refs_1_, f32[256,2048]{1,0:T(8,128)S(1)} %get-tuple-element.154.refs_2_, ...), custom_call_target="tpu_custom_call" | custom-call | flops 10000000000 | bytes 30000000 | tf_op jit(solution)/shard_map/middle_back_kernel/pallas_call | solution.py:832
  51.9 0.6 collective-permute-done.5
  52.5 0.7 collective-permute-done.4
  53.4 3.2 %conv_back_kernel.1 = (f32[256,512]{1,0:T(8,128)S(1)}, bf16[8,176,256]{2,1,0:T(8,128)(2,1)S(1)}, bf16[8,176,256]{2,1,0:T(8,128)(2,1)S(1)}) custom-call(s32[1]{0:T(128)S(6)} %copy.43.refs_0_, bf16[256,2048]{1,0:T(8,128)(2,1)S(1)} %get-tuple-element.164.refs_1_, bf16[3,256,256]{2,1,0:T(8,128)(2,1)S(1)} %get-tuple-element.165.refs_2_, ...), custom_call_target="tpu_custom_call" | custom-call | flops 5000000000 | bytes 15000000 | tf_op jit(solution)/shard_map/conv_back_kernel/pallas_call | solution.py:832
  56.7 1.8 %collective-permute-start.8 = (bf16[2,192,256]{2,1,0:T(8,128)(2,1)S(1)}, bf16[2,192,256]{2,1,0:T(8,128)(2,1)S(1)}, u32[]{:S(2)}, u32[]{:S(2)}) collective-permute-start(bf16[2,192,256]{2,1,0:T(8,128)(2,1)S(1)} %get-tuple-element.182), channel_id=1, source_target_pairs={{0,8},{2,10},{4,12},{6,14},{8,0},{10,2},{12,4},{14,6},{16,24},{18,... | collective-permute-start | bytes 589832 | tf_op jit(solution)/shard_map/ppermute | solution.py:978
  58.5 1.5 %collective-permute-start.7 = (bf16[2,256,256]{2,1,0:T(8,128)(2,1)S(1)}, bf16[2,256,256]{2,1,0:T(8,128)(2,1)S(1)}, u32[]{:S(2)}, u32[]{:S(2)}) collective-permute-start(bf16[2,256,256]{2,1,0:T(8,128)(2,1)S(1)} %get-tuple-element.181), channel_id=1, source_target_pairs={{0,4},{2,6},{4,0},{6,2},{8,12},{10,14},{12,8},{14,10},{16,20},{18,... | collective-permute-start | bytes 786440 | tf_op jit(solution)/shard_map/ppermute | solution.py:978
  60.2 3.9 %glu_back_kernel.1 = (f32[128,512]{1,0:T(8,128)}, bf16[8,80,256]{2,1,0:T(8,128)(2,1)S(1)}, bf16[8,80,256]{2,1,0:T(8,128)(2,1)S(1)}) custom-call(f32[256,512]{1,0:T(8,128)S(1)} %get-tuple-element.172.refs_0_, f32[256,512]{1,0:T(8,128)S(1)} %get-tuple-element.153.refs_1_, f32[256,512]{1,0:T(8,128)S(1)} %get-tuple-element.173.refs_2_, ...), custom_call_target="tpu_custom_call" | custom-call | flops 7000000000 | bytes 21000000 | tf_op jit(solution)/shard_map/glu_back_kernel/pallas_call | solution.py:832
  64.2 2.7 %collective-permute-done.7.refs_1_ = bf16[2,256,256]{2,1,0:T(8,128)(2,1)S(1)} collective-permute-done((bf16[2,256,256]{2,1,0:T(8,128)(2,1)S(1)}, bf16[2,256,256]{2,1,0:T(8,128)(2,1)S(1)}, u32[]{:S(2)}, u32[]{:S(2)}) %collective-permute-start.7) | collective-permute-done | bytes 262176 | tf_op jit(solution)/shard_map/ppermute | solution.py:978
  66.9 1.5 %collective-permute-start.10 = (bf16[4,176,256]{2,1,0:T(8,128)(2,1)S(1)}, bf16[4,176,256]{2,1,0:T(8,128)(2,1)S(1)}, u32[]{:S(2)}, u32[]{:S(2)}) collective-permute-start(bf16[4,176,256]{2,1,0:T(8,128)(2,1)S(1)} %get-tuple-element.196), channel_id=1, source_target_pairs={{0,4},{2,6},{4,0},{6,2},{8,12},{10,14},{12,8},{14,10},{16,20},{18,... | collective-permute-start | bytes 1081352 | tf_op jit(solution)/shard_map/ppermute | solution.py:978
  68.6 0.6 collective-permute-start.11
  69.2 9.0 %collective-permute-done.10 = bf16[4,176,256]{2,1,0:T(8,128)(2,1)S(1)} collective-permute-done((bf16[4,176,256]{2,1,0:T(8,128)(2,1)S(1)}, bf16[4,176,256]{2,1,0:T(8,128)(2,1)S(1)}, u32[]{:S(2)}, u32[]{:S(2)}) %collective-permute-start.10) | collective-permute-done | bytes 360480 | tf_op jit(solution)/shard_map/ppermute | solution.py:978
  78.4 0.4 collective-permute-start.12
  78.7 1.4 %collective-permute-done.11 = bf16[4,80,256]{2,1,0:T(8,128)(2,1)S(1)} collective-permute-done((bf16[4,80,256]{2,1,0:T(8,128)(2,1)S(1)}, bf16[4,80,256]{2,1,0:T(8,128)(2,1)S(1)}, u32[]{:S(2)}, u32[]{:S(2)}) %collective-permute-start.11) | collective-permute-done | bytes 163872 | tf_op jit(solution)/shard_map/ppermute | solution.py:978
  80.1 0.4 collective-permute-start.13
  80.6 2.6 %collective-permute-start.14 = (bf16[1,448,256]{2,1,0:T(8,128)(2,1)S(1)}, bf16[1,448,256]{2,1,0:T(8,128)(2,1)S(1)}, u32[]{:S(2)}, u32[]{:S(2)}) collective-permute-start(bf16[1,448,256]{2,1,0:T(8,128)(2,1)S(1)} %get-tuple-element.216), channel_id=1, source_target_pairs={{0,16},{2,18},{4,20},{6,22},{8,24},{10,26},{12,28},{14,30},{16,0},... | collective-permute-start | bytes 688136 | tf_op jit(solution)/shard_map/ppermute | solution.py:978
  83.2 4.6 %collective-permute-done.12.refs_1_ = bf16[2,176,256]{2,1,0:T(8,128)(2,1)S(1)} collective-permute-done((bf16[2,176,256]{2,1,0:T(8,128)(2,1)S(1)}, bf16[2,176,256]{2,1,0:T(8,128)(2,1)S(1)}, u32[]{:S(2)}, u32[]{:S(2)}) %collective-permute-start.12) | collective-permute-done | bytes 180256 | tf_op jit(solution)/shard_map/ppermute | solution.py:978
  87.8 1.9 %collective-permute-done.13.refs_3_ = bf16[2,80,256]{2,1,0:T(8,128)(2,1)S(1)} collective-permute-done((bf16[2,80,256]{2,1,0:T(8,128)(2,1)S(1)}, bf16[2,80,256]{2,1,0:T(8,128)(2,1)S(1)}, u32[]{:S(2)}, u32[]{:S(2)}) %collective-permute-start.13) | collective-permute-done | bytes 81952 | tf_op jit(solution)/shard_map/ppermute | solution.py:978
  89.7 2.4 %collective-permute-done.14 = bf16[1,448,256]{2,1,0:T(8,128)(2,1)S(1)} collective-permute-done((bf16[1,448,256]{2,1,0:T(8,128)(2,1)S(1)}, bf16[1,448,256]{2,1,0:T(8,128)(2,1)S(1)}, u32[]{:S(2)}, u32[]{:S(2)}) %collective-permute-start.14) | collective-permute-done | bytes 229408 | tf_op jit(solution)/shard_map/ppermute | solution.py:978
  92.1 1.8 %collective-permute-start.15 = (bf16[448,256]{1,0:T(8,128)(2,1)S(1)}, bf16[448,256]{1,0:T(8,128)(2,1)S(1)}, u32[]{:S(2)}, u32[]{:S(2)}) collective-permute-start(bf16[448,256]{1,0:T(8,128)(2,1)S(1)} %fusion.refs_0_), channel_id=1, source_target_pairs={{0,1},{1,0},{2,3},{3,2},{4,5},{5,4},{6,7},{7,6},{8,9},{9,8},{10,11... | collective-permute-start | bytes 688136 | tf_op jit(solution)/shard_map/ppermute | solution.py:975
  93.9 5.7 %collective-permute-done.15.refs_1_ = bf16[448,256]{1,0:T(8,128)(2,1)S(1)} collective-permute-done((bf16[448,256]{1,0:T(8,128)(2,1)S(1)}, bf16[448,256]{1,0:T(8,128)(2,1)S(1)}, u32[]{:S(2)}, u32[]{:S(2)}) %collective-permute-start.15) | collective-permute-done | bytes 229408 | tf_op jit(solution)/shard_map/ppermute | solution.py:975
  99.8 1.6 %collective-permute-start.17 = (bf16[256,256]{1,0:T(8,128)(2,1)S(1)}, bf16[256,256]{1,0:T(8,128)(2,1)S(1)}, u32[]{:S(2)}, u32[]{:S(2)}) collective-permute-start(bf16[256,256]{1,0:T(8,128)(2,1)S(1)} %fusion.1.refs_0_), channel_id=1, source_target_pairs={{0,1},{1,0},{2,3},{3,2},{4,5},{5,4},{6,7},{7,6},{8,9},{9,8},{10,11... | collective-permute-start | bytes 393224 | tf_op jit(solution)/shard_map/ppermute | solution.py:975
  101.4 1.0 finish_early_kernel.1
  102.4 2.4 %collective-permute-done.17.refs_1_ = bf16[256,256]{1,0:T(8,128)(2,1)S(1)} collective-permute-done((bf16[256,256]{1,0:T(8,128)(2,1)S(1)}, bf16[256,256]{1,0:T(8,128)(2,1)S(1)}, u32[]{:S(2)}, u32[]{:S(2)}) %collective-permute-start.17) | collective-permute-done | bytes 131104 | tf_op jit(solution)/shard_map/ppermute | solution.py:975
  104.8 0.8 finish_late_kernel.1
  (23 shorter events, 1.7 us)
Async XLA Ops:
  0.7 7.5 %collective-permute-start = (bf16[128,512]{1,0:T(8,128)(2,1)}, bf16[128,512]{1,0:T(8,128)(2,1)S(1)}, u32[]{:S(2)}, u32[]{:S(2)}) collective-permute-start(bf16[128,512]{1,0:T(8,128)(2,1)} %bitcast.8), channel_id=1, source_target_pairs={{0,1},{1,0},{2,3},{3,2},{4,5},{5,4},{6,7},{7,6},{8,9},{9,8},{10,11... | collective-permute-start | bytes 393224 | tf_op jit(solution)/shard_map/ppermute | solution.py:882
  3.7 6.5 %collective-permute-start.1 = (bf16[128,512]{1,0:T(8,128)(2,1)}, bf16[128,512]{1,0:T(8,128)(2,1)S(1)}, u32[]{:S(2)}, u32[]{:S(2)}) collective-permute-start(bf16[128,512]{1,0:T(8,128)(2,1)} %bitcast.10), channel_id=1, source_target_pairs={{0,1},{1,0},{2,3},{3,2},{4,5},{5,4},{6,7},{7,6},{8,9},{9,8},{10,11... | collective-permute-start | bytes 393224 | tf_op jit(solution)/shard_map/ppermute | solution.py:883
  29.4 9.5 %collective-permute-start.2 = (bf16[8,256,256]{2,1,0:T(8,128)(2,1)S(1)}, bf16[8,256,256]{2,1,0:T(8,128)(2,1)S(1)}, u32[]{:S(2)}, u32[]{:S(2)}) collective-permute-start(bf16[8,256,256]{2,1,0:T(8,128)(2,1)S(1)} %get-tuple-element.144), channel_id=1, source_target_pairs={{0,2},{2,0},{4,6},{6,4},{8,10},{10,8},{12,14},{14,12},{16,18},{18,... | collective-permute-start | bytes 3145736 | tf_op jit(solution)/shard_map/ppermute | solution.py:978
  38.3 2.7 %collective-permute-start.3 = (bf16[8,192,256]{2,1,0:T(8,128)(2,1)S(1)}, bf16[8,192,256]{2,1,0:T(8,128)(2,1)S(1)}, u32[]{:S(2)}, u32[]{:S(2)}) collective-permute-start(bf16[8,192,256]{2,1,0:T(8,128)(2,1)S(1)} %get-tuple-element.149), channel_id=1, source_target_pairs={{0,2},{2,0},{4,6},{6,4},{8,10},{10,8},{12,14},{14,12},{16,18},{18,... | collective-permute-start | bytes 2359304 | tf_op jit(solution)/shard_map/ppermute | solution.py:978
  39.1 14.0 %collective-permute-start.4 = (bf16[4,256,256]{2,1,0:T(8,128)(2,1)S(1)}, bf16[4,256,256]{2,1,0:T(8,128)(2,1)S(1)}, u32[]{:S(2)}, u32[]{:S(2)}) collective-permute-start(bf16[4,256,256]{2,1,0:T(8,128)(2,1)S(1)} %get-tuple-element.157), channel_id=1, source_target_pairs={{0,8},{2,10},{4,12},{6,14},{8,0},{10,2},{12,4},{14,6},{16,24},{18,... | collective-permute-start | bytes 1572872 | tf_op jit(solution)/shard_map/ppermute | solution.py:978
  41.3 11.2 %collective-permute-start.5 = (bf16[4,192,256]{2,1,0:T(8,128)(2,1)S(1)}, bf16[4,192,256]{2,1,0:T(8,128)(2,1)S(1)}, u32[]{:S(2)}, u32[]{:S(2)}) collective-permute-start(bf16[4,192,256]{2,1,0:T(8,128)(2,1)S(1)} %get-tuple-element.158), channel_id=1, source_target_pairs={{0,4},{2,6},{4,0},{6,2},{8,12},{10,14},{12,8},{14,10},{16,20},{18,... | collective-permute-start | bytes 1179656 | tf_op jit(solution)/shard_map/ppermute | solution.py:978
  56.7 3.4 %collective-permute-start.6 = (bf16[8,176,256]{2,1,0:T(8,128)(2,1)S(1)}, bf16[8,176,256]{2,1,0:T(8,128)(2,1)S(1)}, u32[]{:S(2)}, u32[]{:S(2)}) collective-permute-start(bf16[8,176,256]{2,1,0:T(8,128)(2,1)S(1)} %get-tuple-element.168), channel_id=1, source_target_pairs={{0,2},{2,0},{4,6},{6,4},{8,10},{10,8},{12,14},{14,12},{16,18},{18,... | collective-permute-start | bytes 2162696 | tf_op jit(solution)/shard_map/ppermute | solution.py:978
  56.7 7.5 %collective-permute-start.8 = (bf16[2,192,256]{2,1,0:T(8,128)(2,1)S(1)}, bf16[2,192,256]{2,1,0:T(8,128)(2,1)S(1)}, u32[]{:S(2)}, u32[]{:S(2)}) collective-permute-start(bf16[2,192,256]{2,1,0:T(8,128)(2,1)S(1)} %get-tuple-element.182), channel_id=1, source_target_pairs={{0,8},{2,10},{4,12},{6,14},{8,0},{10,2},{12,4},{14,6},{16,24},{18,... | collective-permute-start | bytes 589832 | tf_op jit(solution)/shard_map/ppermute | solution.py:978
  58.5 8.4 %collective-permute-start.7 = (bf16[2,256,256]{2,1,0:T(8,128)(2,1)S(1)}, bf16[2,256,256]{2,1,0:T(8,128)(2,1)S(1)}, u32[]{:S(2)}, u32[]{:S(2)}) collective-permute-start(bf16[2,256,256]{2,1,0:T(8,128)(2,1)S(1)} %get-tuple-element.181), channel_id=1, source_target_pairs={{0,4},{2,6},{4,0},{6,2},{8,12},{10,14},{12,8},{14,10},{16,20},{18,... | collective-permute-start | bytes 786440 | tf_op jit(solution)/shard_map/ppermute | solution.py:978
  64.1 4.4 %collective-permute-start.9 = (bf16[8,80,256]{2,1,0:T(8,128)(2,1)S(1)}, bf16[8,80,256]{2,1,0:T(8,128)(2,1)S(1)}, u32[]{:S(2)}, u32[]{:S(2)}) collective-permute-start(bf16[8,80,256]{2,1,0:T(8,128)(2,1)S(1)} %get-tuple-element.191), channel_id=1, source_target_pairs={{0,2},{2,0},{4,6},{6,4},{8,10},{10,8},{12,14},{14,12},{16,18},{18,... | collective-permute-start | bytes 983048 | tf_op jit(solution)/shard_map/ppermute | solution.py:978
  66.9 11.3 %collective-permute-start.10 = (bf16[4,176,256]{2,1,0:T(8,128)(2,1)S(1)}, bf16[4,176,256]{2,1,0:T(8,128)(2,1)S(1)}, u32[]{:S(2)}, u32[]{:S(2)}) collective-permute-start(bf16[4,176,256]{2,1,0:T(8,128)(2,1)S(1)} %get-tuple-element.196), channel_id=1, source_target_pairs={{0,4},{2,6},{4,0},{6,2},{8,12},{10,14},{12,8},{14,10},{16,20},{18,... | collective-permute-start | bytes 1081352 | tf_op jit(solution)/shard_map/ppermute | solution.py:978
  68.6 11.5 %collective-permute-start.11 = (bf16[4,80,256]{2,1,0:T(8,128)(2,1)S(1)}, bf16[4,80,256]{2,1,0:T(8,128)(2,1)S(1)}, u32[]{:S(2)}, u32[]{:S(2)}) collective-permute-start(bf16[4,80,256]{2,1,0:T(8,128)(2,1)S(1)} %get-tuple-element.201), channel_id=1, source_target_pairs={{0,4},{2,6},{4,0},{6,2},{8,12},{10,14},{12,8},{14,10},{16,20},{18,... | collective-permute-start | bytes 491528 | tf_op jit(solution)/shard_map/ppermute | solution.py:978
  78.4 9.4 %collective-permute-start.12 = (bf16[2,176,256]{2,1,0:T(8,128)(2,1)S(1)}, bf16[2,176,256]{2,1,0:T(8,128)(2,1)S(1)}, u32[]{:S(2)}, u32[]{:S(2)}) collective-permute-start(bf16[2,176,256]{2,1,0:T(8,128)(2,1)S(1)} %get-tuple-element.206), channel_id=1, source_target_pairs={{0,8},{2,10},{4,12},{6,14},{8,0},{10,2},{12,4},{14,6},{16,24},{18,... | collective-permute-start | bytes 540680 | tf_op jit(solution)/shard_map/ppermute | solution.py:978
  80.1 9.5 %collective-permute-start.13 = (bf16[2,80,256]{2,1,0:T(8,128)(2,1)S(1)}, bf16[2,80,256]{2,1,0:T(8,128)(2,1)S(1)}, u32[]{:S(2)}, u32[]{:S(2)}) collective-permute-start(bf16[2,80,256]{2,1,0:T(8,128)(2,1)S(1)} %get-tuple-element.207), channel_id=1, source_target_pairs={{0,8},{2,10},{4,12},{6,14},{8,0},{10,2},{12,4},{14,6},{16,24},{18,... | collective-permute-start | bytes 245768 | tf_op jit(solution)/shard_map/ppermute | solution.py:978
  80.6 11.5 %collective-permute-start.14 = (bf16[1,448,256]{2,1,0:T(8,128)(2,1)S(1)}, bf16[1,448,256]{2,1,0:T(8,128)(2,1)S(1)}, u32[]{:S(2)}, u32[]{:S(2)}) collective-permute-start(bf16[1,448,256]{2,1,0:T(8,128)(2,1)S(1)} %get-tuple-element.216), channel_id=1, source_target_pairs={{0,16},{2,18},{4,20},{6,22},{8,24},{10,26},{12,28},{14,30},{16,0},... | collective-permute-start | bytes 688136 | tf_op jit(solution)/shard_map/ppermute | solution.py:978
  92.1 7.5 %collective-permute-start.15 = (bf16[448,256]{1,0:T(8,128)(2,1)S(1)}, bf16[448,256]{1,0:T(8,128)(2,1)S(1)}, u32[]{:S(2)}, u32[]{:S(2)}) collective-permute-start(bf16[448,256]{1,0:T(8,128)(2,1)S(1)} %fusion.refs_0_), channel_id=1, source_target_pairs={{0,1},{1,0},{2,3},{3,2},{4,5},{5,4},{6,7},{7,6},{8,9},{9,8},{10,11... | collective-permute-start | bytes 688136 | tf_op jit(solution)/shard_map/ppermute | solution.py:975
  93.9 5.9 %collective-permute-start.16 = (bf16[1,256,256]{2,1,0:T(8,128)(2,1)S(1)}, bf16[1,256,256]{2,1,0:T(8,128)(2,1)S(1)}, u32[]{:S(2)}, u32[]{:S(2)}) collective-permute-start(bf16[1,256,256]{2,1,0:T(8,128)(2,1)S(1)} %get-tuple-element.223), channel_id=1, source_target_pairs={{0,16},{2,18},{4,20},{6,22},{8,24},{10,26},{12,28},{14,30},{16,0},... | collective-permute-start | bytes 393224 | tf_op jit(solution)/shard_map/ppermute | solution.py:978
  99.8 5.0 %collective-permute-start.17 = (bf16[256,256]{1,0:T(8,128)(2,1)S(1)}, bf16[256,256]{1,0:T(8,128)(2,1)S(1)}, u32[]{:S(2)}, u32[]{:S(2)}) collective-permute-start(bf16[256,256]{1,0:T(8,128)(2,1)S(1)} %fusion.1.refs_0_), channel_id=1, source_target_pairs={{0,1},{1,0},{2,3},{3,2},{4,5},{5,4},{6,7},{7,6},{8,9},{9,8},{10,11... | collective-permute-start | bytes 393224 | tf_op jit(solution)/shard_map/ppermute | solution.py:975

commit v4 on v3

--- a/solution.py
+++ b/solution.py
@@ -14,11 +14,11 @@
 GROUPS = 16
 F32 = jnp.float32
 BF16 = jnp.bfloat16
-VMEM_BYTES = 40 * 1024 * 1024
+VMEM_BYTES = 28 * 1024 * 1024
 FFN_BITS = (2, 1, 3)
 ATTN_BITS = (1, 2, 3)
 CONV_BITS = (1, 2, 3)
-GLU_BITS = (1, 2, 3)
+GLU_BITS = (2, 1, 3)
 
 
 def mm(a, b):
@@ -82,12 +82,16 @@
 
 
 def for_slots(keep, send, bits, body):
-    def visit(p, c):
-        for sent, out in ((0, keep), (1, send)):
-            body(p, slot_block(p, sent, bits), out)
-        return c
-
-    lax.fori_loop(0, GROUPS // 2, visit, 0)
+    count = GROUPS // 2 // len(send)
+    for i, piece in enumerate(send):
+
+        def visit(q, c, i=i, piece=piece):
+            p = i * count + q
+            body(p, slot_block(p, 0, bits), keep)
+            body(q, slot_block(p, 1, bits), piece)
+            return c
+
+        lax.fori_loop(0, count, visit, 0)
 
 
 def place_rows(grad, keep, send, bits, at, rows):
@@ -97,10 +101,58 @@
     for_slots(keep, send, bits, one)
 
 
+def gated(tokens, at, place, length, gain, shift, glu_b, glu_w, first, joined, after_glu, second):
+    part, width = tokens.shape
+
+    def first_rows(r, c):
+        vhat, _ = normalized(tokens[pl.ds(r, 64), :].astype(F32))
+        first[pl.ds(pl.multiple_of(at + r, 64), 64), :] = (vhat * gain[0] + shift[0]).astype(BF16)
+        return c
+
+    row_blocks(part, 64, first_rows, unroll=2)
+    every = pl.ds(at, part)
+    for n in range(2 * width // TILE):
+        joined[every, col(n)] = mm(first[every, :], glu_w[:, col(n)]) + glu_b[:, col(n)]
+
+    def glu_rows(r, c):
+        rows = pl.ds(pl.multiple_of(at + r, 32), 32)
+        gate = jax.nn.sigmoid(joined[rows, width:])
+        joined[rows, width:] = gate
+        v = tokens[pl.ds(r, 32), :].astype(F32) + joined[rows, :width] * gate
+        after_glu[rows, :] = v
+        vhat, _ = normalized(v)
+        valid = valid_rows(place + r, 32, length)
+        second[rows, :] = ((vhat * gain[1] + shift[1]) * valid).astype(BF16)
+        return c
+
+    row_blocks(part, 32, glu_rows, unroll=2)
+
+
+def open_kernel(lengths, far, first, joined, after_glu, second):
+    mine, gains, shifts, glu_bias, glu_w, conv_w, left_w, point_w = far
+    part = first.shape[0]
+    tokens, gains, shifts = mine(), gains(), shifts()
+    gain = [gains[k : k + 1, :].astype(F32) for k in range(2)]
+    shift = [shifts[k : k + 1, :].astype(F32) for k in range(2)]
+    place = lax.axis_index("head") * part
+    glu_b, glu_w = vector(glu_bias()), glu_w()
+    gated(tokens, 0, place, lengths[0], gain, shift, glu_b, glu_w, first, joined, after_glu, second)
+    for get in (conv_w, left_w, point_w):
+        get()
+
+
 def forward_kernel(
     lengths,
     other,
-    cot_other,
+    mine,
+    own_first,
+    own_joined,
+    own_after_glu,
+    own_second,
+    glu_w,
+    conv_w,
+    left_w,
+    point_w,
     far,
     out_tokens,
     stream,
@@ -116,19 +168,11 @@
     packed,
     probs,
     context,
-    d_after,
-    small,
-    keep,
-    send,
-    third,
-    sides,
     after_attn,
     fifth,
     hidden,
-    cot,
-    d_hidden,
-    d_fifth,
-    grad,
+    third,
+    sides,
 ):
     part, width = other.shape
     seq = 2 * part
@@ -137,69 +181,48 @@
     side = lax.axis_index("head")
     length = lengths[0]
     own = pl.ds(pl.multiple_of(side * part, part), part)
-    opposite = pl.ds(pl.multiple_of((1 - side) * part, part), part)
+    opposite = pl.multiple_of((1 - side) * part, part)
     (
-        mine,
         gains,
         shifts,
         glu_bias,
-        glu_w,
         conv_bias,
-        conv_w,
         left_bias,
-        left_w,
         mid_gain,
         mid_bias,
         depth_w,
         point_bias,
-        point_w,
         qkv_w,
         out_w,
         ffn_in_bias,
         ffn_in_w,
         ffn_out_bias,
         ffn_out_w,
-        cot_mine,
     ) = far
-    stream[opposite, :] = other[...]
-    cot[opposite, :] = cot_other[...]
-    stream[own, :] = mine()[...]
+    for whole, piece in (
+        (stream, mine),
+        (first, own_first),
+        (joined, own_joined),
+        (after_glu, own_after_glu),
+        (second, own_second),
+    ):
+        whole[own, :] = piece[...]
+    stream[pl.ds(opposite, part), :] = other[...]
     gains, shifts = gains(), shifts()
     gain = [gains[k : k + 1, :].astype(F32) for k in range(4)]
     shift = [shifts[k : k + 1, :].astype(F32) for k in range(4)]
-
-    def first_rows(r, c):
-        rows = pl.ds(r, 64)
-        vhat, _ = normalized(stream[rows, :].astype(F32))
-        first[rows, :] = (vhat * gain[0] + shift[0]).astype(BF16)
-        return c
-
-    row_blocks(seq, 64, first_rows, unroll=2)
-    glu_b, glu_w = vector(glu_bias()), glu_w()
-    for n in range(2 * width // TILE):
-        joined[:, col(n)] = mm(first[...], glu_w[:, col(n)]) + glu_b[:, col(n)]
-
-    def glu_rows(r, c):
-        rows = pl.ds(r, 32)
-        gate = jax.nn.sigmoid(joined[rows, width:])
-        joined[rows, width:] = gate
-        v = stream[rows, :].astype(F32) + joined[rows, :width] * gate
-        after_glu[rows, :] = v
-        vhat, _ = normalized(v)
-        second[rows, :] = ((vhat * gain[1] + shift[1]) * valid_rows(r, 32, length)).astype(BF16)
-        return c
-
-    row_blocks(seq, 32, glu_rows, unroll=2)
+    gated(
+        other, opposite, opposite, length, gain, shift, vector(glu_bias()), glu_w, first, joined, after_glu, second
+    )
     blank = jnp.zeros((8, half), F32)
     for k in range(2):
         sides[k, 0:8, :] = blank
         sides[k, 8 + seq : 16 + seq, :] = blank
-    conv_w = conv_w()
     sides[0, 8 : 8 + seq, :] = mm(second[...], conv_w[0])
     sides[1, 8 : 8 + seq, :] = mm(second[...], conv_w[2])
     right_pre[...] = mm(second[...], conv_w[1]) + vector(conv_bias())
     right_pre[...] = right_pre[...] + sides[0, 7 : 7 + seq, :] + sides[1, 9 : 9 + seq, :]
-    left_b, left_w = vector(left_bias()), left_w()
+    left_b = vector(left_bias())
     for n in range(ffn // TILE):
         left_pre[:, col(n)] = mm(second[...], left_w[:, col(n)]) + left_b[:, col(n)]
     mid_g, mid_b, depth_w = vector(mid_gain()), vector(mid_bias()), depth_w()
@@ -230,7 +253,7 @@
 
     lax.fori_loop(0, chunks, depth_lanes, 0)
     after_conv[:, :half] = (
-        after_glu[:, :half] + mm(depth_low[...], point_w()[...]) + vector(point_bias())
+        after_glu[:, :half] + mm(depth_low[...], point_w[...]) + vector(point_bias())
     )
     after_conv[:, half:] = after_glu[:, half:]
 
@@ -290,6 +313,32 @@
             + ffn_out_b[:, col(n)]
         ).astype(BF16)
 
+
+def ffn_back_kernel(
+    cot_other,
+    after_attn,
+    fifth,
+    hidden,
+    ffn_in_w,
+    ffn_out_w,
+    far,
+    d_after,
+    small,
+    keep,
+    send,
+    cot,
+    d_hidden,
+    d_fifth,
+    grad,
+):
+    seq, width = fifth.shape
+    part = seq // 2
+    ffn = hidden.shape[1]
+    side = lax.axis_index("head")
+    cot_mine, gains = far
+    own = pl.ds(pl.multiple_of(side * part, part), part)
+    opposite = pl.ds(pl.multiple_of((1 - side) * part, part), part)
+    cot[opposite, :] = cot_other[...]
     cot[own, :] = cot_mine()[...]
     for n in range(ffn // TILE):
         back = mm_nt(cot[...], ffn_out_w[col(n), :])
@@ -301,17 +350,19 @@
 
     cot_half = cot[:, pl.ds(pl.multiple_of(side * (width // 2), width // 2), width // 2)]
     per_row = ffn // GROUPS
+    gain = gains()[3:4, :].astype(F32)
     sums = [jnp.zeros((8, width), F32)] * 3
     for p in range(GROUPS // 2):
         block = slice(p * seq // 8, (p + 1) * seq // 8)
         vhat, rate = normalized(after_attn[block, :])
         e = d_fifth[block, :]
         given = cot[block, :].astype(F32)
-        d_after[block, :] = given + norm_back(vhat, rate, e * gain[3])
+        d_after[block, :] = given + norm_back(vhat, rate, e * gain)
         sums = [total + part_sums(v) for total, v in zip(sums, (e * vhat, e, given))]
-        for sent, out in ((0, keep), (1, send)):
+        count = GROUPS // 2 // len(send)
+        for sent, out, place in ((0, keep, p), (1, send[p // count], p % count)):
             at = pl.multiple_of(slot_block(p, sent, FFN_BITS) * per_row, per_row)
-            out[p, 0:per_row, :] = mm_tn(hidden[:, pl.ds(at, per_row)], cot_half).astype(BF16)
+            out[place, 0:per_row, :] = mm_tn(hidden[:, pl.ds(at, per_row)], cot_half).astype(BF16)
     for k in range(3):
         small[1:2, k * width : (k + 1) * width] = sum_tokens(sums[k])
 
@@ -336,6 +387,8 @@
     fourth,
     after_conv,
     depth_low,
+    out_w,
+    qkv_w,
     far,
     d_after_conv,
     small,
@@ -350,12 +403,11 @@
 ):
     seq, width = d_after.shape
     side = lax.axis_index("head")
-    out_w, qkv_w, gains = far
+    (gains,) = far
     half = d_sep.shape[1]
     ffn = depth_low.shape[1]
     rows = width // GROUPS
     d_attn[...] = d_after[...].astype(BF16)
-    out_w = out_w()
     for n in range(width // TILE):
         d_context[:, col(n)] = mm_nt(d_attn[...], out_w[col(n), :]).astype(BF16)
     low_lanes = lax.broadcasted_iota(jnp.int32, (1, LANES), 1) < HEAD_DIM
@@ -386,7 +438,6 @@
         return c
 
     lax.fori_loop(0, width // LANES, head_pair, 0)
-    qkv_w = qkv_w()
     for n in range(width // TILE):
         d_fourth[:, col(n)] = mm_nt(d_packed[...], qkv_w[col(n), :])
     gain = gains()[2:3, :].astype(F32)
@@ -433,6 +484,7 @@
     d_after_conv,
     left_pre,
     right_pre,
+    point_w,
     far,
     d_left,
     taps_right,
@@ -450,14 +502,13 @@
     ffn = left_pre.shape[1]
     half = right_pre.shape[1]
     length = lengths[0]
-    point_w, mid_gain, mid_bias, depth_w = far
+    mid_gain, mid_bias, depth_w = far
     chunks = ffn // LANES
     edge = jnp.zeros((8, LANES), F32)
     for k in range(chunks):
         d_depth[k, 0:8, :] = edge
         d_depth[k, 8 + seq : 16 + seq, :] = edge
     d_sep = d_after_conv[:, :half].astype(BF16)
-    point_w = point_w()
     for n in range(ffn // TILE):
         block = mm_nt(d_sep, point_w[col(n), :])
         for m in range(TILE // LANES):
@@ -540,6 +591,8 @@
     d_left,
     taps_right,
     second,
+    left_w,
+    conv_w,
     far,
     d_second,
     keep,
@@ -574,7 +627,6 @@
         ].astype(BF16)
 
     for_slots(keep, send, CONV_BITS, conv_slot)
-    left_w, conv_w = (get() for get in far)
     for n in range(width // TILE):
         total = mm_nt(d_left[...], left_w[col(n), :])
         for tap in range(3):
@@ -592,6 +644,7 @@
     small_ffn,
     small_attn,
     small_conv,
+    glu_w,
     far,
     grad_tokens,
     keep,
@@ -606,8 +659,7 @@
     seq, width = d_second.shape
     part = seq // 2
     side = lax.axis_index("head")
-    gains, glu_w = far
-    gains = gains()
+    gains = far[0]()
     gain = [gains[k : k + 1, :].astype(F32) for k in range(2)]
 
     def glu_rows(r, c):
@@ -633,7 +685,6 @@
     nothing = jnp.zeros((8, width), F32)
     sums = row_blocks(seq, 32, glu_rows, (nothing,) * 4, unroll=2)
     gain_one, shift_one, g_value, g_gate = (sum_tokens(v) for v in sums)
-    glu_w = glu_w()
     for n in range(width // TILE):
         d_first[:, col(n)] = mm_nt(d_joined[...], glu_w[col(n), :])
 
@@ -703,14 +754,16 @@
     for_slots(keep, send, GLU_BITS, small_slot)
 
 
-def add_kernel(*refs):
-    *inputs, far, keep, send = refs
+def add_kernel(keeps, gots, far, keep, send):
     at = 0
-    for kept, got in zip(inputs[::2], inputs[1::2]):
+    for kept, got in zip(keeps, gots):
         rows = kept.shape[1]
-        for out, place in ((keep, 0), (send, 1)):
-            total = kept[place].astype(F32) + got[place].astype(F32)
-            out[0, at : at + rows, :] = total.astype(BF16)
+        half = kept.shape[0] // 2
+        count = kept.shape[0] // len(got)
+        for i in range(kept.shape[0]):
+            total = kept[i].astype(F32) + got[i // count][i % count].astype(F32)
+            out = keep if i < half else send
+            out[i % half, at : at + rows, :] = total.astype(BF16)
         at += rows
 
 
@@ -794,21 +847,29 @@
         point_bias[col(k, LANES)] = block[2 + k, LANES : 2 * LANES]
 
 
-def call(kernel, outs, scratch, near, far, micros=2, scalars=0):
+def call(kernel, outs, scratch, near, far, micros=0, scalars=0, kept=()):
     smem = pl.BlockSpec(memory_space=pltpu.SMEM)
     vmem = pl.BlockSpec(memory_space=pltpu.VMEM)
     anywhere = pl.BlockSpec(memory_space=pltpu.HBM)
 
+    near, inside = jax.tree.flatten(near)
+    outs, outside = jax.tree.flatten(outs, is_leaf=lambda v: isinstance(v, tuple))
+    own = len(outs)
+    outs = outs + [(far[i].shape, far[i].dtype) for i in kept]
+
     def body(*refs):
-        inputs = refs[: len(near)]
+        inputs = inside.unflatten(refs[: len(near)])
         sources = refs[len(near) : len(near) + len(far)]
-        results = refs[len(near) + len(far) : len(near) + len(far) + len(outs)]
-        rest = refs[len(near) + len(far) + len(outs) :]
+        first = len(near) + len(far)
+        results = outside.unflatten(refs[first : first + own])
+        held = refs[first + own : first + len(outs)]
+        rest = refs[first + len(outs) :]
         if not far:
             kernel(*inputs, (), *results, *rest)
             return
         *rest, done = rest
-        buffers = rest[len(scratch) :]
+        fresh = iter(rest[len(scratch) :])
+        buffers = [held[kept.index(i)] if i in kept else next(fresh) for i in range(len(far))]
         copies = [
             pltpu.make_async_copy(source, buffer, done.at[i])
             for i, (source, buffer) in enumerate(zip(sources, buffers))
@@ -827,9 +888,9 @@
 
     temporaries = [pltpu.VMEM(shape, dtype) for shape, dtype in scratch]
     if far:
-        temporaries += [pltpu.VMEM(v.shape, v.dtype) for v in far]
+        temporaries += [pltpu.VMEM(v.shape, v.dtype) for i, v in enumerate(far) if i not in kept]
         temporaries.append(pltpu.SemaphoreType.DMA((len(far),)))
-    return pl.pallas_call(
+    results = pl.pallas_call(
         body,
         out_shape=tuple(jax.ShapeDtypeStruct(shape, dtype) for shape, dtype in outs),
         in_specs=[smem] * scalars + [vmem] * (len(near) - scalars) + [anywhere] * len(far),
@@ -841,6 +902,7 @@
         ),
         name=kernel.__name__,
     )(*near, *[pltpu.with_memory_space_constraint(v, pltpu.HBM) for v in far])
+    return [*outside.unflatten(results[:own]), *results[own:]]
 
 
 def per_device(
@@ -882,12 +944,28 @@
     other = lax.ppermute(mine, "head", swap)
     cot_other = lax.ppermute(cot_mine, "head", swap)
 
-    def slot_outs(rows):
-        return [((GROUPS // 2, rows, TILE), BF16)] * 2
+    def slot_outs(rows, pieces=1):
+        count = GROUPS // 2
+        return [((count, rows, TILE), BF16), [((count // pieces, rows, TILE), BF16)] * pieces]
 
     rows = width // GROUPS
     per_row = ffn // GROUPS
     ffn_rows = per_row + ffn // 2 // TILE * rows
+    own_first, own_joined, own_after_glu, own_second, mine, glu_w, conv_w, left_w, point_w = call(
+        open_kernel,
+        [
+            ((part, width), BF16),
+            ((part, 2 * width), F32),
+            ((part, width), F32),
+            ((part, width), BF16),
+        ],
+        [],
+        [lengths],
+        [mine, norm_gain, norm_bias, glu_bias, glu_weight, conv_weight, left_weight, point_weight],
+        micros=1,
+        scalars=1,
+        kept=(0, 4, 5, 6, 7),
+    )
     (
         out_tokens,
         stream,
@@ -903,10 +981,13 @@
         packed,
         probs,
         context,
-        d_after,
-        small_ffn,
-        keep_ffn,
-        send_ffn,
+        after_attn,
+        fifth,
+        hidden,
+        qkv_w,
+        out_w,
+        ffn_in_w,
+        ffn_out_w,
     ) = call(
         forward_kernel,
         [
@@ -925,91 +1006,113 @@
             ((heads, seq, seq), F32),
             ((seq, width), BF16),
             ((seq, width), F32),
-            ((8, ffn), F32),
-        ]
-        + slot_outs(ffn_rows),
+            ((seq, width), BF16),
+            ((seq, ffn), BF16),
+        ],
         [
             ((ffn // LANES, seq + 16, LANES), F32),
             ((2, seq + 16, half), F32),
-            ((seq, width), F32),
-            ((seq, width), BF16),
-            ((seq, ffn), BF16),
-            ((seq, width), BF16),
-            ((seq, ffn), BF16),
-            ((seq, width), F32),
-            ((width, TILE), F32),
         ],
-        [lengths, other, cot_other],
         [
+            lengths,
+            other,
             mine,
+            own_first,
+            own_joined,
+            own_after_glu,
+            own_second,
+            glu_w,
+            conv_w,
+            left_w,
+            point_w,
+        ],
+        [
             norm_gain,
             norm_bias,
             glu_bias,
-            glu_weight,
             conv_bias,
-            conv_weight,
             left_bias,
-            left_weight,
             mid_gain,
             mid_bias,
             depth_weight,
             point_bias,
-            point_weight,
             qkv_weight,
             out_weight,
             ffn_in_bias,
             ffn_in_weight,
             ffn_out_bias,
             ffn_out_weight,
-            cot_mine,
         ],
-        micros=25,
+        micros=14,
         scalars=1,
+        kept=(9, 10, 12, 14),
     )
+    d_after, small_ffn, keep_ffn, send_ffn = call(
+        ffn_back_kernel,
+        [((seq, width), F32), ((8, ffn), F32)] + slot_outs(ffn_rows),
+        [
+            ((seq, width), BF16),
+            ((seq, ffn), BF16),
+            ((seq, width), F32),
+            ((width, TILE), F32),
+        ],
+        [cot_other, after_attn, fifth, hidden, ffn_in_w, ffn_out_w],
+        [cot_mine, norm_gain],
+        micros=5,
+    )
+
     class Chunk:
         def __init__(self, keep, send, bits):
             self.keep, self.send, self.bits = keep, send, list(bits)
 
         def start(self):
             if not self.bits:
-                self.got = lax.ppermute(self.keep, "head", swap)
+                self.got = [lax.ppermute(self.keep, "head", swap)]
                 return
             step = below << self.bits.pop(0)
-            self.got = lax.ppermute(self.send, "dp", [(i, i ^ step) for i in range(shards)])
-
-        def add(self):
-            n = self.keep.shape[0] // 2
-
-            def total(piece):
-                return (self.keep[piece].astype(F32) + self.got[piece].astype(F32)).astype(BF16)
-
-            if n > 0:
-                self.keep, self.send = total(slice(0, n)), total(slice(n, 2 * n))
-                return
-            total = total(slice(0, 1))[0]
-            step = 1
-            while step < below:
-                total = total + lax.ppermute(total, "dp", [(i, i ^ step) for i in range(shards)])
-                step *= 2
-            self.keep, self.send = total, total
-
-    def wave(held, *chunks, joined=False):
-        gots = [c.got for c in chunks]
-        held, gots = lax.optimization_barrier((held, gots))
+            pairs = [(i, i ^ step) for i in range(shards)]
+            self.got = [lax.ppermute(v, "dp", pairs) for v in self.send]
+
+    def last_sum(keep, got):
+        total = (keep[0].astype(F32) + got[0].astype(F32)).astype(BF16)
+        step = 1
+        while step < below:
+            total = total + lax.ppermute(total, "dp", [(i, i ^ step) for i in range(shards)])
+            step *= 2
+        return total
+
+    def added(*chunks):
+        keep = chunks[0].keep
+        if keep.shape[0] == 1:
+            return last_sum(keep, chunks[0].got[0]), None
+        if len(chunks) == 1 and len(chunks[0].got) < 3:
+            (c,) = chunks
+            n = keep.shape[0] // 2
+            got = c.got if len(c.got) == 2 else (c.got[0][:n], c.got[0][n:])
+            return tuple(
+                (keep[half * n : half * n + n].astype(F32) + got[half].astype(F32)).astype(BF16)
+                for half in range(2)
+            )
+        shape = ((keep.shape[0] // 2, sum(c.keep.shape[1] for c in chunks), TILE), BF16)
+        return call(
+            add_kernel, [shape, shape], [], [[c.keep for c in chunks], [c.got for c in chunks]], []
+        )
+
+    def received(held, *chunks):
+        held, gots = lax.optimization_barrier((held, [c.got for c in chunks]))
         for c, got in zip(chunks, gots):
             c.got = got
-        if joined:
-            total = ((1, sum(c.keep.shape[1] for c in chunks), TILE), BF16)
-            pair = call(add_kernel, [total, total], [], [v for c in chunks for v in (c.keep, c.got)], [])
-            chunks = [Chunk(*pair, chunks[0].bits)]
-        else:
-            for c in chunks:
-                c.add()
-        held, pairs = lax.optimization_barrier((held, [(c.keep, c.send) for c in chunks]))
-        for c, pair in zip(chunks, pairs):
-            c.keep, c.send = pair
+        return held
+
+    def wave(held, *chunks, joined=False):
+        held = received(held, *chunks)
+        groups = [chunks] if joined else [(c,) for c in chunks]
+        nexts = [Chunk(*added(*group), group[0].bits) for group in groups]
+        held, keeps = lax.optimization_barrier((held, [(c.keep, c.send) for c in nexts]))
+        for c, (keep, send) in zip(nexts, keeps):
+            c.keep, c.send = keep, [send]
             c.start()
-        return (held, chunks[0]) if joined else held
+        return (held, *nexts)
 
     ffn_grads = Chunk(keep_ffn, send_ffn, (0, *FFN_BITS))
     ffn_grads.start()
@@ -1024,14 +1127,14 @@
             ((seq, half), BF16),
             ((4, width, TILE), F32),
         ],
-        [d_after, packed, probs, context, fourth, after_conv, depth_low],
-        [out_weight, qkv_weight, norm_gain],
+        [d_after, packed, probs, context, fourth, after_conv, depth_low, out_w, qkv_w],
+        [norm_gain],
         micros=10,
     )
-    d_after_conv = wave(d_after_conv, ffn_grads)
+    d_after_conv, ffn_grads = wave(d_after_conv, ffn_grads)
     attn_grads = Chunk(keep_attn, send_attn, (0, *ATTN_BITS))
     attn_grads.start()
-    d_after_conv = wave(d_after_conv, attn_grads)
+    d_after_conv, attn_grads = wave(d_after_conv, attn_grads)
     d_left, taps_right, small_conv = call(
         middle_back_kernel,
         [((seq, ffn), BF16), ((3, seq, half), BF16), ((16, ffn), F32)],
@@ -1045,27 +1148,27 @@
             ((seq + 16, half), F32),
             ((1, ffn), F32),
         ],
-        [lengths, d_after_conv, left_pre, right_pre],
-        [point_weight, mid_gain, mid_bias, depth_weight],
-        micros=10,
+        [lengths, d_after_conv, left_pre, right_pre, point_w],
+        [mid_gain, mid_bias, depth_weight],
+        micros=4,
         scalars=1,
     )
-    d_left = wave(d_left, ffn_grads, attn_grads)
+    d_left, ffn_grads, attn_grads = wave(d_left, ffn_grads, attn_grads)
     d_second, keep_conv, send_conv = call(
         conv_back_kernel,
-        [((seq, width), F32)] + slot_outs(ffn // 2 // TILE * rows + 3 * rows // 2),
+        [((seq, width), F32)] + slot_outs(ffn // 2 // TILE * rows + 3 * rows // 2, 1),
         [((width, TILE), F32), ((3, width, LANES), F32)],
-        [lengths, d_left, taps_right, second],
-        [left_weight, conv_weight],
+        [lengths, d_left, taps_right, second, left_w, conv_w],
+        [],
         micros=5,
         scalars=1,
     )
     conv_grads = Chunk(keep_conv, send_conv, (0, *CONV_BITS))
     conv_grads.start()
-    d_second = wave(d_second, conv_grads)
+    d_second, conv_grads = wave(d_second, conv_grads)
     grad_tokens, keep_glu, send_glu = call(
         glu_back_kernel,
-        [((part, width), F32)] + slot_outs(width // TILE * rows + 16),
+        [((part, width), F32)] + slot_outs(width // TILE * rows + 16, 2),
         [
             ((seq, 2 * width), BF16),
             ((seq, width), F32),
@@ -1084,20 +1187,22 @@
             small_ffn,
             small_attn,
             small_conv,
+            glu_w,
         ],
-        [norm_gain, glu_weight],
+        [norm_gain],
         micros=7,
     )
     glu_grads = Chunk(keep_glu, send_glu, (0, *GLU_BITS))
     glu_grads.start()
-    held, early = wave(grad_tokens, ffn_grads, attn_grads, joined=True)
-    held = wave(held, glu_grads)
-    held = wave(held, conv_grads)
-    held = wave(held, glu_grads)
+    held = received(grad_tokens, ffn_grads, attn_grads)
+    held, glu_grads = wave(held, glu_grads)
+    held, early = wave(held, ffn_grads, attn_grads, joined=True)
+    held, conv_grads = wave(held, conv_grads)
+    held, glu_grads = wave(held, glu_grads)
     held, late = wave(held, conv_grads, glu_grads, joined=True)
-    held = wave(held, early)
-    held, other = lax.optimization_barrier((held, early.got))
-    grad_tokens = wave(held, late)
+    held, early = wave(held, early)
+    grad_tokens, late = wave(held, late)
+    other = early.got[0]
     ffn_out, ffn_in, out, qkv, point = call(
         finish_early_kernel,
         [
@@ -1145,7 +1250,7 @@
             ((half,), F32),
         ],
         [],
-        [late.keep, late.got],
+        [late.keep, late.got[0]],
         [],
     )
     results = (

time: 106 us -> 97.8 us (0.923)
  waiting for transfers between devices: 37.3 us -> 24.8 us
  starting transfers between devices: 19.5 us -> 22.5 us
  Pallas kernels: 46.2 us -> 47.4 us
    ppermute x16 -> x17, waiting for transfers between devices: 31.5 us -> 23.6 us  [the longest x15 21.1 us: start(): self.got = [lax.ppermute(v, 'dp', pairs) for v in self.send]]
    ppermute x16 -> x17, starting transfers between devices: 16.5 us -> 19.5 us  [the longest x15 16.3 us: start(): self.got = [lax.ppermute(v, 'dp', pairs) for v in self.send]]
    ppermute x1, waiting for transfers between devices: 3.8 us -> 1.18 us  [per_device(): other = lax.ppermute(mine, 'head', swap)]
    ppermute x1, waiting for transfers between devices: 1.98 us -> 0.01 us  [per_device(): cot_other = lax.ppermute(cot_mine, 'head', swap)]
    pallas_call x9 -> x11, Pallas kernels: 46.2 us -> 47.4 us  [call(): pl.pallas_call(body, out_shape=tuple((jax.ShapeDtypeStruct(shape, dtype)...]
  transfers between devices with their start and end apart: 18 -> 19, of which waited for: 13 -> 11; matrix products, arithmetic and copies ran while one was open for 1% -> 1% of each run, Pallas kernels for 22% -> 40%
where the time goes in v4:
time: 97.8 us; the launch traced here: 97.5 us
  Pallas kernels  47.4 us (48%)
  waiting for transfers between devices  24.8 us (25%)
  starting transfers between devices  22.5 us (23%)
  between operations  1.63 us (2%)
  other arithmetic  1.13 us (1%)
    pallas_call x11, Pallas kernels, call(): pl.pallas_call(body, out_shape=tuple((jax.ShapeDtypeStruct(shape, dtype)...  47.4 us
    ppermute x15, waiting for transfers between devices, start(): self.got = [lax.ppermute(v, 'dp', pairs) for v in self.send]  21.1 us
    ppermute x15, starting transfers between devices, start(): self.got = [lax.ppermute(v, 'dp', pairs) for v in self.send]  16.3 us
    ppermute x2, starting transfers between devices, start(): self.got = [lax.ppermute(self.keep, 'head', swap)]  3.11 us
    ppermute x1, starting transfers between devices, per_device(): other = lax.ppermute(mine, 'head', swap)  3 us
    ppermute x2, waiting for transfers between devices, start(): self.got = [lax.ppermute(self.keep, 'head', swap)]  2.49 us
  transfers between devices with their start and end apart: 19, of which 11 were waited for; matrix products, arithmetic and copies ran while one was open for 1% of the time, Pallas kernels for 40%

profile of v4, /device:TPU:0, one launch (start us, length us, event | category | flops | bytes accessed | tf_op | source)
XLA Modules:
  0.0 97.5 jit_solution(8553606645725751332)
XLA Ops:
  0.7 3.0 %collective-permute-start = (bf16[128,512]{1,0:T(8,128)(2,1)}, bf16[128,512]{1,0:T(8,128)(2,1)S(1)}, u32[]{:S(2)}, u32[]{:S(2)}) collective-permute-start(bf16[128,512]{1,0:T(8,128)(2,1)} %bitcast.8), channel_id=1, source_target_pairs={{0,1},{1,0},{2,3},{3,2},{4,5},{5,4},{6,7},{7,6},{8,9},{9,8},{10,11... | collective-permute-start | bytes 393224 | tf_op jit(solution)/shard_map/ppermute | solution.py:944
  4.4 2.6 %open_kernel.1 = (bf16[128,512]{1,0:T(8,128)(2,1)S(1)}, f32[128,1024]{1,0:T(8,128)S(1)}, f32[128,512]{1,0:T(8,128)S(1)}, bf16[128,512]{1,0:T(8,128)(2,1)S(1)}, b...) custom-call(s32[1]{0:T(128)S(6)} %copy.43.refs_0_, ...), custom_call_target="tpu_custom_call" | custom-call | flops 1000000000 | bytes 3000000 | tf_op jit(solution)/shard_map/open_kernel/pallas_call | solution.py:893
  7.0 1.2 %collective-permute-done.refs_1_ = bf16[128,512]{1,0:T(8,128)(2,1)S(1)} collective-permute-done((bf16[128,512]{1,0:T(8,128)(2,1)}, bf16[128,512]{1,0:T(8,128)(2,1)S(1)}, u32[]{:S(2)}, u32[]{:S(2)}) %collective-permute-start) | collective-permute-done | bytes 131104 | tf_op jit(solution)/shard_map/ppermute | solution.py:944
  8.2 14.6 %forward_kernel.1 = (bf16[128,512]{1,0:T(8,128)(2,1)}, bf16[256,512]{1,0:T(8,128)(2,1)S(1)}, bf16[256,512]{1,0:T(8,128)(2,1)S(1)}, f32[256,1024]{1,0:T(8,128)S(1...) custom-call(s32[1]{0:T(128)S(6)} %copy.43.refs_0_, ...), custom_call_target="tpu_custom_call" | custom-call | flops 14000000000 | bytes 42000000 | tf_op jit(solution)/shard_map/forward_kernel/pallas_call | solution.py:893
  22.8 4.8 %ffn_back_kernel.1 = (f32[256,512]{1,0:T(8,128)S(1)}, f32[8,2048]{1,0:T(8,128)S(1)}, bf16[8,256,256]{2,1,0:T(8,128)(2,1)S(1)}, bf16[8,256,256]{2,1,0:T(8,128)(2,1)S(1)}) custom-call(bf16[128,512]{1,0:T(8,128)(2,1)S(1)} %collective-permute-done.1.refs_0_, f32[256,512]{1,0:T(8,128)S(1)} %get-tuple-element.164.refs_1_, ...), custom_call_target="tpu_custom_call" | custom-call | flops 5000000000 | bytes 15000000 | tf_op jit(solution)/shard_map/ffn_back_kernel/pallas_call | solution.py:893
  27.8 7.8 %attention_back_kernel.1 = (f32[256,512]{1,0:T(8,128)S(1)}, f32[8,2048]{1,0:T(8,128)S(1)}, bf16[8,192,256]{2,1,0:T(8,128)(2,1)S(1)}, bf16[8,192,256]{2,1,0:T(8,128)(2,1)S(1)}) custom-call(f32[256,512]{1,0:T(8,128)S(1)} %get-tuple-element.169.refs_0_, bf16[256,1536]{1,0:T(8,128)(2,1)S(1)} %get-tuple-element.170.refs_1_, ...), custom_call_target="tpu_custom_call" | custom-call | flops 10000000000 | bytes 30000000 | tf_op jit(solution)/shard_map/attention_back_kernel/pallas_call | solution.py:893
  35.5 0.6 collective-permute-start.3
  36.4 1.7 %collective-permute-done.3 = bf16[8,192,256]{2,1,0:T(8,128)(2,1)S(1)} collective-permute-done((bf16[8,192,256]{2,1,0:T(8,128)(2,1)S(1)}, bf16[8,192,256]{2,1,0:T(8,128)(2,1)S(1)}, u32[]{:S(2)}, u32[]{:S(2)}) %collective-permute-start.3) | collective-permute-done | bytes 786464 | tf_op jit(solution)/shard_map/ppermute | solution.py:1074
  38.0 2.2 %collective-permute-start.4 = (bf16[4,256,256]{2,1,0:T(8,128)(2,1)S(1)}, bf16[4,256,256]{2,1,0:T(8,128)(2,1)S(1)}, u32[]{:S(2)}, u32[]{:S(2)}) collective-permute-start(bf16[4,256,256]{2,1,0:T(8,128)(2,1)S(1)} %get-tuple-element.192), channel_id=1, source_target_pairs={{0,8},{2,10},{4,12},{6,14},{8,0},{10,2},{12,4},{14,6},{16,24},{18,... | collective-permute-start | bytes 1572872 | tf_op jit(solution)/shard_map/ppermute | solution.py:1074
  40.4 1.6 %collective-permute-start.5 = (bf16[4,192,256]{2,1,0:T(8,128)(2,1)S(1)}, bf16[4,192,256]{2,1,0:T(8,128)(2,1)S(1)}, u32[]{:S(2)}, u32[]{:S(2)}) collective-permute-start(bf16[4,192,256]{2,1,0:T(8,128)(2,1)S(1)} %get-tuple-element.193), channel_id=1, source_target_pairs={{0,4},{2,6},{4,0},{6,2},{8,12},{10,14},{12,8},{14,10},{16,20},{18,... | collective-permute-start | bytes 1179656 | tf_op jit(solution)/shard_map/ppermute | solution.py:1074
  42.0 8.5 %middle_back_kernel.1 = (bf16[256,2048]{1,0:T(8,128)(2,1)S(1)}, bf16[3,256,256]{2,1,0:T(8,128)(2,1)S(1)}, f32[16,2048]{1,0:T(8,128)S(1)}) custom-call(s32[1]{0:T(128)S(6)} %copy.43.refs_0_, f32[256,512]{1,0:T(8,128)S(1)} %get-tuple-element.188.refs_1_, f32[256,2048]{1,0:T(8,128)S(1)} %get-tuple-element.189.refs_2_, ...), custom_call_target="tpu_custom_call" | custom-call | flops 4000000000 | bytes 12000000 | tf_op jit(solution)/shard_map/middle_back_kernel/pallas_call | solution.py:893
  50.5 1.1 %collective-permute-done.5 = bf16[4,192,256]{2,1,0:T(8,128)(2,1)S(1)} collective-permute-done((bf16[4,192,256]{2,1,0:T(8,128)(2,1)S(1)}, bf16[4,192,256]{2,1,0:T(8,128)(2,1)S(1)}, u32[]{:S(2)}, u32[]{:S(2)}) %collective-permute-start.5) | collective-permute-done | bytes 393248 | tf_op jit(solution)/shard_map/ppermute | solution.py:1074
  51.5 1.1 %collective-permute-done.4 = bf16[4,256,256]{2,1,0:T(8,128)(2,1)S(1)} collective-permute-done((bf16[4,256,256]{2,1,0:T(8,128)(2,1)S(1)}, bf16[4,256,256]{2,1,0:T(8,128)(2,1)S(1)}, u32[]{:S(2)}, u32[]{:S(2)}) %collective-permute-start.4) | collective-permute-done | bytes 524320 | tf_op jit(solution)/shard_map/ppermute | solution.py:1074
  52.9 3.2 %conv_back_kernel.1 = (f32[256,512]{1,0:T(8,128)S(1)}, bf16[8,176,256]{2,1,0:T(8,128)(2,1)S(1)}, bf16[8,176,256]{2,1,0:T(8,128)(2,1)S(1)}) custom-call(s32[1]{0:T(128)S(6)} %copy.43.refs_0_, bf16[256,2048]{1,0:T(8,128)(2,1)S(1)} %get-tuple-element.199.refs_1_, bf16[3,256,256]{2,1,0:T(8,128)(2,1)S(1)} %get-tuple-element.200.refs_2_, ...), custom_call_target="tpu_custom_call" | custom-call | flops 5000000000 | bytes 15000000 | tf_op jit(solution)/shard_map/conv_back_kernel/pallas_call | solution.py:893
  56.1 1.8 %collective-permute-start.8 = (bf16[2,192,256]{2,1,0:T(8,128)(2,1)S(1)}, bf16[2,192,256]{2,1,0:T(8,128)(2,1)S(1)}, u32[]{:S(2)}, u32[]{:S(2)}) collective-permute-start(bf16[2,192,256]{2,1,0:T(8,128)(2,1)S(1)} %get-tuple-element.217), channel_id=1, source_target_pairs={{0,8},{2,10},{4,12},{6,14},{8,0},{10,2},{12,4},{14,6},{16,24},{18,... | collective-permute-start | bytes 589832 | tf_op jit(solution)/shard_map/ppermute | solution.py:1074
  57.9 1.5 %collective-permute-start.7 = (bf16[2,256,256]{2,1,0:T(8,128)(2,1)S(1)}, bf16[2,256,256]{2,1,0:T(8,128)(2,1)S(1)}, u32[]{:S(2)}, u32[]{:S(2)}) collective-permute-start(bf16[2,256,256]{2,1,0:T(8,128)(2,1)S(1)} %get-tuple-element.216), channel_id=1, source_target_pairs={{0,4},{2,6},{4,0},{6,2},{8,12},{10,14},{12,8},{14,10},{16,20},{18,... | collective-permute-start | bytes 786440 | tf_op jit(solution)/shard_map/ppermute | solution.py:1074
  59.6 3.9 %glu_back_kernel.1 = (f32[128,512]{1,0:T(8,128)}, bf16[8,80,256]{2,1,0:T(8,128)(2,1)S(1)}, bf16[4,80,256]{2,1,0:T(8,128)(2,1)S(1)}, bf16[4,80,256]{2,1,0:T(8,128)(2,1)S(1)}) custom-call(f32[256,512]{1,0:T(8,128)S(1)} %get-tuple-element.207.refs_0_, f32[256,512]{1,0:T(8,128)S(1)} %get-tuple-element.188.refs_1_, f32[256,512]{1,0:T(8,128)S(1)} %get-tuple-element.208.refs_2_, ...), custom_call_target="tpu_custom_call" | custom-call | flops 7000000000 | bytes 21000000 | tf_op jit(solution)/shard_map/glu_back_kernel/pallas_call | solution.py:893
  64.1 0.5 collective-permute-start.11
  64.7 1.7 %collective-permute-done.7.refs_2_ = bf16[2,256,256]{2,1,0:T(8,128)(2,1)S(1)} collective-permute-done((bf16[2,256,256]{2,1,0:T(8,128)(2,1)S(1)}, bf16[2,256,256]{2,1,0:T(8,128)(2,1)S(1)}, u32[]{:S(2)}, u32[]{:S(2)}) %collective-permute-start.7) | collective-permute-done | bytes 262176 | tf_op jit(solution)/shard_map/ppermute | solution.py:1074
  66.9 2.8 %collective-permute-start.15 = (bf16[1,448,256]{2,1,0:T(8,128)(2,1)S(1)}, bf16[1,448,256]{2,1,0:T(8,128)(2,1)S(1)}, u32[]{:S(2)}, u32[]{:S(2)}) collective-permute-start(bf16[1,448,256]{2,1,0:T(8,128)(2,1)S(1)} %get-tuple-element.256), channel_id=1, source_target_pairs={{0,16},{2,18},{4,20},{6,22},{8,24},{10,26},{12,28},{14,30},{16,0},... | collective-permute-start | bytes 688136 | tf_op jit(solution)/shard_map/ppermute | solution.py:1074
  69.6 4.9 %collective-permute-done.11 = bf16[4,176,256]{2,1,0:T(8,128)(2,1)S(1)} collective-permute-done((bf16[4,176,256]{2,1,0:T(8,128)(2,1)S(1)}, bf16[4,176,256]{2,1,0:T(8,128)(2,1)S(1)}, u32[]{:S(2)}, u32[]{:S(2)}) %collective-permute-start.11) | collective-permute-done | bytes 360480 | tf_op jit(solution)/shard_map/ppermute | solution.py:1074
  74.6 1.9 %collective-permute-done.12 = bf16[4,80,256]{2,1,0:T(8,128)(2,1)S(1)} collective-permute-done((bf16[4,80,256]{2,1,0:T(8,128)(2,1)S(1)}, bf16[4,80,256]{2,1,0:T(8,128)(2,1)S(1)}, u32[]{:S(2)}, u32[]{:S(2)}) %collective-permute-start.12) | collective-permute-done | bytes 163872 | tf_op jit(solution)/shard_map/ppermute | solution.py:1074
  76.6 1.5 %collective-permute-start.14 = (bf16[2,80,256]{2,1,0:T(8,128)(2,1)S(1)}, bf16[2,80,256]{2,1,0:T(8,128)(2,1)S(1)}, u32[]{:S(2)}, u32[]{:S(2)}) collective-permute-start(bf16[2,80,256]{2,1,0:T(8,128)(2,1)S(1)} %get-tuple-element.247), channel_id=1, source_target_pairs={{0,4},{2,6},{4,0},{6,2},{8,12},{10,14},{12,8},{14,10},{16,20},{18,... | collective-permute-start | bytes 245768 | tf_op jit(solution)/shard_map/ppermute | solution.py:1074
  78.1 3.0 %collective-permute-done.14.refs_3_ = bf16[2,80,256]{2,1,0:T(8,128)(2,1)S(1)} collective-permute-done((bf16[2,80,256]{2,1,0:T(8,128)(2,1)S(1)}, bf16[2,80,256]{2,1,0:T(8,128)(2,1)S(1)}, u32[]{:S(2)}, u32[]{:S(2)}) %collective-permute-start.14) | collective-permute-done | bytes 81952 | tf_op jit(solution)/shard_map/ppermute | solution.py:1074
  81.1 0.9 collective-permute-done.13.refs_2_
  82.1 2.9 %collective-permute-start.16 = (bf16[1,256,256]{2,1,0:T(8,128)(2,1)S(1)}, bf16[1,256,256]{2,1,0:T(8,128)(2,1)S(1)}, u32[]{:S(2)}, u32[]{:S(2)}) collective-permute-start(bf16[1,256,256]{2,1,0:T(8,128)(2,1)S(1)} %get-tuple-element.261), channel_id=1, source_target_pairs={{0,16},{2,18},{4,20},{6,22},{8,24},{10,26},{12,28},{14,30},{16,0},... | collective-permute-start | bytes 393224 | tf_op jit(solution)/shard_map/ppermute | solution.py:1074
  85.1 1.6 %collective-permute-start.18 = (bf16[448,256]{1,0:T(8,128)(2,1)S(1)}, bf16[448,256]{1,0:T(8,128)(2,1)S(1)}, u32[]{:S(2)}, u32[]{:S(2)}) collective-permute-start(bf16[448,256]{1,0:T(8,128)(2,1)S(1)} %fusion.refs_0_), channel_id=1, source_target_pairs={{0,1},{1,0},{2,3},{3,2},{4,5},{5,4},{6,7},{7,6},{8,9},{9,8},{10,11... | collective-permute-start | bytes 688136 | tf_op jit(solution)/shard_map/ppermute | solution.py:1070
  86.6 4.8 %collective-permute-done.16 = bf16[1,256,256]{2,1,0:T(8,128)(2,1)S(1)} collective-permute-done((bf16[1,256,256]{2,1,0:T(8,128)(2,1)S(1)}, bf16[1,256,256]{2,1,0:T(8,128)(2,1)S(1)}, u32[]{:S(2)}, u32[]{:S(2)}) %collective-permute-start.16) | collective-permute-done | bytes 131104 | tf_op jit(solution)/shard_map/ppermute | solution.py:1074
  91.5 1.6 %collective-permute-start.17 = (bf16[256,256]{1,0:T(8,128)(2,1)S(1)}, bf16[256,256]{1,0:T(8,128)(2,1)S(1)}, u32[]{:S(2)}, u32[]{:S(2)}) collective-permute-start(bf16[256,256]{1,0:T(8,128)(2,1)S(1)} %fusion.1.refs_0_), channel_id=1, source_target_pairs={{0,1},{1,0},{2,3},{3,2},{4,5},{5,4},{6,7},{7,6},{8,9},{9,8},{10,11... | collective-permute-start | bytes 393224 | tf_op jit(solution)/shard_map/ppermute | solution.py:1070
  93.0 1.0 %finish_early_kernel.1 = (f32[128,512]{1,0:T(8,128)}, f32[32,2048]{1,0:T(8,128)}, f32[32,512]{1,0:T(8,128)}, f32[32,1536]{1,0:T(8,128)}, f32[128,256]{1,0:T(8,128)}) custom-call(bf16[448,256]{1,0:T(8,128)(2,1)S(1)} %fusion.refs_0_, bf16[448,256]{1,0:T(8,128)(2,1)S(1)} %collective-permute-done.18.refs_1_), custom_call_target="tpu_custom_call" | custom-call | tf_op jit(solution)/shard_map/finish_early_kernel/pallas_call | solution.py:893
  94.0 2.5 %collective-permute-done.17.refs_1_ = bf16[256,256]{1,0:T(8,128)(2,1)S(1)} collective-permute-done((bf16[256,256]{1,0:T(8,128)(2,1)S(1)}, bf16[256,256]{1,0:T(8,128)(2,1)S(1)}, u32[]{:S(2)}, u32[]{:S(2)}) %collective-permute-start.17) | collective-permute-done | bytes 131104 | tf_op jit(solution)/shard_map/ppermute | solution.py:1070
  96.5 0.8 finish_late_kernel.1
  (27 shorter events, 2.5 us)
Async XLA Ops:
  0.7 7.5 %collective-permute-start = (bf16[128,512]{1,0:T(8,128)(2,1)}, bf16[128,512]{1,0:T(8,128)(2,1)S(1)}, u32[]{:S(2)}, u32[]{:S(2)}) collective-permute-start(bf16[128,512]{1,0:T(8,128)(2,1)} %bitcast.8), channel_id=1, source_target_pairs={{0,1},{1,0},{2,3},{3,2},{4,5},{5,4},{6,7},{7,6},{8,9},{9,8},{10,11... | collective-permute-start | bytes 393224 | tf_op jit(solution)/shard_map/ppermute | solution.py:944
  3.7 19.2 %collective-permute-start.1 = (bf16[128,512]{1,0:T(8,128)(2,1)}, bf16[128,512]{1,0:T(8,128)(2,1)S(1)}, u32[]{:S(2)}, u32[]{:S(2)}) collective-permute-start(bf16[128,512]{1,0:T(8,128)(2,1)} %bitcast.10), channel_id=1, source_target_pairs={{0,1},{1,0},{2,3},{3,2},{4,5},{5,4},{6,7},{7,6},{8,9},{9,8},{10,11... | collective-permute-start | bytes 393224 | tf_op jit(solution)/shard_map/ppermute | solution.py:945
  27.7 8.4 %collective-permute-start.2 = (bf16[8,256,256]{2,1,0:T(8,128)(2,1)S(1)}, bf16[8,256,256]{2,1,0:T(8,128)(2,1)S(1)}, u32[]{:S(2)}, u32[]{:S(2)}) collective-permute-start(bf16[8,256,256]{2,1,0:T(8,128)(2,1)S(1)} %get-tuple-element.179), channel_id=1, source_target_pairs={{0,2},{2,0},{4,6},{6,4},{8,10},{10,8},{12,14},{14,12},{16,18},{18,... | collective-permute-start | bytes 3145736 | tf_op jit(solution)/shard_map/ppermute | solution.py:1074
  35.5 2.5 %collective-permute-start.3 = (bf16[8,192,256]{2,1,0:T(8,128)(2,1)S(1)}, bf16[8,192,256]{2,1,0:T(8,128)(2,1)S(1)}, u32[]{:S(2)}, u32[]{:S(2)}) collective-permute-start(bf16[8,192,256]{2,1,0:T(8,128)(2,1)S(1)} %get-tuple-element.184), channel_id=1, source_target_pairs={{0,2},{2,0},{4,6},{6,4},{8,10},{10,8},{12,14},{14,12},{16,18},{18,... | collective-permute-start | bytes 2359304 | tf_op jit(solution)/shard_map/ppermute | solution.py:1074
  38.0 14.6 %collective-permute-start.4 = (bf16[4,256,256]{2,1,0:T(8,128)(2,1)S(1)}, bf16[4,256,256]{2,1,0:T(8,128)(2,1)S(1)}, u32[]{:S(2)}, u32[]{:S(2)}) collective-permute-start(bf16[4,256,256]{2,1,0:T(8,128)(2,1)S(1)} %get-tuple-element.192), channel_id=1, source_target_pairs={{0,8},{2,10},{4,12},{6,14},{8,0},{10,2},{12,4},{14,6},{16,24},{18,... | collective-permute-start | bytes 1572872 | tf_op jit(solution)/shard_map/ppermute | solution.py:1074
  40.4 11.2 %collective-permute-start.5 = (bf16[4,192,256]{2,1,0:T(8,128)(2,1)S(1)}, bf16[4,192,256]{2,1,0:T(8,128)(2,1)S(1)}, u32[]{:S(2)}, u32[]{:S(2)}) collective-permute-start(bf16[4,192,256]{2,1,0:T(8,128)(2,1)S(1)} %get-tuple-element.193), channel_id=1, source_target_pairs={{0,4},{2,6},{4,0},{6,2},{8,12},{10,14},{12,8},{14,10},{16,20},{18,... | collective-permute-start | bytes 1179656 | tf_op jit(solution)/shard_map/ppermute | solution.py:1074
  56.1 3.4 %collective-permute-start.6 = (bf16[8,176,256]{2,1,0:T(8,128)(2,1)S(1)}, bf16[8,176,256]{2,1,0:T(8,128)(2,1)S(1)}, u32[]{:S(2)}, u32[]{:S(2)}) collective-permute-start(bf16[8,176,256]{2,1,0:T(8,128)(2,1)S(1)} %get-tuple-element.203), channel_id=1, source_target_pairs={{0,2},{2,0},{4,6},{6,4},{8,10},{10,8},{12,14},{14,12},{16,18},{18,... | collective-permute-start | bytes 2162696 | tf_op jit(solution)/shard_map/ppermute | solution.py:1074
  56.1 8.5 %collective-permute-start.8 = (bf16[2,192,256]{2,1,0:T(8,128)(2,1)S(1)}, bf16[2,192,256]{2,1,0:T(8,128)(2,1)S(1)}, u32[]{:S(2)}, u32[]{:S(2)}) collective-permute-start(bf16[2,192,256]{2,1,0:T(8,128)(2,1)S(1)} %get-tuple-element.217), channel_id=1, source_target_pairs={{0,8},{2,10},{4,12},{6,14},{8,0},{10,2},{12,4},{14,6},{16,24},{18,... | collective-permute-start | bytes 589832 | tf_op jit(solution)/shard_map/ppermute | solution.py:1074
  57.9 8.4 %collective-permute-start.7 = (bf16[2,256,256]{2,1,0:T(8,128)(2,1)S(1)}, bf16[2,256,256]{2,1,0:T(8,128)(2,1)S(1)}, u32[]{:S(2)}, u32[]{:S(2)}) collective-permute-start(bf16[2,256,256]{2,1,0:T(8,128)(2,1)S(1)} %get-tuple-element.216), channel_id=1, source_target_pairs={{0,4},{2,6},{4,0},{6,2},{8,12},{10,14},{12,8},{14,10},{16,20},{18,... | collective-permute-start | bytes 786440 | tf_op jit(solution)/shard_map/ppermute | solution.py:1074
  63.6 2.8 %collective-permute-start.9 = (bf16[4,80,256]{2,1,0:T(8,128)(2,1)S(1)}, bf16[4,80,256]{2,1,0:T(8,128)(2,1)S(1)}, u32[]{:S(2)}, u32[]{:S(2)}) collective-permute-start(bf16[4,80,256]{2,1,0:T(8,128)(2,1)S(1)} %get-tuple-element.219), channel_id=1, source_target_pairs={{0,2},{2,0},{4,6},{6,4},{8,10},{10,8},{12,14},{14,12},{16,18},{18,... | collective-permute-start | bytes 491528 | tf_op jit(solution)/shard_map/ppermute | solution.py:1074
  63.6 2.7 %collective-permute-start.10 = (bf16[4,80,256]{2,1,0:T(8,128)(2,1)S(1)}, bf16[4,80,256]{2,1,0:T(8,128)(2,1)S(1)}, u32[]{:S(2)}, u32[]{:S(2)}) collective-permute-start(bf16[4,80,256]{2,1,0:T(8,128)(2,1)S(1)} %get-tuple-element.220), channel_id=1, source_target_pairs={{0,2},{2,0},{4,6},{6,4},{8,10},{10,8},{12,14},{14,12},{16,18},{18,... | collective-permute-start | bytes 491528 | tf_op jit(solution)/shard_map/ppermute | solution.py:1074
  64.1 10.4 %collective-permute-start.11 = (bf16[4,176,256]{2,1,0:T(8,128)(2,1)S(1)}, bf16[4,176,256]{2,1,0:T(8,128)(2,1)S(1)}, u32[]{:S(2)}, u32[]{:S(2)}) collective-permute-start(bf16[4,176,256]{2,1,0:T(8,128)(2,1)S(1)} %get-tuple-element.236), channel_id=1, source_target_pairs={{0,4},{2,6},{4,0},{6,2},{8,12},{10,14},{12,8},{14,10},{16,20},{18,... | collective-permute-start | bytes 1081352 | tf_op jit(solution)/shard_map/ppermute | solution.py:1074
  66.5 10.0 %collective-permute-start.12 = (bf16[4,80,256]{2,1,0:T(8,128)(2,1)S(1)}, bf16[4,80,256]{2,1,0:T(8,128)(2,1)S(1)}, u32[]{:S(2)}, u32[]{:S(2)}) collective-permute-start(bf16[4,80,256]{2,1,0:T(8,128)(2,1)S(1)} %get-tuple-element.241), channel_id=1, source_target_pairs={{0,8},{2,10},{4,12},{6,14},{8,0},{10,2},{12,4},{14,6},{16,24},{18,... | collective-permute-start | bytes 491528 | tf_op jit(solution)/shard_map/ppermute | solution.py:1074
  66.9 15.2 %collective-permute-start.15 = (bf16[1,448,256]{2,1,0:T(8,128)(2,1)S(1)}, bf16[1,448,256]{2,1,0:T(8,128)(2,1)S(1)}, u32[]{:S(2)}, u32[]{:S(2)}) collective-permute-start(bf16[1,448,256]{2,1,0:T(8,128)(2,1)S(1)} %get-tuple-element.256), channel_id=1, source_target_pairs={{0,16},{2,18},{4,20},{6,22},{8,24},{10,26},{12,28},{14,30},{16,0},... | collective-permute-start | bytes 688136 | tf_op jit(solution)/shard_map/ppermute | solution.py:1074
  76.6 5.5 %collective-permute-start.13 = (bf16[2,176,256]{2,1,0:T(8,128)(2,1)S(1)}, bf16[2,176,256]{2,1,0:T(8,128)(2,1)S(1)}, u32[]{:S(2)}, u32[]{:S(2)}) collective-permute-start(bf16[2,176,256]{2,1,0:T(8,128)(2,1)S(1)} %get-tuple-element.246), channel_id=1, source_target_pairs={{0,8},{2,10},{4,12},{6,14},{8,0},{10,2},{12,4},{14,6},{16,24},{18,... | collective-permute-start | bytes 540680 | tf_op jit(solution)/shard_map/ppermute | solution.py:1074
  76.6 4.5 %collective-permute-start.14 = (bf16[2,80,256]{2,1,0:T(8,128)(2,1)S(1)}, bf16[2,80,256]{2,1,0:T(8,128)(2,1)S(1)}, u32[]{:S(2)}, u32[]{:S(2)}) collective-permute-start(bf16[2,80,256]{2,1,0:T(8,128)(2,1)S(1)} %get-tuple-element.247), channel_id=1, source_target_pairs={{0,4},{2,6},{4,0},{6,2},{8,12},{10,14},{12,8},{14,10},{16,20},{18,... | collective-permute-start | bytes 245768 | tf_op jit(solution)/shard_map/ppermute | solution.py:1074
  82.1 9.3 %collective-permute-start.16 = (bf16[1,256,256]{2,1,0:T(8,128)(2,1)S(1)}, bf16[1,256,256]{2,1,0:T(8,128)(2,1)S(1)}, u32[]{:S(2)}, u32[]{:S(2)}) collective-permute-start(bf16[1,256,256]{2,1,0:T(8,128)(2,1)S(1)} %get-tuple-element.261), channel_id=1, source_target_pairs={{0,16},{2,18},{4,20},{6,22},{8,24},{10,26},{12,28},{14,30},{16,0},... | collective-permute-start | bytes 393224 | tf_op jit(solution)/shard_map/ppermute | solution.py:1074
  85.1 8.0 %collective-permute-start.18 = (bf16[448,256]{1,0:T(8,128)(2,1)S(1)}, bf16[448,256]{1,0:T(8,128)(2,1)S(1)}, u32[]{:S(2)}, u32[]{:S(2)}) collective-permute-start(bf16[448,256]{1,0:T(8,128)(2,1)S(1)} %fusion.refs_0_), channel_id=1, source_target_pairs={{0,1},{1,0},{2,3},{3,2},{4,5},{5,4},{6,7},{7,6},{8,9},{9,8},{10,11... | collective-permute-start | bytes 688136 | tf_op jit(solution)/shard_map/ppermute | solution.py:1070
  91.5 5.0 %collective-permute-start.17 = (bf16[256,256]{1,0:T(8,128)(2,1)S(1)}, bf16[256,256]{1,0:T(8,128)(2,1)S(1)}, u32[]{:S(2)}, u32[]{:S(2)}) collective-permute-start(bf16[256,256]{1,0:T(8,128)(2,1)S(1)} %fusion.1.refs_0_), channel_id=1, source_target_pairs={{0,1},{1,0},{2,3},{3,2},{4,5},{5,4},{6,7},{7,6},{8,9},{9,8},{10,11... | collective-permute-start | bytes 393224 | tf_op jit(solution)/shard_map/ppermute | solution.py:1070

commit v5 on v4

--- a/solution.py
+++ b/solution.py
@@ -15,8 +15,8 @@
 F32 = jnp.float32
 BF16 = jnp.bfloat16
 VMEM_BYTES = 28 * 1024 * 1024
-FFN_BITS = (2, 1, 3)
-ATTN_BITS = (1, 2, 3)
+FFN_BITS = (1, 2, 3)
+ATTN_BITS = (2, 1, 3)
 CONV_BITS = (1, 2, 3)
 GLU_BITS = (2, 1, 3)
 
@@ -81,7 +81,7 @@
     return group ^ (wanted | sent)
 
 
-def for_slots(keep, send, bits, body):
+def for_slots(keep, send, bits, body, unroll=1):
     count = GROUPS // 2 // len(send)
     for i, piece in enumerate(send):
 
@@ -91,12 +91,14 @@
             body(q, slot_block(p, 1, bits), piece)
             return c
 
-        lax.fori_loop(0, count, visit, 0)
-
-
-def place_rows(grad, keep, send, bits, at, rows):
+        lax.fori_loop(0, count, visit, 0, unroll=unroll)
+
+
+def place_rows(grads, keep, send, bits, at, rows):
     def one(p, block, out):
-        out[p, at : at + rows, :] = grad[pl.ds(pl.multiple_of(block * rows, rows), rows), :].astype(BF16)
+        source = pl.ds(pl.multiple_of(block * rows, rows), rows)
+        for j, grad in enumerate(grads):
+            out[p, at + j * rows : at + (j + 1) * rows, :] = grad[source, :].astype(BF16)
 
     for_slots(keep, send, bits, one)
 
@@ -154,7 +156,6 @@
     left_w,
     point_w,
     far,
-    out_tokens,
     stream,
     first,
     joined,
@@ -171,8 +172,12 @@
     after_attn,
     fifth,
     hidden,
+    vhat,
+    rates,
     third,
     sides,
+    mid_row,
+    mask,
 ):
     part, width = other.shape
     seq = 2 * part
@@ -196,7 +201,6 @@
         out_w,
         ffn_in_bias,
         ffn_in_w,
-        ffn_out_bias,
         ffn_out_w,
     ) = far
     for whole, piece in (
@@ -225,19 +229,20 @@
     left_b = vector(left_bias())
     for n in range(ffn // TILE):
         left_pre[:, col(n)] = mm(second[...], left_w[:, col(n)]) + left_b[:, col(n)]
-    mid_g, mid_b, depth_w = vector(mid_gain()), vector(mid_bias()), depth_w()
+    mid_row[0:1, :], mid_row[1:2, :] = vector(mid_gain()), vector(mid_bias())
+    depth_w = depth_w()
     chunks = ffn // LANES
     edge = jnp.zeros((8, LANES), F32)
-    for k in range(chunks):
-        third[k, 0:8, :] = edge
-        third[k, 8 + seq : 16 + seq, :] = edge
+    third[0:8, :] = edge
+    third[8 + seq : 16 + seq, :] = edge
+    mask[...] = (lax.broadcasted_iota(jnp.int32, (seq, LANES), 0) < length).astype(F32)
 
     def mid_rows(r, c):
         rows = pl.ds(r, 16)
-        vhat, _ = normalized(combine(left_pre[rows, :], right_pre[rows, :]))
-        v = (vhat * mid_g + mid_b) * valid_rows(r, 16, length)
+        v, rate = normalized(combine(left_pre[rows, :], right_pre[rows, :]))
+        rates[rows, :] = jnp.broadcast_to(rate, (16, LANES))
         for k in range(chunks):
-            third[k, pl.ds(pl.multiple_of(8 + r, 8), 16), :] = v[:, col(k, LANES)]
+            vhat[k, rows, :] = v[:, col(k, LANES)]
         return c
 
     row_blocks(seq, 16, mid_rows, unroll=2)
@@ -245,9 +250,10 @@
     def depth_lanes(k, c):
         lanes = pl.ds(pl.multiple_of(k * LANES, LANES), LANES)
         taps = depth_w[:, lanes].astype(F32)
-        total = third[k, 4 : 4 + seq, :] * taps[0:1, :]
+        third[8 : 8 + seq, :] = (vhat[k] * mid_row[0:1, lanes] + mid_row[1:2, lanes]) * mask[...]
+        total = third[4 : 4 + seq, :] * taps[0:1, :]
         for j in range(1, 9):
-            total = total + third[k, 4 + j : 4 + j + seq, :] * taps[j : j + 1, :]
+            total = total + third[4 + j : 4 + j + seq, :] * taps[j : j + 1, :]
         depth_low[:, lanes] = total.astype(BF16)
         return c
 
@@ -305,13 +311,7 @@
     for n in range(ffn // TILE):
         pre = mm(fifth[...], ffn_in_w[:, col(n)]) + ffn_in_b[:, col(n)]
         hidden[:, col(n)] = jnp.where(pre > 0.0, pre, 0.0).astype(BF16)
-    ffn_out_b, ffn_out_w = vector(ffn_out_bias()), ffn_out_w()
-    for n in range(width // TILE):
-        out_tokens[:, col(n)] = (
-            after_attn[own, col(n)]
-            + mm(hidden[own, :], ffn_out_w[:, col(n)])
-            + ffn_out_b[:, col(n)]
-        ).astype(BF16)
+    ffn_out_w()
 
 
 def ffn_back_kernel(
@@ -369,8 +369,9 @@
     rows = width // GROUPS
     for j in range(ffn // 2 // TILE):
         at = pl.multiple_of(side * (ffn // 2) + j * TILE, TILE)
-        grad[...] = mm_tn(fifth[...], d_hidden[:, pl.ds(at, TILE)])
-        place_rows(grad, keep, send, FFN_BITS, per_row + j * rows, rows)
+        grad[j] = mm_tn(fifth[...], d_hidden[:, pl.ds(at, TILE)])
+    count = ffn // 2 // TILE
+    place_rows([grad.at[j] for j in range(count)], keep, send, FFN_BITS, per_row, rows)
 
 
 def combine(left_pre, right_pre):
@@ -464,8 +465,7 @@
     small[0:1, 0:width] = sum_tokens(sums[0])
     small[0:1, width : 2 * width] = sum_tokens(sums[1])
     small[0:1, 2 * width : 2 * width + half] = sum_tokens(g_point)
-    for j in range(len(sides)):
-        place_rows(grad.at[j], keep, send, ATTN_BITS, j * rows, rows)
+    place_rows([grad.at[j] for j in range(len(sides))], keep, send, ATTN_BITS, 0, rows)
     sep_half = d_sep[:, pl.ds(pl.multiple_of(side * (half // 2), half // 2), half // 2)]
     per_row = ffn // GROUPS
 
@@ -476,7 +476,7 @@
         out[p, 4 * rows : 4 * rows + per_row // 2, 0:LANES] = g[: per_row // 2]
         out[p, 4 * rows : 4 * rows + per_row // 2, LANES : 2 * LANES] = g[per_row // 2 :]
 
-    for_slots(keep, send, ATTN_BITS, point_slot)
+    for_slots(keep, send, ATTN_BITS, point_slot, unroll=4)
 
 
 def middle_back_kernel(
@@ -484,19 +484,19 @@
     d_after_conv,
     left_pre,
     right_pre,
+    vhat3,
+    rates,
     point_w,
     far,
     d_left,
     taps_right,
     small,
-    vhat3,
-    third,
     d_depth,
     d_third,
-    rates,
     sums,
     d_right,
     mid_row,
+    mask,
 ):
     seq, width = d_after_conv.shape
     ffn = left_pre.shape[1]
@@ -514,39 +514,28 @@
         for m in range(TILE // LANES):
             d_depth[n * (TILE // LANES) + m, 8 : 8 + seq, :] = block[:, col(m, LANES)]
 
-    mid_g, mid_b, depth_w = vector(mid_gain()), vector(mid_bias()), depth_w()
-    mid_row[...] = mid_g
-
-    def mid_rows(r, c):
-        rows = pl.ds(r, 16)
-        vhat, rate = normalized(combine(left_pre[rows, :], right_pre[rows, :]))
-        v = (vhat * mid_g + mid_b) * valid_rows(r, 16, length)
-        rates[rows, :] = jnp.broadcast_to(rate, (16, LANES))
-        for k in range(chunks):
-            third[k, rows, :] = v[:, col(k, LANES)]
-            vhat3[k, rows, :] = vhat[:, col(k, LANES)]
-        return c
-
-    row_blocks(seq, 16, mid_rows, unroll=2)
+    mid_row[0:1, :], mid_row[1:2, :] = vector(mid_gain()), vector(mid_bias())
+    depth_w = depth_w()
+    mask[...] = (lax.broadcasted_iota(jnp.int32, (seq, LANES), 0) < length).astype(F32)
     sums[...] = jnp.zeros(sums.shape, F32)
     step = 64
 
     def depth_lanes(k, c):
         lanes = pl.ds(pl.multiple_of(k * LANES, LANES), LANES)
         taps = depth_w[:, lanes].astype(F32)
-        mid_lanes = mid_row[0:1, lanes]
+        mid_lanes, low_lanes = mid_row[0:1, lanes], mid_row[1:2, lanes]
         totals = [jnp.zeros((8, LANES), F32)] * 11
         for r in range(0, seq, step):
             block = slice(r, r + step)
-            here = third[k, block, :]
+            vhat = vhat3[k, block, :]
+            here = (vhat * mid_lanes + low_lanes) * mask[block, :]
             total = None
             for j in range(9):
                 moved = d_depth[k, 12 - j + r : 12 - j + r + step, :]
                 totals[j] = totals[j] + part_sums(moved * here)
                 term = moved * taps[j : j + 1, :]
                 total = term if total is None else total + term
-            total = total * valid_rows(r, step, length)
-            vhat = vhat3[k, block, :]
+            total = total * mask[block, :]
             totals[9] = totals[9] + part_sums(total * vhat)
             totals[10] = totals[10] + part_sums(total)
             gained = total * mid_lanes
@@ -608,8 +597,8 @@
     rows = width // GROUPS
     for j in range(ffn // 2 // TILE):
         at = pl.multiple_of(side * (ffn // 2) + j * TILE, TILE)
-        grad[...] = mm_tn(second[...], d_left[:, pl.ds(at, TILE)])
-        place_rows(grad, keep, send, CONV_BITS, j * rows, rows)
+        grad[j] = mm_tn(second[...], d_left[:, pl.ds(at, TILE)])
+    place_rows([grad.at[j] for j in range(ffn // 2 // TILE)], keep, send, CONV_BITS, 0, rows)
     start = ffn // 2 // TILE * rows
     half_lanes = pl.ds(pl.multiple_of(side * (half // 2), half // 2), half // 2)
     for tap in range(3):
@@ -646,18 +635,16 @@
     small_conv,
     glu_w,
     far,
-    grad_tokens,
+    d_after_glu,
+    d_first,
     keep,
     send,
     d_joined,
-    d_after_glu,
-    d_first,
     rolled,
     blocks,
     grad,
 ):
     seq, width = d_second.shape
-    part = seq // 2
     side = lax.axis_index("head")
     gains = far[0]()
     gain = [gains[k : k + 1, :].astype(F32) for k in range(2)]
@@ -693,17 +680,14 @@
     columns = [pl.ds(pl.multiple_of(side * width + j * TILE, TILE), TILE) for j in range(width // TILE)]
     for p in range(8):
         block = slice(p * seq // 8, (p + 1) * seq // 8)
-        vhat, rate = normalized(stream[block, :].astype(F32))
+        vhat, _ = normalized(stream[block, :].astype(F32))
         e = d_first[block, :]
-        d_after_glu[block, :] = d_after_glu[block, :] + norm_back(vhat, rate, e * gain[0])
         sums = [total + part_sums(v) for total, v in zip(sums, (e * vhat, e))]
         if p < 2 * len(columns):
             part_rows = slice(p % 2 * (width // 2), (p % 2 + 1) * (width // 2))
             grad[p // 2, part_rows, :] = mm_tn(first[:, part_rows], d_joined[:, columns[p // 2]])
     gain_zero, shift_zero = (sum_tokens(v) for v in sums)
-    grad_tokens[...] = d_after_glu[pl.ds(pl.multiple_of(side * part, part), part), :]
-    for j in range(len(columns)):
-        place_rows(grad.at[j], keep, send, GLU_BITS, j * rows, rows)
+    place_rows([grad.at[j] for j in range(len(columns))], keep, send, GLU_BITS, 0, rows)
 
     blocks[...] = jnp.zeros(blocks.shape, F32)
     rolled[...] = jnp.zeros(rolled.shape, F32)
@@ -752,6 +736,26 @@
         out[p, start : start + 16, :] = blocks[block].astype(BF16)
 
     for_slots(keep, send, GLU_BITS, small_slot)
+
+
+def tokens_kernel(after_attn, hidden, ffn_out_w, d_after_glu, d_first, stream, far, out_tokens, grad_tokens):
+    part, width = out_tokens.shape
+    gains, ffn_out_bias = far
+    at = pl.multiple_of(lax.axis_index("head") * part, part)
+    own = pl.ds(at, part)
+    gain, bias = gains()[0:1, :].astype(F32), vector(ffn_out_bias())
+    for n in range(width // TILE):
+        out_tokens[:, col(n)] = (
+            after_attn[own, col(n)] + mm(hidden[own, :], ffn_out_w[:, col(n)]) + bias[:, col(n)]
+        ).astype(BF16)
+
+    def rows(r, c):
+        block = pl.ds(pl.multiple_of(at + r, 32), 32)
+        vhat, rate = normalized(stream[block, :].astype(F32))
+        grad_tokens[pl.ds(r, 32), :] = d_after_glu[block, :] + norm_back(vhat, rate, d_first[block, :] * gain)
+        return c
+
+    row_blocks(part, 32, rows, unroll=2)
 
 
 def add_kernel(keeps, gots, far, keep, send):
@@ -967,7 +971,6 @@
         kept=(0, 4, 5, 6, 7),
     )
     (
-        out_tokens,
         stream,
         first_norm,
         joined,
@@ -984,6 +987,8 @@
         after_attn,
         fifth,
         hidden,
+        vhat,
+        rates,
         qkv_w,
         out_w,
         ffn_in_w,
@@ -991,7 +996,6 @@
     ) = call(
         forward_kernel,
         [
-            ((part, width), BF16),
             ((seq, width), BF16),
             ((seq, width), BF16),
             ((seq, 2 * width), F32),
@@ -1008,10 +1012,14 @@
             ((seq, width), F32),
             ((seq, width), BF16),
             ((seq, ffn), BF16),
+            ((ffn // LANES, seq, LANES), F32),
+            ((seq, LANES), F32),
         ],
         [
-            ((ffn // LANES, seq + 16, LANES), F32),
+            ((seq + 16, LANES), F32),
             ((2, seq + 16, half), F32),
+            ((2, ffn), F32),
+            ((seq, LANES), F32),
         ],
         [
             lengths,
@@ -1040,12 +1048,11 @@
             out_weight,
             ffn_in_bias,
             ffn_in_weight,
-            ffn_out_bias,
             ffn_out_weight,
         ],
         micros=14,
         scalars=1,
-        kept=(9, 10, 12, 14),
+        kept=(9, 10, 12, 13),
     )
     d_after, small_ffn, keep_ffn, send_ffn = call(
         ffn_back_kernel,
@@ -1054,7 +1061,7 @@
             ((seq, width), BF16),
             ((seq, ffn), BF16),
             ((seq, width), F32),
-            ((width, TILE), F32),
+            ((ffn // 2 // TILE, width, TILE), F32),
         ],
         [cot_other, after_attn, fifth, hidden, ffn_in_w, ffn_out_w],
         [cot_mine, norm_gain],
@@ -1081,11 +1088,11 @@
             step *= 2
         return total
 
-    def added(*chunks):
+    def added(*chunks, whole=False):
         keep = chunks[0].keep
         if keep.shape[0] == 1:
             return last_sum(keep, chunks[0].got[0]), None
-        if len(chunks) == 1 and len(chunks[0].got) < 3:
+        if len(chunks) == 1 and len(chunks[0].got) < 3 and not whole:
             (c,) = chunks
             n = keep.shape[0] // 2
             got = c.got if len(c.got) == 2 else (c.got[0][:n], c.got[0][n:])
@@ -1104,10 +1111,10 @@
             c.got = got
         return held
 
-    def wave(held, *chunks, joined=False):
+    def wave(held, *chunks, joined=False, whole=True):
         held = received(held, *chunks)
         groups = [chunks] if joined else [(c,) for c in chunks]
-        nexts = [Chunk(*added(*group), group[0].bits) for group in groups]
+        nexts = [Chunk(*added(*group, whole=whole), group[0].bits) for group in groups]
         held, keeps = lax.optimization_barrier((held, [(c.keep, c.send) for c in nexts]))
         for c, (keep, send) in zip(nexts, keeps):
             c.keep, c.send = keep, [send]
@@ -1131,48 +1138,44 @@
         [norm_gain],
         micros=10,
     )
-    d_after_conv, ffn_grads = wave(d_after_conv, ffn_grads)
+    d_after_conv, ffn_grads = wave(d_after_conv, ffn_grads, whole=False)
     attn_grads = Chunk(keep_attn, send_attn, (0, *ATTN_BITS))
     attn_grads.start()
-    d_after_conv, attn_grads = wave(d_after_conv, attn_grads)
+    d_after_conv, attn_grads = wave(d_after_conv, attn_grads, whole=True)
     d_left, taps_right, small_conv = call(
         middle_back_kernel,
         [((seq, ffn), BF16), ((3, seq, half), BF16), ((16, ffn), F32)],
         [
-            ((ffn // LANES, seq, LANES), F32),
-            ((ffn // LANES, seq, LANES), F32),
             ((ffn // LANES, seq + 16, LANES), F32),
             ((ffn // LANES, seq, LANES), F32),
-            ((seq, LANES), F32),
             ((2, seq, LANES), F32),
             ((seq + 16, half), F32),
-            ((1, ffn), F32),
+            ((2, ffn), F32),
+            ((seq, LANES), F32),
         ],
-        [lengths, d_after_conv, left_pre, right_pre, point_w],
+        [lengths, d_after_conv, left_pre, right_pre, vhat, rates, point_w],
         [mid_gain, mid_bias, depth_weight],
-        micros=4,
+        micros=0,
         scalars=1,
     )
-    d_left, ffn_grads, attn_grads = wave(d_left, ffn_grads, attn_grads)
     d_second, keep_conv, send_conv = call(
         conv_back_kernel,
         [((seq, width), F32)] + slot_outs(ffn // 2 // TILE * rows + 3 * rows // 2, 1),
-        [((width, TILE), F32), ((3, width, LANES), F32)],
+        [((ffn // 2 // TILE, width, TILE), F32), ((3, width, LANES), F32)],
         [lengths, d_left, taps_right, second, left_w, conv_w],
         [],
-        micros=5,
+        micros=0,
         scalars=1,
     )
     conv_grads = Chunk(keep_conv, send_conv, (0, *CONV_BITS))
     conv_grads.start()
+    d_second, ffn_grads, attn_grads = wave(d_second, ffn_grads, attn_grads, whole=False)
     d_second, conv_grads = wave(d_second, conv_grads)
-    grad_tokens, keep_glu, send_glu = call(
+    d_after_glu, d_first, keep_glu, send_glu = call(
         glu_back_kernel,
-        [((part, width), F32)] + slot_outs(width // TILE * rows + 16, 2),
+        [((seq, width), F32)] * 2 + slot_outs(width // TILE * rows + 16, 2),
         [
             ((seq, 2 * width), BF16),
-            ((seq, width), F32),
-            ((seq, width), F32),
             ((2, 32, LANES), F32),
             ((GROUPS, 16, 2 * LANES), F32),
             ((width // TILE, width, TILE), F32),
@@ -1194,12 +1197,19 @@
     )
     glu_grads = Chunk(keep_glu, send_glu, (0, *GLU_BITS))
     glu_grads.start()
-    held = received(grad_tokens, ffn_grads, attn_grads)
+    held = received(d_after_glu, ffn_grads, attn_grads)
     held, glu_grads = wave(held, glu_grads)
     held, early = wave(held, ffn_grads, attn_grads, joined=True)
     held, conv_grads = wave(held, conv_grads)
-    held, glu_grads = wave(held, glu_grads)
-    held, late = wave(held, conv_grads, glu_grads, joined=True)
+    out_tokens, grad_tokens = call(
+        tokens_kernel,
+        [((part, width), BF16), ((part, width), F32)],
+        [],
+        [after_attn, hidden, ffn_out_w, held, d_first, stream],
+        [norm_gain, ffn_out_bias],
+    )
+    grad_tokens, glu_grads = wave(grad_tokens, glu_grads)
+    held, late = wave(grad_tokens, conv_grads, glu_grads, joined=True)
     held, early = wave(held, early)
     grad_tokens, late = wave(held, late)
     other = early.got[0]

time: 97.8 us -> 87.2 us (0.89)
  waiting for transfers between devices: 24.8 us -> 16.6 us
  Pallas kernels: 47.4 us -> 43.8 us
  starting transfers between devices: 22.5 us -> 24.3 us
    ppermute x15, waiting for transfers between devices: 21.1 us -> 12.9 us  [start(): self.got = [lax.ppermute(v, 'dp', pairs) for v in self.send]]
    pallas_call x11 -> x17, Pallas kernels: 47.4 us -> 43.8 us  [call(): pl.pallas_call(body, out_shape=tuple((jax.ShapeDtypeStruct(shape, dtype)...]
    ppermute x15, starting transfers between devices: 16.3 us -> 18.2 us  [start(): self.got = [lax.ppermute(v, 'dp', pairs) for v in self.send]]
  transfers between devices with their start and end apart: 19 -> 19, of which waited for: 11 -> 10; matrix products, arithmetic and copies ran while one was open for 1% -> 1% of each run, Pallas kernels for 40% -> 45%
where the time goes in v5:
time: 87.2 us; the launch traced here: 86.9 us
  Pallas kernels  43.8 us (50%)
  starting transfers between devices  24.3 us (28%)
  waiting for transfers between devices  16.6 us (19%)
  between operations  1.62 us (2%)
    pallas_call x17, Pallas kernels, call(): pl.pallas_call(body, out_shape=tuple((jax.ShapeDtypeStruct(shape, dtype)...  43.8 us
    ppermute x15, starting transfers between devices, start(): self.got = [lax.ppermute(v, 'dp', pairs) for v in self.send]  18.2 us
    ppermute x15, waiting for transfers between devices, start(): self.got = [lax.ppermute(v, 'dp', pairs) for v in self.send]  12.9 us
    ppermute x2, starting transfers between devices, start(): self.got = [lax.ppermute(self.keep, 'head', swap)]  3.1 us
    ppermute x1, starting transfers between devices, per_device(): other = lax.ppermute(mine, 'head', swap)  3 us
    ppermute x2, waiting for transfers between devices, start(): self.got = [lax.ppermute(self.keep, 'head', swap)]  2.5 us
  transfers between devices with their start and end apart: 19, of which 10 were waited for; matrix products, arithmetic and copies ran while one was open for 1% of the time, Pallas kernels for 45%

profile of v5, /device:TPU:0, one launch (start us, length us, event | category | flops | bytes accessed | tf_op | source)
XLA Modules:
  0.0 86.9 jit_solution(8897129700628771749)
XLA Ops:
  0.7 3.0 %collective-permute-start = (bf16[128,512]{1,0:T(8,128)(2,1)}, bf16[128,512]{1,0:T(8,128)(2,1)S(1)}, u32[]{:S(2)}, u32[]{:S(2)}) collective-permute-start(bf16[128,512]{1,0:T(8,128)(2,1)} %bitcast.8), channel_id=1, source_target_pairs={{0,1},{1,0},{2,3},{3,2},{4,5},{5,4},{6,7},{7,6},{8,9},{9,8},{10,11... | collective-permute-start | bytes 393224 | tf_op jit(solution)/shard_map/ppermute | solution.py:948
  4.4 2.6 %open_kernel.1 = (bf16[128,512]{1,0:T(8,128)(2,1)S(1)}, f32[128,1024]{1,0:T(8,128)S(1)}, f32[128,512]{1,0:T(8,128)S(1)}, bf16[128,512]{1,0:T(8,128)(2,1)S(1)}, b...) custom-call(s32[1]{0:T(128)S(6)} %copy.43.refs_0_, ...), custom_call_target="tpu_custom_call" | custom-call | flops 1000000000 | bytes 3000000 | tf_op jit(solution)/shard_map/open_kernel/pallas_call | solution.py:897
  7.0 1.2 %collective-permute-done.refs_1_ = bf16[128,512]{1,0:T(8,128)(2,1)S(1)} collective-permute-done((bf16[128,512]{1,0:T(8,128)(2,1)}, bf16[128,512]{1,0:T(8,128)(2,1)S(1)}, u32[]{:S(2)}, u32[]{:S(2)}) %collective-permute-start) | collective-permute-done | bytes 131104 | tf_op jit(solution)/shard_map/ppermute | solution.py:948
  8.2 14.2 %forward_kernel.1 = (bf16[256,512]{1,0:T(8,128)(2,1)S(1)}, bf16[256,512]{1,0:T(8,128)(2,1)S(1)}, f32[256,1024]{1,0:T(8,128)S(1)}, f32[256,512]{1,0:T(8,128)S(1)}...) custom-call(s32[1]{0:T(128)S(6)} %copy.43.refs_0_, ...), custom_call_target="tpu_custom_call" | custom-call | flops 14000000000 | bytes 42000000 | tf_op jit(solution)/shard_map/forward_kernel/pallas_call | solution.py:897
  22.5 4.1 %ffn_back_kernel.1 = (f32[256,512]{1,0:T(8,128)S(1)}, f32[8,2048]{1,0:T(8,128)S(1)}, bf16[8,256,256]{2,1,0:T(8,128)(2,1)S(1)}, bf16[8,256,256]{2,1,0:T(8,128)(2,1)S(1)}) custom-call(bf16[128,512]{1,0:T(8,128)(2,1)S(1)} %collective-permute-done.1.refs_0_, f32[256,512]{1,0:T(8,128)S(1)} %get-tuple-element.177.refs_1_.refs_0_, ...), custom_call_target="tpu_custom_call" | custom-call | flops 5000000000 | bytes 15000000 | tf_op jit(solution)/shard_map/ffn_back_kernel/pallas_call | solution.py:897
  26.7 6.4 %attention_back_kernel.1 = (f32[256,512]{1,0:T(8,128)S(1)}, f32[8,2048]{1,0:T(8,128)S(1)}, bf16[8,192,256]{2,1,0:T(8,128)(2,1)S(1)}, bf16[8,192,256]{2,1,0:T(8,128)(2,1)S(1)}) custom-call(f32[256,512]{1,0:T(8,128)S(1)} %get-tuple-element.182.refs_0_, bf16[256,1536]{1,0:T(8,128)(2,1)S(1)} %get-tuple-element.183.refs_1_, ...), custom_call_target="tpu_custom_call" | custom-call | flops 10000000000 | bytes 30000000 | tf_op jit(solution)/shard_map/attention_back_kernel/pallas_call | solution.py:897
  33.9 2.2 %collective-permute-start.4 = (bf16[4,256,256]{2,1,0:T(8,128)(2,1)S(1)}, bf16[4,256,256]{2,1,0:T(8,128)(2,1)S(1)}, u32[]{:S(2)}, u32[]{:S(2)}) collective-permute-start(bf16[4,256,256]{2,1,0:T(8,128)(2,1)S(1)} %get-tuple-element.212), channel_id=1, source_target_pairs={{0,4},{2,6},{4,0},{6,2},{8,12},{10,14},{12,8},{14,10},{16,20},{18,... | collective-permute-start | bytes 1572872 | tf_op jit(solution)/shard_map/ppermute | solution.py:1081
  36.2 1.7 %collective-permute-start.5 = (bf16[4,192,256]{2,1,0:T(8,128)(2,1)S(1)}, bf16[4,192,256]{2,1,0:T(8,128)(2,1)S(1)}, u32[]{:S(2)}, u32[]{:S(2)}) collective-permute-start(bf16[4,192,256]{2,1,0:T(8,128)(2,1)S(1)} %get-tuple-element.213), channel_id=1, source_target_pairs={{0,8},{2,10},{4,12},{6,14},{8,0},{10,2},{12,4},{14,6},{16,24},{18,... | collective-permute-start | bytes 1179656 | tf_op jit(solution)/shard_map/ppermute | solution.py:1081
  37.9 6.1 %middle_back_kernel.1 = (bf16[256,2048]{1,0:T(8,128)(2,1)S(1)}, bf16[3,256,256]{2,1,0:T(8,128)(2,1)S(1)}, f32[16,2048]{1,0:T(8,128)S(1)}) custom-call(s32[1]{0:T(128)S(6)} %copy.43.refs_0_, f32[256,512]{1,0:T(8,128)S(1)} %get-tuple-element.203.refs_1_, f32[256,2048]{1,0:T(8,128)S(1)} %get-tuple-element.204.refs_2_, ...), custom_call_target="tpu_custom_call" | custom-call | tf_op jit(solution)/shard_map/middle_back_kernel/pallas_call | solution.py:897
  44.1 2.4 %conv_back_kernel.1 = (f32[256,512]{1,0:T(8,128)S(1)}, bf16[8,176,256]{2,1,0:T(8,128)(2,1)S(1)}, bf16[8,176,256]{2,1,0:T(8,128)(2,1)S(1)}) custom-call(s32[1]{0:T(128)S(6)} %copy.43.refs_0_, bf16[256,2048]{1,0:T(8,128)(2,1)S(1)} %get-tuple-element.208.refs_1_, bf16[3,256,256]{2,1,0:T(8,128)(2,1)S(1)} %get-tuple-element.209.refs_2_, ...), custom_call_target="tpu_custom_call" | custom-call | tf_op jit(solution)/shard_map/conv_back_kernel/pallas_call | solution.py:897
  46.6 1.0 %collective-permute-done.5 = bf16[4,192,256]{2,1,0:T(8,128)(2,1)S(1)} collective-permute-done((bf16[4,192,256]{2,1,0:T(8,128)(2,1)S(1)}, bf16[4,192,256]{2,1,0:T(8,128)(2,1)S(1)}, u32[]{:S(2)}, u32[]{:S(2)}) %collective-permute-start.5) | collective-permute-done | bytes 393248 | tf_op jit(solution)/shard_map/ppermute | solution.py:1081
  47.6 0.6 collective-permute-done.4
  48.4 1.8 %collective-permute-start.8 = (bf16[2,192,256]{2,1,0:T(8,128)(2,1)S(1)}, bf16[2,192,256]{2,1,0:T(8,128)(2,1)S(1)}, u32[]{:S(2)}, u32[]{:S(2)}) collective-permute-start(bf16[2,192,256]{2,1,0:T(8,128)(2,1)S(1)} %get-tuple-element.236), channel_id=1, source_target_pairs={{0,4},{2,6},{4,0},{6,2},{8,12},{10,14},{12,8},{14,10},{16,20},{18,... | collective-permute-start | bytes 589832 | tf_op jit(solution)/shard_map/ppermute | solution.py:1081
  50.2 1.6 %collective-permute-start.7 = (bf16[2,256,256]{2,1,0:T(8,128)(2,1)S(1)}, bf16[2,256,256]{2,1,0:T(8,128)(2,1)S(1)}, u32[]{:S(2)}, u32[]{:S(2)}) collective-permute-start(bf16[2,256,256]{2,1,0:T(8,128)(2,1)S(1)} %get-tuple-element.235), channel_id=1, source_target_pairs={{0,8},{2,10},{4,12},{6,14},{8,0},{10,2},{12,4},{14,6},{16,24},{18,... | collective-permute-start | bytes 786440 | tf_op jit(solution)/shard_map/ppermute | solution.py:1081
  51.9 0.6 collective-permute-start.11
  52.5 3.0 %glu_back_kernel.1 = (f32[256,512]{1,0:T(8,128)S(1)}, f32[256,512]{1,0:T(8,128)S(1)}, bf16[8,80,256]{2,1,0:T(8,128)(2,1)S(1)}, bf16[4,80,256]{2,1,0:T(8,128)(2,1)S(1)}, bf16[4,80,256]{2,1,0:T(8,128)(2,1)S(1)}) custom-call(f32[256,512]{1,0:T(8,128)S(1)} %get-tuple-element.226.refs_0_, f32[256,512]{1,0:T(8,128)S(1)} %get-tuple-element.203.refs_1_, ...), custom_call_target="tpu_custom_call" | custom-call | flops 7000000000 | bytes 21000000 | tf_op jit(solution)/shard_map/glu_back_kernel/pallas_call | solution.py:897
  56.2 1.0 %collective-permute-done.7.refs_2_ = bf16[2,256,256]{2,1,0:T(8,128)(2,1)S(1)} collective-permute-done((bf16[2,256,256]{2,1,0:T(8,128)(2,1)S(1)}, bf16[2,256,256]{2,1,0:T(8,128)(2,1)S(1)}, u32[]{:S(2)}, u32[]{:S(2)}) %collective-permute-start.7) | collective-permute-done | bytes 262176 | tf_op jit(solution)/shard_map/ppermute | solution.py:1081
  57.4 1.6 %collective-permute-start.12 = (bf16[4,80,256]{2,1,0:T(8,128)(2,1)S(1)}, bf16[4,80,256]{2,1,0:T(8,128)(2,1)S(1)}, u32[]{:S(2)}, u32[]{:S(2)}) collective-permute-start(bf16[4,80,256]{2,1,0:T(8,128)(2,1)S(1)} %get-tuple-element.267), channel_id=1, source_target_pairs={{0,8},{2,10},{4,12},{6,14},{8,0},{10,2},{12,4},{14,6},{16,24},{18,... | collective-permute-start | bytes 491528 | tf_op jit(solution)/shard_map/ppermute | solution.py:1081
  59.1 2.6 %collective-permute-start.15 = (bf16[1,448,256]{2,1,0:T(8,128)(2,1)S(1)}, bf16[1,448,256]{2,1,0:T(8,128)(2,1)S(1)}, u32[]{:S(2)}, u32[]{:S(2)}) collective-permute-start(bf16[1,448,256]{2,1,0:T(8,128)(2,1)S(1)} %get-tuple-element.284), channel_id=1, source_target_pairs={{0,16},{2,18},{4,20},{6,22},{8,24},{10,26},{12,28},{14,30},{16,0},... | collective-permute-start | bytes 688136 | tf_op jit(solution)/shard_map/ppermute | solution.py:1081
  61.8 0.7 collective-permute-done.11.refs_1_
  62.6 1.5 %collective-permute-start.13 = (bf16[2,176,256]{2,1,0:T(8,128)(2,1)S(1)}, bf16[2,176,256]{2,1,0:T(8,128)(2,1)S(1)}, u32[]{:S(2)}, u32[]{:S(2)}) collective-permute-start(bf16[2,176,256]{2,1,0:T(8,128)(2,1)S(1)} %get-tuple-element.274), channel_id=1, source_target_pairs={{0,8},{2,10},{4,12},{6,14},{8,0},{10,2},{12,4},{14,6},{16,24},{18,... | collective-permute-start | bytes 540680 | tf_op jit(solution)/shard_map/ppermute | solution.py:1081
  64.1 2.4 %tokens_kernel.1 = (bf16[128,512]{1,0:T(8,128)(2,1)}, f32[128,512]{1,0:T(8,128)}) custom-call(f32[256,512]{1,0:T(8,128)S(1)} %get-tuple-element.177.refs_1_.refs_0_, bf16[256,2048]{1,0:T(8,128)(2,1)S(1)} %get-tuple-element.178.refs_3_.refs_1_, bf16[2048,512]{1,0:T(8,128)(2,1)S(1)} %get-tuple-element.179.refs_5_.refs_2_, ...), custom_call_target="tpu_custom_call" | custom-call | tf_op jit(solution)/shard_map/tokens_kernel/pallas_call | solution.py:897
  66.5 2.4 %collective-permute-done.12.refs_1_ = bf16[4,80,256]{2,1,0:T(8,128)(2,1)S(1)} collective-permute-done((bf16[4,80,256]{2,1,0:T(8,128)(2,1)S(1)}, bf16[4,80,256]{2,1,0:T(8,128)(2,1)S(1)}, u32[]{:S(2)}, u32[]{:S(2)}) %collective-permute-start.12) | collective-permute-done | bytes 163872 | tf_op jit(solution)/shard_map/ppermute | solution.py:1081
  68.9 1.4 %collective-permute-start.14 = (bf16[2,80,256]{2,1,0:T(8,128)(2,1)S(1)}, bf16[2,80,256]{2,1,0:T(8,128)(2,1)S(1)}, u32[]{:S(2)}, u32[]{:S(2)}) collective-permute-start(bf16[2,80,256]{2,1,0:T(8,128)(2,1)S(1)} %get-tuple-element.275), channel_id=1, source_target_pairs={{0,4},{2,6},{4,0},{6,2},{8,12},{10,14},{12,8},{14,10},{16,20},{18,... | collective-permute-start | bytes 245768 | tf_op jit(solution)/shard_map/ppermute | solution.py:1081
  70.3 3.1 %collective-permute-done.14.refs_3_ = bf16[2,80,256]{2,1,0:T(8,128)(2,1)S(1)} collective-permute-done((bf16[2,80,256]{2,1,0:T(8,128)(2,1)S(1)}, bf16[2,80,256]{2,1,0:T(8,128)(2,1)S(1)}, u32[]{:S(2)}, u32[]{:S(2)}) %collective-permute-start.14) | collective-permute-done | bytes 81952 | tf_op jit(solution)/shard_map/ppermute | solution.py:1081
  73.5 1.7 %collective-permute-start.16 = (bf16[1,256,256]{2,1,0:T(8,128)(2,1)S(1)}, bf16[1,256,256]{2,1,0:T(8,128)(2,1)S(1)}, u32[]{:S(2)}, u32[]{:S(2)}) collective-permute-start(bf16[1,256,256]{2,1,0:T(8,128)(2,1)S(1)} %get-tuple-element.289), channel_id=1, source_target_pairs={{0,16},{2,18},{4,20},{6,22},{8,24},{10,26},{12,28},{14,30},{16,0},... | collective-permute-start | bytes 393224 | tf_op jit(solution)/shard_map/ppermute | solution.py:1081
  75.3 1.6 %collective-permute-start.18 = (bf16[448,256]{1,0:T(8,128)(2,1)S(1)}, bf16[448,256]{1,0:T(8,128)(2,1)S(1)}, u32[]{:S(2)}, u32[]{:S(2)}) collective-permute-start(bf16[448,256]{1,0:T(8,128)(2,1)S(1)} %fusion.refs_0_), channel_id=1, source_target_pairs={{0,1},{1,0},{2,3},{3,2},{4,5},{5,4},{6,7},{7,6},{8,9},{9,8},{10,11... | collective-permute-start | bytes 688136 | tf_op jit(solution)/shard_map/ppermute | solution.py:1077
  76.9 4.0 %collective-permute-done.16 = bf16[1,256,256]{2,1,0:T(8,128)(2,1)S(1)} collective-permute-done((bf16[1,256,256]{2,1,0:T(8,128)(2,1)S(1)}, bf16[1,256,256]{2,1,0:T(8,128)(2,1)S(1)}, u32[]{:S(2)}, u32[]{:S(2)}) %collective-permute-start.16) | collective-permute-done | bytes 131104 | tf_op jit(solution)/shard_map/ppermute | solution.py:1081
  80.9 1.5 %collective-permute-start.17 = (bf16[256,256]{1,0:T(8,128)(2,1)S(1)}, bf16[256,256]{1,0:T(8,128)(2,1)S(1)}, u32[]{:S(2)}, u32[]{:S(2)}) collective-permute-start(bf16[256,256]{1,0:T(8,128)(2,1)S(1)} %fusion.1.refs_0_), channel_id=1, source_target_pairs={{0,1},{1,0},{2,3},{3,2},{4,5},{5,4},{6,7},{7,6},{8,9},{9,8},{10,11... | collective-permute-start | bytes 393224 | tf_op jit(solution)/shard_map/ppermute | solution.py:1077
  82.4 1.0 %finish_early_kernel.1 = (f32[128,512]{1,0:T(8,128)}, f32[32,2048]{1,0:T(8,128)}, f32[32,512]{1,0:T(8,128)}, f32[32,1536]{1,0:T(8,128)}, f32[128,256]{1,0:T(8,128)}) custom-call(bf16[448,256]{1,0:T(8,128)(2,1)S(1)} %fusion.refs_0_, bf16[448,256]{1,0:T(8,128)(2,1)S(1)} %collective-permute-done.18.refs_1_), custom_call_target="tpu_custom_call" | custom-call | tf_op jit(solution)/shard_map/finish_early_kernel/pallas_call | solution.py:897
  83.4 2.5 %collective-permute-done.17.refs_1_ = bf16[256,256]{1,0:T(8,128)(2,1)S(1)} collective-permute-done((bf16[256,256]{1,0:T(8,128)(2,1)S(1)}, bf16[256,256]{1,0:T(8,128)(2,1)S(1)}, u32[]{:S(2)}, u32[]{:S(2)}) %collective-permute-start.17) | collective-permute-done | bytes 131104 | tf_op jit(solution)/shard_map/ppermute | solution.py:1077
  85.9 0.8 finish_late_kernel.1
  (28 shorter events, 2.9 us)
Async XLA Ops:
  0.7 7.5 %collective-permute-start = (bf16[128,512]{1,0:T(8,128)(2,1)}, bf16[128,512]{1,0:T(8,128)(2,1)S(1)}, u32[]{:S(2)}, u32[]{:S(2)}) collective-permute-start(bf16[128,512]{1,0:T(8,128)(2,1)} %bitcast.8), channel_id=1, source_target_pairs={{0,1},{1,0},{2,3},{3,2},{4,5},{5,4},{6,7},{7,6},{8,9},{9,8},{10,11... | collective-permute-start | bytes 393224 | tf_op jit(solution)/shard_map/ppermute | solution.py:948
  3.7 18.8 %collective-permute-start.1 = (bf16[128,512]{1,0:T(8,128)(2,1)}, bf16[128,512]{1,0:T(8,128)(2,1)S(1)}, u32[]{:S(2)}, u32[]{:S(2)}) collective-permute-start(bf16[128,512]{1,0:T(8,128)(2,1)} %bitcast.11), channel_id=1, source_target_pairs={{0,1},{1,0},{2,3},{3,2},{4,5},{5,4},{6,7},{7,6},{8,9},{9,8},{10,11... | collective-permute-start | bytes 393224 | tf_op jit(solution)/shard_map/ppermute | solution.py:949
  26.6 7.0 %collective-permute-start.2 = (bf16[8,256,256]{2,1,0:T(8,128)(2,1)S(1)}, bf16[8,256,256]{2,1,0:T(8,128)(2,1)S(1)}, u32[]{:S(2)}, u32[]{:S(2)}) collective-permute-start(bf16[8,256,256]{2,1,0:T(8,128)(2,1)S(1)} %get-tuple-element.192), channel_id=1, source_target_pairs={{0,2},{2,0},{4,6},{6,4},{8,10},{10,8},{12,14},{14,12},{16,18},{18,... | collective-permute-start | bytes 3145736 | tf_op jit(solution)/shard_map/ppermute | solution.py:1081
  33.0 3.0 %collective-permute-start.3 = (bf16[8,192,256]{2,1,0:T(8,128)(2,1)S(1)}, bf16[8,192,256]{2,1,0:T(8,128)(2,1)S(1)}, u32[]{:S(2)}, u32[]{:S(2)}) collective-permute-start(bf16[8,192,256]{2,1,0:T(8,128)(2,1)S(1)} %get-tuple-element.197), channel_id=1, source_target_pairs={{0,2},{2,0},{4,6},{6,4},{8,10},{10,8},{12,14},{14,12},{16,18},{18,... | collective-permute-start | bytes 2359304 | tf_op jit(solution)/shard_map/ppermute | solution.py:1081
  33.9 14.3 %collective-permute-start.4 = (bf16[4,256,256]{2,1,0:T(8,128)(2,1)S(1)}, bf16[4,256,256]{2,1,0:T(8,128)(2,1)S(1)}, u32[]{:S(2)}, u32[]{:S(2)}) collective-permute-start(bf16[4,256,256]{2,1,0:T(8,128)(2,1)S(1)} %get-tuple-element.212), channel_id=1, source_target_pairs={{0,4},{2,6},{4,0},{6,2},{8,12},{10,14},{12,8},{14,10},{16,20},{18,... | collective-permute-start | bytes 1572872 | tf_op jit(solution)/shard_map/ppermute | solution.py:1081
  36.2 11.4 %collective-permute-start.5 = (bf16[4,192,256]{2,1,0:T(8,128)(2,1)S(1)}, bf16[4,192,256]{2,1,0:T(8,128)(2,1)S(1)}, u32[]{:S(2)}, u32[]{:S(2)}) collective-permute-start(bf16[4,192,256]{2,1,0:T(8,128)(2,1)S(1)} %get-tuple-element.213), channel_id=1, source_target_pairs={{0,8},{2,10},{4,12},{6,14},{8,0},{10,2},{12,4},{14,6},{16,24},{18,... | collective-permute-start | bytes 1179656 | tf_op jit(solution)/shard_map/ppermute | solution.py:1081
  46.4 5.3 %collective-permute-start.6 = (bf16[8,176,256]{2,1,0:T(8,128)(2,1)S(1)}, bf16[8,176,256]{2,1,0:T(8,128)(2,1)S(1)}, u32[]{:S(2)}, u32[]{:S(2)}) collective-permute-start(bf16[8,176,256]{2,1,0:T(8,128)(2,1)S(1)} %get-tuple-element.220), channel_id=1, source_target_pairs={{0,2},{2,0},{4,6},{6,4},{8,10},{10,8},{12,14},{14,12},{16,18},{18,... | collective-permute-start | bytes 2162696 | tf_op jit(solution)/shard_map/ppermute | solution.py:1081
  48.4 7.9 %collective-permute-start.8 = (bf16[2,192,256]{2,1,0:T(8,128)(2,1)S(1)}, bf16[2,192,256]{2,1,0:T(8,128)(2,1)S(1)}, u32[]{:S(2)}, u32[]{:S(2)}) collective-permute-start(bf16[2,192,256]{2,1,0:T(8,128)(2,1)S(1)} %get-tuple-element.236), channel_id=1, source_target_pairs={{0,4},{2,6},{4,0},{6,2},{8,12},{10,14},{12,8},{14,10},{16,20},{18,... | collective-permute-start | bytes 589832 | tf_op jit(solution)/shard_map/ppermute | solution.py:1081
  50.2 7.1 %collective-permute-start.7 = (bf16[2,256,256]{2,1,0:T(8,128)(2,1)S(1)}, bf16[2,256,256]{2,1,0:T(8,128)(2,1)S(1)}, u32[]{:S(2)}, u32[]{:S(2)}) collective-permute-start(bf16[2,256,256]{2,1,0:T(8,128)(2,1)S(1)} %get-tuple-element.235), channel_id=1, source_target_pairs={{0,8},{2,10},{4,12},{6,14},{8,0},{10,2},{12,4},{14,6},{16,24},{18,... | collective-permute-start | bytes 786440 | tf_op jit(solution)/shard_map/ppermute | solution.py:1081
  51.9 10.5 %collective-permute-start.11 = (bf16[4,176,256]{2,1,0:T(8,128)(2,1)S(1)}, bf16[4,176,256]{2,1,0:T(8,128)(2,1)S(1)}, u32[]{:S(2)}, u32[]{:S(2)}) collective-permute-start(bf16[4,176,256]{2,1,0:T(8,128)(2,1)S(1)} %get-tuple-element.257), channel_id=1, source_target_pairs={{0,4},{2,6},{4,0},{6,2},{8,12},{10,14},{12,8},{14,10},{16,20},{18,... | collective-permute-start | bytes 1081352 | tf_op jit(solution)/shard_map/ppermute | solution.py:1081
  55.5 1.8 %collective-permute-start.9 = (bf16[4,80,256]{2,1,0:T(8,128)(2,1)S(1)}, bf16[4,80,256]{2,1,0:T(8,128)(2,1)S(1)}, u32[]{:S(2)}, u32[]{:S(2)}) collective-permute-start(bf16[4,80,256]{2,1,0:T(8,128)(2,1)S(1)} %get-tuple-element.238), channel_id=1, source_target_pairs={{0,2},{2,0},{4,6},{6,4},{8,10},{10,8},{12,14},{14,12},{16,18},{18,... | collective-permute-start | bytes 491528 | tf_op jit(solution)/shard_map/ppermute | solution.py:1081
  55.6 1.7 %collective-permute-start.10 = (bf16[4,80,256]{2,1,0:T(8,128)(2,1)S(1)}, bf16[4,80,256]{2,1,0:T(8,128)(2,1)S(1)}, u32[]{:S(2)}, u32[]{:S(2)}) collective-permute-start(bf16[4,80,256]{2,1,0:T(8,128)(2,1)S(1)} %get-tuple-element.239), channel_id=1, source_target_pairs={{0,2},{2,0},{4,6},{6,4},{8,10},{10,8},{12,14},{14,12},{16,18},{18,... | collective-permute-start | bytes 491528 | tf_op jit(solution)/shard_map/ppermute | solution.py:1081
  57.4 11.5 %collective-permute-start.12 = (bf16[4,80,256]{2,1,0:T(8,128)(2,1)S(1)}, bf16[4,80,256]{2,1,0:T(8,128)(2,1)S(1)}, u32[]{:S(2)}, u32[]{:S(2)}) collective-permute-start(bf16[4,80,256]{2,1,0:T(8,128)(2,1)S(1)} %get-tuple-element.267), channel_id=1, source_target_pairs={{0,8},{2,10},{4,12},{6,14},{8,0},{10,2},{12,4},{14,6},{16,24},{18,... | collective-permute-start | bytes 491528 | tf_op jit(solution)/shard_map/ppermute | solution.py:1081
  59.1 14.4 %collective-permute-start.15 = (bf16[1,448,256]{2,1,0:T(8,128)(2,1)S(1)}, bf16[1,448,256]{2,1,0:T(8,128)(2,1)S(1)}, u32[]{:S(2)}, u32[]{:S(2)}) collective-permute-start(bf16[1,448,256]{2,1,0:T(8,128)(2,1)S(1)} %get-tuple-element.284), channel_id=1, source_target_pairs={{0,16},{2,18},{4,20},{6,22},{8,24},{10,26},{12,28},{14,30},{16,0},... | collective-permute-start | bytes 688136 | tf_op jit(solution)/shard_map/ppermute | solution.py:1081
  62.6 10.9 %collective-permute-start.13 = (bf16[2,176,256]{2,1,0:T(8,128)(2,1)S(1)}, bf16[2,176,256]{2,1,0:T(8,128)(2,1)S(1)}, u32[]{:S(2)}, u32[]{:S(2)}) collective-permute-start(bf16[2,176,256]{2,1,0:T(8,128)(2,1)S(1)} %get-tuple-element.274), channel_id=1, source_target_pairs={{0,8},{2,10},{4,12},{6,14},{8,0},{10,2},{12,4},{14,6},{16,24},{18,... | collective-permute-start | bytes 540680 | tf_op jit(solution)/shard_map/ppermute | solution.py:1081
  68.9 4.5 %collective-permute-start.14 = (bf16[2,80,256]{2,1,0:T(8,128)(2,1)S(1)}, bf16[2,80,256]{2,1,0:T(8,128)(2,1)S(1)}, u32[]{:S(2)}, u32[]{:S(2)}) collective-permute-start(bf16[2,80,256]{2,1,0:T(8,128)(2,1)S(1)} %get-tuple-element.275), channel_id=1, source_target_pairs={{0,4},{2,6},{4,0},{6,2},{8,12},{10,14},{12,8},{14,10},{16,20},{18,... | collective-permute-start | bytes 245768 | tf_op jit(solution)/shard_map/ppermute | solution.py:1081
  73.5 7.3 %collective-permute-start.16 = (bf16[1,256,256]{2,1,0:T(8,128)(2,1)S(1)}, bf16[1,256,256]{2,1,0:T(8,128)(2,1)S(1)}, u32[]{:S(2)}, u32[]{:S(2)}) collective-permute-start(bf16[1,256,256]{2,1,0:T(8,128)(2,1)S(1)} %get-tuple-element.289), channel_id=1, source_target_pairs={{0,16},{2,18},{4,20},{6,22},{8,24},{10,26},{12,28},{14,30},{16,0},... | collective-permute-start | bytes 393224 | tf_op jit(solution)/shard_map/ppermute | solution.py:1081
  75.3 7.1 %collective-permute-start.18 = (bf16[448,256]{1,0:T(8,128)(2,1)S(1)}, bf16[448,256]{1,0:T(8,128)(2,1)S(1)}, u32[]{:S(2)}, u32[]{:S(2)}) collective-permute-start(bf16[448,256]{1,0:T(8,128)(2,1)S(1)} %fusion.refs_0_), channel_id=1, source_target_pairs={{0,1},{1,0},{2,3},{3,2},{4,5},{5,4},{6,7},{7,6},{8,9},{9,8},{10,11... | collective-permute-start | bytes 688136 | tf_op jit(solution)/shard_map/ppermute | solution.py:1077
  80.9 5.0 %collective-permute-start.17 = (bf16[256,256]{1,0:T(8,128)(2,1)S(1)}, bf16[256,256]{1,0:T(8,128)(2,1)S(1)}, u32[]{:S(2)}, u32[]{:S(2)}) collective-permute-start(bf16[256,256]{1,0:T(8,128)(2,1)S(1)} %fusion.1.refs_0_), channel_id=1, source_target_pairs={{0,1},{1,0},{2,3},{3,2},{4,5},{5,4},{6,7},{7,6},{8,9},{9,8},{10,11... | collective-permute-start | bytes 393224 | tf_op jit(solution)/shard_map/ppermute | solution.py:1077

commit v6 on v5

--- a/solution.py
+++ b/solution.py
@@ -127,7 +127,7 @@
         second[rows, :] = ((vhat * gain[1] + shift[1]) * valid).astype(BF16)
         return c
 
-    row_blocks(part, 32, glu_rows, unroll=2)
+    row_blocks(part, 32, glu_rows, unroll=4)
 
 
 def open_kernel(lengths, far, first, joined, after_glu, second):
@@ -245,19 +245,24 @@
             vhat[k, rows, :] = v[:, col(k, LANES)]
         return c
 
-    row_blocks(seq, 16, mid_rows, unroll=2)
+    row_blocks(seq, 16, mid_rows, unroll=8)
 
     def depth_lanes(k, c):
         lanes = pl.ds(pl.multiple_of(k * LANES, LANES), LANES)
         taps = depth_w[:, lanes].astype(F32)
-        third[8 : 8 + seq, :] = (vhat[k] * mid_row[0:1, lanes] + mid_row[1:2, lanes]) * mask[...]
-        total = third[4 : 4 + seq, :] * taps[0:1, :]
-        for j in range(1, 9):
-            total = total + third[4 + j : 4 + j + seq, :] * taps[j : j + 1, :]
-        depth_low[:, lanes] = total.astype(BF16)
+        mid_gains, mid_shifts = mid_row[0:1, lanes], mid_row[1:2, lanes]
+        step = 64
+        for r in range(0, seq, step):
+            block = slice(r, r + step)
+            third[8 + r : 8 + r + step, :] = (vhat[k, block, :] * mid_gains + mid_shifts) * mask[block, :]
+        for r in range(0, seq, step):
+            total = third[4 + r : 4 + r + step, :] * taps[0:1, :]
+            for j in range(1, 9):
+                total = total + third[4 + j + r : 4 + j + r + step, :] * taps[j : j + 1, :]
+            depth_low[r : r + step, lanes] = total.astype(BF16)
         return c
 
-    lax.fori_loop(0, chunks, depth_lanes, 0)
+    lax.fori_loop(0, chunks, depth_lanes, 0, unroll=2)
     after_conv[:, :half] = (
         after_glu[:, :half] + mm(depth_low[...], point_w[...]) + vector(point_bias())
     )
@@ -269,7 +274,7 @@
         fourth[rows, :] = (vhat * gain[2] + shift[2]).astype(BF16)
         return c
 
-    row_blocks(seq, 64, fourth_rows, unroll=2)
+    row_blocks(seq, 64, fourth_rows, unroll=4)
     qkv_w = qkv_w()
     for n in range(3 * width // TILE):
         packed[:, col(n)] = mm(fourth[...], qkv_w[:, col(n)]).astype(BF16)
@@ -295,7 +300,7 @@
         context[:, lanes] = both.T.astype(BF16)
         return c
 
-    lax.fori_loop(0, width // LANES, head_pair, 0)
+    lax.fori_loop(0, width // LANES, head_pair, 0, unroll=4)
     out_w = out_w()
     for n in range(width // TILE):
         after_attn[:, col(n)] = after_conv[:, col(n)] + mm(context[...], out_w[:, col(n)])
@@ -306,7 +311,7 @@
         fifth[rows, :] = (vhat * gain[3] + shift[3]).astype(BF16)
         return c
 
-    row_blocks(seq, 64, fifth_rows, unroll=2)
+    row_blocks(seq, 64, fifth_rows, unroll=4)
     ffn_in_b, ffn_in_w = vector(ffn_in_bias()), ffn_in_w()
     for n in range(ffn // TILE):
         pre = mm(fifth[...], ffn_in_w[:, col(n)]) + ffn_in_b[:, col(n)]
@@ -438,7 +443,7 @@
         d_packed[:, v_lanes] = jnp.where(low_lanes, dv[0], dv[1]).astype(BF16)
         return c
 
-    lax.fori_loop(0, width // LANES, head_pair, 0)
+    lax.fori_loop(0, width // LANES, head_pair, 0, unroll=4)
     for n in range(width // TILE):
         d_fourth[:, col(n)] = mm_nt(d_packed[...], qkv_w[col(n), :])
     gain = gains()[2:3, :].astype(F32)
@@ -497,6 +502,7 @@
     d_right,
     mid_row,
     mask,
+    left_sums,
 ):
     seq, width = d_after_conv.shape
     ffn = left_pre.shape[1]
@@ -546,7 +552,7 @@
             small[j : j + 1, lanes] = sum_tokens(totals[j])
         return c
 
-    lax.fori_loop(0, chunks, depth_lanes, 0)
+    lax.fori_loop(0, chunks, depth_lanes, 0, unroll=2)
     inverse = 1.0 / ffn
     sums[0] = jnp.broadcast_to(jnp.sum(sums[0], axis=-1, keepdims=True) * inverse, (seq, LANES))
     sums[1] = jnp.broadcast_to(jnp.sum(sums[1], axis=-1, keepdims=True) * inverse, (seq, LANES))
@@ -554,14 +560,22 @@
     def combined_lanes(k):
         return (d_third[k] - sums[0] - vhat3[k] * sums[1]) * rates[...]
 
-    def left_lanes(k, c):
-        lanes = pl.ds(pl.multiple_of(k * LANES, LANES), LANES)
-        v = jnp.where(left_pre[:, lanes] > 0.0, combined_lanes(k), 0.0).astype(BF16)
-        d_left[:, lanes] = v
-        small[11:12, lanes] = sum_tokens(v.astype(F32))
-        return c
-
-    lax.fori_loop(0, chunks, left_lanes, 0)
+    left_sums[...] = jnp.zeros(left_sums.shape, F32)
+    for r in range(0, seq, step):
+        block = slice(r, r + step)
+        first, second, rate = sums[0, block, :], sums[1, block, :], rates[block, :]
+
+        def left_lanes(k, c, block=block, first=first, second=second, rate=rate):
+            lanes = pl.ds(pl.multiple_of(k * LANES, LANES), LANES)
+            v = (d_third[k, block, :] - first - vhat3[k, block, :] * second) * rate
+            v = jnp.where(left_pre[block, lanes] > 0.0, v, 0.0).astype(BF16)
+            d_left[block, lanes] = v
+            left_sums[k] = left_sums[k] + part_sums(v.astype(F32))
+            return c
+
+        lax.fori_loop(0, chunks, left_lanes, 0, unroll=2)
+    for k in range(chunks):
+        small[11:12, col(k, LANES)] = sum_tokens(left_sums[k])
     blank = jnp.zeros((8, half), F32)
     d_right[0:8, :] = blank
     d_right[8 + seq : 16 + seq, :] = blank
@@ -670,7 +684,7 @@
         )
 
     nothing = jnp.zeros((8, width), F32)
-    sums = row_blocks(seq, 32, glu_rows, (nothing,) * 4, unroll=2)
+    sums = row_blocks(seq, 32, glu_rows, (nothing,) * 4, unroll=8)
     gain_one, shift_one, g_value, g_gate = (sum_tokens(v) for v in sums)
     for n in range(width // TILE):
         d_first[:, col(n)] = mm_nt(d_joined[...], glu_w[col(n), :])
@@ -1152,6 +1166,7 @@
             ((seq + 16, half), F32),
             ((2, ffn), F32),
             ((seq, LANES), F32),
+            ((ffn // LANES, 8, LANES), F32),
         ],
         [lengths, d_after_conv, left_pre, right_pre, vhat, rates, point_w],
         [mid_gain, mid_bias, depth_weight],

time: 87.2 us -> 82.6 us (0.947)
  Pallas kernels: 43.8 us -> 39.2 us
    pallas_call x17, Pallas kernels: 43.8 us -> 39.2 us  [call(): pl.pallas_call(body, out_shape=tuple((jax.ShapeDtypeStruct(shape, dtype)...]
  transfers between devices with their start and end apart: 19 -> 19, of which waited for: 10 -> 11; matrix products, arithmetic and copies ran while one was open for 1% -> 1% of each run, Pallas kernels for 45% -> 42%
where the time goes in v6:
time: 82.6 us; the launch traced here: 82.2 us
  Pallas kernels  39.2 us (47%)
  starting transfers between devices  24 us (29%)
  waiting for transfers between devices  16.8 us (20%)
  between operations  1.64 us (2%)
    pallas_call x17, Pallas kernels, call(): pl.pallas_call(body, out_shape=tuple((jax.ShapeDtypeStruct(shape, dtype)...  39.2 us
    ppermute x15, starting transfers between devices, start(): self.got = [lax.ppermute(v, 'dp', pairs) for v in self.send]  17.8 us
    ppermute x15, waiting for transfers between devices, start(): self.got = [lax.ppermute(v, 'dp', pairs) for v in self.send]  13.1 us
    ppermute x2, starting transfers between devices, start(): self.got = [lax.ppermute(self.keep, 'head', swap)]  3.08 us
    ppermute x1, starting transfers between devices, per_device(): other = lax.ppermute(mine, 'head', swap)  3 us
    ppermute x2, waiting for transfers between devices, start(): self.got = [lax.ppermute(self.keep, 'head', swap)]  2.51 us
  transfers between devices with their start and end apart: 19, of which 11 were waited for; matrix products, arithmetic and copies ran while one was open for 1% of the time, Pallas kernels for 42%

profile of v6, /device:TPU:0, one launch (start us, length us, event | category | flops | bytes accessed | tf_op | source)
XLA Modules:
  0.0 82.2 jit_solution(16976812580585867710)
XLA Ops:
  0.7 3.0 %collective-permute-start = (bf16[128,512]{1,0:T(8,128)(2,1)}, bf16[128,512]{1,0:T(8,128)(2,1)S(1)}, u32[]{:S(2)}, u32[]{:S(2)}) collective-permute-start(bf16[128,512]{1,0:T(8,128)(2,1)} %bitcast.8), channel_id=1, source_target_pairs={{0,1},{1,0},{2,3},{3,2},{4,5},{5,4},{6,7},{7,6},{8,9},{9,8},{10,11... | collective-permute-start | bytes 393224 | tf_op jit(solution)/shard_map/ppermute | solution.py:962
  4.4 2.6 %open_kernel.1 = (bf16[128,512]{1,0:T(8,128)(2,1)S(1)}, f32[128,1024]{1,0:T(8,128)S(1)}, f32[128,512]{1,0:T(8,128)S(1)}, bf16[128,512]{1,0:T(8,128)(2,1)S(1)}, b...) custom-call(s32[1]{0:T(128)S(6)} %copy.43.refs_0_, ...), custom_call_target="tpu_custom_call" | custom-call | flops 1000000000 | bytes 3000000 | tf_op jit(solution)/shard_map/open_kernel/pallas_call | solution.py:911
  7.0 1.2 %collective-permute-done.refs_1_ = bf16[128,512]{1,0:T(8,128)(2,1)S(1)} collective-permute-done((bf16[128,512]{1,0:T(8,128)(2,1)}, bf16[128,512]{1,0:T(8,128)(2,1)S(1)}, u32[]{:S(2)}, u32[]{:S(2)}) %collective-permute-start) | collective-permute-done | bytes 131104 | tf_op jit(solution)/shard_map/ppermute | solution.py:962
  8.2 11.0 %forward_kernel.1 = (bf16[256,512]{1,0:T(8,128)(2,1)S(1)}, bf16[256,512]{1,0:T(8,128)(2,1)S(1)}, f32[256,1024]{1,0:T(8,128)S(1)}, f32[256,512]{1,0:T(8,128)S(1)}...) custom-call(s32[1]{0:T(128)S(6)} %copy.43.refs_0_, ...), custom_call_target="tpu_custom_call" | custom-call | flops 14000000000 | bytes 42000000 | tf_op jit(solution)/shard_map/forward_kernel/pallas_call | solution.py:911
  19.2 4.1 %ffn_back_kernel.1 = (f32[256,512]{1,0:T(8,128)S(1)}, f32[8,2048]{1,0:T(8,128)S(1)}, bf16[8,256,256]{2,1,0:T(8,128)(2,1)S(1)}, bf16[8,256,256]{2,1,0:T(8,128)(2,1)S(1)}) custom-call(bf16[128,512]{1,0:T(8,128)(2,1)S(1)} %collective-permute-done.1.refs_0_, f32[256,512]{1,0:T(8,128)S(1)} %get-tuple-element.177.refs_1_.refs_0_, ...), custom_call_target="tpu_custom_call" | custom-call | flops 5000000000 | bytes 15000000 | tf_op jit(solution)/shard_map/ffn_back_kernel/pallas_call | solution.py:911
  23.5 5.9 %attention_back_kernel.1 = (f32[256,512]{1,0:T(8,128)S(1)}, f32[8,2048]{1,0:T(8,128)S(1)}, bf16[8,192,256]{2,1,0:T(8,128)(2,1)S(1)}, bf16[8,192,256]{2,1,0:T(8,128)(2,1)S(1)}) custom-call(f32[256,512]{1,0:T(8,128)S(1)} %get-tuple-element.182.refs_0_, bf16[256,1536]{1,0:T(8,128)(2,1)S(1)} %get-tuple-element.183.refs_1_, ...), custom_call_target="tpu_custom_call" | custom-call | flops 10000000000 | bytes 30000000 | tf_op jit(solution)/shard_map/attention_back_kernel/pallas_call | solution.py:911
  30.2 2.1 %collective-permute-start.4 = (bf16[4,256,256]{2,1,0:T(8,128)(2,1)S(1)}, bf16[4,256,256]{2,1,0:T(8,128)(2,1)S(1)}, u32[]{:S(2)}, u32[]{:S(2)}) collective-permute-start(bf16[4,256,256]{2,1,0:T(8,128)(2,1)S(1)} %get-tuple-element.212), channel_id=1, source_target_pairs={{0,4},{2,6},{4,0},{6,2},{8,12},{10,14},{12,8},{14,10},{16,20},{18,... | collective-permute-start | bytes 1572872 | tf_op jit(solution)/shard_map/ppermute | solution.py:1095
  32.5 1.7 %collective-permute-start.5 = (bf16[4,192,256]{2,1,0:T(8,128)(2,1)S(1)}, bf16[4,192,256]{2,1,0:T(8,128)(2,1)S(1)}, u32[]{:S(2)}, u32[]{:S(2)}) collective-permute-start(bf16[4,192,256]{2,1,0:T(8,128)(2,1)S(1)} %get-tuple-element.213), channel_id=1, source_target_pairs={{0,8},{2,10},{4,12},{6,14},{8,0},{10,2},{12,4},{14,6},{16,24},{18,... | collective-permute-start | bytes 1179656 | tf_op jit(solution)/shard_map/ppermute | solution.py:1095
  34.3 6.1 %middle_back_kernel.1 = (bf16[256,2048]{1,0:T(8,128)(2,1)S(1)}, bf16[3,256,256]{2,1,0:T(8,128)(2,1)S(1)}, f32[16,2048]{1,0:T(8,128)S(1)}) custom-call(s32[1]{0:T(128)S(6)} %copy.43.refs_0_, f32[256,512]{1,0:T(8,128)S(1)} %get-tuple-element.203.refs_1_, f32[256,2048]{1,0:T(8,128)S(1)} %get-tuple-element.204.refs_2_, ...), custom_call_target="tpu_custom_call" | custom-call | tf_op jit(solution)/shard_map/middle_back_kernel/pallas_call | solution.py:911
  40.4 2.2 %conv_back_kernel.1 = (f32[256,512]{1,0:T(8,128)S(1)}, bf16[8,176,256]{2,1,0:T(8,128)(2,1)S(1)}, bf16[8,176,256]{2,1,0:T(8,128)(2,1)S(1)}) custom-call(s32[1]{0:T(128)S(6)} %copy.43.refs_0_, bf16[256,2048]{1,0:T(8,128)(2,1)S(1)} %get-tuple-element.208.refs_1_, bf16[3,256,256]{2,1,0:T(8,128)(2,1)S(1)} %get-tuple-element.209.refs_2_, ...), custom_call_target="tpu_custom_call" | custom-call | tf_op jit(solution)/shard_map/conv_back_kernel/pallas_call | solution.py:911
  42.7 1.2 %collective-permute-done.5 = bf16[4,192,256]{2,1,0:T(8,128)(2,1)S(1)} collective-permute-done((bf16[4,192,256]{2,1,0:T(8,128)(2,1)S(1)}, bf16[4,192,256]{2,1,0:T(8,128)(2,1)S(1)}, u32[]{:S(2)}, u32[]{:S(2)}) %collective-permute-start.5) | collective-permute-done | bytes 393248 | tf_op jit(solution)/shard_map/ppermute | solution.py:1095
  44.7 1.8 %collective-permute-start.8 = (bf16[2,192,256]{2,1,0:T(8,128)(2,1)S(1)}, bf16[2,192,256]{2,1,0:T(8,128)(2,1)S(1)}, u32[]{:S(2)}, u32[]{:S(2)}) collective-permute-start(bf16[2,192,256]{2,1,0:T(8,128)(2,1)S(1)} %get-tuple-element.236), channel_id=1, source_target_pairs={{0,4},{2,6},{4,0},{6,2},{8,12},{10,14},{12,8},{14,10},{16,20},{18,... | collective-permute-start | bytes 589832 | tf_op jit(solution)/shard_map/ppermute | solution.py:1095
  46.5 1.6 %collective-permute-start.7 = (bf16[2,256,256]{2,1,0:T(8,128)(2,1)S(1)}, bf16[2,256,256]{2,1,0:T(8,128)(2,1)S(1)}, u32[]{:S(2)}, u32[]{:S(2)}) collective-permute-start(bf16[2,256,256]{2,1,0:T(8,128)(2,1)S(1)} %get-tuple-element.235), channel_id=1, source_target_pairs={{0,8},{2,10},{4,12},{6,14},{8,0},{10,2},{12,4},{14,6},{16,24},{18,... | collective-permute-start | bytes 786440 | tf_op jit(solution)/shard_map/ppermute | solution.py:1095
  48.3 0.6 collective-permute-start.11
  48.8 2.2 %glu_back_kernel.1 = (f32[256,512]{1,0:T(8,128)S(1)}, f32[256,512]{1,0:T(8,128)S(1)}, bf16[8,80,256]{2,1,0:T(8,128)(2,1)S(1)}, bf16[4,80,256]{2,1,0:T(8,128)(2,1)S(1)}, bf16[4,80,256]{2,1,0:T(8,128)(2,1)S(1)}) custom-call(f32[256,512]{1,0:T(8,128)S(1)} %get-tuple-element.226.refs_0_, f32[256,512]{1,0:T(8,128)S(1)} %get-tuple-element.203.refs_1_, ...), custom_call_target="tpu_custom_call" | custom-call | flops 7000000000 | bytes 21000000 | tf_op jit(solution)/shard_map/glu_back_kernel/pallas_call | solution.py:911
  51.7 0.9 %collective-permute-done.8.refs_3_ = bf16[2,192,256]{2,1,0:T(8,128)(2,1)S(1)} collective-permute-done((bf16[2,192,256]{2,1,0:T(8,128)(2,1)S(1)}, bf16[2,192,256]{2,1,0:T(8,128)(2,1)S(1)}, u32[]{:S(2)}, u32[]{:S(2)}) %collective-permute-start.8) | collective-permute-done | bytes 196640 | tf_op jit(solution)/shard_map/ppermute | solution.py:1095
  52.6 1.0 %collective-permute-done.7.refs_2_ = bf16[2,256,256]{2,1,0:T(8,128)(2,1)S(1)} collective-permute-done((bf16[2,256,256]{2,1,0:T(8,128)(2,1)S(1)}, bf16[2,256,256]{2,1,0:T(8,128)(2,1)S(1)}, u32[]{:S(2)}, u32[]{:S(2)}) %collective-permute-start.7) | collective-permute-done | bytes 262176 | tf_op jit(solution)/shard_map/ppermute | solution.py:1095
  53.7 1.6 %collective-permute-start.12 = (bf16[4,80,256]{2,1,0:T(8,128)(2,1)S(1)}, bf16[4,80,256]{2,1,0:T(8,128)(2,1)S(1)}, u32[]{:S(2)}, u32[]{:S(2)}) collective-permute-start(bf16[4,80,256]{2,1,0:T(8,128)(2,1)S(1)} %get-tuple-element.267), channel_id=1, source_target_pairs={{0,8},{2,10},{4,12},{6,14},{8,0},{10,2},{12,4},{14,6},{16,24},{18,... | collective-permute-start | bytes 491528 | tf_op jit(solution)/shard_map/ppermute | solution.py:1095
  55.5 2.7 %collective-permute-start.15 = (bf16[1,448,256]{2,1,0:T(8,128)(2,1)S(1)}, bf16[1,448,256]{2,1,0:T(8,128)(2,1)S(1)}, u32[]{:S(2)}, u32[]{:S(2)}) collective-permute-start(bf16[1,448,256]{2,1,0:T(8,128)(2,1)S(1)} %get-tuple-element.284), channel_id=1, source_target_pairs={{0,16},{2,18},{4,20},{6,22},{8,24},{10,26},{12,28},{14,30},{16,0},... | collective-permute-start | bytes 688136 | tf_op jit(solution)/shard_map/ppermute | solution.py:1095
  58.1 0.7 collective-permute-done.11.refs_1_
  58.9 1.6 %collective-permute-start.13 = (bf16[2,176,256]{2,1,0:T(8,128)(2,1)S(1)}, bf16[2,176,256]{2,1,0:T(8,128)(2,1)S(1)}, u32[]{:S(2)}, u32[]{:S(2)}) collective-permute-start(bf16[2,176,256]{2,1,0:T(8,128)(2,1)S(1)} %get-tuple-element.274), channel_id=1, source_target_pairs={{0,8},{2,10},{4,12},{6,14},{8,0},{10,2},{12,4},{14,6},{16,24},{18,... | collective-permute-start | bytes 540680 | tf_op jit(solution)/shard_map/ppermute | solution.py:1095
  60.4 2.4 %tokens_kernel.1 = (bf16[128,512]{1,0:T(8,128)(2,1)}, f32[128,512]{1,0:T(8,128)}) custom-call(f32[256,512]{1,0:T(8,128)S(1)} %get-tuple-element.177.refs_1_.refs_0_, bf16[256,2048]{1,0:T(8,128)(2,1)S(1)} %get-tuple-element.178.refs_3_.refs_1_, bf16[2048,512]{1,0:T(8,128)(2,1)S(1)} %get-tuple-element.179.refs_5_.refs_2_, ...), custom_call_target="tpu_custom_call" | custom-call | tf_op jit(solution)/shard_map/tokens_kernel/pallas_call | solution.py:911
  62.9 1.9 %collective-permute-done.12.refs_1_ = bf16[4,80,256]{2,1,0:T(8,128)(2,1)S(1)} collective-permute-done((bf16[4,80,256]{2,1,0:T(8,128)(2,1)S(1)}, bf16[4,80,256]{2,1,0:T(8,128)(2,1)S(1)}, u32[]{:S(2)}, u32[]{:S(2)}) %collective-permute-start.12) | collective-permute-done | bytes 163872 | tf_op jit(solution)/shard_map/ppermute | solution.py:1095
  64.8 1.3 %collective-permute-start.14 = (bf16[2,80,256]{2,1,0:T(8,128)(2,1)S(1)}, bf16[2,80,256]{2,1,0:T(8,128)(2,1)S(1)}, u32[]{:S(2)}, u32[]{:S(2)}) collective-permute-start(bf16[2,80,256]{2,1,0:T(8,128)(2,1)S(1)} %get-tuple-element.275), channel_id=1, source_target_pairs={{0,4},{2,6},{4,0},{6,2},{8,12},{10,14},{12,8},{14,10},{16,20},{18,... | collective-permute-start | bytes 245768 | tf_op jit(solution)/shard_map/ppermute | solution.py:1095
  66.0 3.2 %collective-permute-done.14.refs_3_ = bf16[2,80,256]{2,1,0:T(8,128)(2,1)S(1)} collective-permute-done((bf16[2,80,256]{2,1,0:T(8,128)(2,1)S(1)}, bf16[2,80,256]{2,1,0:T(8,128)(2,1)S(1)}, u32[]{:S(2)}, u32[]{:S(2)}) %collective-permute-start.14) | collective-permute-done | bytes 81952 | tf_op jit(solution)/shard_map/ppermute | solution.py:1095
  69.3 1.5 %collective-permute-start.16 = (bf16[1,256,256]{2,1,0:T(8,128)(2,1)S(1)}, bf16[1,256,256]{2,1,0:T(8,128)(2,1)S(1)}, u32[]{:S(2)}, u32[]{:S(2)}) collective-permute-start(bf16[1,256,256]{2,1,0:T(8,128)(2,1)S(1)} %get-tuple-element.289), channel_id=1, source_target_pairs={{0,16},{2,18},{4,20},{6,22},{8,24},{10,26},{12,28},{14,30},{16,0},... | collective-permute-start | bytes 393224 | tf_op jit(solution)/shard_map/ppermute | solution.py:1095
  70.9 1.5 %collective-permute-start.18 = (bf16[448,256]{1,0:T(8,128)(2,1)S(1)}, bf16[448,256]{1,0:T(8,128)(2,1)S(1)}, u32[]{:S(2)}, u32[]{:S(2)}) collective-permute-start(bf16[448,256]{1,0:T(8,128)(2,1)S(1)} %fusion.refs_0_), channel_id=1, source_target_pairs={{0,1},{1,0},{2,3},{3,2},{4,5},{5,4},{6,7},{7,6},{8,9},{9,8},{10,11... | collective-permute-start | bytes 688136 | tf_op jit(solution)/shard_map/ppermute | solution.py:1091
  72.5 3.6 %collective-permute-done.16 = bf16[1,256,256]{2,1,0:T(8,128)(2,1)S(1)} collective-permute-done((bf16[1,256,256]{2,1,0:T(8,128)(2,1)S(1)}, bf16[1,256,256]{2,1,0:T(8,128)(2,1)S(1)}, u32[]{:S(2)}, u32[]{:S(2)}) %collective-permute-start.16) | collective-permute-done | bytes 131104 | tf_op jit(solution)/shard_map/ppermute | solution.py:1095
  76.2 1.5 %collective-permute-start.17 = (bf16[256,256]{1,0:T(8,128)(2,1)S(1)}, bf16[256,256]{1,0:T(8,128)(2,1)S(1)}, u32[]{:S(2)}, u32[]{:S(2)}) collective-permute-start(bf16[256,256]{1,0:T(8,128)(2,1)S(1)} %fusion.1.refs_0_), channel_id=1, source_target_pairs={{0,1},{1,0},{2,3},{3,2},{4,5},{5,4},{6,7},{7,6},{8,9},{9,8},{10,11... | collective-permute-start | bytes 393224 | tf_op jit(solution)/shard_map/ppermute | solution.py:1091
  78.2 1.0 %finish_early_kernel.1 = (f32[128,512]{1,0:T(8,128)}, f32[32,2048]{1,0:T(8,128)}, f32[32,512]{1,0:T(8,128)}, f32[32,1536]{1,0:T(8,128)}, f32[128,256]{1,0:T(8,128)}) custom-call(bf16[448,256]{1,0:T(8,128)(2,1)S(1)} %fusion.refs_0_, bf16[448,256]{1,0:T(8,128)(2,1)S(1)} %collective-permute-done.18.refs_1_), custom_call_target="tpu_custom_call" | custom-call | tf_op jit(solution)/shard_map/finish_early_kernel/pallas_call | solution.py:911
  79.2 2.0 %collective-permute-done.17.refs_1_ = bf16[256,256]{1,0:T(8,128)(2,1)S(1)} collective-permute-done((bf16[256,256]{1,0:T(8,128)(2,1)S(1)}, bf16[256,256]{1,0:T(8,128)(2,1)S(1)}, u32[]{:S(2)}, u32[]{:S(2)}) %collective-permute-start.17) | collective-permute-done | bytes 131104 | tf_op jit(solution)/shard_map/ppermute | solution.py:1091
  81.2 0.8 %finish_late_kernel.1 = (f32[32,2048]{1,0:T(8,128)}, f32[3,32,256]{2,1,0:T(8,128)}, f32[32,1024]{1,0:T(8,128)}, f32[4,32]{1,0:T(4,128)}, f32[4,32]{1,0:T(4,128)}...) custom-call(bf16[256,256]{1,0:T(8,128)(2,1)S(1)} %fusion.1.refs_0_, ...), custom_call_target="tpu_custom_call" | custom-call | tf_op jit(solution)/shard_map/finish_late_kernel/pallas_call | solution.py:911
  (28 shorter events, 3.8 us)
Async XLA Ops:
  0.7 7.5 %collective-permute-start = (bf16[128,512]{1,0:T(8,128)(2,1)}, bf16[128,512]{1,0:T(8,128)(2,1)S(1)}, u32[]{:S(2)}, u32[]{:S(2)}) collective-permute-start(bf16[128,512]{1,0:T(8,128)(2,1)} %bitcast.8), channel_id=1, source_target_pairs={{0,1},{1,0},{2,3},{3,2},{4,5},{5,4},{6,7},{7,6},{8,9},{9,8},{10,11... | collective-permute-start | bytes 393224 | tf_op jit(solution)/shard_map/ppermute | solution.py:962
  3.7 15.6 %collective-permute-start.1 = (bf16[128,512]{1,0:T(8,128)(2,1)}, bf16[128,512]{1,0:T(8,128)(2,1)S(1)}, u32[]{:S(2)}, u32[]{:S(2)}) collective-permute-start(bf16[128,512]{1,0:T(8,128)(2,1)} %bitcast.11), channel_id=1, source_target_pairs={{0,1},{1,0},{2,3},{3,2},{4,5},{5,4},{6,7},{7,6},{8,9},{9,8},{10,11... | collective-permute-start | bytes 393224 | tf_op jit(solution)/shard_map/ppermute | solution.py:963
  23.4 6.6 %collective-permute-start.2 = (bf16[8,256,256]{2,1,0:T(8,128)(2,1)S(1)}, bf16[8,256,256]{2,1,0:T(8,128)(2,1)S(1)}, u32[]{:S(2)}, u32[]{:S(2)}) collective-permute-start(bf16[8,256,256]{2,1,0:T(8,128)(2,1)S(1)} %get-tuple-element.192), channel_id=1, source_target_pairs={{0,2},{2,0},{4,6},{6,4},{8,10},{10,8},{12,14},{14,12},{16,18},{18,... | collective-permute-start | bytes 3145736 | tf_op jit(solution)/shard_map/ppermute | solution.py:1095
  29.4 3.0 %collective-permute-start.3 = (bf16[8,192,256]{2,1,0:T(8,128)(2,1)S(1)}, bf16[8,192,256]{2,1,0:T(8,128)(2,1)S(1)}, u32[]{:S(2)}, u32[]{:S(2)}) collective-permute-start(bf16[8,192,256]{2,1,0:T(8,128)(2,1)S(1)} %get-tuple-element.197), channel_id=1, source_target_pairs={{0,2},{2,0},{4,6},{6,4},{8,10},{10,8},{12,14},{14,12},{16,18},{18,... | collective-permute-start | bytes 2359304 | tf_op jit(solution)/shard_map/ppermute | solution.py:1095
  30.2 14.3 %collective-permute-start.4 = (bf16[4,256,256]{2,1,0:T(8,128)(2,1)S(1)}, bf16[4,256,256]{2,1,0:T(8,128)(2,1)S(1)}, u32[]{:S(2)}, u32[]{:S(2)}) collective-permute-start(bf16[4,256,256]{2,1,0:T(8,128)(2,1)S(1)} %get-tuple-element.212), channel_id=1, source_target_pairs={{0,4},{2,6},{4,0},{6,2},{8,12},{10,14},{12,8},{14,10},{16,20},{18,... | collective-permute-start | bytes 1572872 | tf_op jit(solution)/shard_map/ppermute | solution.py:1095
  32.5 11.4 %collective-permute-start.5 = (bf16[4,192,256]{2,1,0:T(8,128)(2,1)S(1)}, bf16[4,192,256]{2,1,0:T(8,128)(2,1)S(1)}, u32[]{:S(2)}, u32[]{:S(2)}) collective-permute-start(bf16[4,192,256]{2,1,0:T(8,128)(2,1)S(1)} %get-tuple-element.213), channel_id=1, source_target_pairs={{0,8},{2,10},{4,12},{6,14},{8,0},{10,2},{12,4},{14,6},{16,24},{18,... | collective-permute-start | bytes 1179656 | tf_op jit(solution)/shard_map/ppermute | solution.py:1095
  42.6 5.5 %collective-permute-start.6 = (bf16[8,176,256]{2,1,0:T(8,128)(2,1)S(1)}, bf16[8,176,256]{2,1,0:T(8,128)(2,1)S(1)}, u32[]{:S(2)}, u32[]{:S(2)}) collective-permute-start(bf16[8,176,256]{2,1,0:T(8,128)(2,1)S(1)} %get-tuple-element.220), channel_id=1, source_target_pairs={{0,2},{2,0},{4,6},{6,4},{8,10},{10,8},{12,14},{14,12},{16,18},{18,... | collective-permute-start | bytes 2162696 | tf_op jit(solution)/shard_map/ppermute | solution.py:1095
  44.7 7.9 %collective-permute-start.8 = (bf16[2,192,256]{2,1,0:T(8,128)(2,1)S(1)}, bf16[2,192,256]{2,1,0:T(8,128)(2,1)S(1)}, u32[]{:S(2)}, u32[]{:S(2)}) collective-permute-start(bf16[2,192,256]{2,1,0:T(8,128)(2,1)S(1)} %get-tuple-element.236), channel_id=1, source_target_pairs={{0,4},{2,6},{4,0},{6,2},{8,12},{10,14},{12,8},{14,10},{16,20},{18,... | collective-permute-start | bytes 589832 | tf_op jit(solution)/shard_map/ppermute | solution.py:1095
  46.5 7.1 %collective-permute-start.7 = (bf16[2,256,256]{2,1,0:T(8,128)(2,1)S(1)}, bf16[2,256,256]{2,1,0:T(8,128)(2,1)S(1)}, u32[]{:S(2)}, u32[]{:S(2)}) collective-permute-start(bf16[2,256,256]{2,1,0:T(8,128)(2,1)S(1)} %get-tuple-element.235), channel_id=1, source_target_pairs={{0,8},{2,10},{4,12},{6,14},{8,0},{10,2},{12,4},{14,6},{16,24},{18,... | collective-permute-start | bytes 786440 | tf_op jit(solution)/shard_map/ppermute | solution.py:1095
  48.3 10.5 %collective-permute-start.11 = (bf16[4,176,256]{2,1,0:T(8,128)(2,1)S(1)}, bf16[4,176,256]{2,1,0:T(8,128)(2,1)S(1)}, u32[]{:S(2)}, u32[]{:S(2)}) collective-permute-start(bf16[4,176,256]{2,1,0:T(8,128)(2,1)S(1)} %get-tuple-element.257), channel_id=1, source_target_pairs={{0,4},{2,6},{4,0},{6,2},{8,12},{10,14},{12,8},{14,10},{16,20},{18,... | collective-permute-start | bytes 1081352 | tf_op jit(solution)/shard_map/ppermute | solution.py:1095
  51.1 2.5 %collective-permute-start.9 = (bf16[4,80,256]{2,1,0:T(8,128)(2,1)S(1)}, bf16[4,80,256]{2,1,0:T(8,128)(2,1)S(1)}, u32[]{:S(2)}, u32[]{:S(2)}) collective-permute-start(bf16[4,80,256]{2,1,0:T(8,128)(2,1)S(1)} %get-tuple-element.238), channel_id=1, source_target_pairs={{0,2},{2,0},{4,6},{6,4},{8,10},{10,8},{12,14},{14,12},{16,18},{18,... | collective-permute-start | bytes 491528 | tf_op jit(solution)/shard_map/ppermute | solution.py:1095
  51.2 2.5 %collective-permute-start.10 = (bf16[4,80,256]{2,1,0:T(8,128)(2,1)S(1)}, bf16[4,80,256]{2,1,0:T(8,128)(2,1)S(1)}, u32[]{:S(2)}, u32[]{:S(2)}) collective-permute-start(bf16[4,80,256]{2,1,0:T(8,128)(2,1)S(1)} %get-tuple-element.239), channel_id=1, source_target_pairs={{0,2},{2,0},{4,6},{6,4},{8,10},{10,8},{12,14},{14,12},{16,18},{18,... | collective-permute-start | bytes 491528 | tf_op jit(solution)/shard_map/ppermute | solution.py:1095
  53.7 11.0 %collective-permute-start.12 = (bf16[4,80,256]{2,1,0:T(8,128)(2,1)S(1)}, bf16[4,80,256]{2,1,0:T(8,128)(2,1)S(1)}, u32[]{:S(2)}, u32[]{:S(2)}) collective-permute-start(bf16[4,80,256]{2,1,0:T(8,128)(2,1)S(1)} %get-tuple-element.267), channel_id=1, source_target_pairs={{0,8},{2,10},{4,12},{6,14},{8,0},{10,2},{12,4},{14,6},{16,24},{18,... | collective-permute-start | bytes 491528 | tf_op jit(solution)/shard_map/ppermute | solution.py:1095
  55.5 13.9 %collective-permute-start.15 = (bf16[1,448,256]{2,1,0:T(8,128)(2,1)S(1)}, bf16[1,448,256]{2,1,0:T(8,128)(2,1)S(1)}, u32[]{:S(2)}, u32[]{:S(2)}) collective-permute-start(bf16[1,448,256]{2,1,0:T(8,128)(2,1)S(1)} %get-tuple-element.284), channel_id=1, source_target_pairs={{0,16},{2,18},{4,20},{6,22},{8,24},{10,26},{12,28},{14,30},{16,0},... | collective-permute-start | bytes 688136 | tf_op jit(solution)/shard_map/ppermute | solution.py:1095
  58.9 10.4 %collective-permute-start.13 = (bf16[2,176,256]{2,1,0:T(8,128)(2,1)S(1)}, bf16[2,176,256]{2,1,0:T(8,128)(2,1)S(1)}, u32[]{:S(2)}, u32[]{:S(2)}) collective-permute-start(bf16[2,176,256]{2,1,0:T(8,128)(2,1)S(1)} %get-tuple-element.274), channel_id=1, source_target_pairs={{0,8},{2,10},{4,12},{6,14},{8,0},{10,2},{12,4},{14,6},{16,24},{18,... | collective-permute-start | bytes 540680 | tf_op jit(solution)/shard_map/ppermute | solution.py:1095
  64.8 4.5 %collective-permute-start.14 = (bf16[2,80,256]{2,1,0:T(8,128)(2,1)S(1)}, bf16[2,80,256]{2,1,0:T(8,128)(2,1)S(1)}, u32[]{:S(2)}, u32[]{:S(2)}) collective-permute-start(bf16[2,80,256]{2,1,0:T(8,128)(2,1)S(1)} %get-tuple-element.275), channel_id=1, source_target_pairs={{0,4},{2,6},{4,0},{6,2},{8,12},{10,14},{12,8},{14,10},{16,20},{18,... | collective-permute-start | bytes 245768 | tf_op jit(solution)/shard_map/ppermute | solution.py:1095
  69.3 6.8 %collective-permute-start.16 = (bf16[1,256,256]{2,1,0:T(8,128)(2,1)S(1)}, bf16[1,256,256]{2,1,0:T(8,128)(2,1)S(1)}, u32[]{:S(2)}, u32[]{:S(2)}) collective-permute-start(bf16[1,256,256]{2,1,0:T(8,128)(2,1)S(1)} %get-tuple-element.289), channel_id=1, source_target_pairs={{0,16},{2,18},{4,20},{6,22},{8,24},{10,26},{12,28},{14,30},{16,0},... | collective-permute-start | bytes 393224 | tf_op jit(solution)/shard_map/ppermute | solution.py:1095
  70.9 7.3 %collective-permute-start.18 = (bf16[448,256]{1,0:T(8,128)(2,1)S(1)}, bf16[448,256]{1,0:T(8,128)(2,1)S(1)}, u32[]{:S(2)}, u32[]{:S(2)}) collective-permute-start(bf16[448,256]{1,0:T(8,128)(2,1)S(1)} %fusion.refs_0_), channel_id=1, source_target_pairs={{0,1},{1,0},{2,3},{3,2},{4,5},{5,4},{6,7},{7,6},{8,9},{9,8},{10,11... | collective-permute-start | bytes 688136 | tf_op jit(solution)/shard_map/ppermute | solution.py:1091
  76.2 5.0 %collective-permute-start.17 = (bf16[256,256]{1,0:T(8,128)(2,1)S(1)}, bf16[256,256]{1,0:T(8,128)(2,1)S(1)}, u32[]{:S(2)}, u32[]{:S(2)}) collective-permute-start(bf16[256,256]{1,0:T(8,128)(2,1)S(1)} %fusion.1.refs_0_), channel_id=1, source_target_pairs={{0,1},{1,0},{2,3},{3,2},{4,5},{5,4},{6,7},{7,6},{8,9},{9,8},{10,11... | collective-permute-start | bytes 393224 | tf_op jit(solution)/shard_map/ppermute | solution.py:1091

commit v7 on v6

--- a/solution.py
+++ b/solution.py
@@ -131,7 +131,7 @@
 
 
 def open_kernel(lengths, far, first, joined, after_glu, second):
-    mine, gains, shifts, glu_bias, glu_w, conv_w, left_w, point_w = far
+    mine, gains, shifts, glu_bias, glu_w, conv_w = far
     part = first.shape[0]
     tokens, gains, shifts = mine(), gains(), shifts()
     gain = [gains[k : k + 1, :].astype(F32) for k in range(2)]
@@ -139,8 +139,7 @@
     place = lax.axis_index("head") * part
     glu_b, glu_w = vector(glu_bias()), glu_w()
     gated(tokens, 0, place, lengths[0], gain, shift, glu_b, glu_w, first, joined, after_glu, second)
-    for get in (conv_w, left_w, point_w):
-        get()
+    conv_w()
 
 
 def forward_kernel(
@@ -153,8 +152,6 @@
     own_second,
     glu_w,
     conv_w,
-    left_w,
-    point_w,
     far,
     stream,
     first,
@@ -193,10 +190,12 @@
         glu_bias,
         conv_bias,
         left_bias,
+        left_w,
         mid_gain,
         mid_bias,
         depth_w,
         point_bias,
+        point_w,
         qkv_w,
         out_w,
         ffn_in_bias,
@@ -226,7 +225,7 @@
     sides[1, 8 : 8 + seq, :] = mm(second[...], conv_w[2])
     right_pre[...] = mm(second[...], conv_w[1]) + vector(conv_bias())
     right_pre[...] = right_pre[...] + sides[0, 7 : 7 + seq, :] + sides[1, 9 : 9 + seq, :]
-    left_b = vector(left_bias())
+    left_b, left_w = vector(left_bias()), left_w()
     for n in range(ffn // TILE):
         left_pre[:, col(n)] = mm(second[...], left_w[:, col(n)]) + left_b[:, col(n)]
     mid_row[0:1, :], mid_row[1:2, :] = vector(mid_gain()), vector(mid_bias())
@@ -264,7 +263,7 @@
 
     lax.fori_loop(0, chunks, depth_lanes, 0, unroll=2)
     after_conv[:, :half] = (
-        after_glu[:, :half] + mm(depth_low[...], point_w[...]) + vector(point_bias())
+        after_glu[:, :half] + mm(depth_low[...], point_w()[...]) + vector(point_bias())
     )
     after_conv[:, half:] = after_glu[:, half:]
 
@@ -481,34 +480,12 @@
         out[p, 4 * rows : 4 * rows + per_row // 2, 0:LANES] = g[: per_row // 2]
         out[p, 4 * rows : 4 * rows + per_row // 2, LANES : 2 * LANES] = g[per_row // 2 :]
 
-    for_slots(keep, send, ATTN_BITS, point_slot, unroll=4)
-
-
-def middle_back_kernel(
-    lengths,
-    d_after_conv,
-    left_pre,
-    right_pre,
-    vhat3,
-    rates,
-    point_w,
-    far,
-    d_left,
-    taps_right,
-    small,
-    d_depth,
-    d_third,
-    sums,
-    d_right,
-    mid_row,
-    mask,
-    left_sums,
-):
-    seq, width = d_after_conv.shape
-    ffn = left_pre.shape[1]
-    half = right_pre.shape[1]
-    length = lengths[0]
-    mid_gain, mid_bias, depth_w = far
+    for_slots(keep, send, ATTN_BITS, point_slot, unroll=8)
+
+
+def depth_back_kernel(d_after_conv, point_w, far, d_depth):
+    seq = d_after_conv.shape[0]
+    ffn, half = point_w.shape
     chunks = ffn // LANES
     edge = jnp.zeros((8, LANES), F32)
     for k in range(chunks):
@@ -520,6 +497,31 @@
         for m in range(TILE // LANES):
             d_depth[n * (TILE // LANES) + m, 8 : 8 + seq, :] = block[:, col(m, LANES)]
 
+
+def middle_back_kernel(
+    lengths,
+    d_depth,
+    left_pre,
+    right_pre,
+    vhat3,
+    rates,
+    far,
+    d_left,
+    taps_right,
+    small,
+    d_third,
+    sums,
+    d_right,
+    mid_row,
+    mask,
+    left_sums,
+):
+    seq = left_pre.shape[0]
+    ffn = left_pre.shape[1]
+    half = right_pre.shape[1]
+    length = lengths[0]
+    mid_gain, mid_bias, depth_w = far
+    chunks = ffn // LANES
     mid_row[0:1, :], mid_row[1:2, :] = vector(mid_gain()), vector(mid_bias())
     depth_w = depth_w()
     mask[...] = (lax.broadcasted_iota(jnp.int32, (seq, LANES), 0) < length).astype(F32)
@@ -969,7 +971,7 @@
     rows = width // GROUPS
     per_row = ffn // GROUPS
     ffn_rows = per_row + ffn // 2 // TILE * rows
-    own_first, own_joined, own_after_glu, own_second, mine, glu_w, conv_w, left_w, point_w = call(
+    own_first, own_joined, own_after_glu, own_second, mine, glu_w, conv_w = call(
         open_kernel,
         [
             ((part, width), BF16),
@@ -979,10 +981,10 @@
         ],
         [],
         [lengths],
-        [mine, norm_gain, norm_bias, glu_bias, glu_weight, conv_weight, left_weight, point_weight],
+        [mine, norm_gain, norm_bias, glu_bias, glu_weight, conv_weight],
         micros=1,
         scalars=1,
-        kept=(0, 4, 5, 6, 7),
+        kept=(0, 4, 5),
     )
     (
         stream,
@@ -1003,6 +1005,8 @@
         hidden,
         vhat,
         rates,
+        left_w,
+        point_w,
         qkv_w,
         out_w,
         ffn_in_w,
@@ -1045,8 +1049,6 @@
             own_second,
             glu_w,
             conv_w,
-            left_w,
-            point_w,
         ],
         [
             norm_gain,
@@ -1054,10 +1056,12 @@
             glu_bias,
             conv_bias,
             left_bias,
+            left_weight,
             mid_gain,
             mid_bias,
             depth_weight,
             point_bias,
+            point_weight,
             qkv_weight,
             out_weight,
             ffn_in_bias,
@@ -1066,7 +1070,7 @@
         ],
         micros=14,
         scalars=1,
-        kept=(9, 10, 12, 13),
+        kept=(5, 10, 11, 12, 14, 15),
     )
     d_after, small_ffn, keep_ffn, send_ffn = call(
         ffn_back_kernel,
@@ -1155,12 +1159,18 @@
     d_after_conv, ffn_grads = wave(d_after_conv, ffn_grads, whole=False)
     attn_grads = Chunk(keep_attn, send_attn, (0, *ATTN_BITS))
     attn_grads.start()
-    d_after_conv, attn_grads = wave(d_after_conv, attn_grads, whole=True)
+    (d_depth,) = call(
+        depth_back_kernel,
+        [((ffn // LANES, seq + 16, LANES), F32)],
+        [],
+        [d_after_conv, point_w],
+        [],
+    )
+    (d_after_conv, d_depth), attn_grads = wave((d_after_conv, d_depth), attn_grads, whole=True)
     d_left, taps_right, small_conv = call(
         middle_back_kernel,
         [((seq, ffn), BF16), ((3, seq, half), BF16), ((16, ffn), F32)],
         [
-            ((ffn // LANES, seq + 16, LANES), F32),
             ((ffn // LANES, seq, LANES), F32),
             ((2, seq, LANES), F32),
             ((seq + 16, half), F32),
@@ -1168,7 +1178,7 @@
             ((seq, LANES), F32),
             ((ffn // LANES, 8, LANES), F32),
         ],
-        [lengths, d_after_conv, left_pre, right_pre, vhat, rates, point_w],
+        [lengths, d_depth, left_pre, right_pre, vhat, rates],
         [mid_gain, mid_bias, depth_weight],
         micros=0,
         scalars=1,
@@ -1216,6 +1226,9 @@
     held, glu_grads = wave(held, glu_grads)
     held, early = wave(held, ffn_grads, attn_grads, joined=True)
     held, conv_grads = wave(held, conv_grads)
+    held, glu_grads = wave(held, glu_grads)
+    held, late = wave(held, conv_grads, glu_grads, joined=True)
+    held, early = wave(held, early)
     out_tokens, grad_tokens = call(
         tokens_kernel,
         [((part, width), BF16), ((part, width), F32)],
@@ -1223,10 +1236,7 @@
         [after_attn, hidden, ffn_out_w, held, d_first, stream],
         [norm_gain, ffn_out_bias],
     )
-    grad_tokens, glu_grads = wave(grad_tokens, glu_grads)
-    held, late = wave(grad_tokens, conv_grads, glu_grads, joined=True)
-    held, early = wave(held, early)
-    grad_tokens, late = wave(held, late)
+    grad_tokens, late = wave(grad_tokens, late)
     other = early.got[0]
     ffn_out, ffn_in, out, qkv, point = call(
         finish_early_kernel,

time: 82.6 us -> 82.6 us (level)
    pallas_call x17 -> x18, Pallas kernels: 39.2 us -> 38.7 us  [call(): pl.pallas_call(body, out_shape=tuple((jax.ShapeDtypeStruct(shape, dtype)...]
  transfers between devices with their start and end apart: 19 -> 19, of which waited for: 11 -> 11; matrix products, arithmetic and copies ran while one was open for 1% -> 1% of each run, Pallas kernels for 42% -> 41%
where the time goes in v7:
time: 82.6 us; the launch traced here: 82.3 us
  Pallas kernels  38.7 us (47%)
  starting transfers between devices  23.8 us (29%)
  waiting for transfers between devices  17.5 us (21%)
  between operations  1.67 us (2%)
    pallas_call x18, Pallas kernels, call(): pl.pallas_call(body, out_shape=tuple((jax.ShapeDtypeStruct(shape, dtype)...  38.7 us
    ppermute x15, starting transfers between devices, start(): self.got = [lax.ppermute(v, 'dp', pairs) for v in self.send]  17.7 us
    ppermute x15, waiting for transfers between devices, start(): self.got = [lax.ppermute(v, 'dp', pairs) for v in self.send]  13.3 us
    ppermute x2, starting transfers between devices, start(): self.got = [lax.ppermute(self.keep, 'head', swap)]  3.09 us
    ppermute x1, starting transfers between devices, per_device(): other = lax.ppermute(mine, 'head', swap)  3 us
    ppermute x2, waiting for transfers between devices, start(): self.got = [lax.ppermute(self.keep, 'head', swap)]  2.49 us
    ppermute x1, waiting for transfers between devices, per_device(): other = lax.ppermute(mine, 'head', swap)  1.72 us
  transfers between devices with their start and end apart: 19, of which 11 were waited for; matrix products, arithmetic and copies ran while one was open for 1% of the time, Pallas kernels for 41%

profile of v7, /device:TPU:0, one launch (start us, length us, event | category | flops | bytes accessed | tf_op | source)
XLA Modules:
  0.0 82.3 jit_solution(583033473213977165)
XLA Ops:
  0.7 3.0 %collective-permute-start = (bf16[128,512]{1,0:T(8,128)(2,1)}, bf16[128,512]{1,0:T(8,128)(2,1)S(1)}, u32[]{:S(2)}, u32[]{:S(2)}) collective-permute-start(bf16[128,512]{1,0:T(8,128)(2,1)} %bitcast.9), channel_id=1, source_target_pairs={{0,1},{1,0},{2,3},{3,2},{4,5},{5,4},{6,7},{7,6},{8,9},{9,8},{10,11... | collective-permute-start | bytes 393224 | tf_op jit(solution)/shard_map/ppermute | solution.py:964
  4.4 2.1 %open_kernel.1 = (bf16[128,512]{1,0:T(8,128)(2,1)S(1)}, f32[128,1024]{1,0:T(8,128)S(1)}, f32[128,512]{1,0:T(8,128)S(1)}, bf16[128,512]{1,0:T(8,128)(2,1)S(1)}, b...) custom-call(s32[1]{0:T(128)S(6)} %copy.43.refs_0_, ...), custom_call_target="tpu_custom_call" | custom-call | flops 1000000000 | bytes 3000000 | tf_op jit(solution)/shard_map/open_kernel/pallas_call | solution.py:913
  6.5 1.7 %collective-permute-done.refs_1_ = bf16[128,512]{1,0:T(8,128)(2,1)S(1)} collective-permute-done((bf16[128,512]{1,0:T(8,128)(2,1)}, bf16[128,512]{1,0:T(8,128)(2,1)S(1)}, u32[]{:S(2)}, u32[]{:S(2)}) %collective-permute-start) | collective-permute-done | bytes 131104 | tf_op jit(solution)/shard_map/ppermute | solution.py:964
  8.2 11.1 %forward_kernel.1 = (bf16[256,512]{1,0:T(8,128)(2,1)S(1)}, bf16[256,512]{1,0:T(8,128)(2,1)S(1)}, f32[256,1024]{1,0:T(8,128)S(1)}, f32[256,512]{1,0:T(8,128)S(1)}...) custom-call(s32[1]{0:T(128)S(6)} %copy.43.refs_0_, ...), custom_call_target="tpu_custom_call" | custom-call | flops 14000000000 | bytes 42000000 | tf_op jit(solution)/shard_map/forward_kernel/pallas_call | solution.py:913
  19.3 4.1 %ffn_back_kernel.1 = (f32[256,512]{1,0:T(8,128)S(1)}, f32[8,2048]{1,0:T(8,128)S(1)}, bf16[8,256,256]{2,1,0:T(8,128)(2,1)S(1)}, bf16[8,256,256]{2,1,0:T(8,128)(2,1)S(1)}) custom-call(bf16[128,512]{1,0:T(8,128)(2,1)S(1)} %collective-permute-done.1.refs_0_, f32[256,512]{1,0:T(8,128)S(1)} %get-tuple-element.177.refs_1_.refs_0_, ...), custom_call_target="tpu_custom_call" | custom-call | flops 5000000000 | bytes 15000000 | tf_op jit(solution)/shard_map/ffn_back_kernel/pallas_call | solution.py:913
  23.5 5.9 %attention_back_kernel.1 = (f32[256,512]{1,0:T(8,128)S(1)}, f32[8,2048]{1,0:T(8,128)S(1)}, bf16[8,192,256]{2,1,0:T(8,128)(2,1)S(1)}, bf16[8,192,256]{2,1,0:T(8,128)(2,1)S(1)}) custom-call(f32[256,512]{1,0:T(8,128)S(1)} %get-tuple-element.182.refs_0_, bf16[256,1536]{1,0:T(8,128)(2,1)S(1)} %get-tuple-element.183.refs_1_, ...), custom_call_target="tpu_custom_call" | custom-call | flops 10000000000 | bytes 30000000 | tf_op jit(solution)/shard_map/attention_back_kernel/pallas_call | solution.py:913
  30.3 2.2 %collective-permute-start.4 = (bf16[4,256,256]{2,1,0:T(8,128)(2,1)S(1)}, bf16[4,256,256]{2,1,0:T(8,128)(2,1)S(1)}, u32[]{:S(2)}, u32[]{:S(2)}) collective-permute-start(bf16[4,256,256]{2,1,0:T(8,128)(2,1)S(1)} %get-tuple-element.215), channel_id=1, source_target_pairs={{0,4},{2,6},{4,0},{6,2},{8,12},{10,14},{12,8},{14,10},{16,20},{18,... | collective-permute-start | bytes 1572872 | tf_op jit(solution)/shard_map/ppermute | solution.py:1099
  33.1 1.6 %collective-permute-start.5 = (bf16[4,192,256]{2,1,0:T(8,128)(2,1)S(1)}, bf16[4,192,256]{2,1,0:T(8,128)(2,1)S(1)}, u32[]{:S(2)}, u32[]{:S(2)}) collective-permute-start(bf16[4,192,256]{2,1,0:T(8,128)(2,1)S(1)} %get-tuple-element.216), channel_id=1, source_target_pairs={{0,8},{2,10},{4,12},{6,14},{8,0},{10,2},{12,4},{14,6},{16,24},{18,... | collective-permute-start | bytes 1179656 | tf_op jit(solution)/shard_map/ppermute | solution.py:1099
  34.8 5.6 %middle_back_kernel.1 = (bf16[256,2048]{1,0:T(8,128)(2,1)S(1)}, bf16[3,256,256]{2,1,0:T(8,128)(2,1)S(1)}, f32[16,2048]{1,0:T(8,128)S(1)}) custom-call(s32[1]{0:T(128)S(6)} %copy.43.refs_0_, f32[16,272,128]{2,1,0:T(8,128)S(1)} %depth_back_kernel.1.refs_1_, f32[256,2048]{1,0:T(8,128)S(1)} %get-tuple-element.206.refs_2_, ...), custom_call_target="tpu_custom_call" | custom-call | tf_op jit(solution)/shard_map/middle_back_kernel/pallas_call | solution.py:913
  40.4 2.2 %conv_back_kernel.1 = (f32[256,512]{1,0:T(8,128)S(1)}, bf16[8,176,256]{2,1,0:T(8,128)(2,1)S(1)}, bf16[8,176,256]{2,1,0:T(8,128)(2,1)S(1)}) custom-call(s32[1]{0:T(128)S(6)} %copy.43.refs_0_, bf16[256,2048]{1,0:T(8,128)(2,1)S(1)} %get-tuple-element.210.refs_1_, bf16[3,256,256]{2,1,0:T(8,128)(2,1)S(1)} %get-tuple-element.211.refs_2_, ...), custom_call_target="tpu_custom_call" | custom-call | tf_op jit(solution)/shard_map/conv_back_kernel/pallas_call | solution.py:913
  42.7 1.3 %collective-permute-done.5 = bf16[4,192,256]{2,1,0:T(8,128)(2,1)S(1)} collective-permute-done((bf16[4,192,256]{2,1,0:T(8,128)(2,1)S(1)}, bf16[4,192,256]{2,1,0:T(8,128)(2,1)S(1)}, u32[]{:S(2)}, u32[]{:S(2)}) %collective-permute-start.5) | collective-permute-done | bytes 393248 | tf_op jit(solution)/shard_map/ppermute | solution.py:1099
  44.8 1.8 %collective-permute-start.8 = (bf16[2,192,256]{2,1,0:T(8,128)(2,1)S(1)}, bf16[2,192,256]{2,1,0:T(8,128)(2,1)S(1)}, u32[]{:S(2)}, u32[]{:S(2)}) collective-permute-start(bf16[2,192,256]{2,1,0:T(8,128)(2,1)S(1)} %get-tuple-element.240), channel_id=1, source_target_pairs={{0,4},{2,6},{4,0},{6,2},{8,12},{10,14},{12,8},{14,10},{16,20},{18,... | collective-permute-start | bytes 589832 | tf_op jit(solution)/shard_map/ppermute | solution.py:1099
  46.6 1.6 %collective-permute-start.7 = (bf16[2,256,256]{2,1,0:T(8,128)(2,1)S(1)}, bf16[2,256,256]{2,1,0:T(8,128)(2,1)S(1)}, u32[]{:S(2)}, u32[]{:S(2)}) collective-permute-start(bf16[2,256,256]{2,1,0:T(8,128)(2,1)S(1)} %get-tuple-element.239), channel_id=1, source_target_pairs={{0,8},{2,10},{4,12},{6,14},{8,0},{10,2},{12,4},{14,6},{16,24},{18,... | collective-permute-start | bytes 786440 | tf_op jit(solution)/shard_map/ppermute | solution.py:1099
  48.4 0.6 collective-permute-start.11
  48.9 2.2 %glu_back_kernel.1 = (f32[256,512]{1,0:T(8,128)S(1)}, f32[256,512]{1,0:T(8,128)S(1)}, bf16[8,80,256]{2,1,0:T(8,128)(2,1)S(1)}, bf16[4,80,256]{2,1,0:T(8,128)(2,1)S(1)}, bf16[4,80,256]{2,1,0:T(8,128)(2,1)S(1)}) custom-call(f32[256,512]{1,0:T(8,128)S(1)} %get-tuple-element.229.refs_0_, f32[256,512]{1,0:T(8,128)S(1)} %get-tuple-element.230.refs_0_.refs_1_, ...), custom_call_target="tpu_custom_call" | custom-call | flops 7000000000 | bytes 21000000 | tf_op jit(solution)/shard_map/glu_back_kernel/pallas_call | solution.py:913
  51.8 0.9 %collective-permute-done.8.refs_3_ = bf16[2,192,256]{2,1,0:T(8,128)(2,1)S(1)} collective-permute-done((bf16[2,192,256]{2,1,0:T(8,128)(2,1)S(1)}, bf16[2,192,256]{2,1,0:T(8,128)(2,1)S(1)}, u32[]{:S(2)}, u32[]{:S(2)}) %collective-permute-start.8) | collective-permute-done | bytes 196640 | tf_op jit(solution)/shard_map/ppermute | solution.py:1099
  52.7 1.0 %collective-permute-done.7.refs_2_ = bf16[2,256,256]{2,1,0:T(8,128)(2,1)S(1)} collective-permute-done((bf16[2,256,256]{2,1,0:T(8,128)(2,1)S(1)}, bf16[2,256,256]{2,1,0:T(8,128)(2,1)S(1)}, u32[]{:S(2)}, u32[]{:S(2)}) %collective-permute-start.7) | collective-permute-done | bytes 262176 | tf_op jit(solution)/shard_map/ppermute | solution.py:1099
  53.8 1.6 %collective-permute-start.12 = (bf16[4,80,256]{2,1,0:T(8,128)(2,1)S(1)}, bf16[4,80,256]{2,1,0:T(8,128)(2,1)S(1)}, u32[]{:S(2)}, u32[]{:S(2)}) collective-permute-start(bf16[4,80,256]{2,1,0:T(8,128)(2,1)S(1)} %get-tuple-element.268), channel_id=1, source_target_pairs={{0,8},{2,10},{4,12},{6,14},{8,0},{10,2},{12,4},{14,6},{16,24},{18,... | collective-permute-start | bytes 491528 | tf_op jit(solution)/shard_map/ppermute | solution.py:1099
  55.6 2.7 %collective-permute-start.15 = (bf16[1,448,256]{2,1,0:T(8,128)(2,1)S(1)}, bf16[1,448,256]{2,1,0:T(8,128)(2,1)S(1)}, u32[]{:S(2)}, u32[]{:S(2)}) collective-permute-start(bf16[1,448,256]{2,1,0:T(8,128)(2,1)S(1)} %get-tuple-element.285), channel_id=1, source_target_pairs={{0,16},{2,18},{4,20},{6,22},{8,24},{10,26},{12,28},{14,30},{16,0},... | collective-permute-start | bytes 688136 | tf_op jit(solution)/shard_map/ppermute | solution.py:1099
  58.2 0.7 collective-permute-done.11.refs_1_
  59.0 1.5 %collective-permute-start.13 = (bf16[2,176,256]{2,1,0:T(8,128)(2,1)S(1)}, bf16[2,176,256]{2,1,0:T(8,128)(2,1)S(1)}, u32[]{:S(2)}, u32[]{:S(2)}) collective-permute-start(bf16[2,176,256]{2,1,0:T(8,128)(2,1)S(1)} %get-tuple-element.275), channel_id=1, source_target_pairs={{0,8},{2,10},{4,12},{6,14},{8,0},{10,2},{12,4},{14,6},{16,24},{18,... | collective-permute-start | bytes 540680 | tf_op jit(solution)/shard_map/ppermute | solution.py:1099
  60.5 4.3 %collective-permute-done.12.refs_1_ = bf16[4,80,256]{2,1,0:T(8,128)(2,1)S(1)} collective-permute-done((bf16[4,80,256]{2,1,0:T(8,128)(2,1)S(1)}, bf16[4,80,256]{2,1,0:T(8,128)(2,1)S(1)}, u32[]{:S(2)}, u32[]{:S(2)}) %collective-permute-start.12) | collective-permute-done | bytes 163872 | tf_op jit(solution)/shard_map/ppermute | solution.py:1099
  64.8 1.3 %collective-permute-start.14 = (bf16[2,80,256]{2,1,0:T(8,128)(2,1)S(1)}, bf16[2,80,256]{2,1,0:T(8,128)(2,1)S(1)}, u32[]{:S(2)}, u32[]{:S(2)}) collective-permute-start(bf16[2,80,256]{2,1,0:T(8,128)(2,1)S(1)} %get-tuple-element.276), channel_id=1, source_target_pairs={{0,4},{2,6},{4,0},{6,2},{8,12},{10,14},{12,8},{14,10},{16,20},{18,... | collective-permute-start | bytes 245768 | tf_op jit(solution)/shard_map/ppermute | solution.py:1099
  66.1 3.2 %collective-permute-done.14.refs_3_ = bf16[2,80,256]{2,1,0:T(8,128)(2,1)S(1)} collective-permute-done((bf16[2,80,256]{2,1,0:T(8,128)(2,1)S(1)}, bf16[2,80,256]{2,1,0:T(8,128)(2,1)S(1)}, u32[]{:S(2)}, u32[]{:S(2)}) %collective-permute-start.14) | collective-permute-done | bytes 81952 | tf_op jit(solution)/shard_map/ppermute | solution.py:1099
  69.4 1.5 %collective-permute-start.16 = (bf16[1,256,256]{2,1,0:T(8,128)(2,1)S(1)}, bf16[1,256,256]{2,1,0:T(8,128)(2,1)S(1)}, u32[]{:S(2)}, u32[]{:S(2)}) collective-permute-start(bf16[1,256,256]{2,1,0:T(8,128)(2,1)S(1)} %get-tuple-element.293), channel_id=1, source_target_pairs={{0,16},{2,18},{4,20},{6,22},{8,24},{10,26},{12,28},{14,30},{16,0},... | collective-permute-start | bytes 393224 | tf_op jit(solution)/shard_map/ppermute | solution.py:1099
  71.0 1.5 %collective-permute-start.18 = (bf16[448,256]{1,0:T(8,128)(2,1)S(1)}, bf16[448,256]{1,0:T(8,128)(2,1)S(1)}, u32[]{:S(2)}, u32[]{:S(2)}) collective-permute-start(bf16[448,256]{1,0:T(8,128)(2,1)S(1)} %fusion.refs_0_), channel_id=1, source_target_pairs={{0,1},{1,0},{2,3},{3,2},{4,5},{5,4},{6,7},{7,6},{8,9},{9,8},{10,11... | collective-permute-start | bytes 688136 | tf_op jit(solution)/shard_map/ppermute | solution.py:1095
  72.6 2.4 %tokens_kernel.1 = (bf16[128,512]{1,0:T(8,128)(2,1)}, f32[128,512]{1,0:T(8,128)}) custom-call(f32[256,512]{1,0:T(8,128)S(1)} %get-tuple-element.177.refs_1_.refs_0_, bf16[256,2048]{1,0:T(8,128)(2,1)S(1)} %get-tuple-element.178.refs_3_.refs_1_, bf16[2048,512]{1,0:T(8,128)(2,1)S(1)} %get-tuple-element.179.refs_5_.refs_2_, ...), custom_call_target="tpu_custom_call" | custom-call | tf_op jit(solution)/shard_map/tokens_kernel/pallas_call | solution.py:913
  75.0 1.2 %collective-permute-done.16 = bf16[1,256,256]{2,1,0:T(8,128)(2,1)S(1)} collective-permute-done((bf16[1,256,256]{2,1,0:T(8,128)(2,1)S(1)}, bf16[1,256,256]{2,1,0:T(8,128)(2,1)S(1)}, u32[]{:S(2)}, u32[]{:S(2)}) %collective-permute-start.16) | collective-permute-done | bytes 131104 | tf_op jit(solution)/shard_map/ppermute | solution.py:1099
  76.2 1.6 %collective-permute-start.17 = (bf16[256,256]{1,0:T(8,128)(2,1)S(1)}, bf16[256,256]{1,0:T(8,128)(2,1)S(1)}, u32[]{:S(2)}, u32[]{:S(2)}) collective-permute-start(bf16[256,256]{1,0:T(8,128)(2,1)S(1)} %fusion.1.refs_0_), channel_id=1, source_target_pairs={{0,1},{1,0},{2,3},{3,2},{4,5},{5,4},{6,7},{7,6},{8,9},{9,8},{10,11... | collective-permute-start | bytes 393224 | tf_op jit(solution)/shard_map/ppermute | solution.py:1095
  78.3 1.0 %finish_early_kernel.1 = (f32[128,512]{1,0:T(8,128)}, f32[32,2048]{1,0:T(8,128)}, f32[32,512]{1,0:T(8,128)}, f32[32,1536]{1,0:T(8,128)}, f32[128,256]{1,0:T(8,128)}) custom-call(bf16[448,256]{1,0:T(8,128)(2,1)S(1)} %fusion.refs_0_, bf16[448,256]{1,0:T(8,128)(2,1)S(1)} %collective-permute-done.18.refs_1_), custom_call_target="tpu_custom_call" | custom-call | tf_op jit(solution)/shard_map/finish_early_kernel/pallas_call | solution.py:913
  79.3 2.0 %collective-permute-done.17.refs_1_ = bf16[256,256]{1,0:T(8,128)(2,1)S(1)} collective-permute-done((bf16[256,256]{1,0:T(8,128)(2,1)S(1)}, bf16[256,256]{1,0:T(8,128)(2,1)S(1)}, u32[]{:S(2)}, u32[]{:S(2)}) %collective-permute-start.17) | collective-permute-done | bytes 131104 | tf_op jit(solution)/shard_map/ppermute | solution.py:1095
  81.3 0.8 %finish_late_kernel.1 = (f32[32,2048]{1,0:T(8,128)}, f32[3,32,256]{2,1,0:T(8,128)}, f32[32,1024]{1,0:T(8,128)}, f32[4,32]{1,0:T(4,128)}, f32[4,32]{1,0:T(4,128)}...) custom-call(bf16[256,256]{1,0:T(8,128)(2,1)S(1)} %fusion.1.refs_0_, ...), custom_call_target="tpu_custom_call" | custom-call | tf_op jit(solution)/shard_map/finish_late_kernel/pallas_call | solution.py:913
  (29 shorter events, 4.2 us)
Async XLA Ops:
  0.7 7.5 %collective-permute-start = (bf16[128,512]{1,0:T(8,128)(2,1)}, bf16[128,512]{1,0:T(8,128)(2,1)S(1)}, u32[]{:S(2)}, u32[]{:S(2)}) collective-permute-start(bf16[128,512]{1,0:T(8,128)(2,1)} %bitcast.9), channel_id=1, source_target_pairs={{0,1},{1,0},{2,3},{3,2},{4,5},{5,4},{6,7},{7,6},{8,9},{9,8},{10,11... | collective-permute-start | bytes 393224 | tf_op jit(solution)/shard_map/ppermute | solution.py:964
  3.7 15.7 %collective-permute-start.1 = (bf16[128,512]{1,0:T(8,128)(2,1)}, bf16[128,512]{1,0:T(8,128)(2,1)S(1)}, u32[]{:S(2)}, u32[]{:S(2)}) collective-permute-start(bf16[128,512]{1,0:T(8,128)(2,1)} %bitcast.11), channel_id=1, source_target_pairs={{0,1},{1,0},{2,3},{3,2},{4,5},{5,4},{6,7},{7,6},{8,9},{9,8},{10,11... | collective-permute-start | bytes 393224 | tf_op jit(solution)/shard_map/ppermute | solution.py:965
  23.5 6.6 %collective-permute-start.2 = (bf16[8,256,256]{2,1,0:T(8,128)(2,1)S(1)}, bf16[8,256,256]{2,1,0:T(8,128)(2,1)S(1)}, u32[]{:S(2)}, u32[]{:S(2)}) collective-permute-start(bf16[8,256,256]{2,1,0:T(8,128)(2,1)S(1)} %get-tuple-element.192), channel_id=1, source_target_pairs={{0,2},{2,0},{4,6},{6,4},{8,10},{10,8},{12,14},{14,12},{16,18},{18,... | collective-permute-start | bytes 3145736 | tf_op jit(solution)/shard_map/ppermute | solution.py:1099
  29.5 3.5 %collective-permute-start.3 = (bf16[8,192,256]{2,1,0:T(8,128)(2,1)S(1)}, bf16[8,192,256]{2,1,0:T(8,128)(2,1)S(1)}, u32[]{:S(2)}, u32[]{:S(2)}) collective-permute-start(bf16[8,192,256]{2,1,0:T(8,128)(2,1)S(1)} %get-tuple-element.198), channel_id=1, source_target_pairs={{0,2},{2,0},{4,6},{6,4},{8,10},{10,8},{12,14},{14,12},{16,18},{18,... | collective-permute-start | bytes 2359304 | tf_op jit(solution)/shard_map/ppermute | solution.py:1099
  30.3 14.3 %collective-permute-start.4 = (bf16[4,256,256]{2,1,0:T(8,128)(2,1)S(1)}, bf16[4,256,256]{2,1,0:T(8,128)(2,1)S(1)}, u32[]{:S(2)}, u32[]{:S(2)}) collective-permute-start(bf16[4,256,256]{2,1,0:T(8,128)(2,1)S(1)} %get-tuple-element.215), channel_id=1, source_target_pairs={{0,4},{2,6},{4,0},{6,2},{8,12},{10,14},{12,8},{14,10},{16,20},{18,... | collective-permute-start | bytes 1572872 | tf_op jit(solution)/shard_map/ppermute | solution.py:1099
  33.1 10.9 %collective-permute-start.5 = (bf16[4,192,256]{2,1,0:T(8,128)(2,1)S(1)}, bf16[4,192,256]{2,1,0:T(8,128)(2,1)S(1)}, u32[]{:S(2)}, u32[]{:S(2)}) collective-permute-start(bf16[4,192,256]{2,1,0:T(8,128)(2,1)S(1)} %get-tuple-element.216), channel_id=1, source_target_pairs={{0,8},{2,10},{4,12},{6,14},{8,0},{10,2},{12,4},{14,6},{16,24},{18,... | collective-permute-start | bytes 1179656 | tf_op jit(solution)/shard_map/ppermute | solution.py:1099
  42.6 5.6 %collective-permute-start.6 = (bf16[8,176,256]{2,1,0:T(8,128)(2,1)S(1)}, bf16[8,176,256]{2,1,0:T(8,128)(2,1)S(1)}, u32[]{:S(2)}, u32[]{:S(2)}) collective-permute-start(bf16[8,176,256]{2,1,0:T(8,128)(2,1)S(1)} %get-tuple-element.223), channel_id=1, source_target_pairs={{0,2},{2,0},{4,6},{6,4},{8,10},{10,8},{12,14},{14,12},{16,18},{18,... | collective-permute-start | bytes 2162696 | tf_op jit(solution)/shard_map/ppermute | solution.py:1099
  44.8 7.9 %collective-permute-start.8 = (bf16[2,192,256]{2,1,0:T(8,128)(2,1)S(1)}, bf16[2,192,256]{2,1,0:T(8,128)(2,1)S(1)}, u32[]{:S(2)}, u32[]{:S(2)}) collective-permute-start(bf16[2,192,256]{2,1,0:T(8,128)(2,1)S(1)} %get-tuple-element.240), channel_id=1, source_target_pairs={{0,4},{2,6},{4,0},{6,2},{8,12},{10,14},{12,8},{14,10},{16,20},{18,... | collective-permute-start | bytes 589832 | tf_op jit(solution)/shard_map/ppermute | solution.py:1099
  46.6 7.1 %collective-permute-start.7 = (bf16[2,256,256]{2,1,0:T(8,128)(2,1)S(1)}, bf16[2,256,256]{2,1,0:T(8,128)(2,1)S(1)}, u32[]{:S(2)}, u32[]{:S(2)}) collective-permute-start(bf16[2,256,256]{2,1,0:T(8,128)(2,1)S(1)} %get-tuple-element.239), channel_id=1, source_target_pairs={{0,8},{2,10},{4,12},{6,14},{8,0},{10,2},{12,4},{14,6},{16,24},{18,... | collective-permute-start | bytes 786440 | tf_op jit(solution)/shard_map/ppermute | solution.py:1099
  48.4 10.5 %collective-permute-start.11 = (bf16[4,176,256]{2,1,0:T(8,128)(2,1)S(1)}, bf16[4,176,256]{2,1,0:T(8,128)(2,1)S(1)}, u32[]{:S(2)}, u32[]{:S(2)}) collective-permute-start(bf16[4,176,256]{2,1,0:T(8,128)(2,1)S(1)} %get-tuple-element.261), channel_id=1, source_target_pairs={{0,4},{2,6},{4,0},{6,2},{8,12},{10,14},{12,8},{14,10},{16,20},{18,... | collective-permute-start | bytes 1081352 | tf_op jit(solution)/shard_map/ppermute | solution.py:1099
  51.2 2.5 %collective-permute-start.9 = (bf16[4,80,256]{2,1,0:T(8,128)(2,1)S(1)}, bf16[4,80,256]{2,1,0:T(8,128)(2,1)S(1)}, u32[]{:S(2)}, u32[]{:S(2)}) collective-permute-start(bf16[4,80,256]{2,1,0:T(8,128)(2,1)S(1)} %get-tuple-element.242), channel_id=1, source_target_pairs={{0,2},{2,0},{4,6},{6,4},{8,10},{10,8},{12,14},{14,12},{16,18},{18,... | collective-permute-start | bytes 491528 | tf_op jit(solution)/shard_map/ppermute | solution.py:1099
  51.3 2.5 %collective-permute-start.10 = (bf16[4,80,256]{2,1,0:T(8,128)(2,1)S(1)}, bf16[4,80,256]{2,1,0:T(8,128)(2,1)S(1)}, u32[]{:S(2)}, u32[]{:S(2)}) collective-permute-start(bf16[4,80,256]{2,1,0:T(8,128)(2,1)S(1)} %get-tuple-element.243), channel_id=1, source_target_pairs={{0,2},{2,0},{4,6},{6,4},{8,10},{10,8},{12,14},{14,12},{16,18},{18,... | collective-permute-start | bytes 491528 | tf_op jit(solution)/shard_map/ppermute | solution.py:1099
  53.8 11.0 %collective-permute-start.12 = (bf16[4,80,256]{2,1,0:T(8,128)(2,1)S(1)}, bf16[4,80,256]{2,1,0:T(8,128)(2,1)S(1)}, u32[]{:S(2)}, u32[]{:S(2)}) collective-permute-start(bf16[4,80,256]{2,1,0:T(8,128)(2,1)S(1)} %get-tuple-element.268), channel_id=1, source_target_pairs={{0,8},{2,10},{4,12},{6,14},{8,0},{10,2},{12,4},{14,6},{16,24},{18,... | collective-permute-start | bytes 491528 | tf_op jit(solution)/shard_map/ppermute | solution.py:1099
  55.6 13.9 %collective-permute-start.15 = (bf16[1,448,256]{2,1,0:T(8,128)(2,1)S(1)}, bf16[1,448,256]{2,1,0:T(8,128)(2,1)S(1)}, u32[]{:S(2)}, u32[]{:S(2)}) collective-permute-start(bf16[1,448,256]{2,1,0:T(8,128)(2,1)S(1)} %get-tuple-element.285), channel_id=1, source_target_pairs={{0,16},{2,18},{4,20},{6,22},{8,24},{10,26},{12,28},{14,30},{16,0},... | collective-permute-start | bytes 688136 | tf_op jit(solution)/shard_map/ppermute | solution.py:1099
  59.0 10.4 %collective-permute-start.13 = (bf16[2,176,256]{2,1,0:T(8,128)(2,1)S(1)}, bf16[2,176,256]{2,1,0:T(8,128)(2,1)S(1)}, u32[]{:S(2)}, u32[]{:S(2)}) collective-permute-start(bf16[2,176,256]{2,1,0:T(8,128)(2,1)S(1)} %get-tuple-element.275), channel_id=1, source_target_pairs={{0,8},{2,10},{4,12},{6,14},{8,0},{10,2},{12,4},{14,6},{16,24},{18,... | collective-permute-start | bytes 540680 | tf_op jit(solution)/shard_map/ppermute | solution.py:1099
  64.8 4.5 %collective-permute-start.14 = (bf16[2,80,256]{2,1,0:T(8,128)(2,1)S(1)}, bf16[2,80,256]{2,1,0:T(8,128)(2,1)S(1)}, u32[]{:S(2)}, u32[]{:S(2)}) collective-permute-start(bf16[2,80,256]{2,1,0:T(8,128)(2,1)S(1)} %get-tuple-element.276), channel_id=1, source_target_pairs={{0,4},{2,6},{4,0},{6,2},{8,12},{10,14},{12,8},{14,10},{16,20},{18,... | collective-permute-start | bytes 245768 | tf_op jit(solution)/shard_map/ppermute | solution.py:1099
  69.4 6.8 %collective-permute-start.16 = (bf16[1,256,256]{2,1,0:T(8,128)(2,1)S(1)}, bf16[1,256,256]{2,1,0:T(8,128)(2,1)S(1)}, u32[]{:S(2)}, u32[]{:S(2)}) collective-permute-start(bf16[1,256,256]{2,1,0:T(8,128)(2,1)S(1)} %get-tuple-element.293), channel_id=1, source_target_pairs={{0,16},{2,18},{4,20},{6,22},{8,24},{10,26},{12,28},{14,30},{16,0},... | collective-permute-start | bytes 393224 | tf_op jit(solution)/shard_map/ppermute | solution.py:1099
  71.0 7.3 %collective-permute-start.18 = (bf16[448,256]{1,0:T(8,128)(2,1)S(1)}, bf16[448,256]{1,0:T(8,128)(2,1)S(1)}, u32[]{:S(2)}, u32[]{:S(2)}) collective-permute-start(bf16[448,256]{1,0:T(8,128)(2,1)S(1)} %fusion.refs_0_), channel_id=1, source_target_pairs={{0,1},{1,0},{2,3},{3,2},{4,5},{5,4},{6,7},{7,6},{8,9},{9,8},{10,11... | collective-permute-start | bytes 688136 | tf_op jit(solution)/shard_map/ppermute | solution.py:1095
  76.2 5.0 %collective-permute-start.17 = (bf16[256,256]{1,0:T(8,128)(2,1)S(1)}, bf16[256,256]{1,0:T(8,128)(2,1)S(1)}, u32[]{:S(2)}, u32[]{:S(2)}) collective-permute-start(bf16[256,256]{1,0:T(8,128)(2,1)S(1)} %fusion.1.refs_0_), channel_id=1, source_target_pairs={{0,1},{1,0},{2,3},{3,2},{4,5},{5,4},{6,7},{7,6},{8,9},{9,8},{10,11... | collective-permute-start | bytes 393224 | tf_op jit(solution)/shard_map/ppermute | solution.py:1095

commit v8 on v6

--- a/solution.py
+++ b/solution.py
@@ -131,7 +131,7 @@
 
 
 def open_kernel(lengths, far, first, joined, after_glu, second):
-    mine, gains, shifts, glu_bias, glu_w, conv_w, left_w, point_w = far
+    mine, gains, shifts, glu_bias, glu_w, conv_w = far
     part = first.shape[0]
     tokens, gains, shifts = mine(), gains(), shifts()
     gain = [gains[k : k + 1, :].astype(F32) for k in range(2)]
@@ -139,8 +139,7 @@
     place = lax.axis_index("head") * part
     glu_b, glu_w = vector(glu_bias()), glu_w()
     gated(tokens, 0, place, lengths[0], gain, shift, glu_b, glu_w, first, joined, after_glu, second)
-    for get in (conv_w, left_w, point_w):
-        get()
+    conv_w()
 
 
 def forward_kernel(
@@ -153,8 +152,6 @@
     own_second,
     glu_w,
     conv_w,
-    left_w,
-    point_w,
     far,
     stream,
     first,
@@ -193,10 +190,12 @@
         glu_bias,
         conv_bias,
         left_bias,
+        left_w,
         mid_gain,
         mid_bias,
         depth_w,
         point_bias,
+        point_w,
         qkv_w,
         out_w,
         ffn_in_bias,
@@ -226,7 +225,7 @@
     sides[1, 8 : 8 + seq, :] = mm(second[...], conv_w[2])
     right_pre[...] = mm(second[...], conv_w[1]) + vector(conv_bias())
     right_pre[...] = right_pre[...] + sides[0, 7 : 7 + seq, :] + sides[1, 9 : 9 + seq, :]
-    left_b = vector(left_bias())
+    left_b, left_w = vector(left_bias()), left_w()
     for n in range(ffn // TILE):
         left_pre[:, col(n)] = mm(second[...], left_w[:, col(n)]) + left_b[:, col(n)]
     mid_row[0:1, :], mid_row[1:2, :] = vector(mid_gain()), vector(mid_bias())
@@ -264,7 +263,7 @@
 
     lax.fori_loop(0, chunks, depth_lanes, 0, unroll=2)
     after_conv[:, :half] = (
-        after_glu[:, :half] + mm(depth_low[...], point_w[...]) + vector(point_bias())
+        after_glu[:, :half] + mm(depth_low[...], point_w()[...]) + vector(point_bias())
     )
     after_conv[:, half:] = after_glu[:, half:]
 
@@ -481,7 +480,7 @@
         out[p, 4 * rows : 4 * rows + per_row // 2, 0:LANES] = g[: per_row // 2]
         out[p, 4 * rows : 4 * rows + per_row // 2, LANES : 2 * LANES] = g[per_row // 2 :]
 
-    for_slots(keep, send, ATTN_BITS, point_slot, unroll=4)
+    for_slots(keep, send, ATTN_BITS, point_slot, unroll=8)
 
 
 def middle_back_kernel(
@@ -969,7 +968,7 @@
     rows = width // GROUPS
     per_row = ffn // GROUPS
     ffn_rows = per_row + ffn // 2 // TILE * rows
-    own_first, own_joined, own_after_glu, own_second, mine, glu_w, conv_w, left_w, point_w = call(
+    own_first, own_joined, own_after_glu, own_second, mine, glu_w, conv_w = call(
         open_kernel,
         [
             ((part, width), BF16),
@@ -979,10 +978,10 @@
         ],
         [],
         [lengths],
-        [mine, norm_gain, norm_bias, glu_bias, glu_weight, conv_weight, left_weight, point_weight],
+        [mine, norm_gain, norm_bias, glu_bias, glu_weight, conv_weight],
         micros=1,
         scalars=1,
-        kept=(0, 4, 5, 6, 7),
+        kept=(0, 4, 5),
     )
     (
         stream,
@@ -1003,6 +1002,8 @@
         hidden,
         vhat,
         rates,
+        left_w,
+        point_w,
         qkv_w,
         out_w,
         ffn_in_w,
@@ -1045,8 +1046,6 @@
             own_second,
             glu_w,
             conv_w,
-            left_w,
-            point_w,
         ],
         [
             norm_gain,
@@ -1054,10 +1053,12 @@
             glu_bias,
             conv_bias,
             left_bias,
+            left_weight,
             mid_gain,
             mid_bias,
             depth_weight,
             point_bias,
+            point_weight,
             qkv_weight,
             out_weight,
             ffn_in_bias,
@@ -1066,7 +1067,7 @@
         ],
         micros=14,
         scalars=1,
-        kept=(9, 10, 12, 13),
+        kept=(5, 10, 11, 12, 14, 15),
     )
     d_after, small_ffn, keep_ffn, send_ffn = call(
         ffn_back_kernel,
@@ -1216,6 +1217,9 @@
     held, glu_grads = wave(held, glu_grads)
     held, early = wave(held, ffn_grads, attn_grads, joined=True)
     held, conv_grads = wave(held, conv_grads)
+    held, glu_grads = wave(held, glu_grads)
+    held, late = wave(held, conv_grads, glu_grads, joined=True)
+    held, early = wave(held, early)
     out_tokens, grad_tokens = call(
         tokens_kernel,
         [((part, width), BF16), ((part, width), F32)],
@@ -1223,10 +1227,7 @@
         [after_attn, hidden, ffn_out_w, held, d_first, stream],
         [norm_gain, ffn_out_bias],
     )
-    grad_tokens, glu_grads = wave(grad_tokens, glu_grads)
-    held, late = wave(grad_tokens, conv_grads, glu_grads, joined=True)
-    held, early = wave(held, early)
-    grad_tokens, late = wave(held, late)
+    grad_tokens, late = wave(grad_tokens, late)
     other = early.got[0]
     ffn_out, ffn_in, out, qkv, point = call(
         finish_early_kernel,

time: 82.6 us -> 82.7 us (level)
  transfers between devices with their start and end apart: 19 -> 19, of which waited for: 11 -> 11; matrix products, arithmetic and copies ran while one was open for 1% -> 1% of each run, Pallas kernels for 42% -> 41%
where the time goes in v8:
time: 82.7 us; the launch traced here: 82.3 us
  Pallas kernels  38.5 us (47%)
  starting transfers between devices  24 us (29%)
  waiting for transfers between devices  17.6 us (21%)
  between operations  1.64 us (2%)
    pallas_call x17, Pallas kernels, call(): pl.pallas_call(body, out_shape=tuple((jax.ShapeDtypeStruct(shape, dtype)...  38.5 us
    ppermute x15, starting transfers between devices, start(): self.got = [lax.ppermute(v, 'dp', pairs) for v in self.send]  17.8 us
    ppermute x15, waiting for transfers between devices, start(): self.got = [lax.ppermute(v, 'dp', pairs) for v in self.send]  13.4 us
    ppermute x2, starting transfers between devices, start(): self.got = [lax.ppermute(self.keep, 'head', swap)]  3.09 us
    ppermute x1, starting transfers between devices, per_device(): other = lax.ppermute(mine, 'head', swap)  3 us
    ppermute x2, waiting for transfers between devices, start(): self.got = [lax.ppermute(self.keep, 'head', swap)]  2.49 us
    ppermute x1, waiting for transfers between devices, per_device(): other = lax.ppermute(mine, 'head', swap)  1.72 us
  transfers between devices with their start and end apart: 19, of which 11 were waited for; matrix products, arithmetic and copies ran while one was open for 1% of the time, Pallas kernels for 41%

profile of v8, /device:TPU:0, one launch (start us, length us, event | category | flops | bytes accessed | tf_op | source)
XLA Modules:
  0.0 82.3 jit_solution(5463536769964689788)
XLA Ops:
  0.7 3.0 %collective-permute-start = (bf16[128,512]{1,0:T(8,128)(2,1)}, bf16[128,512]{1,0:T(8,128)(2,1)S(1)}, u32[]{:S(2)}, u32[]{:S(2)}) collective-permute-start(bf16[128,512]{1,0:T(8,128)(2,1)} %bitcast.9), channel_id=1, source_target_pairs={{0,1},{1,0},{2,3},{3,2},{4,5},{5,4},{6,7},{7,6},{8,9},{9,8},{10,11... | collective-permute-start | bytes 393224 | tf_op jit(solution)/shard_map/ppermute | solution.py:961
  4.4 2.1 %open_kernel.1 = (bf16[128,512]{1,0:T(8,128)(2,1)S(1)}, f32[128,1024]{1,0:T(8,128)S(1)}, f32[128,512]{1,0:T(8,128)S(1)}, bf16[128,512]{1,0:T(8,128)(2,1)S(1)}, b...) custom-call(s32[1]{0:T(128)S(6)} %copy.43.refs_0_, ...), custom_call_target="tpu_custom_call" | custom-call | flops 1000000000 | bytes 3000000 | tf_op jit(solution)/shard_map/open_kernel/pallas_call | solution.py:910
  6.5 1.7 %collective-permute-done.refs_1_ = bf16[128,512]{1,0:T(8,128)(2,1)S(1)} collective-permute-done((bf16[128,512]{1,0:T(8,128)(2,1)}, bf16[128,512]{1,0:T(8,128)(2,1)S(1)}, u32[]{:S(2)}, u32[]{:S(2)}) %collective-permute-start) | collective-permute-done | bytes 131104 | tf_op jit(solution)/shard_map/ppermute | solution.py:961
  8.2 11.1 %forward_kernel.1 = (bf16[256,512]{1,0:T(8,128)(2,1)S(1)}, bf16[256,512]{1,0:T(8,128)(2,1)S(1)}, f32[256,1024]{1,0:T(8,128)S(1)}, f32[256,512]{1,0:T(8,128)S(1)}...) custom-call(s32[1]{0:T(128)S(6)} %copy.43.refs_0_, ...), custom_call_target="tpu_custom_call" | custom-call | flops 14000000000 | bytes 42000000 | tf_op jit(solution)/shard_map/forward_kernel/pallas_call | solution.py:910
  19.3 4.1 %ffn_back_kernel.1 = (f32[256,512]{1,0:T(8,128)S(1)}, f32[8,2048]{1,0:T(8,128)S(1)}, bf16[8,256,256]{2,1,0:T(8,128)(2,1)S(1)}, bf16[8,256,256]{2,1,0:T(8,128)(2,1)S(1)}) custom-call(bf16[128,512]{1,0:T(8,128)(2,1)S(1)} %collective-permute-done.1.refs_0_, f32[256,512]{1,0:T(8,128)S(1)} %get-tuple-element.175.refs_1_.refs_0_, ...), custom_call_target="tpu_custom_call" | custom-call | flops 5000000000 | bytes 15000000 | tf_op jit(solution)/shard_map/ffn_back_kernel/pallas_call | solution.py:910
  23.5 5.9 %attention_back_kernel.1 = (f32[256,512]{1,0:T(8,128)S(1)}, f32[8,2048]{1,0:T(8,128)S(1)}, bf16[8,192,256]{2,1,0:T(8,128)(2,1)S(1)}, bf16[8,192,256]{2,1,0:T(8,128)(2,1)S(1)}) custom-call(f32[256,512]{1,0:T(8,128)S(1)} %get-tuple-element.180.refs_0_, bf16[256,1536]{1,0:T(8,128)(2,1)S(1)} %get-tuple-element.181.refs_1_, ...), custom_call_target="tpu_custom_call" | custom-call | flops 10000000000 | bytes 30000000 | tf_op jit(solution)/shard_map/attention_back_kernel/pallas_call | solution.py:910
  30.3 2.2 %collective-permute-start.4 = (bf16[4,256,256]{2,1,0:T(8,128)(2,1)S(1)}, bf16[4,256,256]{2,1,0:T(8,128)(2,1)S(1)}, u32[]{:S(2)}, u32[]{:S(2)}) collective-permute-start(bf16[4,256,256]{2,1,0:T(8,128)(2,1)S(1)} %get-tuple-element.212), channel_id=1, source_target_pairs={{0,4},{2,6},{4,0},{6,2},{8,12},{10,14},{12,8},{14,10},{16,20},{18,... | collective-permute-start | bytes 1572872 | tf_op jit(solution)/shard_map/ppermute | solution.py:1096
  32.6 1.7 %collective-permute-start.5 = (bf16[4,192,256]{2,1,0:T(8,128)(2,1)S(1)}, bf16[4,192,256]{2,1,0:T(8,128)(2,1)S(1)}, u32[]{:S(2)}, u32[]{:S(2)}) collective-permute-start(bf16[4,192,256]{2,1,0:T(8,128)(2,1)S(1)} %get-tuple-element.213), channel_id=1, source_target_pairs={{0,8},{2,10},{4,12},{6,14},{8,0},{10,2},{12,4},{14,6},{16,24},{18,... | collective-permute-start | bytes 1179656 | tf_op jit(solution)/shard_map/ppermute | solution.py:1096
  34.4 5.9 %middle_back_kernel.1 = (bf16[256,2048]{1,0:T(8,128)(2,1)S(1)}, bf16[3,256,256]{2,1,0:T(8,128)(2,1)S(1)}, f32[16,2048]{1,0:T(8,128)S(1)}) custom-call(s32[1]{0:T(128)S(6)} %copy.43.refs_0_, f32[256,512]{1,0:T(8,128)S(1)} %get-tuple-element.201.refs_1_, f32[256,2048]{1,0:T(8,128)S(1)} %get-tuple-element.202.refs_2_, ...), custom_call_target="tpu_custom_call" | custom-call | tf_op jit(solution)/shard_map/middle_back_kernel/pallas_call | solution.py:910
  40.3 2.2 %conv_back_kernel.1 = (f32[256,512]{1,0:T(8,128)S(1)}, bf16[8,176,256]{2,1,0:T(8,128)(2,1)S(1)}, bf16[8,176,256]{2,1,0:T(8,128)(2,1)S(1)}) custom-call(s32[1]{0:T(128)S(6)} %copy.43.refs_0_, bf16[256,2048]{1,0:T(8,128)(2,1)S(1)} %get-tuple-element.207.refs_1_, bf16[3,256,256]{2,1,0:T(8,128)(2,1)S(1)} %get-tuple-element.208.refs_2_, ...), custom_call_target="tpu_custom_call" | custom-call | tf_op jit(solution)/shard_map/conv_back_kernel/pallas_call | solution.py:910
  42.6 1.4 %collective-permute-done.5 = bf16[4,192,256]{2,1,0:T(8,128)(2,1)S(1)} collective-permute-done((bf16[4,192,256]{2,1,0:T(8,128)(2,1)S(1)}, bf16[4,192,256]{2,1,0:T(8,128)(2,1)S(1)}, u32[]{:S(2)}, u32[]{:S(2)}) %collective-permute-start.5) | collective-permute-done | bytes 393248 | tf_op jit(solution)/shard_map/ppermute | solution.py:1096
  44.8 1.8 %collective-permute-start.8 = (bf16[2,192,256]{2,1,0:T(8,128)(2,1)S(1)}, bf16[2,192,256]{2,1,0:T(8,128)(2,1)S(1)}, u32[]{:S(2)}, u32[]{:S(2)}) collective-permute-start(bf16[2,192,256]{2,1,0:T(8,128)(2,1)S(1)} %get-tuple-element.236), channel_id=1, source_target_pairs={{0,4},{2,6},{4,0},{6,2},{8,12},{10,14},{12,8},{14,10},{16,20},{18,... | collective-permute-start | bytes 589832 | tf_op jit(solution)/shard_map/ppermute | solution.py:1096
  46.6 1.6 %collective-permute-start.7 = (bf16[2,256,256]{2,1,0:T(8,128)(2,1)S(1)}, bf16[2,256,256]{2,1,0:T(8,128)(2,1)S(1)}, u32[]{:S(2)}, u32[]{:S(2)}) collective-permute-start(bf16[2,256,256]{2,1,0:T(8,128)(2,1)S(1)} %get-tuple-element.235), channel_id=1, source_target_pairs={{0,8},{2,10},{4,12},{6,14},{8,0},{10,2},{12,4},{14,6},{16,24},{18,... | collective-permute-start | bytes 786440 | tf_op jit(solution)/shard_map/ppermute | solution.py:1096
  48.4 0.6 collective-permute-start.11
  48.9 2.2 %glu_back_kernel.1 = (f32[256,512]{1,0:T(8,128)S(1)}, f32[256,512]{1,0:T(8,128)S(1)}, bf16[8,80,256]{2,1,0:T(8,128)(2,1)S(1)}, bf16[4,80,256]{2,1,0:T(8,128)(2,1)S(1)}, bf16[4,80,256]{2,1,0:T(8,128)(2,1)S(1)}) custom-call(f32[256,512]{1,0:T(8,128)S(1)} %get-tuple-element.226.refs_0_, f32[256,512]{1,0:T(8,128)S(1)} %get-tuple-element.201.refs_1_, ...), custom_call_target="tpu_custom_call" | custom-call | flops 7000000000 | bytes 21000000 | tf_op jit(solution)/shard_map/glu_back_kernel/pallas_call | solution.py:910
  51.8 0.9 %collective-permute-done.8.refs_3_ = bf16[2,192,256]{2,1,0:T(8,128)(2,1)S(1)} collective-permute-done((bf16[2,192,256]{2,1,0:T(8,128)(2,1)S(1)}, bf16[2,192,256]{2,1,0:T(8,128)(2,1)S(1)}, u32[]{:S(2)}, u32[]{:S(2)}) %collective-permute-start.8) | collective-permute-done | bytes 196640 | tf_op jit(solution)/shard_map/ppermute | solution.py:1096
  52.7 1.0 %collective-permute-done.7.refs_2_ = bf16[2,256,256]{2,1,0:T(8,128)(2,1)S(1)} collective-permute-done((bf16[2,256,256]{2,1,0:T(8,128)(2,1)S(1)}, bf16[2,256,256]{2,1,0:T(8,128)(2,1)S(1)}, u32[]{:S(2)}, u32[]{:S(2)}) %collective-permute-start.7) | collective-permute-done | bytes 262176 | tf_op jit(solution)/shard_map/ppermute | solution.py:1096
  53.8 1.6 %collective-permute-start.12 = (bf16[4,80,256]{2,1,0:T(8,128)(2,1)S(1)}, bf16[4,80,256]{2,1,0:T(8,128)(2,1)S(1)}, u32[]{:S(2)}, u32[]{:S(2)}) collective-permute-start(bf16[4,80,256]{2,1,0:T(8,128)(2,1)S(1)} %get-tuple-element.264), channel_id=1, source_target_pairs={{0,8},{2,10},{4,12},{6,14},{8,0},{10,2},{12,4},{14,6},{16,24},{18,... | collective-permute-start | bytes 491528 | tf_op jit(solution)/shard_map/ppermute | solution.py:1096
  55.6 2.7 %collective-permute-start.15 = (bf16[1,448,256]{2,1,0:T(8,128)(2,1)S(1)}, bf16[1,448,256]{2,1,0:T(8,128)(2,1)S(1)}, u32[]{:S(2)}, u32[]{:S(2)}) collective-permute-start(bf16[1,448,256]{2,1,0:T(8,128)(2,1)S(1)} %get-tuple-element.281), channel_id=1, source_target_pairs={{0,16},{2,18},{4,20},{6,22},{8,24},{10,26},{12,28},{14,30},{16,0},... | collective-permute-start | bytes 688136 | tf_op jit(solution)/shard_map/ppermute | solution.py:1096
  58.2 0.7 collective-permute-done.11.refs_1_
  59.0 1.5 %collective-permute-start.13 = (bf16[2,176,256]{2,1,0:T(8,128)(2,1)S(1)}, bf16[2,176,256]{2,1,0:T(8,128)(2,1)S(1)}, u32[]{:S(2)}, u32[]{:S(2)}) collective-permute-start(bf16[2,176,256]{2,1,0:T(8,128)(2,1)S(1)} %get-tuple-element.271), channel_id=1, source_target_pairs={{0,8},{2,10},{4,12},{6,14},{8,0},{10,2},{12,4},{14,6},{16,24},{18,... | collective-permute-start | bytes 540680 | tf_op jit(solution)/shard_map/ppermute | solution.py:1096
  60.5 4.3 %collective-permute-done.12.refs_1_ = bf16[4,80,256]{2,1,0:T(8,128)(2,1)S(1)} collective-permute-done((bf16[4,80,256]{2,1,0:T(8,128)(2,1)S(1)}, bf16[4,80,256]{2,1,0:T(8,128)(2,1)S(1)}, u32[]{:S(2)}, u32[]{:S(2)}) %collective-permute-start.12) | collective-permute-done | bytes 163872 | tf_op jit(solution)/shard_map/ppermute | solution.py:1096
  64.8 1.3 %collective-permute-start.14 = (bf16[2,80,256]{2,1,0:T(8,128)(2,1)S(1)}, bf16[2,80,256]{2,1,0:T(8,128)(2,1)S(1)}, u32[]{:S(2)}, u32[]{:S(2)}) collective-permute-start(bf16[2,80,256]{2,1,0:T(8,128)(2,1)S(1)} %get-tuple-element.272), channel_id=1, source_target_pairs={{0,4},{2,6},{4,0},{6,2},{8,12},{10,14},{12,8},{14,10},{16,20},{18,... | collective-permute-start | bytes 245768 | tf_op jit(solution)/shard_map/ppermute | solution.py:1096
  66.1 3.2 %collective-permute-done.14.refs_3_ = bf16[2,80,256]{2,1,0:T(8,128)(2,1)S(1)} collective-permute-done((bf16[2,80,256]{2,1,0:T(8,128)(2,1)S(1)}, bf16[2,80,256]{2,1,0:T(8,128)(2,1)S(1)}, u32[]{:S(2)}, u32[]{:S(2)}) %collective-permute-start.14) | collective-permute-done | bytes 81952 | tf_op jit(solution)/shard_map/ppermute | solution.py:1096
  69.4 1.5 %collective-permute-start.16 = (bf16[1,256,256]{2,1,0:T(8,128)(2,1)S(1)}, bf16[1,256,256]{2,1,0:T(8,128)(2,1)S(1)}, u32[]{:S(2)}, u32[]{:S(2)}) collective-permute-start(bf16[1,256,256]{2,1,0:T(8,128)(2,1)S(1)} %get-tuple-element.289), channel_id=1, source_target_pairs={{0,16},{2,18},{4,20},{6,22},{8,24},{10,26},{12,28},{14,30},{16,0},... | collective-permute-start | bytes 393224 | tf_op jit(solution)/shard_map/ppermute | solution.py:1096
  71.0 1.5 %collective-permute-start.18 = (bf16[448,256]{1,0:T(8,128)(2,1)S(1)}, bf16[448,256]{1,0:T(8,128)(2,1)S(1)}, u32[]{:S(2)}, u32[]{:S(2)}) collective-permute-start(bf16[448,256]{1,0:T(8,128)(2,1)S(1)} %fusion.refs_0_), channel_id=1, source_target_pairs={{0,1},{1,0},{2,3},{3,2},{4,5},{5,4},{6,7},{7,6},{8,9},{9,8},{10,11... | collective-permute-start | bytes 688136 | tf_op jit(solution)/shard_map/ppermute | solution.py:1092
  72.6 2.4 %tokens_kernel.1 = (bf16[128,512]{1,0:T(8,128)(2,1)}, f32[128,512]{1,0:T(8,128)}) custom-call(f32[256,512]{1,0:T(8,128)S(1)} %get-tuple-element.175.refs_1_.refs_0_, bf16[256,2048]{1,0:T(8,128)(2,1)S(1)} %get-tuple-element.176.refs_3_.refs_1_, bf16[2048,512]{1,0:T(8,128)(2,1)S(1)} %get-tuple-element.177.refs_5_.refs_2_, ...), custom_call_target="tpu_custom_call" | custom-call | tf_op jit(solution)/shard_map/tokens_kernel/pallas_call | solution.py:910
  75.0 1.2 %collective-permute-done.16 = bf16[1,256,256]{2,1,0:T(8,128)(2,1)S(1)} collective-permute-done((bf16[1,256,256]{2,1,0:T(8,128)(2,1)S(1)}, bf16[1,256,256]{2,1,0:T(8,128)(2,1)S(1)}, u32[]{:S(2)}, u32[]{:S(2)}) %collective-permute-start.16) | collective-permute-done | bytes 131104 | tf_op jit(solution)/shard_map/ppermute | solution.py:1096
  76.2 1.6 %collective-permute-start.17 = (bf16[256,256]{1,0:T(8,128)(2,1)S(1)}, bf16[256,256]{1,0:T(8,128)(2,1)S(1)}, u32[]{:S(2)}, u32[]{:S(2)}) collective-permute-start(bf16[256,256]{1,0:T(8,128)(2,1)S(1)} %fusion.1.refs_0_), channel_id=1, source_target_pairs={{0,1},{1,0},{2,3},{3,2},{4,5},{5,4},{6,7},{7,6},{8,9},{9,8},{10,11... | collective-permute-start | bytes 393224 | tf_op jit(solution)/shard_map/ppermute | solution.py:1092
  78.3 1.0 %finish_early_kernel.1 = (f32[128,512]{1,0:T(8,128)}, f32[32,2048]{1,0:T(8,128)}, f32[32,512]{1,0:T(8,128)}, f32[32,1536]{1,0:T(8,128)}, f32[128,256]{1,0:T(8,128)}) custom-call(bf16[448,256]{1,0:T(8,128)(2,1)S(1)} %fusion.refs_0_, bf16[448,256]{1,0:T(8,128)(2,1)S(1)} %collective-permute-done.18.refs_1_), custom_call_target="tpu_custom_call" | custom-call | tf_op jit(solution)/shard_map/finish_early_kernel/pallas_call | solution.py:910
  79.3 2.0 %collective-permute-done.17.refs_1_ = bf16[256,256]{1,0:T(8,128)(2,1)S(1)} collective-permute-done((bf16[256,256]{1,0:T(8,128)(2,1)S(1)}, bf16[256,256]{1,0:T(8,128)(2,1)S(1)}, u32[]{:S(2)}, u32[]{:S(2)}) %collective-permute-start.17) | collective-permute-done | bytes 131104 | tf_op jit(solution)/shard_map/ppermute | solution.py:1092
  81.3 0.8 %finish_late_kernel.1 = (f32[32,2048]{1,0:T(8,128)}, f32[3,32,256]{2,1,0:T(8,128)}, f32[32,1024]{1,0:T(8,128)}, f32[4,32]{1,0:T(4,128)}, f32[4,32]{1,0:T(4,128)}...) custom-call(bf16[256,256]{1,0:T(8,128)(2,1)S(1)} %fusion.1.refs_0_, ...), custom_call_target="tpu_custom_call" | custom-call | tf_op jit(solution)/shard_map/finish_late_kernel/pallas_call | solution.py:910
  (28 shorter events, 3.8 us)
Async XLA Ops:
  0.7 7.5 %collective-permute-start = (bf16[128,512]{1,0:T(8,128)(2,1)}, bf16[128,512]{1,0:T(8,128)(2,1)S(1)}, u32[]{:S(2)}, u32[]{:S(2)}) collective-permute-start(bf16[128,512]{1,0:T(8,128)(2,1)} %bitcast.9), channel_id=1, source_target_pairs={{0,1},{1,0},{2,3},{3,2},{4,5},{5,4},{6,7},{7,6},{8,9},{9,8},{10,11... | collective-permute-start | bytes 393224 | tf_op jit(solution)/shard_map/ppermute | solution.py:961
  3.7 15.7 %collective-permute-start.1 = (bf16[128,512]{1,0:T(8,128)(2,1)}, bf16[128,512]{1,0:T(8,128)(2,1)S(1)}, u32[]{:S(2)}, u32[]{:S(2)}) collective-permute-start(bf16[128,512]{1,0:T(8,128)(2,1)} %bitcast.11), channel_id=1, source_target_pairs={{0,1},{1,0},{2,3},{3,2},{4,5},{5,4},{6,7},{7,6},{8,9},{9,8},{10,11... | collective-permute-start | bytes 393224 | tf_op jit(solution)/shard_map/ppermute | solution.py:962
  23.5 6.6 %collective-permute-start.2 = (bf16[8,256,256]{2,1,0:T(8,128)(2,1)S(1)}, bf16[8,256,256]{2,1,0:T(8,128)(2,1)S(1)}, u32[]{:S(2)}, u32[]{:S(2)}) collective-permute-start(bf16[8,256,256]{2,1,0:T(8,128)(2,1)S(1)} %get-tuple-element.190), channel_id=1, source_target_pairs={{0,2},{2,0},{4,6},{6,4},{8,10},{10,8},{12,14},{14,12},{16,18},{18,... | collective-permute-start | bytes 3145736 | tf_op jit(solution)/shard_map/ppermute | solution.py:1096
  29.5 3.0 %collective-permute-start.3 = (bf16[8,192,256]{2,1,0:T(8,128)(2,1)S(1)}, bf16[8,192,256]{2,1,0:T(8,128)(2,1)S(1)}, u32[]{:S(2)}, u32[]{:S(2)}) collective-permute-start(bf16[8,192,256]{2,1,0:T(8,128)(2,1)S(1)} %get-tuple-element.195), channel_id=1, source_target_pairs={{0,2},{2,0},{4,6},{6,4},{8,10},{10,8},{12,14},{14,12},{16,18},{18,... | collective-permute-start | bytes 2359304 | tf_op jit(solution)/shard_map/ppermute | solution.py:1096
  30.3 14.3 %collective-permute-start.4 = (bf16[4,256,256]{2,1,0:T(8,128)(2,1)S(1)}, bf16[4,256,256]{2,1,0:T(8,128)(2,1)S(1)}, u32[]{:S(2)}, u32[]{:S(2)}) collective-permute-start(bf16[4,256,256]{2,1,0:T(8,128)(2,1)S(1)} %get-tuple-element.212), channel_id=1, source_target_pairs={{0,4},{2,6},{4,0},{6,2},{8,12},{10,14},{12,8},{14,10},{16,20},{18,... | collective-permute-start | bytes 1572872 | tf_op jit(solution)/shard_map/ppermute | solution.py:1096
  32.6 11.4 %collective-permute-start.5 = (bf16[4,192,256]{2,1,0:T(8,128)(2,1)S(1)}, bf16[4,192,256]{2,1,0:T(8,128)(2,1)S(1)}, u32[]{:S(2)}, u32[]{:S(2)}) collective-permute-start(bf16[4,192,256]{2,1,0:T(8,128)(2,1)S(1)} %get-tuple-element.213), channel_id=1, source_target_pairs={{0,8},{2,10},{4,12},{6,14},{8,0},{10,2},{12,4},{14,6},{16,24},{18,... | collective-permute-start | bytes 1179656 | tf_op jit(solution)/shard_map/ppermute | solution.py:1096
  42.5 5.7 %collective-permute-start.6 = (bf16[8,176,256]{2,1,0:T(8,128)(2,1)S(1)}, bf16[8,176,256]{2,1,0:T(8,128)(2,1)S(1)}, u32[]{:S(2)}, u32[]{:S(2)}) collective-permute-start(bf16[8,176,256]{2,1,0:T(8,128)(2,1)S(1)} %get-tuple-element.220), channel_id=1, source_target_pairs={{0,2},{2,0},{4,6},{6,4},{8,10},{10,8},{12,14},{14,12},{16,18},{18,... | collective-permute-start | bytes 2162696 | tf_op jit(solution)/shard_map/ppermute | solution.py:1096
  44.8 7.9 %collective-permute-start.8 = (bf16[2,192,256]{2,1,0:T(8,128)(2,1)S(1)}, bf16[2,192,256]{2,1,0:T(8,128)(2,1)S(1)}, u32[]{:S(2)}, u32[]{:S(2)}) collective-permute-start(bf16[2,192,256]{2,1,0:T(8,128)(2,1)S(1)} %get-tuple-element.236), channel_id=1, source_target_pairs={{0,4},{2,6},{4,0},{6,2},{8,12},{10,14},{12,8},{14,10},{16,20},{18,... | collective-permute-start | bytes 589832 | tf_op jit(solution)/shard_map/ppermute | solution.py:1096
  46.6 7.1 %collective-permute-start.7 = (bf16[2,256,256]{2,1,0:T(8,128)(2,1)S(1)}, bf16[2,256,256]{2,1,0:T(8,128)(2,1)S(1)}, u32[]{:S(2)}, u32[]{:S(2)}) collective-permute-start(bf16[2,256,256]{2,1,0:T(8,128)(2,1)S(1)} %get-tuple-element.235), channel_id=1, source_target_pairs={{0,8},{2,10},{4,12},{6,14},{8,0},{10,2},{12,4},{14,6},{16,24},{18,... | collective-permute-start | bytes 786440 | tf_op jit(solution)/shard_map/ppermute | solution.py:1096
  48.4 10.5 %collective-permute-start.11 = (bf16[4,176,256]{2,1,0:T(8,128)(2,1)S(1)}, bf16[4,176,256]{2,1,0:T(8,128)(2,1)S(1)}, u32[]{:S(2)}, u32[]{:S(2)}) collective-permute-start(bf16[4,176,256]{2,1,0:T(8,128)(2,1)S(1)} %get-tuple-element.257), channel_id=1, source_target_pairs={{0,4},{2,6},{4,0},{6,2},{8,12},{10,14},{12,8},{14,10},{16,20},{18,... | collective-permute-start | bytes 1081352 | tf_op jit(solution)/shard_map/ppermute | solution.py:1096
  51.2 2.5 %collective-permute-start.9 = (bf16[4,80,256]{2,1,0:T(8,128)(2,1)S(1)}, bf16[4,80,256]{2,1,0:T(8,128)(2,1)S(1)}, u32[]{:S(2)}, u32[]{:S(2)}) collective-permute-start(bf16[4,80,256]{2,1,0:T(8,128)(2,1)S(1)} %get-tuple-element.238), channel_id=1, source_target_pairs={{0,2},{2,0},{4,6},{6,4},{8,10},{10,8},{12,14},{14,12},{16,18},{18,... | collective-permute-start | bytes 491528 | tf_op jit(solution)/shard_map/ppermute | solution.py:1096
  51.3 2.5 %collective-permute-start.10 = (bf16[4,80,256]{2,1,0:T(8,128)(2,1)S(1)}, bf16[4,80,256]{2,1,0:T(8,128)(2,1)S(1)}, u32[]{:S(2)}, u32[]{:S(2)}) collective-permute-start(bf16[4,80,256]{2,1,0:T(8,128)(2,1)S(1)} %get-tuple-element.239), channel_id=1, source_target_pairs={{0,2},{2,0},{4,6},{6,4},{8,10},{10,8},{12,14},{14,12},{16,18},{18,... | collective-permute-start | bytes 491528 | tf_op jit(solution)/shard_map/ppermute | solution.py:1096
  53.8 11.0 %collective-permute-start.12 = (bf16[4,80,256]{2,1,0:T(8,128)(2,1)S(1)}, bf16[4,80,256]{2,1,0:T(8,128)(2,1)S(1)}, u32[]{:S(2)}, u32[]{:S(2)}) collective-permute-start(bf16[4,80,256]{2,1,0:T(8,128)(2,1)S(1)} %get-tuple-element.264), channel_id=1, source_target_pairs={{0,8},{2,10},{4,12},{6,14},{8,0},{10,2},{12,4},{14,6},{16,24},{18,... | collective-permute-start | bytes 491528 | tf_op jit(solution)/shard_map/ppermute | solution.py:1096
  55.6 13.9 %collective-permute-start.15 = (bf16[1,448,256]{2,1,0:T(8,128)(2,1)S(1)}, bf16[1,448,256]{2,1,0:T(8,128)(2,1)S(1)}, u32[]{:S(2)}, u32[]{:S(2)}) collective-permute-start(bf16[1,448,256]{2,1,0:T(8,128)(2,1)S(1)} %get-tuple-element.281), channel_id=1, source_target_pairs={{0,16},{2,18},{4,20},{6,22},{8,24},{10,26},{12,28},{14,30},{16,0},... | collective-permute-start | bytes 688136 | tf_op jit(solution)/shard_map/ppermute | solution.py:1096
  59.0 10.4 %collective-permute-start.13 = (bf16[2,176,256]{2,1,0:T(8,128)(2,1)S(1)}, bf16[2,176,256]{2,1,0:T(8,128)(2,1)S(1)}, u32[]{:S(2)}, u32[]{:S(2)}) collective-permute-start(bf16[2,176,256]{2,1,0:T(8,128)(2,1)S(1)} %get-tuple-element.271), channel_id=1, source_target_pairs={{0,8},{2,10},{4,12},{6,14},{8,0},{10,2},{12,4},{14,6},{16,24},{18,... | collective-permute-start | bytes 540680 | tf_op jit(solution)/shard_map/ppermute | solution.py:1096
  64.8 4.5 %collective-permute-start.14 = (bf16[2,80,256]{2,1,0:T(8,128)(2,1)S(1)}, bf16[2,80,256]{2,1,0:T(8,128)(2,1)S(1)}, u32[]{:S(2)}, u32[]{:S(2)}) collective-permute-start(bf16[2,80,256]{2,1,0:T(8,128)(2,1)S(1)} %get-tuple-element.272), channel_id=1, source_target_pairs={{0,4},{2,6},{4,0},{6,2},{8,12},{10,14},{12,8},{14,10},{16,20},{18,... | collective-permute-start | bytes 245768 | tf_op jit(solution)/shard_map/ppermute | solution.py:1096
  69.4 6.8 %collective-permute-start.16 = (bf16[1,256,256]{2,1,0:T(8,128)(2,1)S(1)}, bf16[1,256,256]{2,1,0:T(8,128)(2,1)S(1)}, u32[]{:S(2)}, u32[]{:S(2)}) collective-permute-start(bf16[1,256,256]{2,1,0:T(8,128)(2,1)S(1)} %get-tuple-element.289), channel_id=1, source_target_pairs={{0,16},{2,18},{4,20},{6,22},{8,24},{10,26},{12,28},{14,30},{16,0},... | collective-permute-start | bytes 393224 | tf_op jit(solution)/shard_map/ppermute | solution.py:1096
  71.0 7.3 %collective-permute-start.18 = (bf16[448,256]{1,0:T(8,128)(2,1)S(1)}, bf16[448,256]{1,0:T(8,128)(2,1)S(1)}, u32[]{:S(2)}, u32[]{:S(2)}) collective-permute-start(bf16[448,256]{1,0:T(8,128)(2,1)S(1)} %fusion.refs_0_), channel_id=1, source_target_pairs={{0,1},{1,0},{2,3},{3,2},{4,5},{5,4},{6,7},{7,6},{8,9},{9,8},{10,11... | collective-permute-start | bytes 688136 | tf_op jit(solution)/shard_map/ppermute | solution.py:1092
  76.2 5.0 %collective-permute-start.17 = (bf16[256,256]{1,0:T(8,128)(2,1)S(1)}, bf16[256,256]{1,0:T(8,128)(2,1)S(1)}, u32[]{:S(2)}, u32[]{:S(2)}) collective-permute-start(bf16[256,256]{1,0:T(8,128)(2,1)S(1)} %fusion.1.refs_0_), channel_id=1, source_target_pairs={{0,1},{1,0},{2,3},{3,2},{4,5},{5,4},{6,7},{7,6},{8,9},{9,8},{10,11... | collective-permute-start | bytes 393224 | tf_op jit(solution)/shard_map/ppermute | solution.py:1092
